TPU v7x, 32 devices: a whole 2x2x4 slice. The times are simulated.
32 devices in a mesh: dp: 4 (over y, x), context: 8 (over z, core).
Axes of the slice: x: 2, y: 2, z: 4, core: 2. Of those that a mesh axis runs over, the one named last changes fastest.
Arguments:
- projected: bfloat16 [4096, 6144], P(('dp', 'context')), may hold values from -6 to 6
- short_taps: float32 [3, 6144], replicated, may hold values from -4 to 4
- long_filter: float32 [2048, 1024], P('context'), may hold values from -1.5 to 1.5
- skip_gain: float32 [2048], P('context'), may hold values from -4 to 4
- out_proj: bfloat16 [2048, 2048], P('dp'), may hold values from -0.125 to 0.125
- cotangent: bfloat16 [4096, 2048], P(('dp', 'context')), may hold values from -25 to 25
Outputs:
- grad_inputs: bfloat16 [4096, 6144], P(('dp', 'context'))
- grad_taps: float32 [3, 6144], replicated
- grad_filter: float32 [2048, 1024], P('context', 'dp')
- grad_skip: float32 [2048], P('context')
- grad_proj: float32 [2048, 2048], P(('dp', 'context'))
All inputs are finite; a program needn't handle non-finite values.
Results may differ from a plain program's by a relative error of at most 0.012.
Values may be sent and summed in bfloat16 or wider, within the bound.
No kernel may reach another device: no remote copies, remote signals or barrier semaphores. Data moves between devices by JAX's collectives and lax.ppermute only.
A program may use at most 128 MiB of HBM per device.

v0:
```python
import math

import jax
import jax.numpy as jnp
from jax import lax
from jax.sharding import PartitionSpec as P

PRECISE = lax.Precision.HIGH


def passed_along(value, axis, steps):
    count = lax.axis_size(axis)
    initial, last = (max(0, -steps), min(count, count - steps))
    return lax.ppermute(value, axis, [(source, source + steps) for source in range(initial, last)])


def angle_table(first_count, second_count, period):
    first_idx = lax.broadcasted_iota(jnp.int32, (first_count, second_count), 0)
    second_idx = lax.broadcasted_iota(jnp.int32, (first_count, second_count), 1)
    phases = first_idx * second_idx % period
    angles = phases.astype(jnp.float32) * (-2.0 * math.pi / period)
    return (jnp.cos(angles), jnp.sin(angles))


def make_tables(seq_len):
    radix_size = min(128, seq_len)
    blocks = 2 * seq_len // radix_size
    half_blocks = blocks // 2
    outer_re, outer_im = angle_table(blocks, blocks, blocks)
    twist = angle_table(blocks, radix_size, blocks * radix_size)
    inner_re, inner_im = angle_table(radix_size, radix_size, radix_size)
    first_table = jnp.concatenate([outer_re[:, :half_blocks], outer_im[:, :half_blocks]], 0)
    inner_fwd = jnp.concatenate(
        [jnp.concatenate([inner_re, inner_im], 1), jnp.concatenate([-inner_im, inner_re], 1)], 0
    )
    inner_back = jnp.concatenate(
        [jnp.concatenate([inner_re, -inner_im], 1), jnp.concatenate([inner_im, inner_re], 1)], 0
    )
    last_table = jnp.concatenate([outer_re[:half_blocks, :], outer_im[:half_blocks, :]], 1)
    return (first_table, twist, inner_fwd, inner_back, last_table)


def forward_spectrum(signal, tables):
    first_table, (twist_re, twist_im), inner_fwd, inner_back, last_table = tables
    blocks = twist_re.shape[0]
    radix_size = twist_re.shape[1]
    shaped = signal.reshape(signal.shape[0], blocks // 2, radix_size)
    first = jnp.einsum("kn,cnm->ckm", first_table, shaped, precision=PRECISE)
    first_re = first[:, :blocks]
    first_im = first[:, blocks:]
    turned = jnp.concatenate(
        [first_re * twist_re - first_im * twist_im, first_re * twist_im + first_im * twist_re], 2
    )
    return jnp.einsum("ckn,nm->ckm", turned, inner_fwd, precision=PRECISE)


def spectral_product(left, right, conjugate_left):
    width = left.shape[2] // 2
    left_re, left_im = (left[:, :, :width], left[:, :, width:])
    right_re, right_im = (right[:, :, :width], right[:, :, width:])
    if conjugate_left:
        return jnp.concatenate(
            [left_re * right_re + left_im * right_im, left_re * right_im - left_im * right_re], 2
        )
    return jnp.concatenate(
        [left_re * right_re - left_im * right_im, left_re * right_im + left_im * right_re], 2
    )


def inverse_real(spectrum, tables):
    first_table, (twist_re, twist_im), inner_fwd, inner_back, last_table = tables
    blocks = twist_re.shape[0]
    radix_size = twist_re.shape[1]
    undo = jnp.einsum("ckn,nm->ckm", spectrum, inner_back, precision=PRECISE)
    undo_re = undo[:, :, :radix_size]
    undo_im = undo[:, :, radix_size:]
    back = jnp.concatenate(
        [undo_re * twist_re + undo_im * twist_im, undo_im * twist_re - undo_re * twist_im], 1
    )
    result = jnp.einsum("nk,ckm->cnm", last_table, back, precision=PRECISE)
    return result.reshape(spectrum.shape[0], blocks // 2 * radix_size) / (blocks * radix_size)


def body(projected, short_taps, long_filter, skip_gain, out_proj, cotangent):
    tok_rows = projected.shape[0]
    chan_all = projected.shape[1] // 3
    prev_rows = passed_along(projected[tok_rows - 2 :], "context", 1)
    extended = jnp.concatenate([prev_rows, projected], 0).astype(jnp.float32)
    current = extended[2:]
    once_back = extended[1 : tok_rows + 1]
    twice_back = extended[:tok_rows]
    mixed = short_taps[0] * current + short_taps[1] * once_back + short_taps[2] * twice_back
    query = mixed[:, :chan_all].astype(jnp.bfloat16)
    keyed = mixed[:, chan_all : 2 * chan_all].astype(jnp.bfloat16)
    valued = mixed[:, 2 * chan_all :].astype(jnp.bfloat16)
    product = (keyed.astype(jnp.float32) * valued.astype(jnp.float32)).astype(jnp.bfloat16)
    product_chan = lax.all_to_all(product.T, "context", split_axis=0, concat_axis=1, tiled=True)
    seq_len = product_chan.shape[1]
    tables = make_tables(seq_len)
    prod_f = product_chan.astype(jnp.float32)
    filter_spec = forward_spectrum(long_filter, tables)
    prod_spec = forward_spectrum(prod_f, tables)
    long_chan = (
        inverse_real(spectral_product(filter_spec, prod_spec, False), tables)
        + skip_gain[:, None] * prod_f
    )
    long_tok = lax.all_to_all(
        long_chan.astype(jnp.bfloat16), "context", split_axis=1, concat_axis=0, tiled=True
    ).T
    gate = (query.astype(jnp.float32) * long_tok.astype(jnp.float32)).astype(jnp.bfloat16)
    grad_gate = lax.dot_general(
        cotangent,
        lax.all_gather(out_proj, "dp", axis=0, tiled=True),
        (((1,), (1,)), ((), ())),
        preferred_element_type=jnp.float32,
    ).astype(jnp.bfloat16)
    grad_rows = lax.psum_scatter(
        lax.dot_general(
            gate, cotangent, (((0,), (0,)), ((), ())), preferred_element_type=jnp.float32
        ),
        ("dp", "context"),
        scatter_dimension=0,
        tiled=True,
    )
    grad_query = grad_gate.astype(jnp.float32) * long_tok.astype(jnp.float32)
    grad_long = (grad_gate.astype(jnp.float32) * query.astype(jnp.float32)).astype(jnp.bfloat16)
    grad_chan = lax.all_to_all(
        grad_long.T, "context", split_axis=0, concat_axis=1, tiled=True
    ).astype(jnp.float32)
    grad_spec = forward_spectrum(grad_chan, tables)
    back_chan = (
        inverse_real(spectral_product(filter_spec, grad_spec, True), tables)
        + skip_gain[:, None] * grad_chan
    )
    filter_local = inverse_real(spectral_product(prod_spec, grad_spec, True), tables)
    grad_product = lax.all_to_all(
        back_chan.astype(jnp.bfloat16), "context", split_axis=1, concat_axis=0, tiled=True
    ).T
    scale_factor = 1.0 / math.sqrt(seq_len * lax.axis_size("dp"))
    grad_filter = (
        lax.psum_scatter(filter_local, "dp", scatter_dimension=1, tiled=True) * scale_factor
    )
    grad_skip = lax.psum(jnp.sum(grad_chan * prod_f, axis=1), "dp") * scale_factor
    grad_key = grad_product.astype(jnp.float32) * valued.astype(jnp.float32)
    grad_value = grad_product.astype(jnp.float32) * keyed.astype(jnp.float32)
    grad_mixed = jnp.concatenate([grad_query, grad_key, grad_value], 1)
    next_rows = passed_along(grad_mixed[:2].astype(jnp.bfloat16), "context", -1).astype(jnp.float32)
    grad_ext = jnp.concatenate([grad_mixed, next_rows], 0)
    grad_inputs = (
        short_taps[0] * grad_ext[:tok_rows]
        + short_taps[1] * grad_ext[1 : tok_rows + 1]
        + short_taps[2] * grad_ext[2:]
    ).astype(jnp.bfloat16)
    taps_terms = jnp.stack(
        [
            jnp.sum(grad_mixed * current, 0),
            jnp.sum(grad_mixed * once_back, 0),
            jnp.sum(grad_mixed * twice_back, 0),
        ]
    )
    grad_taps = lax.psum(taps_terms, ("dp", "context")) * scale_factor
    return (grad_inputs, grad_taps, grad_filter, grad_skip, grad_rows * scale_factor)


def solution(mesh):
    placed = (
        P(("dp", "context"), None),
        P(),
        P("context", None),
        P("context"),
        P("dp", None),
        P(("dp", "context"), None),
    )
    return jax.shard_map(
        body,
        mesh=mesh,
        in_specs=placed,
        out_specs=(
            P(("dp", "context"), None),
            P(),
            P("context", "dp"),
            P("context"),
            P(("dp", "context"), None),
        ),
        check_vma=False,
    )
```

profile of v0, /device:TPU:0, one launch (start us, length us, event | category | flops | bytes accessed | tf_op | source)
XLA Modules:
  0.0 625.7 jit_solution(3541810269681701199)
XLA Ops:
  7.2 0.7 all-gather.2.cloned.1.call-update
  7.9 0.9 slice.124
  8.8 2.4 collective-permute-start
  11.2 1.1 fusion.109
  12.9 1.7 copy-done.1
  14.6 1.0 add_convert_fusion
  15.6 84.6 %all-gather.2.cloned.1.call-done = bf16[2048,2048]{1,0:T(8,128)(2,1)} async-done(((bf16[512,2048]{1,0:T(8,128)(2,1)}), bf16[2048,2048]{1,0:T(8,128)(2,1)}) %all-gather.2.cloned.1.call-update) | async-done | bytes 8388624 | tf_op jit(solution)/shard_map/all_gather | solution.py:113
  100.2 6.3 fusion.21
  106.5 1.0 copy-done.11
  107.6 1.0 copy.71
  108.6 4.6 all-to-all-start.2
  113.4 1.4 copy.77
  115.5 3.7 convolution_bitcast_fusion.2
  119.2 9.4 %all-to-all-done.2 = bf16[8,256,128]{2,1,0:T(8,128)(2,1)S(1)} async-done(((bf16[8,256,128]{2,1,0:T(8,128)(2,1)}), bf16[8,256,128]{2,1,0:T(8,128)(2,1)S(1)}, u32[]{:S(2)}, u32[]{:S(2)}) %all-to-all-start.2) | async-done | bytes 524320 | tf_op jit(solution)/shard_map/all_to_all | solution.py:127
  128.6 1.4 convolution_bitcast_fusion
  130.0 1.0 copy-done.7
  131.0 0.9 multiply_subtract_fusion.8
  131.8 0.7 pad_maximum_fusion
  132.6 4.2 fusion.16
  136.8 4.2 fusion.12
  141.0 0.9 multiply_add_fusion.3
  142.0 1.0 copy-done.5
  143.0 2.8 pad_maximum_fusion.4
  145.8 5.5 copy.61
  151.3 4.0 fusion.68
  156.0 3.2 fusion.46
  159.3 17.8 %all_to_all.52 = bf16[256,8,128]{2,0,1:T(8,128)(2,1)S(1)} all-to-all(bf16[256,8,128]{2,0,1:T(8,128)(2,1)S(1)} %copy.52), channel_id=1, replica_groups=mesh['dp'=4,'context'=8] {'context'}, dimensions={1} | all-to-all | bytes 1048576 | tf_op jit(solution)/shard_map/all_to_all | solution.py:136
  177.1 1.3 copy.74
  178.4 2.8 convert_multiply_fusion.5
  181.5 17.8 %all_to_all.53 = bf16[8,256,128]{2,1,0:T(8,128)(2,1)S(1)} all-to-all(bf16[8,256,128]{2,1,0:T(8,128)(2,1)S(1)} %bitcast.96), channel_id=1, replica_groups=mesh['dp'=4,'context'=8] {'context'}, dimensions={0} | all-to-all | bytes 1048576 | tf_op jit(solution)/shard_map/all_to_all | solution.py:97
  199.2 0.8 copy-done.15
  200.0 1.4 convolution_bitcast_fusion.1
  202.2 4.1 fusion.14
  206.3 4.4 multiply_add_fusion.1
  210.8 4.6 pad_maximum_fusion.5
  215.3 5.5 copy.64
  220.9 6.1 fusion.66
  227.0 2.3 pad_maximum_fusion.2
  229.3 5.6 copy.58
  234.9 4.3 fusion.70
  239.2 2.8 multiply_add_fusion
  242.0 3.2 fusion.43
  245.3 17.8 %all_to_all.54 = bf16[256,8,128]{2,0,1:T(8,128)(2,1)S(1)} all-to-all(bf16[256,8,128]{2,0,1:T(8,128)(2,1)S(1)} %copy.43), channel_id=1, replica_groups=mesh['dp'=4,'context'=8] {'context'}, dimensions={1} | all-to-all | bytes 1048576 | tf_op jit(solution)/shard_map/all_to_all | solution.py:107
  263.1 1.1 convert_element_type.197
  264.1 2.6 copy.70
  266.7 1.7 bitcast_multiply_fusion
  268.6 1.3 collective-permute-start.1
  269.9 1.8 collective-permute-done.1
  272.1 1.6 copy-done.2
  273.7 3.0 multiply_reduce_fusion.2
  276.7 0.7 pad_maximum_fusion.12
  277.5 3.5 fusion.22
  281.0 1.2 copy.98
  282.2 9.1 %fusion.53 = f32[2048,2048]{1,0:T(8,128)} fusion(bf16[128,2048]{1,0:T(8,128)(2,1)S(1)} %copy-done, f32[2048,128]{0,1:T(8,128)S(1)} %copy-done.10, bf16[128,6144]{1,0:T(8,128)(2,1)} %copy-done.12), kind=kOutput, calls=%fused_computation.82 | convolution fusion | flops 1074528256 | bytes 18874368 | tf_op jit(solution)/shard_map/dot_general | solution.py:118
  291.4 1.0 copy-done.14
  292.6 1.1 fusion.52
  293.7 8.9 %psum.15 = f32[256]{0:T(256)S(1)} all-reduce(f32[256]{0:T(256)S(1)} %fusion.52), channel_id=1, replica_groups=mesh['dp'=4,'context'=8] {'dp'}, use_global_device_ids=true, to_apply=%region_6.7 | all-reduce | flops 256 | bytes 2048 | tf_op jit(solution)/shard_map/psum | solution.py:143
  302.6 0.6 broadcast_multiply_fusion.3
  303.2 93.5 %all-reduce.2.cloned.1.call-done = f32[3,6144]{1,0:T(4,128)} async-done(((f32[3,6144]{1,0:T(4,128)}), f32[3,6144]{1,0:T(4,128)}) %all-reduce.2.cloned.1.call-update) | async-done | bytes 73744 | tf_op jit(solution)/shard_map/psum | solution.py:161
  396.7 1.6 broadcast_multiply_fusion.2
  398.2 29.9 %reduce-scatter.3.cloned.1.call-done = f32[256,256]{1,0:T(8,128)} async-done(((f32[256,1024]{1,0:T(8,128)}), f32[256,256]{1,0:T(8,128)}) %reduce-scatter.3.cloned.1.call-update) | async-done | bytes 262160 | tf_op jit(solution)/shard_map/reduce_scatter | solution.py:141
  428.2 1.7 broadcast_multiply_fusion.1
  429.8 187.3 %reduce-scatter.5.cloned.1.call-done = f32[64,2048]{1,0:T(8,128)} async-done(((f32[2048,2048]{1,0:T(8,128)}), f32[64,2048]{1,0:T(8,128)}) %reduce-scatter.5.cloned.1.call-update) | async-done | bytes 524304 | tf_op jit(solution)/shard_map/reduce_scatter | solution.py:117
  617.1 1.9 broadcast_multiply_fusion
  (68 shorter events, 4.4 us)
Async XLA Ops:
  7.2 93.1 %copy-start = (bf16[128,2048]{1,0:T(8,128)(2,1)S(1)}, bf16[128,2048]{1,0:T(8,128)(2,1)}, u32[]{:S(2)}) copy-start(bf16[128,2048]{1,0:T(8,128)(2,1)} %param.11) | copy-start | bytes 1572868
  7.2 5.3 copy-start.20
  7.2 93.0 %all-gather.2.cloned.1.call-start = ((), (), s32[]{:S(2)}) async-start(), calls=%async_computation.6 | async-start | bytes 10485760 | tf_op jit(solution)/shard_map/all_gather | solution.py:113
  8.8 3.6 collective-permute-start
  12.9 1.7 copy-start.1
  15.6 90.9 %copy-start.12 = (bf16[128,6144]{1,0:T(8,128)(2,1)}, bf16[128,6144]{1,0:T(8,128)(2,1)S(1)}, u32[]{:S(2)}) copy-start(bf16[128,6144]{1,0:T(8,128)(2,1)S(1)} %add_convert_fusion) | copy-start | bytes 4718596
  106.5 1.0 copy-start.11
  108.6 20.0 %all-to-all-start.2 = ((bf16[8,256,128]{2,1,0:T(8,128)(2,1)}), bf16[8,256,128]{2,1,0:T(8,128)(2,1)S(1)}, u32[]{:S(2)}, u32[]{:S(2)}) async-start(bf16[8,256,128]{2,1,0:T(8,128)(2,1)} %bitcast.17), calls=%async_computation.2 | async-start | bytes 1048576 | tf_op jit(solution)/shard_map/all_to_all | solution.py:127
  113.2 283.5 %all-reduce.2.cloned.1.call-start = ((), (), s32[]{:S(2)}) async-start(), calls=%async_computation.7 | async-start | bytes 196608 | tf_op jit(solution)/shard_map/psum | solution.py:161
  128.6 27.2 %copy-start.13 = (bf16[8,256,128]{2,1,0:T(8,128)(2,1)}, bf16[8,256,128]{2,1,0:T(8,128)(2,1)S(1)}, u32[]{:S(2)}) copy-start(bf16[8,256,128]{2,1,0:T(8,128)(2,1)S(1)} %all-to-all-done.2) | copy-start | bytes 1572868
  128.6 2.4 copy-start.7
  136.8 4.2 copy-start.3
  141.0 1.9 copy-start.5
  155.3 0.7 copy-start.21
  199.2 0.8 copy-start.15
  202.2 4.1 copy-start.4
  202.2 4.1 copy-start.6
  220.9 6.1 copy-start.18
  220.9 6.1 copy-start.19
  234.9 4.3 copy-start.8
  239.2 2.8 copy-start.16
  263.1 5.3 copy-start.9
  268.6 3.1 collective-permute-start.1
  271.7 1.9 copy-start.2
  277.4 150.8 %reduce-scatter.3.cloned.1.call-start = ((), (), s32[]{:S(2)}) async-start(), calls=%async_computation.8 | async-start | bytes 1310720 | tf_op jit(solution)/shard_map/reduce_scatter | solution.py:141
  277.5 4.8 copy-start.10
  282.2 334.9 %reduce-scatter.5.cloned.1.call-start = ((), (), s32[]{:S(2)}) async-start(), calls=%async_computation.9 | async-start | bytes 17301504 | tf_op jit(solution)/shard_map/reduce_scatter | solution.py:117
  291.4 1.0 copy-start.14
  291.4 1.2 copy-start.17
Sparse Core Ops, SparseCore 0:
  9.9 90.2 all-gather.1
  277.5 119.1 all-reduce.1
  399.6 28.5 reduce-scatter.2
  430.4 186.6 reduce-scatter.4
where the time goes:
time: 631 us; the launch traced here: 626 us
  waiting for transfers between devices  407 us (65%)
  blocking collectives  62.2 us (10%)
  matrix products  58.6 us (9%)
  other arithmetic  39.6 us (6%)
  local copies, waits for them, and re-layouts  35.2 us (6%)
  between operations  14.4 us (2%)
  starting transfers between devices  8.41 us (1%)
    reduce_scatter x1, waiting for transfers between devices, body(): lax.psum_scatter(lax.dot_general(gate, cotangent, (((0,), (0,)), ((), ())...  187 us
    psum x1, waiting for transfers between devices, body(): grad_taps = lax.psum(taps_terms, ('dp', 'context')) * scale_factor  93.5 us
    all_gather x1, waiting for transfers between devices, body(): lax.all_gather(out_proj, 'dp', axis=0, tiled=True)  84.6 us
    reduce_scatter x1, waiting for transfers between devices, body(): lax.psum_scatter(filter_local, 'dp', scatter_dimension=1, tiled=True)  29.9 us
    all_to_all x1, blocking collectives, body(): lax.all_to_all(back_chan.astype(jnp.bfloat16), 'context', split_axis=1, c...  17.8 us
    all_to_all x1, blocking collectives, body(): lax.all_to_all(product.T, 'context', split_axis=0, concat_axis=1, tiled=T...  17.8 us
    all_to_all x1, blocking collectives, body(): lax.all_to_all(long_chan.astype(jnp.bfloat16), 'context', split_axis=1, c...  17.8 us
    dot_general x3, matrix products, inverse_real(): undo = jnp.einsum('ckn,nm->ckm', spectrum, inner_back, precision=PRECISE)  14.4 us
  transfers between devices with their start and end apart: 7, of which 6 were waited for; matrix products, arithmetic and copies ran while one was open for 5% of the time, Pallas kernels for 0%

commit v1 on v0

v1 whole, which is shorter than its diff:
```python
import math

import jax
import jax.numpy as jnp
from jax import lax
from jax.experimental import pallas as pl
from jax.experimental.pallas import tpu as pltpu
from jax.sharding import PartitionSpec as P

BF16 = jnp.bfloat16
F32 = jnp.float32


def passed_along(value, axis, steps):
    count = lax.axis_size(axis)
    initial, last = (max(0, -steps), min(count, count - steps))
    return lax.ppermute(value, axis, [(source, source + steps) for source in range(initial, last)])


def swapped(value, axis, mask):
    return lax.ppermute(value, axis, [(i, i ^ mask) for i in range(lax.axis_size(axis))])


def exchanged(pieces, axis):
    return [pieces[0]] + [swapped(pieces[k], axis, k) for k in range(1, len(pieces))]


def rows_down(values, steps, before):
    row = lax.broadcasted_iota(jnp.int32, values.shape, 0)
    moved = pltpu.roll(values, steps, axis=0)
    if steps == 1:
        return jnp.where(row == 0, before[1:2], moved)
    return jnp.where(row == 0, before[0:1], jnp.where(row == 1, before[1:2], moved))


def rows_up(values, steps, after):
    count = values.shape[0]
    row = lax.broadcasted_iota(jnp.int32, values.shape, 0)
    moved = pltpu.roll(values, count - steps, axis=0)
    if steps == 1:
        return jnp.where(row == count - 1, after[0:1], moved)
    return jnp.where(row == count - 1, after[1:2], jnp.where(row == count - 2, after[0:1], moved))


def short_kernel(parts, chans, me_ref, proj_ref, prev_ref, taps_ref, *outs):
    query_refs, product_refs = outs[:parts], outs[parts : 2 * parts]
    keyed_ref, valued_ref = outs[2 * parts :]
    blk = chans // parts
    me = me_ref[0]
    for k in range(parts):
        start = (me ^ k) * blk

        def mixed(stream):
            cols = pl.ds(pl.multiple_of(start + stream * chans, blk), blk)
            values = proj_ref[:, cols].astype(F32)
            before = prev_ref[:, cols]
            taps = taps_ref[:, cols]
            return (
                taps[0:1] * values
                + taps[1:2] * rows_down(values, 1, before)
                + taps[2:3] * rows_down(values, 2, before)
            ).astype(BF16)

        own = pl.ds(pl.multiple_of(start, blk), blk)
        query_refs[k][...] = mixed(0)
        keyed, valued = (mixed(1), mixed(2))
        keyed_ref[:, own] = keyed
        valued_ref[:, own] = valued
        product_refs[k][...] = (keyed.astype(F32) * valued.astype(F32)).astype(BF16)


def final_kernel(parts, chans, me_ref, *refs):
    query_grads, product_grads = refs[:parts], refs[parts : 2 * parts]
    keyed_ref, valued_ref, after_ref, proj_ref, prev_ref, taps_ref = refs[2 * parts : 2 * parts + 6]
    out_ref = refs[2 * parts + 6]
    share_refs = refs[2 * parts + 7 :]
    blk = chans // parts
    rows = proj_ref.shape[0]
    me = me_ref[0]
    for k in range(parts):
        start = (me ^ k) * blk
        own = pl.ds(pl.multiple_of(start, blk), blk)
        other = pl.ds(pl.multiple_of(start + chans, blk), blk)
        back = product_grads[k][0:rows].astype(F32)
        back_after = product_grads[k][rows : rows + 2].astype(F32)
        grads = (
            (query_grads[k][0:rows].astype(F32), query_grads[k][rows : rows + 2].astype(F32)),
            (back * valued_ref[:, own].astype(F32), back_after * after_ref[:, other]),
            (back * keyed_ref[:, own].astype(F32), back_after * after_ref[:, own]),
        )
        sums = []
        for stream, (grad, grad_after) in enumerate(grads):
            cols = pl.ds(pl.multiple_of(start + stream * chans, blk), blk)
            taps = taps_ref[:, cols]
            out_ref[:, cols] = (
                taps[0:1] * grad
                + taps[1:2] * rows_up(grad, 1, grad_after)
                + taps[2:3] * rows_up(grad, 2, grad_after)
            ).astype(BF16)
            values = proj_ref[:, cols].astype(F32)
            before = prev_ref[:, cols]
            sums.append(jnp.sum(grad * values, 0, keepdims=True))
            sums.append(jnp.sum(grad * rows_down(values, 1, before), 0, keepdims=True))
            sums.append(jnp.sum(grad * rows_down(values, 2, before), 0, keepdims=True))
        for i, term in enumerate(sums):
            share_refs[k][i : i + 1, :] = term


VMEM = pl.BlockSpec(memory_space=pltpu.VMEM)
SMEM = pl.BlockSpec(memory_space=pltpu.SMEM)


def cost(*arrays):
    moved = sum(math.prod(a.shape) * a.dtype.itemsize for a in arrays)
    return pl.CostEstimate(flops=8 * moved, transcendentals=0, bytes_accessed=moved)


def short_convs(me, projected, prev_rows, taps, parts):
    rows, width = projected.shape
    chans = width // 3
    piece = jax.ShapeDtypeStruct((rows, chans // parts), BF16)
    whole = jax.ShapeDtypeStruct((rows, chans), BF16)
    outs = pl.pallas_call(
        lambda *refs: short_kernel(parts, chans, *refs),
        out_shape=[piece] * (2 * parts) + [whole] * 2,
        in_specs=[SMEM, VMEM, VMEM, VMEM],
        out_specs=[VMEM] * (2 * parts + 2),
        compiler_params=pltpu.CompilerParams(vmem_limit_bytes=40 * 2**20),
        cost_estimate=cost(projected, projected, projected),
        name="short_convs",
    )(me, projected, prev_rows, taps)
    return (outs[:parts], outs[parts : 2 * parts], outs[-2], outs[-1])


def stream_grads(me, query_grads, product_grads, keyed, valued, after, projected, prev_rows, taps):
    parts = len(query_grads)
    rows, width = projected.shape
    chans = width // 3
    share = jax.ShapeDtypeStruct((9, chans // parts), F32)
    outs = pl.pallas_call(
        lambda *refs: final_kernel(parts, chans, *refs),
        out_shape=[jax.ShapeDtypeStruct((rows, width), BF16)] + [share] * parts,
        in_specs=[SMEM] + [VMEM] * (2 * parts + 6),
        out_specs=[VMEM] * (1 + parts),
        compiler_params=pltpu.CompilerParams(vmem_limit_bytes=40 * 2**20),
        cost_estimate=cost(projected, projected, projected),
        name="stream_grads",
    )(me, *query_grads, *product_grads, keyed, valued, after, projected, prev_rows, taps)
    return (outs[0], outs[1:])


def shifted(values, before):
    rows = values.shape[0]
    down = jnp.concatenate([before, values], 0)
    return [down[i : i + rows] for i in range(3)]


def reordered(blocks, me):
    picks = [lax.dynamic_index_in_dim(blocks, me ^ k, 0, False) for k in range(blocks.shape[0])]
    return picks


def plain_short_convs(me, projected, prev_rows, taps, parts):
    chans = projected.shape[1] // 3
    blk = chans // parts
    two_back, once_back, current = shifted(projected.astype(F32), prev_rows)
    mixed = (taps[0] * current + taps[1] * once_back + taps[2] * two_back).astype(BF16)
    query, keyed, valued = (mixed[:, i * chans : (i + 1) * chans] for i in range(3))
    product = (keyed.astype(F32) * valued.astype(F32)).astype(BF16)

    def cut(values):
        return reordered(values.reshape(-1, parts, blk).transpose(1, 0, 2), me[0])

    return (cut(query), cut(product), keyed, valued)


def plain_stream_grads(
    me, query_grads, product_grads, keyed, valued, after, projected, prev_rows, taps
):
    parts = len(query_grads)
    rows, width = projected.shape
    blk = width // 3 // parts

    def joined(pieces):
        blocks = jnp.stack(reordered(jnp.stack(pieces), me[0])).astype(F32)
        return blocks.transpose(1, 0, 2).reshape(rows + 2, parts * blk)

    back = joined(product_grads)
    keyed_all = jnp.concatenate([keyed.astype(F32), after[:, : parts * blk]], 0)
    valued_all = jnp.concatenate([valued.astype(F32), after[:, parts * blk :]], 0)
    grads = jnp.concatenate([joined(query_grads), back * valued_all, back * keyed_all], 1)
    own = grads[:rows]
    out = (taps[0] * own + taps[1] * grads[1 : rows + 1] + taps[2] * grads[2:]).astype(BF16)
    two_back, once_back, current = shifted(projected.astype(F32), prev_rows)
    sums = [jnp.sum(own * values, 0) for values in (current, once_back, two_back)]
    blocks = jnp.stack(sums).reshape(3, 3, parts, blk).transpose(2, 1, 0, 3).reshape(parts, 9, blk)
    return (out, reordered(blocks, me[0]))


def table(places, first, freqs, seq_len):
    inner = min(32, freqs)
    outer = freqs // inner

    def waves(odd):
        phases = odd[:, None] * places[None, :] % (4 * seq_len)
        angles = phases.astype(F32) * (2.0 * math.pi / (4 * seq_len))
        return (jnp.cos(angles), jnp.sin(angles))

    outer_cos, outer_sin = waves(2 * (first + inner * jnp.arange(outer)))
    inner_cos, inner_sin = waves(2 * jnp.arange(inner) + 1)
    oc, os = (outer_cos[:, None], outer_sin[:, None])
    ic, is_ = (inner_cos[None], inner_sin[None])
    both = jnp.stack([oc * ic - os * is_, -(os * ic + oc * is_)])
    return both.astype(BF16).reshape(2 * freqs, places.shape[0])


def dot(left, right, left_dim, right_dim):
    return lax.dot_general(
        left, right, (((left_dim,), (right_dim,)), ((), ())), preferred_element_type=F32
    )


def spectral_product(left, right, conjugate_left):
    half = left.shape[0] // 2
    left_re, left_im = (left[:half], left[half:])
    right_re, right_im = (right[:half], right[half:])
    if conjugate_left:
        real = left_re * right_re + left_im * right_im
        imag = left_re * right_im - left_im * right_re
    else:
        real = left_re * right_re - left_im * right_im
        imag = left_re * right_im + left_im * right_re
    return jnp.concatenate([real, imag], 0).astype(BF16)


def long_terms(first, freqs, places, lags, long_filter, product, grad_long):
    seq_len = places.shape[0]
    own = table(places, first, freqs, seq_len)
    plain = table(lags, first, freqs, seq_len)
    filter_spec = dot(plain, long_filter, 1, 1)
    product_spec = dot(own, product, 1, 0)
    grad_spec = dot(own, grad_long, 1, 0)
    out = dot(own, spectral_product(filter_spec, product_spec, False), 0, 0)
    back = dot(own, spectral_product(filter_spec, grad_spec, True), 0, 0)
    lag_grad = dot(spectral_product(product_spec, grad_spec, True), plain, 0, 0)
    return (out, back, lag_grad)


def own_rows(weights, parts_dp, parts_ctx):
    ratio = parts_ctx // parts_dp
    context = lax.axis_index("context")
    block = weights.shape[0] // ratio
    half = lax.dynamic_slice_in_dim(weights, (context % ratio) * block, block, 0)
    holder = context // ratio
    found = half
    for k in range(1, parts_dp):
        pairs = [
            ((c // ratio) * parts_ctx + c, ((c // ratio) ^ k) * parts_ctx + c)
            for c in range(parts_ctx)
        ]
        sent = lax.ppermute(half, ("dp", "context"), pairs)
        found = jnp.where(lax.axis_index("dp") == (holder ^ k), sent, found)
    return found


def gathered(value, axis):
    pieces = [value]
    for k in range(2, lax.axis_size(axis), 2):
        pieces.append(swapped(value, axis, k))
    out = []
    for piece in pieces:
        out += [piece, swapped(piece, axis, 1)]
    return jnp.concatenate(out, 0)


def summed_blocks(value, axis, dim):
    count = lax.axis_size(axis)
    size = value.shape[dim] // count
    me = lax.axis_index(axis)
    total = lax.dynamic_slice_in_dim(value, me * size, size, dim)
    for k in range(1, count):
        sent = lax.dynamic_slice_in_dim(value, (me ^ k) * size, size, dim).astype(BF16)
        total = total + swapped(sent, axis, k).astype(F32)
    return total


def body(projected, short_taps, long_filter, skip_gain, out_proj, cotangent):
    rows, width = projected.shape
    chans = width // 3
    parts_dp, parts = (lax.axis_size("dp"), lax.axis_size("context"))
    blk = chans // parts
    seq_len = rows * parts
    me = lax.axis_index("context")
    me_arr = me.astype(jnp.int32)[None]
    scale_factor = 1.0 / math.sqrt(seq_len * parts_dp)

    prev_rows = passed_along(projected[rows - 2 :], "context", 1).astype(F32)
    cot_seq = gathered(cotangent, "context")
    weights = own_rows(out_proj, parts_dp, parts)
    wide = blk % 128 == 0 and rows % 16 == 0
    query_out, product_out, keyed, valued = (short_convs if wide else plain_short_convs)(
        me_arr, projected, prev_rows, short_taps, parts
    )
    after = passed_along(
        jnp.concatenate([keyed[:2], valued[:2]], 1), "context", -1
    ).astype(F32)
    product = jnp.concatenate(exchanged(product_out, "context"), 0)
    query = jnp.concatenate(exchanged(query_out, "context"), 0).astype(F32)

    lags = jnp.arange(seq_len)
    order = (jnp.arange(parts) ^ me)[:, None] * rows + jnp.arange(rows)[None, :]
    places = order.reshape(seq_len)
    grad_gate = dot(cot_seq, weights, 1, 1).astype(BF16).astype(F32)
    grad_long = (grad_gate * query).astype(BF16)
    filter_b = long_filter.astype(BF16)
    freqs = seq_len if seq_len <= 1024 else 256
    if freqs == seq_len:
        terms = long_terms(0, freqs, places, lags, filter_b, product, grad_long)
    else:

        def step(carry, first):
            new = long_terms(first, freqs, places, lags, filter_b, product, grad_long)
            return (tuple(a + b for a, b in zip(carry, new)), None)

        zero = jnp.zeros((seq_len, blk), F32)
        start = (zero, zero, jnp.zeros((blk, seq_len), F32))
        terms, _ = lax.scan(step, start, jnp.arange(0, seq_len, freqs))
    out_sum, back_sum, lag_sum = terms
    inverse = 1.0 / seq_len
    product_f, grad_long_f = (product.astype(F32), grad_long.astype(F32))
    long_out = (out_sum * inverse + skip_gain[None, :] * product_f).astype(BF16).astype(F32)
    grad_product = (back_sum * inverse + skip_gain[None, :] * grad_long_f).astype(BF16)
    gate = (query * long_out).astype(BF16)
    grad_query = (grad_gate * long_out).astype(BF16)

    follows = (jnp.arange(parts) ^ me) + 1
    picks = (follows[:, None] == (jnp.arange(parts) ^ me)[None, :]).astype(F32)

    def with_next(values):
        blocks = values.reshape(parts, rows, blk)
        heads = blocks[:, :2].astype(F32)
        after_rows = jnp.sum(picks[:, :, None, None] * heads[None], 1).astype(BF16)
        return [jnp.concatenate([blocks[k], after_rows[k]], 0) for k in range(parts)]

    query_grads = exchanged(with_next(grad_query), "context")
    product_grads = exchanged(with_next(grad_product), "context")
    grad_inputs, shares = (stream_grads if wide else plain_stream_grads)(
        me_arr, query_grads, product_grads, keyed, valued, after, projected, prev_rows, short_taps
    )

    proj_part = summed_blocks(dot(gate, cot_seq, 0, 0), "dp", 0).astype(BF16)
    rank = [
        (d * parts + c, c * parts_dp + d) for d in range(parts_dp) for c in range(parts)
    ]
    grad_proj = lax.ppermute(proj_part, ("dp", "context"), rank).astype(F32) * scale_factor
    grad_filter = summed_blocks(lag_sum, "dp", 1) * (scale_factor * inverse)
    skip_part = jnp.sum(grad_long_f * product_f, 0, keepdims=True)
    grad_skip = skip_part
    for k in range(1, parts_dp):
        grad_skip = grad_skip + swapped(skip_part, "dp", k)

    tap_sum = sum(exchanged(shares, "context"))
    tap_all = tap_sum
    for k in range(1, parts_dp):
        tap_all = tap_all + swapped(tap_sum, "dp", k)
    taps = jnp.stack(exchanged([tap_all * scale_factor] * parts, "context"))
    bit = 1
    while bit < parts:
        view = taps.reshape(parts // (2 * bit), 2, bit, 9, blk)
        taps = jnp.where(me & bit != 0, view[:, ::-1], view).reshape(parts, 9, blk)
        bit *= 2
    grad_taps = taps.reshape(parts, 3, 3, blk).transpose(2, 1, 0, 3).reshape(3, width)
    return (grad_inputs, grad_taps, grad_filter, grad_skip[0] * scale_factor, grad_proj)


def solution(mesh):
    placed = (
        P(("dp", "context"), None),
        P(),
        P("context", None),
        P("context"),
        P("dp", None),
        P(("dp", "context"), None),
    )
    return jax.shard_map(
        body,
        mesh=mesh,
        in_specs=placed,
        out_specs=(
            P(("dp", "context"), None),
            P(),
            P("context", "dp"),
            P("context"),
            P(("dp", "context"), None),
        ),
        check_vma=False,
    )
```

time: 631 us -> 276 us (0.44)
  the two profiles are of different devices: /device:TPU:0 before, /device:TPU:2 now
where the time goes in v1:
time: 276 us; the launch traced here: 275 us
  waiting for transfers between devices  160 us (58%)
  starting transfers between devices  68.3 us (25%)
  other arithmetic  14.2 us (5%)
  matrix products  14.2 us (5%)
  local copies, waits for them, and re-layouts  11.7 us (4%)
  Pallas kernels  5.55 us (2%)
    ppermute x61, waiting for transfers between devices, swapped(): lax.ppermute(value, axis, [(i, i ^ mask) for i in range(lax.axis_size(axi...  107 us
    ppermute x61, starting transfers between devices, swapped(): lax.ppermute(value, axis, [(i, i ^ mask) for i in range(lax.axis_size(axi...  60 us
    ppermute x3, waiting for transfers between devices, own_rows(): sent = lax.ppermute(half, ('dp', 'context'), pairs)  41.4 us
    dot_general x8, matrix products, dot(): lax.dot_general(left, right, (((left_dim,), (right_dim,)), ((), ())), pre...  14.2 us
    ppermute x1, waiting for transfers between devices, body(): lax.ppermute(proj_part, ('dp', 'context'), rank).astype(F32) * scale_factor  9.75 us
    unnamed x50, local copies, waits for them, and re-layouts  8.69 us
  transfers between devices with their start and end apart: 67, of which 34 were waited for; matrix products, arithmetic and copies ran while one was open for 10% of the time, Pallas kernels for 1%

profile of v1, /device:TPU:2, one launch (start us, length us, event | category | flops | bytes accessed | tf_op | source)
XLA Modules:
  0.0 275.4 jit_solution(1012440372588373140)
XLA Ops:
  0.6 1.6 collective-permute-start.1
  2.3 2.6 collective-permute-start.3
  5.8 2.1 collective-permute-start.10
  8.0 1.9 constant_dynamic-update-slice_fusion.7
  10.0 2.1 fusion.55
  12.2 3.4 %subtract_convert_fusion = (bf16[1,32,32,1024]{3,2,1,0:T(8,128)(2,1)S(1)}, bf16[1,32,32,1024]{3,2,1,0:T(8,128)(2,1)S(1)}, bf16[1,32,32,1024]{3,2,1,0:T(8,128)(2,1)S(1)}, bf16[1,32,32,1024]{3,2,1,0:T(8,128)(2,1)S(1)}) fusion(f32[32,1024]{1,0:T(8,128)S(1)} %get-tuple-element.125, f32[32,1024]{1,0:T(8,128)S(1)} %get-tuple-element.124, ...), kind=kLoop, calls=%fused_computation.3 | loop fusion | flops 18874368 | bytes 9437184 | tf_op jit(solution)/shard_map/convert.6
  16.8 2.6 fusion.30
  19.5 2.4 pad_maximum_fusion
  21.9 1.4 copy-done.1
  23.3 1.5 short_convs.1
  24.8 2.6 collective-permute-start.11
  27.5 1.3 collective-permute-start.39
  28.8 1.8 collective-permute-done.39
  30.6 8.1 %collective-permute-start.5 = (bf16[128,2048]{1,0:T(8,128)(2,1)}, bf16[128,2048]{1,0:T(8,128)(2,1)S(1)}, u32[]{:S(2)}, u32[]{:S(2)}) collective-permute-start(bf16[128,2048]{1,0:T(8,128)(2,1)} %param.11), channel_id=1, source_target_pairs={{0,6},{1,7},{2,4},{3,5},{4,2},{5,3},{6,0},{7,1},{8,14},{9,15},{10,... | collective-permute-start | bytes 1572872 | tf_op jit(solution)/shard_map/ppermute | solution.py:21
  38.8 13.9 %collective-permute-done.12 = bf16[128,256]{1,0:T(8,128)(2,1)S(1)} collective-permute-done((bf16[128,256]{1,0:T(8,128)(2,1)S(1)}, bf16[128,256]{1,0:T(8,128)(2,1)S(1)}, u32[]{:S(2)}, u32[]{:S(2)}) %collective-permute-start.12) | collective-permute-done | bytes 65568 | tf_op jit(solution)/shard_map/ppermute | solution.py:21
  52.8 4.2 %collective-permute-done.13 = bf16[128,256]{1,0:T(8,128)(2,1)S(1)} collective-permute-done((bf16[128,256]{1,0:T(8,128)(2,1)S(1)}, bf16[128,256]{1,0:T(8,128)(2,1)S(1)}, u32[]{:S(2)}, u32[]{:S(2)}) %collective-permute-start.13) | collective-permute-done | bytes 65568 | tf_op jit(solution)/shard_map/ppermute | solution.py:21
  57.7 5.4 %collective-permute-done.14 = bf16[128,256]{1,0:T(8,128)(2,1)S(1)} collective-permute-done((bf16[128,256]{1,0:T(8,128)(2,1)S(1)}, bf16[128,256]{1,0:T(8,128)(2,1)S(1)}, u32[]{:S(2)}, u32[]{:S(2)}) %collective-permute-start.14) | collective-permute-done | bytes 65568 | tf_op jit(solution)/shard_map/ppermute | solution.py:21
  63.5 5.6 %collective-permute-done.15 = bf16[128,256]{1,0:T(8,128)(2,1)S(1)} collective-permute-done((bf16[128,256]{1,0:T(8,128)(2,1)S(1)}, bf16[128,256]{1,0:T(8,128)(2,1)S(1)}, u32[]{:S(2)}, u32[]{:S(2)}) %collective-permute-start.15) | collective-permute-done | bytes 65568 | tf_op jit(solution)/shard_map/ppermute | solution.py:21
  69.1 2.4 collective-permute-start.16
  71.5 3.7 %collective-permute-done.16 = bf16[128,256]{1,0:T(8,128)(2,1)S(1)} collective-permute-done((bf16[128,256]{1,0:T(8,128)(2,1)S(1)}, bf16[128,256]{1,0:T(8,128)(2,1)S(1)}, u32[]{:S(2)}, u32[]{:S(2)}) %collective-permute-start.16) | collective-permute-done | bytes 65568 | tf_op jit(solution)/shard_map/ppermute | solution.py:21
  76.1 4.5 %collective-permute-done.17 = bf16[128,256]{1,0:T(8,128)(2,1)S(1)} collective-permute-done((bf16[128,256]{1,0:T(8,128)(2,1)S(1)}, bf16[128,256]{1,0:T(8,128)(2,1)S(1)}, u32[]{:S(2)}, u32[]{:S(2)}) %collective-permute-start.17) | collective-permute-done | bytes 65568 | tf_op jit(solution)/shard_map/ppermute | solution.py:21
  80.7 3.6 %fusion.65 = f32[2048,256]{1,0:T(8,128)S(1)} fusion(bf16[2048,1024]{1,0:T(8,128)(2,1)} %bitcast.81, bf16[1024,256]{1,0:T(8,128)(2,1)S(1)} %constant_dynamic-update-slice_fusion.8), kind=kOutput, calls=%fused_computation.189 | convolution fusion | flops 1073741824 | bytes 6815744 | tf_op jit(solution)/shard_map/dot_general | solution.py:218
  84.4 4.5 %collective-permute-done.26 = bf16[128,256]{1,0:T(8,128)(2,1)S(1)} collective-permute-done((bf16[128,256]{1,0:T(8,128)(2,1)S(1)}, bf16[128,256]{1,0:T(8,128)(2,1)S(1)}, u32[]{:S(2)}, u32[]{:S(2)}) %collective-permute-start.26) | collective-permute-done | bytes 65568 | tf_op jit(solution)/shard_map/ppermute | solution.py:21
  88.8 4.3 %collective-permute-done.27 = bf16[128,256]{1,0:T(8,128)(2,1)S(1)} collective-permute-done((bf16[128,256]{1,0:T(8,128)(2,1)S(1)}, bf16[128,256]{1,0:T(8,128)(2,1)S(1)}, u32[]{:S(2)}, u32[]{:S(2)}) %collective-permute-start.27) | collective-permute-done | bytes 65568 | tf_op jit(solution)/shard_map/ppermute | solution.py:21
  94.2 5.0 %collective-permute-done.28 = bf16[128,256]{1,0:T(8,128)(2,1)S(1)} collective-permute-done((bf16[128,256]{1,0:T(8,128)(2,1)S(1)}, bf16[128,256]{1,0:T(8,128)(2,1)S(1)}, u32[]{:S(2)}, u32[]{:S(2)}) %collective-permute-start.28) | collective-permute-done | bytes 65568 | tf_op jit(solution)/shard_map/ppermute | solution.py:21
  99.3 5.9 %collective-permute-done.29 = bf16[128,256]{1,0:T(8,128)(2,1)S(1)} collective-permute-done((bf16[128,256]{1,0:T(8,128)(2,1)S(1)}, bf16[128,256]{1,0:T(8,128)(2,1)S(1)}, u32[]{:S(2)}, u32[]{:S(2)}) %collective-permute-start.29) | collective-permute-done | bytes 65568 | tf_op jit(solution)/shard_map/ppermute | solution.py:21
  105.2 1.8 collective-permute-start.30
  107.0 4.3 %collective-permute-done.30 = bf16[128,256]{1,0:T(8,128)(2,1)S(1)} collective-permute-done((bf16[128,256]{1,0:T(8,128)(2,1)S(1)}, bf16[128,256]{1,0:T(8,128)(2,1)S(1)}, u32[]{:S(2)}, u32[]{:S(2)}) %collective-permute-start.30) | collective-permute-done | bytes 65568 | tf_op jit(solution)/shard_map/ppermute | solution.py:21
  111.6 5.2 %collective-permute-done.31 = bf16[128,256]{1,0:T(8,128)(2,1)S(1)} collective-permute-done((bf16[128,256]{1,0:T(8,128)(2,1)S(1)}, bf16[128,256]{1,0:T(8,128)(2,1)S(1)}, u32[]{:S(2)}, u32[]{:S(2)}) %collective-permute-start.31) | collective-permute-done | bytes 65568 | tf_op jit(solution)/shard_map/ppermute | solution.py:21
  121.1 1.5 collective-permute-start.9
  124.6 41.4 %collective-permute-done.9 = bf16[256,2048]{1,0:T(8,128)(2,1)S(1)} collective-permute-done((bf16[256,2048]{1,0:T(8,128)(2,1)S(1)}, bf16[256,2048]{1,0:T(8,128)(2,1)S(1)}, u32[]{:S(2)}, u32[]{:S(2)}) %collective-permute-start.9) | collective-permute-done | bytes 1048608 | tf_op jit(solution)/shard_map/ppermute | solution.py:261
  166.0 1.4 convolution_convert_fusion
  167.4 1.3 fusion.61
  170.0 1.5 fusion.7
  172.9 1.3 fusion.6
  174.6 1.4 collective-permute-start.37
  176.0 4.8 %collective-permute-start.35 = (bf16[130,256]{1,0:T(8,128)(2,1)S(1)}, bf16[130,256]{1,0:T(8,128)(2,1)S(1)}, u32[]{:S(2)}, u32[]{:S(2)}) collective-permute-start(bf16[130,256]{1,0:T(8,128)(2,1)S(1)} %pad_maximum_fusion.14), channel_id=1, source_target_pairs={{0,4},{1,5},{2,6},{3,7},{4,0},{5,1},{6,2},{7,3},{8,12},{9,13},{10,... | collective-permute-start | bytes 199688 | tf_op jit(solution)/shard_map/ppermute | solution.py:21
  181.5 1.3 collective-permute-start.32
  182.8 3.2 %collective-permute-done.36.refs_14_ = bf16[130,256]{1,0:T(8,128)(2,1)S(1)} collective-permute-done((bf16[130,256]{1,0:T(8,128)(2,1)S(1)}, bf16[130,256]{1,0:T(8,128)(2,1)S(1)}, u32[]{:S(2)}, u32[]{:S(2)}) %collective-permute-start.36) | collective-permute-done | bytes 66592 | tf_op jit(solution)/shard_map/ppermute | solution.py:21
  187.7 1.9 collective-permute-start.23
  189.6 2.7 collective-permute-start.21
  192.3 1.7 collective-permute-start.19
  194.7 3.7 %collective-permute-done.22.refs_6_ = bf16[130,256]{1,0:T(8,128)(2,1)S(1)} collective-permute-done((bf16[130,256]{1,0:T(8,128)(2,1)S(1)}, bf16[130,256]{1,0:T(8,128)(2,1)S(1)}, u32[]{:S(2)}, u32[]{:S(2)}) %collective-permute-start.22) | collective-permute-done | bytes 66592 | tf_op jit(solution)/shard_map/ppermute | solution.py:21
  198.4 1.5 collective-permute-done.21.refs_5_
  201.2 4.1 %stream_grads.1 = (bf16[128,6144]{1,0:T(8,128)(2,1)}, f32[9,256]{1,0:T(8,128)S(1)}, f32[9,256]{1,0:T(8,128)S(1)}, f32[9,256]{1,0:T(8,128)S(1)}, f32[9,256]{1,0:T...) custom-call(s32[1]{0:T(128)} %bitcast.refs_0_, ...), custom_call_target="tpu_custom_call" | custom-call | flops 37748736 | bytes 4718592 | tf_op jit(solution)/shard_map/stream_grads/pallas_call | solution.py:140
  206.5 1.9 collective-permute-start.42
  208.7 2.3 collective-permute-start.44
  211.0 1.4 collective-permute-start.45
  212.4 2.2 collective-permute-start.46
  217.7 2.0 collective-permute-start.48
  221.7 1.7 collective-permute-start.62
  225.2 1.8 collective-permute-start.65
  229.1 3.7 %collective-permute-done.51 = f32[9,256]{1,0:T(8,128)S(1)} collective-permute-done((f32[9,256]{1,0:T(8,128)S(1)}, f32[9,256]{1,0:T(8,128)S(1)}, u32[]{:S(2)}, u32[]{:S(2)}) %collective-permute-start.51) | collective-permute-done | bytes 9248 | tf_op jit(solution)/shard_map/ppermute | solution.py:21
  232.8 3.2 %collective-permute-done.52 = f32[9,256]{1,0:T(8,128)S(1)} collective-permute-done((f32[9,256]{1,0:T(8,128)S(1)}, f32[9,256]{1,0:T(8,128)S(1)}, u32[]{:S(2)}, u32[]{:S(2)}) %collective-permute-start.52) | collective-permute-done | bytes 9248 | tf_op jit(solution)/shard_map/ppermute | solution.py:21
  236.0 4.6 %collective-permute-done.53 = f32[9,256]{1,0:T(8,128)S(1)} collective-permute-done((f32[9,256]{1,0:T(8,128)S(1)}, f32[9,256]{1,0:T(8,128)S(1)}, u32[]{:S(2)}, u32[]{:S(2)}) %collective-permute-start.53) | collective-permute-done | bytes 9248 | tf_op jit(solution)/shard_map/ppermute | solution.py:21
  240.6 4.1 %collective-permute-done.54 = f32[9,256]{1,0:T(8,128)S(1)} collective-permute-done((f32[9,256]{1,0:T(8,128)S(1)}, f32[9,256]{1,0:T(8,128)S(1)}, u32[]{:S(2)}, u32[]{:S(2)}) %collective-permute-start.54) | collective-permute-done | bytes 9248 | tf_op jit(solution)/shard_map/ppermute | solution.py:21
  244.7 1.6 collective-permute-start.55
  246.3 3.9 %collective-permute-done.55 = f32[9,256]{1,0:T(8,128)S(1)} collective-permute-done((f32[9,256]{1,0:T(8,128)S(1)}, f32[9,256]{1,0:T(8,128)S(1)}, u32[]{:S(2)}, u32[]{:S(2)}) %collective-permute-start.55) | collective-permute-done | bytes 9248 | tf_op jit(solution)/shard_map/ppermute | solution.py:21
  250.3 5.0 %collective-permute-done.56 = f32[9,256]{1,0:T(8,128)S(1)} collective-permute-done((f32[9,256]{1,0:T(8,128)S(1)}, f32[9,256]{1,0:T(8,128)S(1)}, u32[]{:S(2)}, u32[]{:S(2)}) %collective-permute-start.56) | collective-permute-done | bytes 9248 | tf_op jit(solution)/shard_map/ppermute | solution.py:21
  256.5 1.6 collective-permute-start.59
  258.1 1.4 add_convert_fusion.3
  259.5 1.9 collective-permute-start.66
  263.1 1.7 add_multiply_fusion
  264.8 9.7 %collective-permute-done.66 = bf16[64,2048]{1,0:T(8,128)(2,1)S(1)} collective-permute-done((bf16[64,2048]{1,0:T(8,128)(2,1)S(1)}, bf16[64,2048]{1,0:T(8,128)(2,1)S(1)}, u32[]{:S(2)}, u32[]{:S(2)}) %collective-permute-start.66) | collective-permute-done | bytes 262176 | tf_op jit(solution)/shard_map/ppermute | solution.py:355
  (192 shorter events, 34.0 us)
Async XLA Ops:
  0.6 116.9 %collective-permute-start.1 = (bf16[128,2048]{1,0:T(8,128)(2,1)}, bf16[128,2048]{1,0:T(8,128)(2,1)}, u32[]{:S(2)}, u32[]{:S(2)}) collective-permute-start(bf16[128,2048]{1,0:T(8,128)(2,1)} %param.11), channel_id=1, source_target_pairs={{0,2},{1,3},{2,0},{3,1},{4,6},{5,7},{6,4},{7,5},{8,10},{9,11},{10,... | collective-permute-start | bytes 1572872 | tf_op jit(solution)/shard_map/ppermute | solution.py:21
  2.3 115.3 %collective-permute-start = (bf16[128,2048]{1,0:T(8,128)(2,1)}, bf16[128,2048]{1,0:T(8,128)(2,1)}, u32[]{:S(2)}, u32[]{:S(2)}) collective-permute-start(bf16[128,2048]{1,0:T(8,128)(2,1)} %param.11), channel_id=1, source_target_pairs={{0,1},{1,0},{2,3},{3,2},{4,5},{5,4},{6,7},{7,6},{8,9},{9,8},{10,11... | collective-permute-start | bytes 1572872 | tf_op jit(solution)/shard_map/ppermute | solution.py:21
  2.3 116.1 %collective-permute-start.3 = (bf16[128,2048]{1,0:T(8,128)(2,1)}, bf16[128,2048]{1,0:T(8,128)(2,1)}, u32[]{:S(2)}, u32[]{:S(2)}) collective-permute-start(bf16[128,2048]{1,0:T(8,128)(2,1)} %param.11), channel_id=1, source_target_pairs={{0,4},{1,5},{2,6},{3,7},{4,0},{5,1},{6,2},{7,3},{8,12},{9,13},{10,... | collective-permute-start | bytes 1572872 | tf_op jit(solution)/shard_map/ppermute | solution.py:21
  5.8 16.1 %collective-permute-start.10 = (bf16[2,6144]{1,0:T(2,128)(2,1)S(1)}, bf16[2,6144]{1,0:T(2,128)(2,1)S(1)}, u32[]{:S(2)}, u32[]{:S(2)}) collective-permute-start(bf16[2,6144]{1,0:T(2,128)(2,1)S(1)} %slice.152), channel_id=1, source_target_pairs={{0,1},{1,2},{2,3},{3,4},{4,5},{5,6},{6,7},{8,9},{9,10},{10,11},{11... | collective-permute-start | bytes 73736 | tf_op jit(solution)/shard_map/ppermute | solution.py:17
  24.8 13.9 %collective-permute-start.11 = (bf16[128,256]{1,0:T(8,128)(2,1)S(1)}, bf16[128,256]{1,0:T(8,128)(2,1)S(1)}, u32[]{:S(2)}, u32[]{:S(2)}) collective-permute-start(bf16[128,256]{1,0:T(8,128)(2,1)S(1)} %get-tuple-element.33), channel_id=1, source_target_pairs={{0,1},{1,0},{2,3},{3,2},{4,5},{5,4},{6,7},{7,6},{8,9},{9,8},{10,11... | collective-permute-start | bytes 196616 | tf_op jit(solution)/shard_map/ppermute | solution.py:21
  30.6 90.5 %collective-permute-start.5 = (bf16[128,2048]{1,0:T(8,128)(2,1)}, bf16[128,2048]{1,0:T(8,128)(2,1)S(1)}, u32[]{:S(2)}, u32[]{:S(2)}) collective-permute-start(bf16[128,2048]{1,0:T(8,128)(2,1)} %param.11), channel_id=1, source_target_pairs={{0,6},{1,7},{2,4},{3,5},{4,2},{5,3},{6,0},{7,1},{8,14},{9,15},{10,... | collective-permute-start | bytes 1572872 | tf_op jit(solution)/shard_map/ppermute | solution.py:21
  38.7 14.0 %collective-permute-start.12 = (bf16[128,256]{1,0:T(8,128)(2,1)S(1)}, bf16[128,256]{1,0:T(8,128)(2,1)S(1)}, u32[]{:S(2)}, u32[]{:S(2)}) collective-permute-start(bf16[128,256]{1,0:T(8,128)(2,1)S(1)} %get-tuple-element.34), channel_id=1, source_target_pairs={{0,2},{1,3},{2,0},{3,1},{4,6},{5,7},{6,4},{7,5},{8,10},{9,11},{10,... | collective-permute-start | bytes 196616 | tf_op jit(solution)/shard_map/ppermute | solution.py:21
  52.8 4.2 %collective-permute-start.13 = (bf16[128,256]{1,0:T(8,128)(2,1)S(1)}, bf16[128,256]{1,0:T(8,128)(2,1)S(1)}, u32[]{:S(2)}, u32[]{:S(2)}) collective-permute-start(bf16[128,256]{1,0:T(8,128)(2,1)S(1)} %get-tuple-element.35), channel_id=1, source_target_pairs={{0,3},{1,2},{2,1},{3,0},{4,7},{5,6},{6,5},{7,4},{8,11},{9,10},{10,... | collective-permute-start | bytes 196616 | tf_op jit(solution)/shard_map/ppermute | solution.py:21
  57.0 6.1 %collective-permute-start.14 = (bf16[128,256]{1,0:T(8,128)(2,1)S(1)}, bf16[128,256]{1,0:T(8,128)(2,1)S(1)}, u32[]{:S(2)}, u32[]{:S(2)}) collective-permute-start(bf16[128,256]{1,0:T(8,128)(2,1)S(1)} %get-tuple-element.36), channel_id=1, source_target_pairs={{0,4},{1,5},{2,6},{3,7},{4,0},{5,1},{6,2},{7,3},{8,12},{9,13},{10,... | collective-permute-start | bytes 196616 | tf_op jit(solution)/shard_map/ppermute | solution.py:21
  63.1 6.0 %collective-permute-start.15 = (bf16[128,256]{1,0:T(8,128)(2,1)S(1)}, bf16[128,256]{1,0:T(8,128)(2,1)S(1)}, u32[]{:S(2)}, u32[]{:S(2)}) collective-permute-start(bf16[128,256]{1,0:T(8,128)(2,1)S(1)} %get-tuple-element.37), channel_id=1, source_target_pairs={{0,5},{1,4},{2,7},{3,6},{4,1},{5,0},{6,3},{7,2},{8,13},{9,12},{10,... | collective-permute-start | bytes 196616 | tf_op jit(solution)/shard_map/ppermute | solution.py:21
  69.1 6.1 %collective-permute-start.16 = (bf16[128,256]{1,0:T(8,128)(2,1)S(1)}, bf16[128,256]{1,0:T(8,128)(2,1)S(1)}, u32[]{:S(2)}, u32[]{:S(2)}) collective-permute-start(bf16[128,256]{1,0:T(8,128)(2,1)S(1)} %get-tuple-element.38), channel_id=1, source_target_pairs={{0,6},{1,7},{2,4},{3,5},{4,2},{5,3},{6,0},{7,1},{8,14},{9,15},{10,... | collective-permute-start | bytes 196616 | tf_op jit(solution)/shard_map/ppermute | solution.py:21
  75.1 5.5 %collective-permute-start.17 = (bf16[128,256]{1,0:T(8,128)(2,1)S(1)}, bf16[128,256]{1,0:T(8,128)(2,1)S(1)}, u32[]{:S(2)}, u32[]{:S(2)}) collective-permute-start(bf16[128,256]{1,0:T(8,128)(2,1)S(1)} %get-tuple-element.39), channel_id=1, source_target_pairs={{0,7},{1,6},{2,5},{3,4},{4,3},{5,2},{6,1},{7,0},{8,15},{9,14},{10,... | collective-permute-start | bytes 196616 | tf_op jit(solution)/shard_map/ppermute | solution.py:21
  80.6 3.6 %collective-permute-start.25 = (bf16[128,256]{1,0:T(8,128)(2,1)S(1)}, bf16[128,256]{1,0:T(8,128)(2,1)S(1)}, u32[]{:S(2)}, u32[]{:S(2)}) collective-permute-start(bf16[128,256]{1,0:T(8,128)(2,1)S(1)} %get-tuple-element.41), channel_id=1, source_target_pairs={{0,1},{1,0},{2,3},{3,2},{4,5},{5,4},{6,7},{7,6},{8,9},{9,8},{10,11... | collective-permute-start | bytes 196616 | tf_op jit(solution)/shard_map/ppermute | solution.py:21
  84.3 4.6 %collective-permute-start.26 = (bf16[128,256]{1,0:T(8,128)(2,1)S(1)}, bf16[128,256]{1,0:T(8,128)(2,1)S(1)}, u32[]{:S(2)}, u32[]{:S(2)}) collective-permute-start(bf16[128,256]{1,0:T(8,128)(2,1)S(1)} %get-tuple-element.42), channel_id=1, source_target_pairs={{0,2},{1,3},{2,0},{3,1},{4,6},{5,7},{6,4},{7,5},{8,10},{9,11},{10,... | collective-permute-start | bytes 196616 | tf_op jit(solution)/shard_map/ppermute | solution.py:21
  88.8 4.3 %collective-permute-start.27 = (bf16[128,256]{1,0:T(8,128)(2,1)S(1)}, bf16[128,256]{1,0:T(8,128)(2,1)S(1)}, u32[]{:S(2)}, u32[]{:S(2)}) collective-permute-start(bf16[128,256]{1,0:T(8,128)(2,1)S(1)} %get-tuple-element.43), channel_id=1, source_target_pairs={{0,3},{1,2},{2,1},{3,0},{4,7},{5,6},{6,5},{7,4},{8,11},{9,10},{10,... | collective-permute-start | bytes 196616 | tf_op jit(solution)/shard_map/ppermute | solution.py:21
  93.1 6.1 %collective-permute-start.28 = (bf16[128,256]{1,0:T(8,128)(2,1)S(1)}, bf16[128,256]{1,0:T(8,128)(2,1)S(1)}, u32[]{:S(2)}, u32[]{:S(2)}) collective-permute-start(bf16[128,256]{1,0:T(8,128)(2,1)S(1)} %get-tuple-element.44), channel_id=1, source_target_pairs={{0,4},{1,5},{2,6},{3,7},{4,0},{5,1},{6,2},{7,3},{8,12},{9,13},{10,... | collective-permute-start | bytes 196616 | tf_op jit(solution)/shard_map/ppermute | solution.py:21
  99.2 5.9 %collective-permute-start.29 = (bf16[128,256]{1,0:T(8,128)(2,1)S(1)}, bf16[128,256]{1,0:T(8,128)(2,1)S(1)}, u32[]{:S(2)}, u32[]{:S(2)}) collective-permute-start(bf16[128,256]{1,0:T(8,128)(2,1)S(1)} %get-tuple-element.45), channel_id=1, source_target_pairs={{0,5},{1,4},{2,7},{3,6},{4,1},{5,0},{6,3},{7,2},{8,13},{9,12},{10,... | collective-permute-start | bytes 196616 | tf_op jit(solution)/shard_map/ppermute | solution.py:21
  105.2 6.1 %collective-permute-start.30 = (bf16[128,256]{1,0:T(8,128)(2,1)S(1)}, bf16[128,256]{1,0:T(8,128)(2,1)S(1)}, u32[]{:S(2)}, u32[]{:S(2)}) collective-permute-start(bf16[128,256]{1,0:T(8,128)(2,1)S(1)} %get-tuple-element.46), channel_id=1, source_target_pairs={{0,6},{1,7},{2,4},{3,5},{4,2},{5,3},{6,0},{7,1},{8,14},{9,15},{10,... | collective-permute-start | bytes 196616 | tf_op jit(solution)/shard_map/ppermute | solution.py:21
  111.3 5.5 %collective-permute-start.31 = (bf16[128,256]{1,0:T(8,128)(2,1)S(1)}, bf16[128,256]{1,0:T(8,128)(2,1)S(1)}, u32[]{:S(2)}, u32[]{:S(2)}) collective-permute-start(bf16[128,256]{1,0:T(8,128)(2,1)S(1)} %get-tuple-element.47), channel_id=1, source_target_pairs={{0,7},{1,6},{2,5},{3,4},{4,3},{5,2},{6,1},{7,0},{8,15},{9,14},{10,... | collective-permute-start | bytes 196616 | tf_op jit(solution)/shard_map/ppermute | solution.py:21
  116.8 7.8 %collective-permute-start.7 = (bf16[256,2048]{1,0:T(8,128)(2,1)S(1)}, bf16[256,2048]{1,0:T(8,128)(2,1)S(1)}, u32[]{:S(2)}, u32[]{:S(2)}) collective-permute-start(bf16[256,2048]{1,0:T(8,128)(2,1)S(1)} %constant_dynamic-slice_fusion), channel_id=1, source_target_pairs={{0,24},{1,25},{10,18},{11,19},{20,12},{21,13},{30,6},{31,7}} | collective-permute-start | bytes 3145736 | tf_op jit(solution)/shard_map/ppermute | solution.py:261
  117.5 5.1 %collective-permute-start.2 = (bf16[128,2048]{1,0:T(8,128)(2,1)}, bf16[128,2048]{1,0:T(8,128)(2,1)S(1)}, u32[]{:S(2)}, u32[]{:S(2)}) collective-permute-start(bf16[128,2048]{1,0:T(8,128)(2,1)} %collective-permute-done.1), channel_id=1, source_target_pairs={{0,1},{1,0},{2,3},{3,2},{4,5},{5,4},{6,7},{7,6},{8,9},{9,8},{10,11... | collective-permute-start | bytes 1572872 | tf_op jit(solution)/shard_map/ppermute | solution.py:21
  117.6 7.0 %collective-permute-start.8 = (bf16[256,2048]{1,0:T(8,128)(2,1)S(1)}, bf16[256,2048]{1,0:T(8,128)(2,1)S(1)}, u32[]{:S(2)}, u32[]{:S(2)}) collective-permute-start(bf16[256,2048]{1,0:T(8,128)(2,1)S(1)} %constant_dynamic-slice_fusion), channel_id=1, source_target_pairs={{0,16},{1,17},{10,26},{11,27},{20,4},{21,5},{30,14},{31,15}} | collective-permute-start | bytes 3145736 | tf_op jit(solution)/shard_map/ppermute | solution.py:261
  118.4 5.5 %collective-permute-start.4 = (bf16[128,2048]{1,0:T(8,128)(2,1)}, bf16[128,2048]{1,0:T(8,128)(2,1)S(1)}, u32[]{:S(2)}, u32[]{:S(2)}) collective-permute-start(bf16[128,2048]{1,0:T(8,128)(2,1)} %collective-permute-done.3), channel_id=1, source_target_pairs={{0,1},{1,0},{2,3},{3,2},{4,5},{5,4},{6,7},{7,6},{8,9},{9,8},{10,11... | collective-permute-start | bytes 1572872 | tf_op jit(solution)/shard_map/ppermute | solution.py:21
  121.1 44.9 %collective-permute-start.9 = (bf16[256,2048]{1,0:T(8,128)(2,1)S(1)}, bf16[256,2048]{1,0:T(8,128)(2,1)S(1)}, u32[]{:S(2)}, u32[]{:S(2)}) collective-permute-start(bf16[256,2048]{1,0:T(8,128)(2,1)S(1)} %constant_dynamic-slice_fusion), channel_id=1, source_target_pairs={{0,8},{1,9},{10,2},{11,3},{20,28},{21,29},{30,22},{31,23}} | collective-permute-start | bytes 3145736 | tf_op jit(solution)/shard_map/ppermute | solution.py:261
  174.5 6.5 %collective-permute-start.38 = (bf16[130,256]{1,0:T(8,128)(2,1)S(1)}, bf16[130,256]{1,0:T(8,128)(2,1)S(1)}, u32[]{:S(2)}, u32[]{:S(2)}) collective-permute-start(bf16[130,256]{1,0:T(8,128)(2,1)S(1)} %pad_maximum_fusion.17), channel_id=1, source_target_pairs={{0,7},{1,6},{2,5},{3,4},{4,3},{5,2},{6,1},{7,0},{8,15},{9,14},{10,... | collective-permute-start | bytes 199688 | tf_op jit(solution)/shard_map/ppermute | solution.py:21
  174.6 7.0 %collective-permute-start.37 = (bf16[130,256]{1,0:T(8,128)(2,1)S(1)}, bf16[130,256]{1,0:T(8,128)(2,1)S(1)}, u32[]{:S(2)}, u32[]{:S(2)}) collective-permute-start(bf16[130,256]{1,0:T(8,128)(2,1)S(1)} %pad_maximum_fusion.16), channel_id=1, source_target_pairs={{0,6},{1,7},{2,4},{3,5},{4,2},{5,3},{6,0},{7,1},{8,14},{9,15},{10,... | collective-permute-start | bytes 199688 | tf_op jit(solution)/shard_map/ppermute | solution.py:21
  175.9 10.1 %collective-permute-start.36 = (bf16[130,256]{1,0:T(8,128)(2,1)S(1)}, bf16[130,256]{1,0:T(8,128)(2,1)S(1)}, u32[]{:S(2)}, u32[]{:S(2)}) collective-permute-start(bf16[130,256]{1,0:T(8,128)(2,1)S(1)} %pad_maximum_fusion.15), channel_id=1, source_target_pairs={{0,5},{1,4},{2,7},{3,6},{4,1},{5,0},{6,3},{7,2},{8,13},{9,12},{10,... | collective-permute-start | bytes 199688 | tf_op jit(solution)/shard_map/ppermute | solution.py:21
  176.0 11.7 %collective-permute-start.35 = (bf16[130,256]{1,0:T(8,128)(2,1)S(1)}, bf16[130,256]{1,0:T(8,128)(2,1)S(1)}, u32[]{:S(2)}, u32[]{:S(2)}) collective-permute-start(bf16[130,256]{1,0:T(8,128)(2,1)S(1)} %pad_maximum_fusion.14), channel_id=1, source_target_pairs={{0,4},{1,5},{2,6},{3,7},{4,0},{5,1},{6,2},{7,3},{8,12},{9,13},{10,... | collective-permute-start | bytes 199688 | tf_op jit(solution)/shard_map/ppermute | solution.py:21
  180.8 8.8 %collective-permute-start.34 = (bf16[130,256]{1,0:T(8,128)(2,1)S(1)}, bf16[130,256]{1,0:T(8,128)(2,1)S(1)}, u32[]{:S(2)}, u32[]{:S(2)}) collective-permute-start(bf16[130,256]{1,0:T(8,128)(2,1)S(1)} %pad_maximum_fusion.13), channel_id=1, source_target_pairs={{0,3},{1,2},{2,1},{3,0},{4,7},{5,6},{6,5},{7,4},{8,11},{9,10},{10,... | collective-permute-start | bytes 199688 | tf_op jit(solution)/shard_map/ppermute | solution.py:21
  180.9 8.7 %collective-permute-start.33 = (bf16[130,256]{1,0:T(8,128)(2,1)S(1)}, bf16[130,256]{1,0:T(8,128)(2,1)S(1)}, u32[]{:S(2)}, u32[]{:S(2)}) collective-permute-start(bf16[130,256]{1,0:T(8,128)(2,1)S(1)} %pad_maximum_fusion.12), channel_id=1, source_target_pairs={{0,2},{1,3},{2,0},{3,1},{4,6},{5,7},{6,4},{7,5},{8,10},{9,11},{10,... | collective-permute-start | bytes 199688 | tf_op jit(solution)/shard_map/ppermute | solution.py:21
  181.5 10.8 %collective-permute-start.32 = (bf16[130,256]{1,0:T(8,128)(2,1)S(1)}, bf16[130,256]{1,0:T(8,128)(2,1)S(1)}, u32[]{:S(2)}, u32[]{:S(2)}) collective-permute-start(bf16[130,256]{1,0:T(8,128)(2,1)S(1)} %pad_maximum_fusion.11), channel_id=1, source_target_pairs={{0,1},{1,0},{2,3},{3,2},{4,5},{5,4},{6,7},{7,6},{8,9},{9,8},{10,11... | collective-permute-start | bytes 199688 | tf_op jit(solution)/shard_map/ppermute | solution.py:21
  186.0 6.3 %collective-permute-start.24 = (bf16[130,256]{1,0:T(8,128)(2,1)S(1)}, bf16[130,256]{1,0:T(8,128)(2,1)S(1)}, u32[]{:S(2)}, u32[]{:S(2)}) collective-permute-start(bf16[130,256]{1,0:T(8,128)(2,1)S(1)} %pad_maximum_fusion.9), channel_id=1, source_target_pairs={{0,7},{1,6},{2,5},{3,4},{4,3},{5,2},{6,1},{7,0},{8,15},{9,14},{10,... | collective-permute-start | bytes 199688 | tf_op jit(solution)/shard_map/ppermute | solution.py:21
  187.7 7.0 %collective-permute-start.23 = (bf16[130,256]{1,0:T(8,128)(2,1)S(1)}, bf16[130,256]{1,0:T(8,128)(2,1)S(1)}, u32[]{:S(2)}, u32[]{:S(2)}) collective-permute-start(bf16[130,256]{1,0:T(8,128)(2,1)S(1)} %pad_maximum_fusion.8), channel_id=1, source_target_pairs={{0,6},{1,7},{2,4},{3,5},{4,2},{5,3},{6,0},{7,1},{8,14},{9,15},{10,... | collective-permute-start | bytes 199688 | tf_op jit(solution)/shard_map/ppermute | solution.py:21
  189.5 8.8 %collective-permute-start.22 = (bf16[130,256]{1,0:T(8,128)(2,1)S(1)}, bf16[130,256]{1,0:T(8,128)(2,1)S(1)}, u32[]{:S(2)}, u32[]{:S(2)}) collective-permute-start(bf16[130,256]{1,0:T(8,128)(2,1)S(1)} %pad_maximum_fusion.7), channel_id=1, source_target_pairs={{0,5},{1,4},{2,7},{3,6},{4,1},{5,0},{6,3},{7,2},{8,13},{9,12},{10,... | collective-permute-start | bytes 199688 | tf_op jit(solution)/shard_map/ppermute | solution.py:21
  189.6 10.3 %collective-permute-start.21 = (bf16[130,256]{1,0:T(8,128)(2,1)S(1)}, bf16[130,256]{1,0:T(8,128)(2,1)S(1)}, u32[]{:S(2)}, u32[]{:S(2)}) collective-permute-start(bf16[130,256]{1,0:T(8,128)(2,1)S(1)} %pad_maximum_fusion.6), channel_id=1, source_target_pairs={{0,4},{1,5},{2,6},{3,7},{4,0},{5,1},{6,2},{7,3},{8,12},{9,13},{10,... | collective-permute-start | bytes 199688 | tf_op jit(solution)/shard_map/ppermute | solution.py:21
  192.3 7.6 %collective-permute-start.20 = (bf16[130,256]{1,0:T(8,128)(2,1)S(1)}, bf16[130,256]{1,0:T(8,128)(2,1)S(1)}, u32[]{:S(2)}, u32[]{:S(2)}) collective-permute-start(bf16[130,256]{1,0:T(8,128)(2,1)S(1)} %pad_maximum_fusion.5), channel_id=1, source_target_pairs={{0,3},{1,2},{2,1},{3,0},{4,7},{5,6},{6,5},{7,4},{8,11},{9,10},{10,... | collective-permute-start | bytes 199688 | tf_op jit(solution)/shard_map/ppermute | solution.py:21
  192.3 8.9 %collective-permute-start.19 = (bf16[130,256]{1,0:T(8,128)(2,1)S(1)}, bf16[130,256]{1,0:T(8,128)(2,1)S(1)}, u32[]{:S(2)}, u32[]{:S(2)}) collective-permute-start(bf16[130,256]{1,0:T(8,128)(2,1)S(1)} %pad_maximum_fusion.4), channel_id=1, source_target_pairs={{0,2},{1,3},{2,0},{3,1},{4,6},{5,7},{6,4},{7,5},{8,10},{9,11},{10,... | collective-permute-start | bytes 199688 | tf_op jit(solution)/shard_map/ppermute | solution.py:21
  194.7 6.5 %collective-permute-start.18 = (bf16[130,256]{1,0:T(8,128)(2,1)S(1)}, bf16[130,256]{1,0:T(8,128)(2,1)S(1)}, u32[]{:S(2)}, u32[]{:S(2)}) collective-permute-start(bf16[130,256]{1,0:T(8,128)(2,1)S(1)} %pad_maximum_fusion.3), channel_id=1, source_target_pairs={{0,1},{1,0},{2,3},{3,2},{4,5},{5,4},{6,7},{7,6},{8,9},{9,8},{10,11... | collective-permute-start | bytes 199688 | tf_op jit(solution)/shard_map/ppermute | solution.py:21
  205.2 5.7 %collective-permute-start.40 = (f32[9,256]{1,0:T(8,128)S(1)}, f32[9,256]{1,0:T(8,128)S(1)}, u32[]{:S(2)}, u32[]{:S(2)}) collective-permute-start(f32[9,256]{1,0:T(8,128)S(1)} %get-tuple-element.52), channel_id=1, source_target_pairs={{0,1},{1,0},{2,3},{3,2},{4,5},{5,4},{6,7},{7,6},{8,9},{9,8},{10,11... | collective-permute-start | bytes 27656 | tf_op jit(solution)/shard_map/ppermute | solution.py:21
  205.2 7.2 %collective-permute-start.41 = (f32[9,256]{1,0:T(8,128)S(1)}, f32[9,256]{1,0:T(8,128)S(1)}, u32[]{:S(2)}, u32[]{:S(2)}) collective-permute-start(f32[9,256]{1,0:T(8,128)S(1)} %get-tuple-element.53), channel_id=1, source_target_pairs={{0,2},{1,3},{2,0},{3,1},{4,6},{5,7},{6,4},{7,5},{8,10},{9,11},{10,... | collective-permute-start | bytes 27656 | tf_op jit(solution)/shard_map/ppermute | solution.py:21
  206.5 9.0 %collective-permute-start.42 = (f32[9,256]{1,0:T(8,128)S(1)}, f32[9,256]{1,0:T(8,128)S(1)}, u32[]{:S(2)}, u32[]{:S(2)}) collective-permute-start(f32[9,256]{1,0:T(8,128)S(1)} %get-tuple-element.54), channel_id=1, source_target_pairs={{0,3},{1,2},{2,1},{3,0},{4,7},{5,6},{6,5},{7,4},{8,11},{9,10},{10,... | collective-permute-start | bytes 27656 | tf_op jit(solution)/shard_map/ppermute | solution.py:21
  208.4 7.1 %collective-permute-start.43 = (f32[9,256]{1,0:T(8,128)S(1)}, f32[9,256]{1,0:T(8,128)S(1)}, u32[]{:S(2)}, u32[]{:S(2)}) collective-permute-start(f32[9,256]{1,0:T(8,128)S(1)} %get-tuple-element.55), channel_id=1, source_target_pairs={{0,4},{1,5},{2,6},{3,7},{4,0},{5,1},{6,2},{7,3},{8,12},{9,13},{10,... | collective-permute-start | bytes 27656 | tf_op jit(solution)/shard_map/ppermute | solution.py:21
  208.7 7.3 %collective-permute-start.44 = (f32[9,256]{1,0:T(8,128)S(1)}, f32[9,256]{1,0:T(8,128)S(1)}, u32[]{:S(2)}, u32[]{:S(2)}) collective-permute-start(f32[9,256]{1,0:T(8,128)S(1)} %get-tuple-element.56), channel_id=1, source_target_pairs={{0,5},{1,4},{2,7},{3,6},{4,1},{5,0},{6,3},{7,2},{8,13},{9,12},{10,... | collective-permute-start | bytes 27656 | tf_op jit(solution)/shard_map/ppermute | solution.py:21
  211.0 5.5 %collective-permute-start.45 = (f32[9,256]{1,0:T(8,128)S(1)}, f32[9,256]{1,0:T(8,128)S(1)}, u32[]{:S(2)}, u32[]{:S(2)}) collective-permute-start(f32[9,256]{1,0:T(8,128)S(1)} %get-tuple-element.57), channel_id=1, source_target_pairs={{0,6},{1,7},{2,4},{3,5},{4,2},{5,3},{6,0},{7,1},{8,14},{9,15},{10,... | collective-permute-start | bytes 27656 | tf_op jit(solution)/shard_map/ppermute | solution.py:21
  212.4 5.0 %collective-permute-start.46 = (f32[9,256]{1,0:T(8,128)S(1)}, f32[9,256]{1,0:T(8,128)S(1)}, u32[]{:S(2)}, u32[]{:S(2)}) collective-permute-start(f32[9,256]{1,0:T(8,128)S(1)} %get-tuple-element.58), channel_id=1, source_target_pairs={{0,7},{1,6},{2,5},{3,4},{4,3},{5,2},{6,1},{7,0},{8,15},{9,14},{10,... | collective-permute-start | bytes 27656 | tf_op jit(solution)/shard_map/ppermute | solution.py:21
  215.5 9.7 %collective-permute-start.60 = (f32[1,256]{1,0:T(1,128)S(1)}, f32[1,256]{1,0:T(1,128)S(1)}, u32[]{:S(2)}, u32[]{:S(2)}) collective-permute-start(f32[1,256]{1,0:T(1,128)S(1)} %bitcast.90), channel_id=1, source_target_pairs={{0,8},{8,0},{16,24},{24,16},{1,9},{9,1},{17,25},{25,17},{2,10},{10... | collective-permute-start | bytes 3080 | tf_op jit(solution)/shard_map/ppermute | solution.py:21
  215.5 11.4 %collective-permute-start.61 = (f32[1,256]{1,0:T(1,128)S(1)}, f32[1,256]{1,0:T(1,128)S(1)}, u32[]{:S(2)}, u32[]{:S(2)}) collective-permute-start(f32[1,256]{1,0:T(1,128)S(1)} %bitcast.91), channel_id=1, source_target_pairs={{0,16},{8,24},{16,0},{24,8},{1,17},{9,25},{17,1},{25,9},{2,18},{10... | collective-permute-start | bytes 3080 | tf_op jit(solution)/shard_map/ppermute | solution.py:21
  217.4 4.3 %collective-permute-start.47 = (f32[9,256]{1,0:T(8,128)S(1)}, f32[9,256]{1,0:T(8,128)S(1)}, u32[]{:S(2)}, u32[]{:S(2)}) collective-permute-start(f32[9,256]{1,0:T(8,128)S(1)} %add_add_fusion), channel_id=1, source_target_pairs={{0,8},{8,0},{16,24},{24,16},{1,9},{9,1},{17,25},{25,17},{2,10},{10... | collective-permute-start | bytes 27656 | tf_op jit(solution)/shard_map/ppermute | solution.py:21
  217.7 5.7 %collective-permute-start.48 = (f32[9,256]{1,0:T(8,128)S(1)}, f32[9,256]{1,0:T(8,128)S(1)}, u32[]{:S(2)}, u32[]{:S(2)}) collective-permute-start(f32[9,256]{1,0:T(8,128)S(1)} %add_add_fusion), channel_id=1, source_target_pairs={{0,16},{8,24},{16,0},{24,8},{1,17},{9,25},{17,1},{25,9},{2,18},{10... | collective-permute-start | bytes 27656 | tf_op jit(solution)/shard_map/ppermute | solution.py:21
  219.7 4.6 %collective-permute-start.49 = (f32[9,256]{1,0:T(8,128)S(1)}, f32[9,256]{1,0:T(8,128)S(1)}, u32[]{:S(2)}, u32[]{:S(2)}) collective-permute-start(f32[9,256]{1,0:T(8,128)S(1)} %add_add_fusion), channel_id=1, source_target_pairs={{0,24},{8,16},{16,8},{24,0},{1,25},{9,17},{17,9},{25,1},{2,26},{10... | collective-permute-start | bytes 27656 | tf_op jit(solution)/shard_map/ppermute | solution.py:21
  221.7 6.2 %collective-permute-start.62 = (f32[1,256]{1,0:T(1,128)S(1)}, f32[1,256]{1,0:T(1,128)S(1)}, u32[]{:S(2)}, u32[]{:S(2)}) collective-permute-start(f32[1,256]{1,0:T(1,128)S(1)} %bitcast.92), channel_id=1, source_target_pairs={{0,24},{8,16},{16,8},{24,0},{1,25},{9,17},{17,9},{25,1},{2,26},{10... | collective-permute-start | bytes 3080 | tf_op jit(solution)/shard_map/ppermute | solution.py:21
  223.4 33.1 %collective-permute-start.63 = (bf16[64,2048]{1,0:T(8,128)(2,1)}, bf16[64,2048]{1,0:T(8,128)(2,1)}, u32[]{:S(2)}, u32[]{:S(2)}) collective-permute-start(bf16[64,2048]{1,0:T(8,128)(2,1)} %get-tuple-element.69), channel_id=1, source_target_pairs={{0,8},{8,0},{16,24},{24,16},{1,9},{9,1},{17,25},{25,17},{2,10},{10... | collective-permute-start | bytes 786440 | tf_op jit(solution)/shard_map/ppermute | solution.py:21
  224.3 33.8 %collective-permute-start.64 = (bf16[64,2048]{1,0:T(8,128)(2,1)}, bf16[64,2048]{1,0:T(8,128)(2,1)}, u32[]{:S(2)}, u32[]{:S(2)}) collective-permute-start(bf16[64,2048]{1,0:T(8,128)(2,1)} %get-tuple-element.71), channel_id=1, source_target_pairs={{0,16},{8,24},{16,0},{24,8},{1,17},{9,25},{17,1},{25,9},{2,18},{10... | collective-permute-start | bytes 786440 | tf_op jit(solution)/shard_map/ppermute | solution.py:21
  225.2 32.9 %collective-permute-start.65 = (bf16[64,2048]{1,0:T(8,128)(2,1)}, bf16[64,2048]{1,0:T(8,128)(2,1)}, u32[]{:S(2)}, u32[]{:S(2)}) collective-permute-start(bf16[64,2048]{1,0:T(8,128)(2,1)} %get-tuple-element.70), channel_id=1, source_target_pairs={{0,24},{8,16},{16,8},{24,0},{1,25},{9,17},{17,9},{25,1},{2,26},{10... | collective-permute-start | bytes 786440 | tf_op jit(solution)/shard_map/ppermute | solution.py:21
  227.0 35.2 %collective-permute-start.57 = (bf16[256,256]{1,0:T(8,128)(2,1)}, bf16[256,256]{1,0:T(8,128)(2,1)S(1)}, u32[]{:S(2)}, u32[]{:S(2)}) collective-permute-start(bf16[256,256]{1,0:T(8,128)(2,1)} %get-tuple-element.74), channel_id=1, source_target_pairs={{0,8},{8,0},{16,24},{24,16},{1,9},{9,1},{17,25},{25,17},{2,10},{10... | collective-permute-start | bytes 393224 | tf_op jit(solution)/shard_map/ppermute | solution.py:21
  229.1 3.7 %collective-permute-start.51 = (f32[9,256]{1,0:T(8,128)S(1)}, f32[9,256]{1,0:T(8,128)S(1)}, u32[]{:S(2)}, u32[]{:S(2)}) collective-permute-start(f32[9,256]{1,0:T(8,128)S(1)} %get-tuple-element.62), channel_id=1, source_target_pairs={{0,2},{1,3},{2,0},{3,1},{4,6},{5,7},{6,4},{7,5},{8,10},{9,11},{10,... | collective-permute-start | bytes 27656 | tf_op jit(solution)/shard_map/ppermute | solution.py:21
  232.8 3.2 %collective-permute-start.52 = (f32[9,256]{1,0:T(8,128)S(1)}, f32[9,256]{1,0:T(8,128)S(1)}, u32[]{:S(2)}, u32[]{:S(2)}) collective-permute-start(f32[9,256]{1,0:T(8,128)S(1)} %get-tuple-element.62), channel_id=1, source_target_pairs={{0,3},{1,2},{2,1},{3,0},{4,7},{5,6},{6,5},{7,4},{8,11},{9,10},{10,... | collective-permute-start | bytes 27656 | tf_op jit(solution)/shard_map/ppermute | solution.py:21
  236.0 4.6 %collective-permute-start.53 = (f32[9,256]{1,0:T(8,128)S(1)}, f32[9,256]{1,0:T(8,128)S(1)}, u32[]{:S(2)}, u32[]{:S(2)}) collective-permute-start(f32[9,256]{1,0:T(8,128)S(1)} %get-tuple-element.62), channel_id=1, source_target_pairs={{0,4},{1,5},{2,6},{3,7},{4,0},{5,1},{6,2},{7,3},{8,12},{9,13},{10,... | collective-permute-start | bytes 27656 | tf_op jit(solution)/shard_map/ppermute | solution.py:21
  240.6 4.1 %collective-permute-start.54 = (f32[9,256]{1,0:T(8,128)S(1)}, f32[9,256]{1,0:T(8,128)S(1)}, u32[]{:S(2)}, u32[]{:S(2)}) collective-permute-start(f32[9,256]{1,0:T(8,128)S(1)} %get-tuple-element.62), channel_id=1, source_target_pairs={{0,5},{1,4},{2,7},{3,6},{4,1},{5,0},{6,3},{7,2},{8,13},{9,12},{10,... | collective-permute-start | bytes 27656 | tf_op jit(solution)/shard_map/ppermute | solution.py:21
  244.7 5.5 %collective-permute-start.55 = (f32[9,256]{1,0:T(8,128)S(1)}, f32[9,256]{1,0:T(8,128)S(1)}, u32[]{:S(2)}, u32[]{:S(2)}) collective-permute-start(f32[9,256]{1,0:T(8,128)S(1)} %get-tuple-element.62), channel_id=1, source_target_pairs={{0,6},{1,7},{2,4},{3,5},{4,2},{5,3},{6,0},{7,1},{8,14},{9,15},{10,... | collective-permute-start | bytes 27656 | tf_op jit(solution)/shard_map/ppermute | solution.py:21
  250.2 5.0 %collective-permute-start.56 = (f32[9,256]{1,0:T(8,128)S(1)}, f32[9,256]{1,0:T(8,128)S(1)}, u32[]{:S(2)}, u32[]{:S(2)}) collective-permute-start(f32[9,256]{1,0:T(8,128)S(1)} %get-tuple-element.62), channel_id=1, source_target_pairs={{0,7},{1,6},{2,5},{3,4},{4,3},{5,2},{6,1},{7,0},{8,15},{9,14},{10,... | collective-permute-start | bytes 27656 | tf_op jit(solution)/shard_map/ppermute | solution.py:21
  255.2 7.9 %collective-permute-start.58 = (bf16[256,256]{1,0:T(8,128)(2,1)}, bf16[256,256]{1,0:T(8,128)(2,1)}, u32[]{:S(2)}, u32[]{:S(2)}) collective-permute-start(bf16[256,256]{1,0:T(8,128)(2,1)} %get-tuple-element.76), channel_id=1, source_target_pairs={{0,16},{8,24},{16,0},{24,8},{1,17},{9,25},{17,1},{25,9},{2,18},{10... | collective-permute-start | bytes 393224 | tf_op jit(solution)/shard_map/ppermute | solution.py:21
  256.5 6.6 %collective-permute-start.59 = (bf16[256,256]{1,0:T(8,128)(2,1)}, bf16[256,256]{1,0:T(8,128)(2,1)S(1)}, u32[]{:S(2)}, u32[]{:S(2)}) collective-permute-start(bf16[256,256]{1,0:T(8,128)(2,1)} %get-tuple-element.75), channel_id=1, source_target_pairs={{0,24},{8,16},{16,8},{24,0},{1,25},{9,17},{17,9},{25,1},{2,26},{10... | collective-permute-start | bytes 393224 | tf_op jit(solution)/shard_map/ppermute | solution.py:21
  259.5 15.0 %collective-permute-start.66 = (bf16[64,2048]{1,0:T(8,128)(2,1)S(1)}, bf16[64,2048]{1,0:T(8,128)(2,1)S(1)}, u32[]{:S(2)}, u32[]{:S(2)}) collective-permute-start(bf16[64,2048]{1,0:T(8,128)(2,1)S(1)} %add_convert_fusion.3), channel_id=1, source_target_pairs={{0,0},{1,4},{2,8},{3,12},{4,16},{5,20},{6,24},{7,28},{8,1},{9,5},{... | collective-permute-start | bytes 786440 | tf_op jit(solution)/shard_map/ppermute | solution.py:355
  (14 other events, 180.4 us)

commit v2 on v1

v2 whole, which is shorter than its diff:
```python
import math

import jax
import jax.numpy as jnp
from jax import lax
from jax.experimental import pallas as pl
from jax.experimental.pallas import tpu as pltpu
from jax.sharding import PartitionSpec as P

BF16 = jnp.bfloat16
F32 = jnp.float32


def swapped(value, axis, mask):
    return lax.ppermute(value, axis, [(i, i ^ mask) for i in range(lax.axis_size(axis))])


def rows_down(values, steps):
    row = lax.broadcasted_iota(jnp.int32, values.shape, 0)
    return jnp.where(row < steps, 0.0, pltpu.roll(values, steps, axis=0))


def rows_up(values, steps):
    count = values.shape[0]
    row = lax.broadcasted_iota(jnp.int32, values.shape, 0)
    return jnp.where(row >= count - steps, 0.0, pltpu.roll(values, count - steps, axis=0))


def flat(ref):
    return ref[...].reshape(-1, ref.shape[-1]).astype(F32)


def short_kernel(query_in, key_in, value_in, taps_ref, query_ref, keyed_ref, valued_ref, product_ref):
    def mixed(ref, stream):
        values = flat(ref)
        taps = taps_ref[stream]
        total = taps[0:1] * values + taps[1:2] * rows_down(values, 1)
        return (total + taps[2:3] * rows_down(values, 2)).astype(BF16)

    query_ref[...] = mixed(query_in, 0)
    keyed, valued = (mixed(key_in, 1), mixed(value_in, 2))
    keyed_ref[...] = keyed
    valued_ref[...] = valued
    product_ref[...] = (keyed.astype(F32) * valued.astype(F32)).astype(BF16)


def final_kernel(*refs):
    query_in, key_in, value_in, taps_ref, gate_grad, long_ref, back_ref, keyed_ref, valued_ref = refs[:9]
    out_refs, sums_ref = refs[9:12], refs[12]
    back = back_ref[...].astype(F32)
    for stream, ref in enumerate((query_in, key_in, value_in)):
        if stream == 0:
            grad = gate_grad[...].astype(F32) * long_ref[...].astype(F32)
        elif stream == 1:
            grad = back * valued_ref[...].astype(F32)
        else:
            grad = back * keyed_ref[...].astype(F32)
        taps = taps_ref[stream]
        total = taps[0:1] * grad + taps[1:2] * rows_up(grad, 1) + taps[2:3] * rows_up(grad, 2)
        out_refs[stream][...] = total.astype(BF16).reshape(out_refs[stream].shape)
        values = flat(ref)
        for j in range(3):
            moved = rows_down(values, j) if j else values
            sums_ref[stream, j : j + 1, :] = jnp.sum(grad * moved, 0, keepdims=True)


def cost(*arrays):
    moved = sum(math.prod(a.shape) * a.dtype.itemsize for a in arrays)
    return pl.CostEstimate(flops=8 * moved, transcendentals=0, bytes_accessed=moved)


def stream_specs(parts, rows, tile):
    return [
        pl.BlockSpec((parts, None, rows, tile), lambda j, s=s: (0, s, 0, j)) for s in range(3)
    ]


def short_convs(streams, taps):
    parts, _, rows, blk = streams.shape
    seq_len = parts * rows
    tile = min(128, blk)
    plane = pl.BlockSpec((seq_len, tile), lambda j: (0, j))
    return pl.pallas_call(
        short_kernel,
        out_shape=[jax.ShapeDtypeStruct((seq_len, blk), BF16)] * 4,
        grid=(blk // tile,),
        in_specs=stream_specs(parts, rows, tile)
        + [pl.BlockSpec((3, 3, tile), lambda j: (0, 0, j))],
        out_specs=[plane] * 4,
        compiler_params=pltpu.CompilerParams(vmem_limit_bytes=48 * 2**20),
        cost_estimate=cost(streams, streams),
        name="short_convs",
    )(streams, streams, streams, taps)


def stream_grads(streams, taps, grad_gate, long_out, back, keyed, valued):
    parts, _, rows, blk = streams.shape
    seq_len = parts * rows
    tile = min(128, blk)
    plane = pl.BlockSpec((seq_len, tile), lambda j: (0, j))
    piece = pl.BlockSpec((parts, rows, tile), lambda j: (0, 0, j))
    rank_three = pl.BlockSpec((3, 3, tile), lambda j: (0, 0, j))
    return pl.pallas_call(
        final_kernel,
        out_shape=[jax.ShapeDtypeStruct((parts, rows, blk), BF16)] * 3
        + [jax.ShapeDtypeStruct((3, 3, blk), F32)],
        grid=(blk // tile,),
        in_specs=stream_specs(parts, rows, tile) + [rank_three] + [plane] * 5,
        out_specs=[piece] * 3 + [rank_three],
        compiler_params=pltpu.CompilerParams(vmem_limit_bytes=56 * 2**20),
        cost_estimate=cost(streams, streams),
        name="stream_grads",
    )(streams, streams, streams, taps, grad_gate, long_out, back, keyed, valued)


def table(first, freqs, seq_len):
    places = jnp.arange(seq_len)
    inner = min(32, freqs)
    outer = freqs // inner

    def waves(odd):
        phases = odd[:, None] * places[None, :] % (4 * seq_len)
        angles = phases.astype(F32) * (2.0 * math.pi / (4 * seq_len))
        return (jnp.cos(angles), jnp.sin(angles))

    outer_cos, outer_sin = waves(2 * (first + inner * jnp.arange(outer)))
    inner_cos, inner_sin = waves(2 * jnp.arange(inner) + 1)
    oc, os = (outer_cos[:, None], outer_sin[:, None])
    ic, is_ = (inner_cos[None], inner_sin[None])
    both = jnp.stack([oc * ic - os * is_, -(os * ic + oc * is_)])
    return both.astype(BF16).reshape(2 * freqs, seq_len)


def dot(left, right, left_dim, right_dim):
    return lax.dot_general(
        left, right, (((left_dim,), (right_dim,)), ((), ())), preferred_element_type=F32
    )


def spectral_product(left, right, conjugate_left):
    half = left.shape[0] // 2
    left_re, left_im = (left[:half], left[half:])
    right_re, right_im = (right[:half], right[half:])
    if conjugate_left:
        real = left_re * right_re + left_im * right_im
        imag = left_re * right_im - left_im * right_re
    else:
        real = left_re * right_re - left_im * right_im
        imag = left_re * right_im + left_im * right_re
    return jnp.concatenate([real, imag], 0).astype(BF16)


def long_terms(first, freqs, long_filter, product, grad_long):
    waves = table(first, freqs, product.shape[0])
    filter_spec = dot(waves, long_filter, 1, 1)
    product_spec = dot(waves, product, 1, 0)
    grad_spec = dot(waves, grad_long, 1, 0)
    out = dot(waves, spectral_product(filter_spec, product_spec, False), 0, 0)
    back = dot(waves, spectral_product(filter_spec, grad_spec, True), 0, 0)
    lag_grad = dot(spectral_product(product_spec, grad_spec, True), waves, 0, 0)
    return (out, back, lag_grad)


def own_rows(weights, parts_dp, parts_ctx):
    ratio = parts_ctx // parts_dp
    context = lax.axis_index("context")
    block = weights.shape[0] // ratio
    half = lax.dynamic_slice_in_dim(weights, (context % ratio) * block, block, 0)
    holder = context // ratio
    found = half
    for k in range(1, parts_dp):
        pairs = [
            ((c // ratio) * parts_ctx + c, ((c // ratio) ^ k) * parts_ctx + c)
            for c in range(parts_ctx)
        ]
        sent = lax.ppermute(half, ("dp", "context"), pairs)
        found = jnp.where(lax.axis_index("dp") == (holder ^ k), sent, found)
    return found


def summed_blocks(value, axis, dim):
    count = lax.axis_size(axis)
    size = value.shape[dim] // count
    me = lax.axis_index(axis)
    total = lax.dynamic_slice_in_dim(value, me * size, size, dim)
    for k in range(1, count):
        sent = lax.dynamic_slice_in_dim(value, (me ^ k) * size, size, dim).astype(BF16)
        total = total + swapped(sent, axis, k).astype(F32)
    return total


def body(projected, short_taps, long_filter, skip_gain, out_proj, cotangent):
    rows, width = projected.shape
    chans = width // 3
    parts_dp, parts = (lax.axis_size("dp"), lax.axis_size("context"))
    blk = chans // parts
    seq_len = rows * parts
    me = lax.axis_index("context")
    scale_factor = 1.0 / math.sqrt(seq_len * parts_dp)

    groups = [list(range(core, parts, 2)) for core in range(2)]
    cot_own = lax.all_gather(cotangent, "context", axis=0, tiled=True, axis_index_groups=groups)
    cot_other = swapped(cot_own, "context", 1)
    weights = own_rows(out_proj, parts_dp, parts)
    blocks = projected.reshape(rows, 3, parts, blk).transpose(2, 1, 0, 3)
    streams = lax.all_to_all(blocks, "context", split_axis=0, concat_axis=0, tiled=True)
    taps = lax.dynamic_slice_in_dim(short_taps.reshape(3, 3, chans), me * blk, blk, 2)
    taps = taps.transpose(1, 0, 2)
    query, keyed, valued, product = short_convs(streams, taps)

    first_core = me % 2 == 0

    def by_core(own, other):
        shape = (parts // 2, 1, rows, -1)
        even = jnp.where(first_core, own, other).reshape(shape)
        odd = jnp.where(first_core, other, own).reshape(shape)
        return jnp.concatenate([even, odd], 1).reshape(seq_len, -1)

    grad_gate = by_core(
        dot(cot_own, weights, 1, 1).astype(BF16), dot(cot_other, weights, 1, 1).astype(BF16)
    )
    grad_long = (grad_gate.astype(F32) * query.astype(F32)).astype(BF16)
    filter_b = long_filter.astype(BF16)
    freqs = seq_len if seq_len <= 1024 else 256
    if freqs == seq_len:
        terms = long_terms(0, freqs, filter_b, product, grad_long)
    else:

        def step(carry, first):
            new = long_terms(first, freqs, filter_b, product, grad_long)
            return (tuple(a + b for a, b in zip(carry, new)), None)

        zero = jnp.zeros((seq_len, blk), F32)
        start = (zero, zero, jnp.zeros((blk, seq_len), F32))
        terms, _ = lax.scan(step, start, jnp.arange(0, seq_len, freqs))
    out_sum, back_sum, lag_sum = terms
    inverse = 1.0 / seq_len
    product_f, grad_long_f = (product.astype(F32), grad_long.astype(F32))
    long_out = (out_sum * inverse + skip_gain[None, :] * product_f).astype(BF16)
    grad_product = (back_sum * inverse + skip_gain[None, :] * grad_long_f).astype(BF16)
    gate = (query.astype(F32) * long_out.astype(F32)).astype(BF16)

    *grads, tap_sums = stream_grads(
        streams, taps, grad_gate, long_out, grad_product, keyed, valued
    )
    sent = jnp.stack(grads, 1)
    back = lax.all_to_all(sent, "context", split_axis=0, concat_axis=0, tiled=True)
    grad_inputs = back.transpose(2, 1, 0, 3).reshape(rows, width)

    pairs = gate.reshape(parts // 2, 2, rows, blk)
    even, odd = (pairs[:, i].reshape(seq_len // 2, blk) for i in range(2))
    proj_sum = dot(jnp.where(first_core, even, odd), cot_own, 0, 0) + dot(
        jnp.where(first_core, odd, even), cot_other, 0, 0
    )
    proj_part = summed_blocks(proj_sum, "dp", 0).astype(BF16)
    rank = [
        (d * parts + c, c * parts_dp + d) for d in range(parts_dp) for c in range(parts)
    ]
    grad_proj = lax.ppermute(proj_part, ("dp", "context"), rank).astype(F32) * scale_factor
    grad_filter = summed_blocks(lag_sum, "dp", 1) * (scale_factor * inverse)

    skip_sum = jnp.sum(grad_long_f * product_f, 0, keepdims=True)
    small = jnp.concatenate([tap_sums.reshape(9, blk), skip_sum], 0)
    small_all = small
    for k in range(1, parts_dp):
        small_all = small_all + swapped(small, "dp", k)
    small_all = small_all * scale_factor
    grad_skip = small_all[9]
    every = jnp.broadcast_to(small_all[None, :9], (parts, 9, blk))
    taps_out = lax.all_to_all(every, "context", split_axis=0, concat_axis=0, tiled=True)
    grad_taps = taps_out.reshape(parts, 3, 3, blk).transpose(2, 1, 0, 3).reshape(3, width)
    return (grad_inputs, grad_taps, grad_filter, grad_skip, grad_proj)


def solution(mesh):
    placed = (
        P(("dp", "context"), None),
        P(),
        P("context", None),
        P("context"),
        P("dp", None),
        P(("dp", "context"), None),
    )
    return jax.shard_map(
        body,
        mesh=mesh,
        in_specs=placed,
        out_specs=(
            P(("dp", "context"), None),
            P(),
            P("context", "dp"),
            P("context"),
            P(("dp", "context"), None),
        ),
        check_vma=False,
    )
```

time: 276 us -> 203 us (0.74)
  the two profiles are of different devices: /device:TPU:2 before, /device:TPU:5 now
where the time goes in v2:
time: 203 us; the launch traced here: 202 us
  waiting for transfers between devices  93 us (46%)
  starting transfers between devices  36.1 us (18%)
  matrix products  22.6 us (11%)
  local copies, waits for them, and re-layouts  16.4 us (8%)
  between operations  14.5 us (7%)
  other arithmetic  12.3 us (6%)
  Pallas kernels  7.08 us (3%)
    all_gather x1, waiting for transfers between devices, body(): lax.all_gather(cotangent, 'context', axis=0, tiled=True, axis_index_group...  65.3 us
    dot_general x10, matrix products, dot(): lax.dot_general(left, right, (((left_dim,), (right_dim,)), ((), ())), pre...  22.6 us
    ppermute x1, waiting for transfers between devices, body(): lax.ppermute(proj_part, ('dp', 'context'), rank).astype(F32) * scale_factor  15.4 us
    ppermute x1, starting transfers between devices, body(): lax.ppermute(proj_part, ('dp', 'context'), rank).astype(F32) * scale_factor  8.69 us
    ppermute x10, starting transfers between devices, swapped(): lax.ppermute(value, axis, [(i, i ^ mask) for i in range(lax.axis_size(axi...  8.62 us
    ppermute x10, waiting for transfers between devices, swapped(): lax.ppermute(value, axis, [(i, i ^ mask) for i in range(lax.axis_size(axi...  8.51 us
    unnamed x43, local copies, waits for them, and re-layouts  7.92 us
    all_to_all x1, starting transfers between devices, body(): lax.all_to_all(blocks, 'context', split_axis=0, concat_axis=0, tiled=True)  5.55 us
  transfers between devices with their start and end apart: 18, of which 6 were waited for; matrix products, arithmetic and copies ran while one was open for 15% of the time, Pallas kernels for 1%

profile of v2, /device:TPU:5, one launch (start us, length us, event | category | flops | bytes accessed | tf_op | source)
XLA Modules:
  0.0 201.9 jit_solution(965587305183879838)
XLA Ops:
  7.2 0.7 all-gather.2.cloned.1.call-update
  7.9 1.9 copy.26
  9.8 1.6 copy.27
  11.4 5.5 %all-to-all-start = ((bf16[8,3,128,256]{3,2,1,0:T(8,128)(2,1)}), bf16[8,3,128,256]{3,2,1,0:T(8,128)(2,1)S(1)}, u32[]{:S(2)}, u32[]{:S(2)}) async-start(bf16[8,3,128,256]{3,2,1,0:T(8,128)(2,1)} %bitcast.1), calls=%async_computation | async-start | bytes 3145728 | tf_op jit(solution)/shard_map/all_to_all | solution.py:206
  17.0 2.4 %constant_dynamic-slice_fusion = bf16[256,2048]{1,0:T(8,128)(2,1)} fusion(bf16[512,2048]{1,0:T(8,128)(2,1)} %param.10, s32[]{:T(128)S(6)} %select_n.130), kind=kLoop, calls=%fused_computation.80 | loop fusion | bytes 2097156 | tf_op jit(solution)/shard_map/dynamic_slice | solution.py:168
  19.3 0.7 collective-permute-start
  20.0 1.3 collective-permute-start.1
  21.3 1.7 collective-permute-start.2
  23.1 65.3 %all-gather.2.cloned.1.call-done = bf16[512,2048]{1,0:T(8,128)(2,1)} async-done(((bf16[128,2048]{1,0:T(8,128)(2,1)}), bf16[512,2048]{1,0:T(8,128)(2,1)}) %all-gather.2.cloned.1.call-update) | async-done | bytes 2097168 | tf_op jit(solution)/shard_map/all_gather | solution.py:202
  88.4 0.5 collective-permute-start.3
  88.8 1.1 fusion.32
  90.0 1.5 subtract_convert_fusion
  91.5 0.4 pad_maximum_fusion
  91.9 0.8 copy-done.15
  92.8 2.6 %fusion.17 = f32[2048,256]{1,0:T(8,128)} fusion(bf16[2048,1024]{1,0:T(8,128)(2,1)S(1)} %bitcast.52, f32[256,1024]{1,0:T(8,128)S(1)} %copy-done.15), kind=kOutput, calls=%fused_computation.44 | convolution fusion | flops 1074003968 | bytes 7340032 | tf_op jit(solution)/shard_map/dot_general | solution.py:135
  95.4 2.9 %select_select_fusion = bf16[256,2048]{1,0:T(8,128)(2,1)} fusion(bf16[256,2048]{1,0:T(8,128)(2,1)S(1)} %collective-permute-done, bf16[256,2048]{1,0:T(8,128)(2,1)} %collective-permute-done.1, bf16[256,2048]{1,0:T(8,128)(2,1)} %collective-permute-done.2, pred[]{:T(512)S(6)} %eq.21, pred[]{:T(512)S(6)} %eq.20, pred[]{:T(512)S(6)} %eq.19, ...), kind=kLoop, calls=%fused_computation.37 | loop fusion | flops 1572864 | bytes 5242887 | tf_op jit(solution)/shard_map/jit(_where)/select_n | solution.py:177
  98.4 2.1 %short_convs.1 = (bf16[1024,256]{1,0:T(8,128)(2,1)S(1)}, bf16[1024,256]{1,0:T(8,128)(2,1)S(1)}, bf16[1024,256]{1,0:T(8,128)(2,1)S(1)}, bf16[1024,256]{1,0:T(8,128)(2,1)S(1)}) custom-call(bf16[8,3,128,256]{3,2,1,0:T(8,128)(2,1)S(1)} %all-to-all-done.query_in.key_in.value_in.refs_0_.refs_1_.refs_2_, ...), custom_call_target="tpu_custom_call" | custom-call | flops 25165824 | bytes 3145728 | tf_op jit(solution)/shard_map/short_convs/pallas_call | solution.py:83
  100.5 0.6 copy-done.7
  101.1 2.7 %fusion.39 = f32[2048,256]{1,0:T(8,128)} fusion(bf16[2048,1024]{1,0:T(8,128)(2,1)S(1)} %bitcast.54, bf16[1024,256]{1,0:T(8,128)(2,1)S(1)} %get-tuple-element.13), kind=kOutput, calls=%fused_computation.86 | convolution fusion | flops 1073741824 | bytes 6815744 | tf_op jit(solution)/shard_map/dot_general | solution.py:135
  103.8 2.5 %convolution_convert_fusion = bf16[256,512]{1,0:T(8,128)(2,1)S(1)} fusion(bf16[256,2048]{1,0:T(8,128)(2,1)S(1)} %copy-done.14, bf16[512,2048]{1,0:T(8,128)(2,1)} %collective-permute-done.3), kind=kOutput, calls=%fused_computation.16 | convolution fusion | flops 537001984 | bytes 3407872 | tf_op jit(solution)/shard_map/dot_general | solution.py:135
  106.3 0.8 select_bitcast_fusion.1
  107.1 0.1 copy.35
  107.2 0.1 copy.36
  107.4 0.3 fusion.6
  107.7 3.6 %fusion.40 = f32[2048,256]{1,0:T(8,128)S(1)} fusion(bf16[2048,1024]{1,0:T(8,128)(2,1)} %bitcast.53, bf16[1024,256]{1,0:T(8,128)(2,1)S(1)} %get-tuple-element.37), kind=kOutput, calls=%fused_computation.87 | convolution fusion | flops 1073741824 | bytes 6815744 | tf_op jit(solution)/shard_map/dot_general | solution.py:135
  111.3 0.3 add_convert_fusion.1
  111.6 1.3 copy-done.13
  112.9 1.4 add_convert_fusion
  114.3 1.0 copy-done.8
  115.3 2.3 %fusion.5 = (bf16[1024,256]{1,0:T(8,128)(2,1)}, bf16[1024,256]{1,0:T(8,128)(2,1)}) fusion(bf16[1024,256]{1,0:T(8,128)(2,1)S(1)} %get-tuple-element.14, bf16[1024,256]{1,0:T(8,128)(2,1)S(1)} %get-tuple-element.13, f32[256]{0:T(256)S(1)} %copy-done.19, bf16[2048,1024]{1,0:T(8,128)(2,1)S(1)} %bitcast.55, bf16[1024,256]{1,0:T(8,128)(2,1)S(1)} %get-tuple-element.47, ...), kind=kOutput, calls=%fused_computation.19 | convolution fusion | flops 1078198272 | bytes 7341056 | tf_op jit(solution)/shard_map/dot_general | solution.py:135
  117.6 2.1 %fusion.2.refs_6_ = bf16[1024,256]{1,0:T(8,128)(2,1)} fusion(bf16[2048,1024]{1,0:T(8,128)(2,1)S(1)} %bitcast.56, bf16[1024,256]{1,0:T(8,128)(2,1)S(1)} %get-tuple-element.37, bf16[1024,256]{1,0:T(8,128)(2,1)S(1)} %get-tuple-element.41, bf16[1024,256]{1,0:T(8,128)(2,1)S(1)} %get-tuple-element.40, f32[256]{0:T(256)S(1)} %copy-done.19), kind=kOutput, calls=%fused_computation.14 | convolution fusion | flops 1077149696 | bytes 6292480 | tf_op jit(solution)/shard_map/dot_general | solution.py:135
  119.7 5.0 %stream_grads.1 = (bf16[8,128,256]{2,1,0:T(8,128)(2,1)}, bf16[8,128,256]{2,1,0:T(8,128)(2,1)}, bf16[8,128,256]{2,1,0:T(8,128)(2,1)}, f32[3,3,256]{2,1,0:T(4,128)}) custom-call(bf16[8,3,128,256]{3,2,1,0:T(8,128)(2,1)} %copy-done.1, bf16[8,3,128,256]{3,2,1,0:T(8,128)(2,1)} %copy-done.1, bf16[8,3,128,256]{3,2,1,0:T(8,128)(2,1)} %copy-done.1, ...), custom_call_target="tpu_custom_call" | custom-call | flops 25165824 | bytes 3145728 | tf_op jit(solution)/shard_map/stream_grads/pallas_call | solution.py:103
  124.7 0.7 reshape.183
  125.4 0.1 collective-permute-start.4
  125.5 1.4 collective-permute-start.5
  126.9 1.2 collective-permute-start.6
  128.2 2.3 %collective-permute-done.6 = f32[10,256]{1,0:T(8,128)S(1)} collective-permute-done((f32[10,256]{1,0:T(8,128)S(1)}, f32[10,256]{1,0:T(8,128)S(1)}, u32[]{:S(2)}, u32[]{:S(2)}) %collective-permute-start.6) | collective-permute-done | bytes 10272 | tf_op jit(solution)/shard_map/ppermute | solution.py:15
  130.4 0.7 broadcast_in_dim.5
  131.1 5.0 %all-to-all-start.2 = ((f32[8,9,256]{2,1,0:T(8,128)}), f32[8,9,256]{2,1,0:T(8,128)S(1)}, u32[]{:S(2)}, u32[]{:S(2)}) async-start(f32[8,9,256]{2,1,0:T(8,128)} %broadcast_in_dim.5), calls=%async_computation.2 | async-start | bytes 262144 | tf_op jit(solution)/shard_map/all_to_all | solution.py:270
  136.1 1.5 pad_maximum_fusion.1
  137.7 1.2 copy.30
  138.9 3.1 %all-to-all-done.2 = f32[8,9,256]{2,1,0:T(8,128)S(1)} async-done(((f32[8,9,256]{2,1,0:T(8,128)}), f32[8,9,256]{2,1,0:T(8,128)S(1)}, u32[]{:S(2)}, u32[]{:S(2)}) %all-to-all-start.2) | async-done | bytes 73760 | tf_op jit(solution)/shard_map/all_to_all | solution.py:270
  142.0 4.5 %all-to-all-start.1 = ((bf16[8,3,128,256]{3,2,1,0:T(8,128)(2,1)}), bf16[8,3,128,256]{3,2,1,0:T(8,128)(2,1)S(1)}, u32[]{:S(2)}, u32[]{:S(2)}) async-start(bf16[8,3,128,256]{3,2,1,0:T(8,128)(2,1)} %copy.30), calls=%async_computation.1 | async-start | bytes 3145728 | tf_op jit(solution)/shard_map/all_to_all | solution.py:247
  146.5 2.3 %fusion.41 = f32[256,2048]{1,0:T(8,128)S(1)} fusion(bf16[512,256]{1,0:T(8,128)(2,1)S(1)} %bitcast.62, bf16[512,2048]{1,0:T(8,128)(2,1)} %all-gather.2.cloned.1.call-done), kind=kOutput, calls=%fused_computation.88 | convolution fusion | flops 536870912 | bytes 4456448 | tf_op jit(solution)/shard_map/dot_general | solution.py:135
  148.8 2.5 %convolution_add_fusion = f32[256,2048]{1,0:T(8,128)S(1)} fusion(f32[256,2048]{1,0:T(8,128)S(1)} %fusion.41, bf16[512,256]{1,0:T(8,128)(2,1)S(1)} %bitcast.61, bf16[512,2048]{1,0:T(8,128)(2,1)} %collective-permute-done.3), kind=kOutput, calls=%fused_computation.3 | convolution fusion | flops 537395200 | bytes 6553600 | tf_op jit(solution)/shard_map/dot_general | solution.py:135
  151.3 0.1 dynamic-slice_convert_fusion.2
  151.4 0.1 collective-permute-start.10
  151.5 1.5 collective-permute-start.11
  153.0 1.2 collective-permute-start.12
  154.1 1.3 fusion.13
  155.5 0.1 collective-permute-start.7
  155.6 1.4 collective-permute-start.8
  157.1 2.0 collective-permute-done.10
  159.1 1.2 collective-permute-start.9
  160.3 4.2 %collective-permute-done.12 = bf16[64,2048]{1,0:T(8,128)(2,1)S(1)} collective-permute-done((bf16[64,2048]{1,0:T(8,128)(2,1)S(1)}, bf16[64,2048]{1,0:T(8,128)(2,1)S(1)}, u32[]{:S(2)}, u32[]{:S(2)}) %collective-permute-start.12) | collective-permute-done | bytes 262176 | tf_op jit(solution)/shard_map/ppermute | solution.py:15
  164.5 0.1 add_convert_fusion.3
  164.6 8.7 %collective-permute-start.13 = (bf16[64,2048]{1,0:T(8,128)(2,1)S(1)}, bf16[64,2048]{1,0:T(8,128)(2,1)S(1)}, u32[]{:S(2)}, u32[]{:S(2)}) collective-permute-start(bf16[64,2048]{1,0:T(8,128)(2,1)S(1)} %add_convert_fusion.3), channel_id=1, source_target_pairs={{0,0},{1,4},{2,8},{3,12},{4,16},{5,20},{6,24},{7,28},{8,1},{9,5},{... | collective-permute-start | bytes 786440 | tf_op jit(solution)/shard_map/ppermute | solution.py:259
  173.3 0.6 slice.53
  173.9 1.7 add_multiply_fusion
  175.7 0.7 copy.37
  176.4 15.4 %collective-permute-done.13 = bf16[64,2048]{1,0:T(8,128)(2,1)S(1)} collective-permute-done((bf16[64,2048]{1,0:T(8,128)(2,1)S(1)}, bf16[64,2048]{1,0:T(8,128)(2,1)S(1)}, u32[]{:S(2)}, u32[]{:S(2)}) %collective-permute-start.13) | collective-permute-done | bytes 262176 | tf_op jit(solution)/shard_map/ppermute | solution.py:259
  191.8 0.8 convert_multiply_fusion.5
  192.6 0.9 copy.31
  193.5 1.6 copy.34
  (59 shorter events, 0.4 us)
Async XLA Ops:
  7.2 82.8 %copy-start = (f32[3,6144]{1,0:T(4,128)S(1)}, f32[3,6144]{1,0:T(4,128)}, u32[]{:S(2)}) copy-start(f32[3,6144]{1,0:T(4,128)} %param.7) | copy-start | bytes 221188
  7.2 81.2 %all-gather.2.cloned.1.call-start = ((), (), s32[]{:S(2)}) async-start(), calls=%async_computation.3 | async-start | bytes 2621440 | tf_op jit(solution)/shard_map/all_gather | solution.py:202
  11.4 86.9 %all-to-all-start = ((bf16[8,3,128,256]{3,2,1,0:T(8,128)(2,1)}), bf16[8,3,128,256]{3,2,1,0:T(8,128)(2,1)S(1)}, u32[]{:S(2)}, u32[]{:S(2)}) async-start(bf16[8,3,128,256]{3,2,1,0:T(8,128)(2,1)} %bitcast.1), calls=%async_computation | async-start | bytes 3145728 | tf_op jit(solution)/shard_map/all_to_all | solution.py:206
  19.3 76.1 %collective-permute-start = (bf16[256,2048]{1,0:T(8,128)(2,1)}, bf16[256,2048]{1,0:T(8,128)(2,1)S(1)}, u32[]{:S(2)}, u32[]{:S(2)}) collective-permute-start(bf16[256,2048]{1,0:T(8,128)(2,1)} %constant_dynamic-slice_fusion), channel_id=1, source_target_pairs={{0,24},{1,25},{10,18},{11,19},{20,12},{21,13},{30,6},{31,7}} | collective-permute-start | bytes 3145736 | tf_op jit(solution)/shard_map/ppermute | solution.py:176
  20.0 75.4 %collective-permute-start.1 = (bf16[256,2048]{1,0:T(8,128)(2,1)}, bf16[256,2048]{1,0:T(8,128)(2,1)}, u32[]{:S(2)}, u32[]{:S(2)}) collective-permute-start(bf16[256,2048]{1,0:T(8,128)(2,1)} %constant_dynamic-slice_fusion), channel_id=1, source_target_pairs={{0,16},{1,17},{10,26},{11,27},{20,4},{21,5},{30,14},{31,15}} | collective-permute-start | bytes 3145736 | tf_op jit(solution)/shard_map/ppermute | solution.py:176
  21.3 74.1 %collective-permute-start.2 = (bf16[256,2048]{1,0:T(8,128)(2,1)}, bf16[256,2048]{1,0:T(8,128)(2,1)}, u32[]{:S(2)}, u32[]{:S(2)}) collective-permute-start(bf16[256,2048]{1,0:T(8,128)(2,1)} %constant_dynamic-slice_fusion), channel_id=1, source_target_pairs={{0,8},{1,9},{10,2},{11,3},{20,28},{21,29},{30,22},{31,23}} | collective-permute-start | bytes 3145736 | tf_op jit(solution)/shard_map/ppermute | solution.py:176
  88.4 15.4 %collective-permute-start.3 = (bf16[512,2048]{1,0:T(8,128)(2,1)}, bf16[512,2048]{1,0:T(8,128)(2,1)}, u32[]{:S(2)}, u32[]{:S(2)}) collective-permute-start(bf16[512,2048]{1,0:T(8,128)(2,1)} %all-gather.2.cloned.1.call-done), channel_id=1, source_target_pairs={{0,1},{1,0},{2,3},{3,2},{4,5},{5,4},{6,7},{7,6},{8,9},{9,8},{10,11... | collective-permute-start | bytes 6291464 | tf_op jit(solution)/shard_map/ppermute | solution.py:15
  90.0 8.3 %copy-start.4 = (f32[3,3,256]{2,1,0:T(4,128)}, f32[3,3,256]{2,1,0:T(4,128)S(1)}, u32[]{:S(2)}) copy-start(f32[3,3,256]{2,1,0:T(4,128)S(1)} %dynamic-slice_bitcast_fusion.taps_ref.refs_3_) | copy-start | bytes 27652
  91.5 1.2 copy-start.15
  91.9 3.5 %copy-start.6 = (bf16[2,32,32,1024]{3,2,1,0:T(8,128)(2,1)}, bf16[2,32,32,1024]{3,2,1,0:T(8,128)(2,1)S(1)}, u32[]{:S(2)}) copy-start(bf16[2,32,32,1024]{3,2,1,0:T(8,128)(2,1)S(1)} %pad_maximum_fusion) | copy-start | bytes 12582916
  92.8 2.7 %copy-start.11 = (bf16[512,2048]{1,0:T(8,128)(2,1)S(1)}, bf16[512,2048]{1,0:T(8,128)(2,1)}, u32[]{:S(2)}) copy-start(bf16[512,2048]{1,0:T(8,128)(2,1)} %param.10) | copy-start | bytes 6291460
  98.3 2.1 %copy-start.1 = (bf16[8,3,128,256]{3,2,1,0:T(8,128)(2,1)}, bf16[8,3,128,256]{3,2,1,0:T(8,128)(2,1)S(1)}, u32[]{:S(2)}) copy-start(bf16[8,3,128,256]{3,2,1,0:T(8,128)(2,1)S(1)} %all-to-all-done.query_in.key_in.value_in.refs_0_.refs_1_.refs_2_) | copy-start | bytes 4718596
  98.4 2.8 %copy-start.7 = (bf16[2,32,32,1024]{3,2,1,0:T(8,128)(2,1)S(1)}, bf16[2,32,32,1024]{3,2,1,0:T(8,128)(2,1)}, u32[]{:S(2)}) copy-start(bf16[2,32,32,1024]{3,2,1,0:T(8,128)(2,1)} %copy-done.6) | copy-start | bytes 12582916
  100.5 3.3 %copy-start.2 = (bf16[1024,256]{1,0:T(8,128)(2,1)}, bf16[1024,256]{1,0:T(8,128)(2,1)S(1)}, u32[]{:S(2)}) copy-start(bf16[1024,256]{1,0:T(8,128)(2,1)S(1)} %get-tuple-element.15.refs_7_) | copy-start | bytes 1572868
  100.5 3.3 %copy-start.3 = (bf16[1024,256]{1,0:T(8,128)(2,1)}, bf16[1024,256]{1,0:T(8,128)(2,1)S(1)}, u32[]{:S(2)}) copy-start(bf16[1024,256]{1,0:T(8,128)(2,1)S(1)} %get-tuple-element.16.refs_8_) | copy-start | bytes 1572868
  101.1 2.7 %copy-start.14 = (bf16[256,2048]{1,0:T(8,128)(2,1)S(1)}, bf16[256,2048]{1,0:T(8,128)(2,1)}, u32[]{:S(2)}) copy-start(bf16[256,2048]{1,0:T(8,128)(2,1)} %select_select_fusion) | copy-start | bytes 3145732
  103.8 2.5 %copy-start.12 = (bf16[512,2048]{1,0:T(8,128)(2,1)S(1)}, bf16[512,2048]{1,0:T(8,128)(2,1)}, u32[]{:S(2)}) copy-start(bf16[512,2048]{1,0:T(8,128)(2,1)} %all-gather.2.cloned.1.call-done) | copy-start | bytes 6291460
  107.4 3.9 %copy-start.10 = (bf16[4,2,128,256]{3,2,1,0:T(8,128)(2,1)}, bf16[4,2,128,256]{3,2,1,0:T(8,128)(2,1)S(1)}, u32[]{:S(2)}) copy-start(bf16[4,2,128,256]{3,2,1,0:T(8,128)(2,1)S(1)} %pad_maximum_fusion.2) | copy-start | bytes 1572868
  107.7 3.6 %copy-start.5 = (f32[2048,256]{1,0:T(8,128)S(1)}, f32[2048,256]{1,0:T(8,128)}, u32[]{:S(2)}) copy-start(f32[2048,256]{1,0:T(8,128)} %fusion.17) | copy-start | bytes 6291460
  111.3 1.6 copy-start.13
  112.9 2.4 %copy-start.8 = (bf16[2,32,32,1024]{3,2,1,0:T(8,128)(2,1)S(1)}, bf16[2,32,32,1024]{3,2,1,0:T(8,128)(2,1)}, u32[]{:S(2)}) copy-start(bf16[2,32,32,1024]{3,2,1,0:T(8,128)(2,1)} %copy-done.6) | copy-start | bytes 12582916
  112.9 2.4 %copy-start.19 = (f32[256]{0:T(256)S(1)}, f32[256]{0:T(256)}, u32[]{:S(2)}) copy-start(f32[256]{0:T(256)} %param.9) | copy-start | bytes 3076
  125.4 2.7 %collective-permute-start.4 = (f32[10,256]{1,0:T(8,128)S(1)}, f32[10,256]{1,0:T(8,128)S(1)}, u32[]{:S(2)}, u32[]{:S(2)}) collective-permute-start(f32[10,256]{1,0:T(8,128)S(1)} %pad_maximum_fusion.3), channel_id=1, source_target_pairs={{0,8},{8,0},{16,24},{24,16},{1,9},{9,1},{17,25},{25,17},{2,10},{10... | collective-permute-start | bytes 30728 | tf_op jit(solution)/shard_map/ppermute | solution.py:15
  125.5 2.7 %collective-permute-start.5 = (f32[10,256]{1,0:T(8,128)S(1)}, f32[10,256]{1,0:T(8,128)S(1)}, u32[]{:S(2)}, u32[]{:S(2)}) collective-permute-start(f32[10,256]{1,0:T(8,128)S(1)} %pad_maximum_fusion.3), channel_id=1, source_target_pairs={{0,16},{8,24},{16,0},{24,8},{1,17},{9,25},{17,1},{25,9},{2,18},{10... | collective-permute-start | bytes 30728 | tf_op jit(solution)/shard_map/ppermute | solution.py:15
  126.9 3.5 %collective-permute-start.6 = (f32[10,256]{1,0:T(8,128)S(1)}, f32[10,256]{1,0:T(8,128)S(1)}, u32[]{:S(2)}, u32[]{:S(2)}) collective-permute-start(f32[10,256]{1,0:T(8,128)S(1)} %pad_maximum_fusion.3), channel_id=1, source_target_pairs={{0,24},{8,16},{16,8},{24,0},{1,25},{9,17},{17,9},{25,1},{2,26},{10... | collective-permute-start | bytes 30728 | tf_op jit(solution)/shard_map/ppermute | solution.py:15
  131.1 10.9 %all-to-all-start.2 = ((f32[8,9,256]{2,1,0:T(8,128)}), f32[8,9,256]{2,1,0:T(8,128)S(1)}, u32[]{:S(2)}, u32[]{:S(2)}) async-start(f32[8,9,256]{2,1,0:T(8,128)} %broadcast_in_dim.5), calls=%async_computation.2 | async-start | bytes 262144 | tf_op jit(solution)/shard_map/all_to_all | solution.py:270
  138.9 7.5 %copy-start.17 = (bf16[1024,256]{1,0:T(8,128)(2,1)S(1)}, bf16[1024,256]{1,0:T(8,128)(2,1)}, u32[]{:S(2)}) copy-start(bf16[1024,256]{1,0:T(8,128)(2,1)} %get-tuple-element.62) | copy-start | bytes 1572868
  142.0 50.6 %all-to-all-start.1 = ((bf16[8,3,128,256]{3,2,1,0:T(8,128)(2,1)}), bf16[8,3,128,256]{3,2,1,0:T(8,128)(2,1)S(1)}, u32[]{:S(2)}, u32[]{:S(2)}) async-start(bf16[8,3,128,256]{3,2,1,0:T(8,128)(2,1)} %copy.30), calls=%async_computation.1 | async-start | bytes 3145728 | tf_op jit(solution)/shard_map/all_to_all | solution.py:247
  148.8 5.3 %copy-start.9 = (bf16[2,32,32,1024]{3,2,1,0:T(8,128)(2,1)S(1)}, bf16[2,32,32,1024]{3,2,1,0:T(8,128)(2,1)}, u32[]{:S(2)}) copy-start(bf16[2,32,32,1024]{3,2,1,0:T(8,128)(2,1)} %copy-done.6) | copy-start | bytes 12582916
  148.8 5.3 %copy-start.16 = (bf16[1024,256]{1,0:T(8,128)(2,1)S(1)}, bf16[1024,256]{1,0:T(8,128)(2,1)}, u32[]{:S(2)}) copy-start(bf16[1024,256]{1,0:T(8,128)(2,1)} %get-tuple-element.39) | copy-start | bytes 1572868
  151.4 7.6 %collective-permute-start.10 = (bf16[64,2048]{1,0:T(8,128)(2,1)S(1)}, bf16[64,2048]{1,0:T(8,128)(2,1)S(1)}, u32[]{:S(2)}, u32[]{:S(2)}) collective-permute-start(bf16[64,2048]{1,0:T(8,128)(2,1)S(1)} %get-tuple-element.44), channel_id=1, source_target_pairs={{0,8},{8,0},{16,24},{24,16},{1,9},{9,1},{17,25},{25,17},{2,10},{10... | collective-permute-start | bytes 786440 | tf_op jit(solution)/shard_map/ppermute | solution.py:15
  151.5 8.8 %collective-permute-start.11 = (bf16[64,2048]{1,0:T(8,128)(2,1)S(1)}, bf16[64,2048]{1,0:T(8,128)(2,1)S(1)}, u32[]{:S(2)}, u32[]{:S(2)}) collective-permute-start(bf16[64,2048]{1,0:T(8,128)(2,1)S(1)} %get-tuple-element.46), channel_id=1, source_target_pairs={{0,16},{8,24},{16,0},{24,8},{1,17},{9,25},{17,1},{25,9},{2,18},{10... | collective-permute-start | bytes 786440 | tf_op jit(solution)/shard_map/ppermute | solution.py:15
  153.0 11.5 %collective-permute-start.12 = (bf16[64,2048]{1,0:T(8,128)(2,1)S(1)}, bf16[64,2048]{1,0:T(8,128)(2,1)S(1)}, u32[]{:S(2)}, u32[]{:S(2)}) collective-permute-start(bf16[64,2048]{1,0:T(8,128)(2,1)S(1)} %get-tuple-element.45), channel_id=1, source_target_pairs={{0,24},{8,16},{16,8},{24,0},{1,25},{9,17},{17,9},{25,1},{2,26},{10... | collective-permute-start | bytes 786440 | tf_op jit(solution)/shard_map/ppermute | solution.py:15
  155.4 9.2 %copy-start.18 = (f32[256,1024]{1,0:T(8,128)}, f32[256,1024]{1,0:T(8,128)S(1)}, u32[]{:S(2)}) copy-start(f32[256,1024]{1,0:T(8,128)S(1)} %fusion.13) | copy-start | bytes 3145732
  155.5 18.4 %collective-permute-start.7 = (bf16[256,256]{1,0:T(8,128)(2,1)S(1)}, bf16[256,256]{1,0:T(8,128)(2,1)S(1)}, u32[]{:S(2)}, u32[]{:S(2)}) collective-permute-start(bf16[256,256]{1,0:T(8,128)(2,1)S(1)} %get-tuple-element.49), channel_id=1, source_target_pairs={{0,8},{8,0},{16,24},{24,16},{1,9},{9,1},{17,25},{25,17},{2,10},{10... | collective-permute-start | bytes 393224 | tf_op jit(solution)/shard_map/ppermute | solution.py:15
  155.6 18.2 %collective-permute-start.8 = (bf16[256,256]{1,0:T(8,128)(2,1)S(1)}, bf16[256,256]{1,0:T(8,128)(2,1)S(1)}, u32[]{:S(2)}, u32[]{:S(2)}) collective-permute-start(bf16[256,256]{1,0:T(8,128)(2,1)S(1)} %get-tuple-element.51), channel_id=1, source_target_pairs={{0,16},{8,24},{16,0},{24,8},{1,17},{9,25},{17,1},{25,9},{2,18},{10... | collective-permute-start | bytes 393224 | tf_op jit(solution)/shard_map/ppermute | solution.py:15
  159.1 14.8 %collective-permute-start.9 = (bf16[256,256]{1,0:T(8,128)(2,1)S(1)}, bf16[256,256]{1,0:T(8,128)(2,1)S(1)}, u32[]{:S(2)}, u32[]{:S(2)}) collective-permute-start(bf16[256,256]{1,0:T(8,128)(2,1)S(1)} %get-tuple-element.50), channel_id=1, source_target_pairs={{0,24},{8,16},{16,8},{24,0},{1,25},{9,17},{17,9},{25,1},{2,26},{10... | collective-permute-start | bytes 393224 | tf_op jit(solution)/shard_map/ppermute | solution.py:15
  164.6 27.2 %collective-permute-start.13 = (bf16[64,2048]{1,0:T(8,128)(2,1)S(1)}, bf16[64,2048]{1,0:T(8,128)(2,1)S(1)}, u32[]{:S(2)}, u32[]{:S(2)}) collective-permute-start(bf16[64,2048]{1,0:T(8,128)(2,1)S(1)} %add_convert_fusion.3), channel_id=1, source_target_pairs={{0,0},{1,4},{2,8},{3,12},{4,16},{5,20},{6,24},{7,28},{8,1},{9,5},{... | collective-permute-start | bytes 786440 | tf_op jit(solution)/shard_map/ppermute | solution.py:259
Sparse Core Ops, SparseCore 0:
  9.6 78.7 all-gather.1

commit v3 on v2

v3 whole, which is shorter than its diff:
```python
import math

import jax
import jax.numpy as jnp
from jax import lax
from jax.experimental import pallas as pl
from jax.experimental.pallas import tpu as pltpu
from jax.sharding import PartitionSpec as P

BF16 = jnp.bfloat16
F32 = jnp.float32


def passed_along(value, axis, steps):
    count = lax.axis_size(axis)
    initial, last = (max(0, -steps), min(count, count - steps))
    return lax.ppermute(value, axis, [(source, source + steps) for source in range(initial, last)])


def swapped(value, axis, mask):
    return lax.ppermute(value, axis, [(i, i ^ mask) for i in range(lax.axis_size(axis))])


VMEM = pl.BlockSpec(memory_space=pltpu.VMEM)
SMEM = pl.BlockSpec(memory_space=pltpu.SMEM)


def rows_down(values, steps, before):
    row = lax.broadcasted_iota(jnp.int32, values.shape, 0)
    moved = pltpu.roll(values, steps, axis=0)
    if steps == 1:
        return jnp.where(row == 0, before[1:2], moved)
    return jnp.where(row == 0, before[0:1], jnp.where(row == 1, before[1:2], moved))


def rows_up(values, steps, after):
    count = values.shape[0]
    row = lax.broadcasted_iota(jnp.int32, values.shape, 0)
    moved = pltpu.roll(values, count - steps, axis=0)
    if steps == 1:
        return jnp.where(row == count - 1, after[0:1], moved)
    return jnp.where(row == count - 1, after[1:2], jnp.where(row == count - 2, after[0:1], moved))


def call(kernel, name, outs, smem, *args):
    moved = sum(math.prod(a.shape) * a.dtype.itemsize for a in args)
    return pl.pallas_call(
        kernel,
        out_shape=outs,
        in_specs=[SMEM] * smem + [VMEM] * (len(args) - smem),
        out_specs=[VMEM] * len(outs),
        compiler_params=pltpu.CompilerParams(vmem_limit_bytes=40 * 2**20),
        cost_estimate=pl.CostEstimate(flops=8 * moved, transcendentals=0, bytes_accessed=2 * moved),
        name=name,
    )(*args)


def columns(index, size):
    return slice(index * size, (index + 1) * size)


def short_kernel(proj_ref, prev_ref, taps_ref, query_ref, keyed_ref, valued_ref, product_ref):
    parts, _, blk = query_ref.shape
    for b in range(parts):

        def mixed(stream):
            cols = columns(stream * parts + b, blk)
            values = proj_ref[:, cols].astype(F32)
            before = prev_ref[:, cols]
            taps = taps_ref[:, cols]
            total = taps[0:1] * values + taps[1:2] * rows_down(values, 1, before)
            return (total + taps[2:3] * rows_down(values, 2, before)).astype(BF16)

        query_ref[b] = mixed(0)
        keyed, valued = (mixed(1), mixed(2))
        keyed_ref[b] = keyed
        valued_ref[b] = valued
        product_ref[b] = (keyed.astype(F32) * valued.astype(F32)).astype(BF16)


def grad_long_kernel(me_ref, query_ref, *refs):
    pieces, (gate_grad_ref, grad_long_ref) = refs[:-2], refs[-2:]
    parts, _, blk = query_ref.shape
    ratio = parts // len(pieces)
    for k, piece in enumerate(pieces):
        for i in range(ratio):
            b = (me_ref[0] ^ k) * ratio + i
            values = piece[:, columns(i, blk)]
            gate_grad_ref[b] = values
            grad_long_ref[b] = (values.astype(F32) * query_ref[b].astype(F32)).astype(BF16)


def gate_kernel(me_ref, query_ref, long_ref, *pieces):
    parts, _, blk = query_ref.shape
    ratio = parts // len(pieces)
    for k, piece in enumerate(pieces):
        for i in range(ratio):
            b = (me_ref[0] ^ k) * ratio + i
            gate = query_ref[b].astype(F32) * long_ref[b].astype(F32)
            piece[:, columns(i, blk)] = gate.astype(BF16)


def final_kernel(*refs):
    proj_ref, prev_ref, taps_ref, gate_grad_ref, long_ref, back_ref, keyed_ref, valued_ref = refs[:8]
    query_after_ref, pair_after_ref, out_ref, sums_ref = refs[8:]
    parts, rows, blk = long_ref.shape
    for b in range(parts):
        back = back_ref[b, 0:rows].astype(F32)
        back_after = back_ref[b, rows : rows + 2].astype(F32)
        grads = (
            (
                gate_grad_ref[b].astype(F32) * long_ref[b].astype(F32),
                query_after_ref[b],
            ),
            (back * valued_ref[b].astype(F32), back_after * pair_after_ref[1, b]),
            (back * keyed_ref[b].astype(F32), back_after * pair_after_ref[0, b]),
        )
        for stream, (grad, after) in enumerate(grads):
            cols = columns(stream * parts + b, blk)
            taps = taps_ref[:, cols]
            total = taps[0:1] * grad + taps[1:2] * rows_up(grad, 1, after)
            out_ref[:, cols] = (total + taps[2:3] * rows_up(grad, 2, after)).astype(BF16)
            values = proj_ref[:, cols].astype(F32)
            before = prev_ref[:, cols]
            for j in range(3):
                moved = rows_down(values, j, before) if j else values
                term = jnp.sum(grad * moved, 0, keepdims=True)
                sums_ref[b, 3 * stream + j : 3 * stream + j + 1, :] = term


def table(first, freqs, seq_len):
    places = jnp.arange(seq_len)
    inner = min(32, freqs)
    outer = freqs // inner

    def waves(odd):
        phases = odd[:, None] * places[None, :] % (4 * seq_len)
        angles = phases.astype(F32) * (2.0 * math.pi / (4 * seq_len))
        return (jnp.cos(angles), jnp.sin(angles))

    outer_cos, outer_sin = waves(2 * (first + inner * jnp.arange(outer)))
    inner_cos, inner_sin = waves(2 * jnp.arange(inner) + 1)
    oc, os = (outer_cos[:, None], outer_sin[:, None])
    ic, is_ = (inner_cos[None], inner_sin[None])
    both = jnp.stack([oc * ic - os * is_, -(os * ic + oc * is_)])
    return both.astype(BF16).reshape(2 * freqs, seq_len)


def dot(left, right, left_dim, right_dim):
    return lax.dot_general(
        left, right, (((left_dim,), (right_dim,)), ((), ())), preferred_element_type=F32
    )


def spectral_product(left, right, conjugate_left):
    half = left.shape[0] // 2
    left_re, left_im = (left[:half], left[half:])
    right_re, right_im = (right[:half], right[half:])
    if conjugate_left:
        real = left_re * right_re + left_im * right_im
        imag = left_re * right_im - left_im * right_re
    else:
        real = left_re * right_re - left_im * right_im
        imag = left_re * right_im + left_im * right_re
    return jnp.concatenate([real, imag], 0).astype(BF16)


def long_terms(first, freqs, long_filter, product, grad_long):
    waves = table(first, freqs, product.shape[0])
    filter_spec = dot(waves, long_filter, 1, 1)
    product_spec = dot(waves, product, 1, 0)
    grad_spec = dot(waves, grad_long, 1, 0)
    out = dot(waves, spectral_product(filter_spec, product_spec, False), 0, 0)
    back = dot(waves, spectral_product(filter_spec, grad_spec, True), 0, 0)
    lag_grad = dot(spectral_product(product_spec, grad_spec, True), waves, 0, 0)
    return (out, back, lag_grad)


def summed_blocks(value, axis, dim):
    count = lax.axis_size(axis)
    size = value.shape[dim] // count
    me = lax.axis_index(axis)
    total = lax.dynamic_slice_in_dim(value, me * size, size, dim)
    for k in range(1, count):
        sent = lax.dynamic_slice_in_dim(value, (me ^ k) * size, size, dim).astype(BF16)
        total = total + swapped(sent, axis, k).astype(F32)
    return total


def own_share(partial, parts):
    blocks = partial.reshape(parts // 2, 2, -1, partial.shape[-1])
    core = lax.axis_index("context") % 2
    mine = lax.dynamic_index_in_dim(blocks, core, 1, False)
    other = lax.dynamic_index_in_dim(blocks, 1 - core, 1, False).astype(BF16)
    pair = (mine + swapped(other, "context", 1).astype(F32)).astype(BF16)
    groups = [list(range(core, parts, 2)) for core in range(2)]
    came = lax.all_to_all(
        pair, "context", split_axis=0, concat_axis=0, tiled=True, axis_index_groups=groups
    )
    return jnp.sum(came.astype(F32), 0)


def to_channels(blocks):
    came = lax.all_to_all(blocks, "context", split_axis=0, concat_axis=0, tiled=True)
    return came.reshape(-1, came.shape[-1])


def to_positions(blocks):
    return lax.all_to_all(blocks, "context", split_axis=0, concat_axis=0, tiled=True)


def body(projected, short_taps, long_filter, skip_gain, out_proj, cotangent):
    rows, width = projected.shape
    chans = width // 3
    parts_dp, parts = (lax.axis_size("dp"), lax.axis_size("context"))
    blk = chans // parts
    seq_len = rows * parts
    scale_factor = 1.0 / math.sqrt(seq_len * parts_dp)
    me_dp = lax.axis_index("dp").astype(jnp.int32)[None]
    plane = jax.ShapeDtypeStruct((parts, rows, blk), BF16)

    prev_rows = passed_along(projected[rows - 2 :], "context", 1).astype(F32)
    cots = [cotangent] + [swapped(cotangent, "dp", k) for k in range(1, parts_dp)]
    query, keyed, valued, product_out = call(
        short_kernel, "short_convs", [plane] * 4, 0, projected, prev_rows, short_taps
    )
    heads = jnp.stack([keyed[:, :2], valued[:, :2]])
    pair_after = passed_along(heads, "context", -1).astype(F32)
    product = to_channels(product_out)

    found = [dot(cot, out_proj, 1, 1).astype(BF16) for cot in cots]
    found = [found[0]] + [swapped(found[k], "dp", k) for k in range(1, parts_dp)]
    gate_grad, grad_long_out = call(
        grad_long_kernel, "grad_long", [plane] * 2, 1, me_dp, query, *found
    )
    grad_long = to_channels(grad_long_out)

    filter_b = long_filter.astype(BF16)
    freqs = seq_len if seq_len <= 1024 else 256
    if freqs == seq_len:
        terms = long_terms(0, freqs, filter_b, product, grad_long)
    else:

        def step(carry, first):
            new = long_terms(first, freqs, filter_b, product, grad_long)
            return (tuple(a + b for a, b in zip(carry, new)), None)

        zero = jnp.zeros((seq_len, blk), F32)
        start = (zero, zero, jnp.zeros((blk, seq_len), F32))
        terms, _ = lax.scan(step, start, jnp.arange(0, seq_len, freqs))
    out_sum, back_sum, lag_sum = terms
    inverse = 1.0 / seq_len
    product_f, grad_long_f = (product.astype(F32), grad_long.astype(F32))
    long_chan = (out_sum * inverse + skip_gain[None, :] * product_f).astype(BF16)
    long_out = to_positions(long_chan.reshape(parts, rows, blk))
    back_chan = (back_sum * inverse + skip_gain[None, :] * grad_long_f).astype(BF16)
    back_blocks = back_chan.reshape(parts, rows, blk)
    next_heads = jnp.concatenate([back_blocks[1:, :2], jnp.zeros((1, 2, blk), BF16)], 0)
    grad_product = to_positions(jnp.concatenate([back_blocks, next_heads], 1))

    piece = jax.ShapeDtypeStruct((rows, chans // parts_dp), BF16)
    gates = call(gate_kernel, "gate", [piece] * parts_dp, 1, me_dp, query, long_out)
    gates = [gates[0]] + [swapped(gates[k], "dp", k) for k in range(1, parts_dp)]
    proj_sum = dot(jnp.concatenate(gates, 0), jnp.concatenate(cots, 0), 0, 0)
    grad_proj = own_share(proj_sum, parts) * scale_factor

    query_heads = gate_grad[:, :2].astype(F32) * long_out[:, :2].astype(F32)
    query_after = passed_along(query_heads, "context", -1)
    grad_inputs, tap_sums = call(
        final_kernel,
        "stream_grads",
        [
            jax.ShapeDtypeStruct((rows, width), BF16),
            jax.ShapeDtypeStruct((parts, 9, blk), F32),
        ],
        0,
        projected,
        prev_rows,
        short_taps,
        gate_grad,
        long_out,
        grad_product,
        keyed,
        valued,
        query_after,
        pair_after,
    )

    grad_filter = summed_blocks(lag_sum, "dp", 1) * (scale_factor * inverse)
    skip_sum = jnp.sum(grad_long_f * product_f, 0, keepdims=True)
    grad_skip = skip_sum
    for k in range(1, parts_dp):
        grad_skip = grad_skip + swapped(skip_sum, "dp", k)

    shares = lax.all_to_all(tap_sums, "context", split_axis=0, concat_axis=0, tiled=True)
    share = jnp.sum(shares, 0)
    total = share
    for k in range(1, parts_dp):
        total = total + swapped(share, "dp", k)
    every = jnp.broadcast_to((total * scale_factor)[None], (parts, 9, blk))
    taps_out = lax.all_to_all(every, "context", split_axis=0, concat_axis=0, tiled=True)
    grad_taps = taps_out.reshape(parts, 3, 3, blk).transpose(2, 1, 0, 3).reshape(3, width)
    return (grad_inputs, grad_taps, grad_filter, grad_skip[0] * scale_factor, grad_proj)


def solution(mesh):
    placed = (
        P(("dp", "context"), None),
        P(),
        P("context", None),
        P("context"),
        P("dp", None),
        P(("dp", "context"), None),
    )
    return jax.shard_map(
        body,
        mesh=mesh,
        in_specs=placed,
        out_specs=(
            P(("dp", "context"), None),
            P(),
            P("context", "dp"),
            P("context"),
            P(("dp", "context"), None),
        ),
        check_vma=False,
    )
```

time: 203 us -> 187 us (0.921)
  the two profiles are of different devices: /device:TPU:5 before, /device:TPU:0 now
where the time goes in v3:
time: 187 us; the launch traced here: 185 us
  starting transfers between devices  51.3 us (27%)
  waiting for transfers between devices  49.9 us (27%)
  matrix products  31.7 us (17%)
  other arithmetic  20.9 us (11%)
  local copies, waits for them, and re-layouts  13.2 us (7%)
  blocking collectives  9.16 us (5%)
  Pallas kernels  7.74 us (4%)
    dot_general x11, matrix products, dot(): lax.dot_general(left, right, (((left_dim,), (right_dim,)), ((), ())), pre...  31.7 us
    ppermute x19, starting transfers between devices, swapped(): lax.ppermute(value, axis, [(i, i ^ mask) for i in range(lax.axis_size(axi...  22.2 us
    all_to_all x2, waiting for transfers between devices, to_positions(): lax.all_to_all(blocks, 'context', split_axis=0, concat_axis=0, tiled=True)  18.5 us
    ppermute x19, waiting for transfers between devices, swapped(): lax.ppermute(value, axis, [(i, i ^ mask) for i in range(lax.axis_size(axi...  14.5 us
    all_to_all x2, starting transfers between devices, to_channels(): lax.all_to_all(blocks, 'context', split_axis=0, concat_axis=0, tiled=True)  11.1 us
    unnamed x43, local copies, waits for them, and re-layouts  9.43 us
    all_to_all x1, blocking collectives, body(): lax.all_to_all(tap_sums, 'context', split_axis=0, concat_axis=0, tiled=True)  9.16 us
    pallas_call x4, Pallas kernels, call(): pl.pallas_call(kernel, out_shape=outs, in_specs=[SMEM] * smem + [VMEM] *...  7.74 us
  transfers between devices with their start and end apart: 28, of which 13 were waited for; matrix products, arithmetic and copies ran while one was open for 26% of the time, Pallas kernels for 4%

profile of v3, /device:TPU:0, one launch (start us, length us, event | category | flops | bytes accessed | tf_op | source)
XLA Modules:
  0.0 185.1 jit_solution(15862192743146091350)
XLA Ops:
  0.6 3.0 %collective-permute-start.1 = (bf16[128,2048]{1,0:T(8,128)(2,1)}, bf16[128,2048]{1,0:T(8,128)(2,1)}, u32[]{:S(2)}, u32[]{:S(2)}) collective-permute-start(bf16[128,2048]{1,0:T(8,128)(2,1)} %param.11), channel_id=1, source_target_pairs={{0,8},{8,0},{16,24},{24,16},{1,9},{9,1},{17,25},{25,17},{2,10},{10... | collective-permute-start | bytes 1572872 | tf_op jit(solution)/shard_map/ppermute | solution.py:21
  3.6 1.5 collective-permute-start.3
  5.2 0.9 slice.42
  6.1 1.3 collective-permute-start
  7.4 1.1 fusion.48
  8.6 3.4 %multiply_subtract_fusion = (bf16[1,32,32,1024]{3,2,1,0:T(8,128)(2,1)}, bf16[1,32,32,1024]{3,2,1,0:T(8,128)(2,1)}) fusion(f32[32,1024]{1,0:T(8,128)S(1)} %get-tuple-element.45, f32[32,1024]{1,0:T(8,128)S(1)} %get-tuple-element.48, f32[32,1024]{1,0:T(8,128)S(1)} %get-tuple-element.44, f32[32,1024]{1,0:T(8,128)S(1)} %get-tuple-element.49), kind=kLoop, calls=%fused_computation.2 | loop fusion | flops 9437184 | bytes 4718592 | tf_op jit(solution)/shard_map/sub | solution.py:145
  12.0 1.2 short_convs.1
  14.9 6.2 %all-to-all-start = ((bf16[8,128,256]{2,1,0:T(8,128)(2,1)}), bf16[8,128,256]{2,1,0:T(8,128)(2,1)}, u32[]{:S(2)}, u32[]{:S(2)}) async-start(bf16[8,128,256]{2,1,0:T(8,128)(2,1)} %copy-done.9), calls=%async_computation | async-start | bytes 1048576 | tf_op jit(solution)/shard_map/all_to_all | solution.py:204
  21.1 2.5 %convolution_convert_fusion.2 = bf16[128,512]{1,0:T(8,128)(2,1)} fusion(bf16[128,2048]{1,0:T(8,128)(2,1)} %collective-permute-done.1, bf16[512,2048]{1,0:T(8,128)(2,1)S(1)} %copy-done), kind=kOutput, calls=%fused_computation.23 | convolution fusion | flops 268500992 | bytes 2752512 | tf_op jit(solution)/shard_map/dot_general | solution.py:150
  23.7 1.5 collective-permute-start.2
  25.2 3.4 %collective-permute-done.3 = bf16[128,2048]{1,0:T(8,128)(2,1)} collective-permute-done((bf16[128,2048]{1,0:T(8,128)(2,1)}, bf16[128,2048]{1,0:T(8,128)(2,1)}, u32[]{:S(2)}, u32[]{:S(2)}) %collective-permute-start.3) | collective-permute-done | bytes 524320 | tf_op jit(solution)/shard_map/ppermute | solution.py:21
  28.6 2.5 %convolution_convert_fusion.1 = bf16[128,512]{1,0:T(8,128)(2,1)} fusion(bf16[128,2048]{1,0:T(8,128)(2,1)} %collective-permute-done.3, bf16[512,2048]{1,0:T(8,128)(2,1)S(1)} %copy-done), kind=kOutput, calls=%fused_computation.22 | convolution fusion | flops 268500992 | bytes 2752512 | tf_op jit(solution)/shard_map/dot_general | solution.py:150
  31.1 1.5 collective-permute-start.4
  32.6 1.9 %convolution_convert_fusion = bf16[128,512]{1,0:T(8,128)(2,1)S(1)} fusion(bf16[128,2048]{1,0:T(8,128)(2,1)} %collective-permute-done.5, bf16[512,2048]{1,0:T(8,128)(2,1)S(1)} %copy-done), kind=kOutput, calls=%fused_computation.21 | convolution fusion | flops 268500992 | bytes 2752512 | tf_op jit(solution)/shard_map/dot_general | solution.py:150
  35.5 2.2 %collective-permute-done.4.refs_2_ = bf16[128,512]{1,0:T(8,128)(2,1)} collective-permute-done((bf16[128,512]{1,0:T(8,128)(2,1)}, bf16[128,512]{1,0:T(8,128)(2,1)}, u32[]{:S(2)}, u32[]{:S(2)}) %collective-permute-start.4) | collective-permute-done | bytes 131104 | tf_op jit(solution)/shard_map/ppermute | solution.py:21
  37.7 2.8 %collective-permute-done.6.refs_3_ = bf16[128,512]{1,0:T(8,128)(2,1)S(1)} collective-permute-done((bf16[128,512]{1,0:T(8,128)(2,1)S(1)}, bf16[128,512]{1,0:T(8,128)(2,1)S(1)}, u32[]{:S(2)}, u32[]{:S(2)}) %collective-permute-start.6) | collective-permute-done | bytes 131104 | tf_op jit(solution)/shard_map/ppermute | solution.py:21
  40.5 1.8 grad_long.1
  42.3 0.8 copy-done.7
  43.1 4.9 %all-to-all-start.2 = ((bf16[8,128,256]{2,1,0:T(8,128)(2,1)}), bf16[8,128,256]{2,1,0:T(8,128)(2,1)S(1)}, u32[]{:S(2)}, u32[]{:S(2)}) async-start(bf16[8,128,256]{2,1,0:T(8,128)(2,1)} %get-tuple-element.20), calls=%async_computation.2 | async-start | bytes 1048576 | tf_op jit(solution)/shard_map/all_to_all | solution.py:204
  48.0 2.7 %maximum_convert_fusion = bf16[2,32,32,1024]{3,2,1,0:T(8,128)(2,1)S(1)} fusion(bf16[1,32,32,1024]{3,2,1,0:T(8,128)(2,1)} %get-tuple-element.41, bf16[1,32,32,1024]{3,2,1,0:T(8,128)(2,1)} %get-tuple-element.40), kind=kLoop, calls=%fused_computation | loop fusion | flops 2097152 | bytes 8388608 | tf_op jit(solution)/shard_map/convert_element_type | solution.py:146
  50.7 2.7 %fusion.33 = f32[2048,256]{1,0:T(8,128)} fusion(bf16[2048,1024]{1,0:T(8,128)(2,1)S(1)} %bitcast.43, f32[256,1024]{1,0:T(8,128)S(1)} %copy-done.18), kind=kOutput, calls=%fused_computation.53 | convolution fusion | flops 1074003968 | bytes 7340032 | tf_op jit(solution)/shard_map/dot_general | solution.py:150
  53.4 3.7 %fusion.55 = f32[2048,256]{1,0:T(8,128)} fusion(bf16[2048,1024]{1,0:T(8,128)(2,1)S(1)} %bitcast.44, bf16[1024,256]{1,0:T(8,128)(2,1)} %bitcast.2), kind=kOutput, calls=%fused_computation.95 | convolution fusion | flops 1073741824 | bytes 6815744 | tf_op jit(solution)/shard_map/dot_general | solution.py:150
  57.2 6.2 %all-to-all-done.2 = bf16[8,128,256]{2,1,0:T(8,128)(2,1)S(1)} async-done(((bf16[8,128,256]{2,1,0:T(8,128)(2,1)}), bf16[8,128,256]{2,1,0:T(8,128)(2,1)S(1)}, u32[]{:S(2)}, u32[]{:S(2)}) %all-to-all-start.2) | async-done | bytes 524320 | tf_op jit(solution)/shard_map/all_to_all | solution.py:204
  63.4 3.7 %fusion.56 = f32[2048,256]{1,0:T(8,128)S(1)} fusion(bf16[2048,1024]{1,0:T(8,128)(2,1)} %bitcast.45, bf16[1024,256]{1,0:T(8,128)(2,1)S(1)} %bitcast.51), kind=kOutput, calls=%fused_computation.96 | convolution fusion | flops 1073741824 | bytes 6815744 | tf_op jit(solution)/shard_map/dot_general | solution.py:150
  67.1 1.6 add_convert_fusion
  68.8 1.6 copy-done.13
  70.4 3.1 %fusion.12 = bf16[1024,256]{1,0:T(8,128)(2,1)} fusion(bf16[2048,1024]{1,0:T(8,128)(2,1)S(1)} %bitcast.48, bf16[1024,256]{1,0:T(8,128)(2,1)S(1)} %get-tuple-element.35, bf16[1024,256]{1,0:T(8,128)(2,1)S(1)} %get-tuple-element.36, bf16[1024,256]{1,0:T(8,128)(2,1)} %bitcast.2, f32[256]{0:T(256)S(1)} %copy-done.20), kind=kOutput, calls=%fused_computation.20 | convolution fusion | flops 1077149696 | bytes 6292480 | tf_op jit(solution)/shard_map/dot_general | solution.py:150
  73.6 3.5 %all-to-all-start.1 = ((bf16[8,128,256]{2,1,0:T(8,128)(2,1)}), bf16[8,128,256]{2,1,0:T(8,128)(2,1)S(1)}, u32[]{:S(2)}, u32[]{:S(2)}) async-start(bf16[8,128,256]{2,1,0:T(8,128)(2,1)} %bitcast.55), calls=%async_computation.1 | async-start | bytes 1048576 | tf_op jit(solution)/shard_map/all_to_all | solution.py:209
  77.1 3.5 %add_convert_fusion.1 = (bf16[1024,256]{1,0:T(8,128)(2,1)}, bf16[1024,256]{1,0:T(8,128)(2,1)}) fusion(f32[2048,256]{1,0:T(8,128)} %copy-done.14, f32[2048,256]{1,0:T(8,128)} %fusion.33), kind=kLoop, calls=%fused_computation.42 | loop fusion | flops 2097152 | bytes 5242880 | tf_op jit(solution)/shard_map/convert.2
  80.6 11.8 %all-to-all-done.1.refs_4_.long_ref = bf16[8,128,256]{2,1,0:T(8,128)(2,1)S(1)} async-done(((bf16[8,128,256]{2,1,0:T(8,128)(2,1)}), bf16[8,128,256]{2,1,0:T(8,128)(2,1)S(1)}, u32[]{:S(2)}, u32[]{:S(2)}) %all-to-all-start.1) | async-done | bytes 524320 | tf_op jit(solution)/shard_map/all_to_all | solution.py:209
  93.1 1.8 collective-permute-start.19
  95.0 1.6 collective-permute-start.18
  96.6 3.9 %fusion.11 = bf16[1024,256]{1,0:T(8,128)(2,1)S(1)} fusion(bf16[2048,1024]{1,0:T(8,128)(2,1)} %bitcast.46, bf16[1024,256]{1,0:T(8,128)(2,1)} %get-tuple-element.32, bf16[1024,256]{1,0:T(8,128)(2,1)} %get-tuple-element.31, bf16[1024,256]{1,0:T(8,128)(2,1)} %bitcast.52, f32[256]{0:T(256)S(1)} %copy-done.20), kind=kOutput, calls=%fused_computation.19 | convolution fusion | flops 1077149696 | bytes 6292480 | tf_op jit(solution)/shard_map/dot_general | solution.py:150
  100.5 0.8 fusion.25
  101.4 3.5 %all-to-all-start.3 = ((bf16[8,130,256]{2,1,0:T(8,128)(2,1)}), bf16[8,130,256]{2,1,0:T(8,128)(2,1)S(1)}, u32[]{:S(2)}, u32[]{:S(2)}) async-start(bf16[8,130,256]{2,1,0:T(8,128)(2,1)} %fusion.25), calls=%async_computation.3 | async-start | bytes 1114112 | tf_op jit(solution)/shard_map/all_to_all | solution.py:209
  105.0 3.0 %fusion = f32[512,2048]{1,0:T(8,128)S(1)} fusion(bf16[128,2048]{1,0:T(8,128)(2,1)} %collective-permute-done.5, bf16[128,2048]{1,0:T(8,128)(2,1)} %collective-permute-done.3, bf16[128,2048]{1,0:T(8,128)(2,1)} %collective-permute-done.1, bf16[128,2048]{1,0:T(8,128)(2,1)} %param.11, bf16[128,512]{1,0:T(8,128)(2,1)} %collective-permute-done.20, ...), kind=kOutput, calls=%fused_computation.3 | convolution fusion | flops 1084227584 | bytes 6815744 | tf_op jit(solution)/shard_map/dot_general | solution.py:150
  108.0 1.3 fusion.14
  110.5 1.3 collective-permute-start.8
  112.6 1.5 collective-permute-start.7
  114.1 6.8 %all-to-all-done.3.refs_5_ = bf16[8,130,256]{2,1,0:T(8,128)(2,1)S(1)} async-done(((bf16[8,130,256]{2,1,0:T(8,128)(2,1)}), bf16[8,130,256]{2,1,0:T(8,128)(2,1)S(1)}, u32[]{:S(2)}, u32[]{:S(2)}) %all-to-all-start.3) | async-done | bytes 532512 | tf_op jit(solution)/shard_map/all_to_all | solution.py:209
  120.9 1.4 copy-done.2
  122.3 1.0 copy-done.4
  123.4 1.0 copy-done.6
  124.4 1.0 copy-done.8
  125.4 3.9 %stream_grads.1 = (bf16[128,6144]{1,0:T(8,128)(2,1)}, f32[8,9,256]{2,1,0:T(8,128)S(1)}) custom-call(bf16[128,6144]{1,0:T(8,128)(2,1)S(1)} %copy-done.2, f32[2,6144]{1,0:T(2,128)S(1)} %convert_element_type.123.prev_ref.refs_1_, f32[3,6144]{1,0:T(4,128)S(1)} %copy-done.10, bf16[8,128,256]{2,1,0:T(8,128)(2,1)S(1)} %copy-done.8, ...), custom_call_target="tpu_custom_call" | custom-call | flops 34996224 | bytes 8749056 | tf_op jit(solution)/shard_map/stream_grads/pallas_call | solution.py:47
  129.3 9.2 %all_to_all.35 = f32[8,9,256]{2,1,0:T(8,128)S(1)} all-to-all(f32[8,9,256]{2,1,0:T(8,128)S(1)} %get-tuple-element.24), channel_id=1, replica_groups=mesh['dp'=4,'context'=8] {'context'}, dimensions={0} | all-to-all | bytes 147456 | tf_op jit(solution)/shard_map/all_to_all | solution.py:295
  138.6 1.8 collective-permute-start.10
  140.4 1.6 collective-permute-start.9
  142.1 1.1 collective-permute-done.11
  143.2 0.9 collective-permute-done.9
  144.9 3.4 %all-to-all-start.5 = ((f32[8,9,256]{2,1,0:T(8,128)}), f32[8,9,256]{2,1,0:T(8,128)S(1)}, u32[]{:S(2)}, u32[]{:S(2)}) async-start(f32[8,9,256]{2,1,0:T(8,128)} %broadcast_in_dim.7), calls=%async_computation.5 | async-start | bytes 262144 | tf_op jit(solution)/shard_map/all_to_all | solution.py:301
  148.2 3.2 %fusion.8 = bf16[4,64,2048]{2,1,0:T(8,128)(2,1)} fusion(bf16[4,64,2048]{2,1,0:T(8,128)(2,1)} %collective-permute-done.21, f32[4,2,64,2048]{3,2,1,0:T(8,128)} %bitcast.50, s32[]{:T(128)S(6)} %select_n.61), kind=kLoop, calls=%fused_computation.12 | loop fusion | flops 1572864 | bytes 4194308 | tf_op jit(solution)/shard_map/convert_element_type | solution.py:195
  151.4 3.5 %all-to-all-done.5 = f32[8,9,256]{2,1,0:T(8,128)S(1)} async-done(((f32[8,9,256]{2,1,0:T(8,128)}), f32[8,9,256]{2,1,0:T(8,128)S(1)}, u32[]{:S(2)}, u32[]{:S(2)}) %all-to-all-start.5) | async-done | bytes 73760 | tf_op jit(solution)/shard_map/all_to_all | solution.py:301
  154.9 3.5 %all-to-all-start.6 = ((bf16[4,64,2048]{2,1,0:T(8,128)(2,1)}), bf16[4,64,2048]{2,1,0:T(8,128)(2,1)S(1)}, u32[]{:S(2)}, u32[]{:S(2)}) async-start(bf16[4,64,2048]{2,1,0:T(8,128)(2,1)} %fusion.8), calls=%async_computation.6 | async-start | bytes 2097152 | tf_op jit(solution)/shard_map/all_to_all | solution.py:197
  158.5 1.4 multiply_reduce_fusion
  159.9 1.4 collective-permute-start.17
  161.3 1.7 collective-permute-start.16
  163.4 3.8 %fusion.21 = f32[256,1024]{1,0:T(8,128)S(1)} fusion(bf16[2048,1024]{1,0:T(8,128)(2,1)} %bitcast.47, bf16[1024,256]{1,0:T(8,128)(2,1)} %get-tuple-element.30, bf16[1024,256]{1,0:T(8,128)(2,1)} %get-tuple-element.29), kind=kOutput, calls=%fused_computation.34 | convolution fusion | flops 1075838976 | bytes 6291456 | tf_op jit(solution)/shard_map/dot_general | solution.py:150
  167.3 1.4 collective-permute-start.14
  168.7 1.7 collective-permute-start.13
  171.4 2.4 %collective-permute-done.14 = bf16[256,256]{1,0:T(8,128)(2,1)S(1)} collective-permute-done((bf16[256,256]{1,0:T(8,128)(2,1)S(1)}, bf16[256,256]{1,0:T(8,128)(2,1)S(1)}, u32[]{:S(2)}, u32[]{:S(2)}) %collective-permute-start.14) | collective-permute-done | bytes 131104 | tf_op jit(solution)/shard_map/ppermute | solution.py:21
  173.9 1.3 collective-permute-done.13
  177.0 7.2 %all-to-all-done.6 = bf16[4,64,2048]{2,1,0:T(8,128)(2,1)S(1)} async-done(((bf16[4,64,2048]{2,1,0:T(8,128)(2,1)}), bf16[4,64,2048]{2,1,0:T(8,128)(2,1)S(1)}, u32[]{:S(2)}, u32[]{:S(2)}) %all-to-all-start.6) | async-done | bytes 1048608 | tf_op jit(solution)/shard_map/all_to_all | solution.py:197
  184.3 0.8 broadcast_multiply_fusion
  (79 shorter events, 9.7 us)
Async XLA Ops:
  0.6 20.5 %copy-start = (bf16[512,2048]{1,0:T(8,128)(2,1)S(1)}, bf16[512,2048]{1,0:T(8,128)(2,1)}, u32[]{:S(2)}) copy-start(bf16[512,2048]{1,0:T(8,128)(2,1)} %param.10) | copy-start | bytes 6291460
  0.6 20.5 %collective-permute-start.1 = (bf16[128,2048]{1,0:T(8,128)(2,1)}, bf16[128,2048]{1,0:T(8,128)(2,1)}, u32[]{:S(2)}, u32[]{:S(2)}) collective-permute-start(bf16[128,2048]{1,0:T(8,128)(2,1)} %param.11), channel_id=1, source_target_pairs={{0,8},{8,0},{16,24},{24,16},{1,9},{9,1},{17,25},{25,17},{2,10},{10... | collective-permute-start | bytes 1572872 | tf_op jit(solution)/shard_map/ppermute | solution.py:21
  3.6 24.9 %collective-permute-start.3 = (bf16[128,2048]{1,0:T(8,128)(2,1)}, bf16[128,2048]{1,0:T(8,128)(2,1)}, u32[]{:S(2)}, u32[]{:S(2)}) collective-permute-start(bf16[128,2048]{1,0:T(8,128)(2,1)} %param.11), channel_id=1, source_target_pairs={{0,16},{8,24},{16,0},{24,8},{1,17},{9,25},{17,1},{25,9},{2,18},{10... | collective-permute-start | bytes 1572872 | tf_op jit(solution)/shard_map/ppermute | solution.py:21
  5.2 27.5 %collective-permute-start.5 = (bf16[128,2048]{1,0:T(8,128)(2,1)}, bf16[128,2048]{1,0:T(8,128)(2,1)}, u32[]{:S(2)}, u32[]{:S(2)}) collective-permute-start(bf16[128,2048]{1,0:T(8,128)(2,1)} %param.11), channel_id=1, source_target_pairs={{0,24},{8,16},{16,8},{24,0},{1,25},{9,17},{17,9},{25,1},{2,26},{10... | collective-permute-start | bytes 1572872 | tf_op jit(solution)/shard_map/ppermute | solution.py:21
  6.1 5.9 %collective-permute-start = (bf16[2,6144]{1,0:T(2,128)(2,1)S(1)}, bf16[2,6144]{1,0:T(2,128)(2,1)S(1)}, u32[]{:S(2)}, u32[]{:S(2)}) collective-permute-start(bf16[2,6144]{1,0:T(2,128)(2,1)S(1)} %slice.42), channel_id=1, source_target_pairs={{0,1},{1,2},{2,3},{3,4},{4,5},{5,6},{6,7},{8,9},{9,10},{10,11},{11... | collective-permute-start | bytes 73736 | tf_op jit(solution)/shard_map/ppermute | solution.py:17
  8.5 3.5 %copy-start.1 = (bf16[128,6144]{1,0:T(8,128)(2,1)S(1)}, bf16[128,6144]{1,0:T(8,128)(2,1)}, u32[]{:S(2)}) copy-start(bf16[128,6144]{1,0:T(8,128)(2,1)} %refs_0_.1) | copy-start | bytes 4718596
  8.6 3.5 %copy-start.10 = (f32[3,6144]{1,0:T(4,128)S(1)}, f32[3,6144]{1,0:T(4,128)}, u32[]{:S(2)}) copy-start(f32[3,6144]{1,0:T(4,128)} %refs_2_.1) | copy-start | bytes 221188
  13.3 0.8 copy-start.5
  14.1 0.8 copy-start.9
  14.9 16.2 %copy-start.3 = (bf16[8,128,256]{2,1,0:T(8,128)(2,1)}, bf16[8,128,256]{2,1,0:T(8,128)(2,1)S(1)}, u32[]{:S(2)}) copy-start(bf16[8,128,256]{2,1,0:T(8,128)(2,1)S(1)} %get-tuple-element.21.refs_6_) | copy-start | bytes 1572868
  14.9 28.2 %all-to-all-start = ((bf16[8,128,256]{2,1,0:T(8,128)(2,1)}), bf16[8,128,256]{2,1,0:T(8,128)(2,1)}, u32[]{:S(2)}, u32[]{:S(2)}) async-start(bf16[8,128,256]{2,1,0:T(8,128)(2,1)} %copy-done.9), calls=%async_computation | async-start | bytes 1048576 | tf_op jit(solution)/shard_map/all_to_all | solution.py:204
  23.7 10.9 %copy-start.19 = (bf16[128,2048]{1,0:T(8,128)(2,1)S(1)}, bf16[128,2048]{1,0:T(8,128)(2,1)}, u32[]{:S(2)}) copy-start(bf16[128,2048]{1,0:T(8,128)(2,1)} %param.11) | copy-start | bytes 1572868
  23.7 11.8 %collective-permute-start.2 = (bf16[128,512]{1,0:T(8,128)(2,1)}, bf16[128,512]{1,0:T(8,128)(2,1)S(1)}, u32[]{:S(2)}, u32[]{:S(2)}) collective-permute-start(bf16[128,512]{1,0:T(8,128)(2,1)} %convolution_convert_fusion.2), channel_id=1, source_target_pairs={{0,8},{8,0},{16,24},{24,16},{1,9},{9,1},{17,25},{25,17},{2,10},{10... | collective-permute-start | bytes 393224 | tf_op jit(solution)/shard_map/ppermute | solution.py:21
  31.1 6.5 %collective-permute-start.4 = (bf16[128,512]{1,0:T(8,128)(2,1)}, bf16[128,512]{1,0:T(8,128)(2,1)}, u32[]{:S(2)}, u32[]{:S(2)}) collective-permute-start(bf16[128,512]{1,0:T(8,128)(2,1)} %convolution_convert_fusion.1), channel_id=1, source_target_pairs={{0,16},{8,24},{16,0},{24,8},{1,17},{9,25},{17,1},{25,9},{2,18},{10... | collective-permute-start | bytes 393224 | tf_op jit(solution)/shard_map/ppermute | solution.py:21
  34.5 5.9 %collective-permute-start.6 = (bf16[128,512]{1,0:T(8,128)(2,1)S(1)}, bf16[128,512]{1,0:T(8,128)(2,1)S(1)}, u32[]{:S(2)}, u32[]{:S(2)}) collective-permute-start(bf16[128,512]{1,0:T(8,128)(2,1)S(1)} %convolution_convert_fusion), channel_id=1, source_target_pairs={{0,24},{8,16},{16,8},{24,0},{1,25},{9,17},{17,9},{25,1},{2,26},{10... | collective-permute-start | bytes 393224 | tf_op jit(solution)/shard_map/ppermute | solution.py:21
  42.3 0.8 copy-start.7
  43.1 20.2 %all-to-all-start.2 = ((bf16[8,128,256]{2,1,0:T(8,128)(2,1)}), bf16[8,128,256]{2,1,0:T(8,128)(2,1)S(1)}, u32[]{:S(2)}, u32[]{:S(2)}) async-start(bf16[8,128,256]{2,1,0:T(8,128)(2,1)} %get-tuple-element.20), calls=%async_computation.2 | async-start | bytes 1048576 | tf_op jit(solution)/shard_map/all_to_all | solution.py:204
  48.0 2.7 %copy-start.18 = (f32[256,1024]{1,0:T(8,128)S(1)}, f32[256,1024]{1,0:T(8,128)}, u32[]{:S(2)}) copy-start(f32[256,1024]{1,0:T(8,128)} %param.8) | copy-start | bytes 3145732
  50.7 2.7 %copy-start.12 = (bf16[2,32,32,1024]{3,2,1,0:T(8,128)(2,1)}, bf16[2,32,32,1024]{3,2,1,0:T(8,128)(2,1)S(1)}, u32[]{:S(2)}) copy-start(bf16[2,32,32,1024]{3,2,1,0:T(8,128)(2,1)S(1)} %maximum_convert_fusion) | copy-start | bytes 12582916
  63.4 3.7 %copy-start.16 = (bf16[8,128,256]{2,1,0:T(8,128)(2,1)}, bf16[8,128,256]{2,1,0:T(8,128)(2,1)S(1)}, u32[]{:S(2)}) copy-start(bf16[8,128,256]{2,1,0:T(8,128)(2,1)S(1)} %all-to-all-done.2) | copy-start | bytes 1572868
  63.4 3.7 %copy-start.11 = (f32[2048,256]{1,0:T(8,128)S(1)}, f32[2048,256]{1,0:T(8,128)}, u32[]{:S(2)}) copy-start(f32[2048,256]{1,0:T(8,128)} %fusion.33) | copy-start | bytes 6291460
  63.4 3.7 %copy-start.17 = (f32[2048,256]{1,0:T(8,128)S(1)}, f32[2048,256]{1,0:T(8,128)}, u32[]{:S(2)}) copy-start(f32[2048,256]{1,0:T(8,128)} %fusion.55) | copy-start | bytes 6291460
  67.1 1.7 copy-start.14
  67.1 3.3 %copy-start.13 = (bf16[2,32,32,1024]{3,2,1,0:T(8,128)(2,1)S(1)}, bf16[2,32,32,1024]{3,2,1,0:T(8,128)(2,1)}, u32[]{:S(2)}) copy-start(bf16[2,32,32,1024]{3,2,1,0:T(8,128)(2,1)} %copy-done.12) | copy-start | bytes 12582916
  67.1 3.3 %copy-start.20 = (f32[256]{0:T(256)S(1)}, f32[256]{0:T(256)}, u32[]{:S(2)}) copy-start(f32[256]{0:T(256)} %param.9) | copy-start | bytes 3076
  73.6 18.8 %all-to-all-start.1 = ((bf16[8,128,256]{2,1,0:T(8,128)(2,1)}), bf16[8,128,256]{2,1,0:T(8,128)(2,1)S(1)}, u32[]{:S(2)}, u32[]{:S(2)}) async-start(bf16[8,128,256]{2,1,0:T(8,128)(2,1)} %bitcast.55), calls=%async_computation.1 | async-start | bytes 1048576 | tf_op jit(solution)/shard_map/all_to_all | solution.py:209
  93.1 11.8 %collective-permute-start.20 = (bf16[128,512]{1,0:T(8,128)(2,1)}, bf16[128,512]{1,0:T(8,128)(2,1)}, u32[]{:S(2)}, u32[]{:S(2)}) collective-permute-start(bf16[128,512]{1,0:T(8,128)(2,1)} %get-tuple-element.28), channel_id=1, source_target_pairs={{0,24},{8,16},{16,8},{24,0},{1,25},{9,17},{17,9},{25,1},{2,26},{10... | collective-permute-start | bytes 393224 | tf_op jit(solution)/shard_map/ppermute | solution.py:21
  93.1 11.8 %collective-permute-start.19 = (bf16[128,512]{1,0:T(8,128)(2,1)}, bf16[128,512]{1,0:T(8,128)(2,1)}, u32[]{:S(2)}, u32[]{:S(2)}) collective-permute-start(bf16[128,512]{1,0:T(8,128)(2,1)} %get-tuple-element.27), channel_id=1, source_target_pairs={{0,16},{8,24},{16,0},{24,8},{1,17},{9,25},{17,1},{25,9},{2,18},{10... | collective-permute-start | bytes 393224 | tf_op jit(solution)/shard_map/ppermute | solution.py:21
  95.0 10.0 %collective-permute-start.18 = (bf16[128,512]{1,0:T(8,128)(2,1)}, bf16[128,512]{1,0:T(8,128)(2,1)}, u32[]{:S(2)}, u32[]{:S(2)}) collective-permute-start(bf16[128,512]{1,0:T(8,128)(2,1)} %get-tuple-element.26), channel_id=1, source_target_pairs={{0,8},{8,0},{16,24},{24,16},{1,9},{9,1},{17,25},{25,17},{2,10},{10... | collective-permute-start | bytes 393224 | tf_op jit(solution)/shard_map/ppermute | solution.py:21
  101.4 19.5 %all-to-all-start.3 = ((bf16[8,130,256]{2,1,0:T(8,128)(2,1)}), bf16[8,130,256]{2,1,0:T(8,128)(2,1)S(1)}, u32[]{:S(2)}, u32[]{:S(2)}) async-start(bf16[8,130,256]{2,1,0:T(8,128)(2,1)} %fusion.25), calls=%async_computation.3 | async-start | bytes 1114112 | tf_op jit(solution)/shard_map/all_to_all | solution.py:209
  108.0 6.2 %copy-start.15 = (f32[512,2048]{1,0:T(8,128)}, f32[512,2048]{1,0:T(8,128)S(1)}, u32[]{:S(2)}) copy-start(f32[512,2048]{1,0:T(8,128)S(1)} %fusion) | copy-start | bytes 12582916
  109.3 39.0 %collective-permute-start.21 = (bf16[4,64,2048]{2,1,0:T(8,128)(2,1)}, bf16[4,64,2048]{2,1,0:T(8,128)(2,1)}, u32[]{:S(2)}, u32[]{:S(2)}) collective-permute-start(bf16[4,64,2048]{2,1,0:T(8,128)(2,1)} %fusion.14), channel_id=1, source_target_pairs={{0,1},{1,0},{2,3},{3,2},{4,5},{5,4},{6,7},{7,6},{8,9},{9,8},{10,11... | collective-permute-start | bytes 3145736 | tf_op jit(solution)/shard_map/ppermute | solution.py:21
  110.5 3.6 %collective-permute-start.8 = (bf16[2,8,2,256]{3,2,1,0:T(2,128)(2,1)S(1)}, bf16[2,8,2,256]{3,2,1,0:T(2,128)(2,1)S(1)}, u32[]{:S(2)}, u32[]{:S(2)}) collective-permute-start(bf16[2,8,2,256]{3,2,1,0:T(2,128)(2,1)S(1)} %pad_maximum_fusion), channel_id=1, source_target_pairs={{1,0},{2,1},{3,2},{4,3},{5,4},{6,5},{7,6},{9,8},{10,9},{11,10},{12... | collective-permute-start | bytes 49160 | tf_op jit(solution)/shard_map/ppermute | solution.py:17
  112.6 8.3 %collective-permute-start.7 = (f32[8,2,256]{2,1,0:T(2,128)S(1)}, f32[8,2,256]{2,1,0:T(2,128)S(1)}, u32[]{:S(2)}, u32[]{:S(2)}) collective-permute-start(f32[8,2,256]{2,1,0:T(2,128)S(1)} %convert_multiply_fusion), channel_id=1, source_target_pairs={{1,0},{2,1},{3,2},{4,3},{5,4},{6,5},{7,6},{9,8},{10,9},{11,10},{12... | collective-permute-start | bytes 49160 | tf_op jit(solution)/shard_map/ppermute | solution.py:17
  120.9 1.4 copy-start.2
  122.3 1.0 copy-start.4
  123.4 1.0 copy-start.6
  124.4 1.0 copy-start.8
  138.5 4.7 %collective-permute-start.11 = (f32[9,256]{1,0:T(8,128)S(1)}, f32[9,256]{1,0:T(8,128)S(1)}, u32[]{:S(2)}, u32[]{:S(2)}) collective-permute-start(f32[9,256]{1,0:T(8,128)S(1)} %reduce_sum.27), channel_id=1, source_target_pairs={{0,24},{8,16},{16,8},{24,0},{1,25},{9,17},{17,9},{25,1},{2,26},{10... | collective-permute-start | bytes 27656 | tf_op jit(solution)/shard_map/ppermute | solution.py:21
  138.6 4.6 %collective-permute-start.10 = (f32[9,256]{1,0:T(8,128)S(1)}, f32[9,256]{1,0:T(8,128)S(1)}, u32[]{:S(2)}, u32[]{:S(2)}) collective-permute-start(f32[9,256]{1,0:T(8,128)S(1)} %reduce_sum.27), channel_id=1, source_target_pairs={{0,16},{8,24},{16,0},{24,8},{1,17},{9,25},{17,1},{25,9},{2,18},{10... | collective-permute-start | bytes 27656 | tf_op jit(solution)/shard_map/ppermute | solution.py:21
  140.4 3.7 %collective-permute-start.9 = (f32[9,256]{1,0:T(8,128)S(1)}, f32[9,256]{1,0:T(8,128)S(1)}, u32[]{:S(2)}, u32[]{:S(2)}) collective-permute-start(f32[9,256]{1,0:T(8,128)S(1)} %reduce_sum.27), channel_id=1, source_target_pairs={{0,8},{8,0},{16,24},{24,16},{1,9},{9,1},{17,25},{25,17},{2,10},{10... | collective-permute-start | bytes 27656 | tf_op jit(solution)/shard_map/ppermute | solution.py:21
  144.9 10.1 %all-to-all-start.5 = ((f32[8,9,256]{2,1,0:T(8,128)}), f32[8,9,256]{2,1,0:T(8,128)S(1)}, u32[]{:S(2)}, u32[]{:S(2)}) async-start(f32[8,9,256]{2,1,0:T(8,128)} %broadcast_in_dim.7), calls=%async_computation.5 | async-start | bytes 262144 | tf_op jit(solution)/shard_map/all_to_all | solution.py:301
  154.9 29.2 %all-to-all-start.6 = ((bf16[4,64,2048]{2,1,0:T(8,128)(2,1)}), bf16[4,64,2048]{2,1,0:T(8,128)(2,1)S(1)}, u32[]{:S(2)}, u32[]{:S(2)}) async-start(bf16[4,64,2048]{2,1,0:T(8,128)(2,1)} %fusion.8), calls=%async_computation.6 | async-start | bytes 2097152 | tf_op jit(solution)/shard_map/all_to_all | solution.py:197
  159.9 10.6 %collective-permute-start.17 = (f32[1,256]{1,0:T(1,128)S(1)}, f32[1,256]{1,0:T(1,128)S(1)}, u32[]{:S(2)}, u32[]{:S(2)}) collective-permute-start(f32[1,256]{1,0:T(1,128)S(1)} %bitcast.59), channel_id=1, source_target_pairs={{0,24},{8,16},{16,8},{24,0},{1,25},{9,17},{17,9},{25,1},{2,26},{10... | collective-permute-start | bytes 3080 | tf_op jit(solution)/shard_map/ppermute | solution.py:21
  161.3 9.5 %collective-permute-start.16 = (f32[1,256]{1,0:T(1,128)S(1)}, f32[1,256]{1,0:T(1,128)S(1)}, u32[]{:S(2)}, u32[]{:S(2)}) collective-permute-start(f32[1,256]{1,0:T(1,128)S(1)} %bitcast.60), channel_id=1, source_target_pairs={{0,16},{8,24},{16,0},{24,8},{1,17},{9,25},{17,1},{25,9},{2,18},{10... | collective-permute-start | bytes 3080 | tf_op jit(solution)/shard_map/ppermute | solution.py:21
  163.1 7.8 %collective-permute-start.15 = (f32[1,256]{1,0:T(1,128)S(1)}, f32[1,256]{1,0:T(1,128)S(1)}, u32[]{:S(2)}, u32[]{:S(2)}) collective-permute-start(f32[1,256]{1,0:T(1,128)S(1)} %bitcast.61), channel_id=1, source_target_pairs={{0,8},{8,0},{16,24},{24,16},{1,9},{9,1},{17,25},{25,17},{2,10},{10... | collective-permute-start | bytes 3080 | tf_op jit(solution)/shard_map/ppermute | solution.py:21
  167.3 6.6 %collective-permute-start.14 = (bf16[256,256]{1,0:T(8,128)(2,1)S(1)}, bf16[256,256]{1,0:T(8,128)(2,1)S(1)}, u32[]{:S(2)}, u32[]{:S(2)}) collective-permute-start(bf16[256,256]{1,0:T(8,128)(2,1)S(1)} %get-tuple-element.38), channel_id=1, source_target_pairs={{0,24},{8,16},{16,8},{24,0},{1,25},{9,17},{17,9},{25,1},{2,26},{10... | collective-permute-start | bytes 393224 | tf_op jit(solution)/shard_map/ppermute | solution.py:21
  168.7 6.4 %collective-permute-start.13 = (bf16[256,256]{1,0:T(8,128)(2,1)S(1)}, bf16[256,256]{1,0:T(8,128)(2,1)S(1)}, u32[]{:S(2)}, u32[]{:S(2)}) collective-permute-start(bf16[256,256]{1,0:T(8,128)(2,1)S(1)} %get-tuple-element.39), channel_id=1, source_target_pairs={{0,16},{8,24},{16,0},{24,8},{1,17},{9,25},{17,1},{25,9},{2,18},{10... | collective-permute-start | bytes 393224 | tf_op jit(solution)/shard_map/ppermute | solution.py:21
  170.5 5.0 %collective-permute-start.12 = (bf16[256,256]{1,0:T(8,128)(2,1)S(1)}, bf16[256,256]{1,0:T(8,128)(2,1)S(1)}, u32[]{:S(2)}, u32[]{:S(2)}) collective-permute-start(bf16[256,256]{1,0:T(8,128)(2,1)S(1)} %get-tuple-element.37), channel_id=1, source_target_pairs={{0,8},{8,0},{16,24},{24,16},{1,9},{9,1},{17,25},{25,17},{2,10},{10... | collective-permute-start | bytes 393224 | tf_op jit(solution)/shard_map/ppermute | solution.py:21

commit v4 on v3

--- a/solution.py
+++ b/solution.py
@@ -124,8 +124,7 @@
             before = prev_ref[:, cols]
             for j in range(3):
                 moved = rows_down(values, j, before) if j else values
-                term = jnp.sum(grad * moved, 0, keepdims=True)
-                sums_ref[b, 3 * stream + j : 3 * stream + j + 1, :] = term
+                sums_ref[j : j + 1, cols] = jnp.sum(grad * moved, 0, keepdims=True)
 
 
 def table(first, freqs, seq_len):
@@ -165,8 +164,11 @@
     return jnp.concatenate([real, imag], 0).astype(BF16)
 
 
-def long_terms(first, freqs, long_filter, product, grad_long):
-    waves = table(first, freqs, product.shape[0])
+def ordered(value, *first):
+    return lax.optimization_barrier((value, *first))[0]
+
+
+def transforms(waves, long_filter, product, grad_long):
     filter_spec = dot(waves, long_filter, 1, 1)
     product_spec = dot(waves, product, 1, 0)
     grad_spec = dot(waves, grad_long, 1, 0)
@@ -174,6 +176,23 @@
     back = dot(waves, spectral_product(filter_spec, grad_spec, True), 0, 0)
     lag_grad = dot(spectral_product(product_spec, grad_spec, True), waves, 0, 0)
     return (out, back, lag_grad)
+
+
+def all_sum(value, axis, bits):
+    for pair in [bits[i : i + 2] for i in range(0, len(bits), 2)]:
+        sums = [value]
+        for bit in pair:
+            sums += [swapped(value, axis, bit)]
+        if len(pair) == 2:
+            far = swapped(value, axis, pair[0] + pair[1])
+            value = (sums[0] + sums[1]) + (sums[2] + far)
+        else:
+            value = sums[0] + sums[1]
+    return value
+
+
+def bits_of(count, first=1):
+    return [1 << i for i in range(count.bit_length() - 1) if 1 << i >= first]
 
 
 def summed_blocks(value, axis, dim):
@@ -193,11 +212,12 @@
     mine = lax.dynamic_index_in_dim(blocks, core, 1, False)
     other = lax.dynamic_index_in_dim(blocks, 1 - core, 1, False).astype(BF16)
     pair = (mine + swapped(other, "context", 1).astype(F32)).astype(BF16)
-    groups = [list(range(core, parts, 2)) for core in range(2)]
-    came = lax.all_to_all(
-        pair, "context", split_axis=0, concat_axis=0, tiled=True, axis_index_groups=groups
-    )
-    return jnp.sum(came.astype(F32), 0)
+    row = lax.axis_index("context") // 2
+    total = lax.dynamic_index_in_dim(pair, row, 0, False).astype(F32)
+    for k in range(1, parts // 2):
+        sent = lax.dynamic_index_in_dim(pair, row ^ k, 0, False)
+        total = total + swapped(sent, "context", 2 * k).astype(F32)
+    return (pair, total)
 
 
 def to_channels(blocks):
@@ -228,41 +248,63 @@
     pair_after = passed_along(heads, "context", -1).astype(F32)
     product = to_channels(product_out)
 
-    found = [dot(cot, out_proj, 1, 1).astype(BF16) for cot in cots]
+    filter_b = long_filter.astype(BF16)
+    inverse = 1.0 / seq_len
+    straight = seq_len <= 1024
+    weights = out_proj
+    if straight:
+        waves = table(0, seq_len, seq_len)
+        filter_spec = dot(waves, filter_b, 1, 1)
+        weights = ordered(out_proj, filter_spec)
+    found = [dot(cot, weights, 1, 1).astype(BF16) for cot in cots]
     found = [found[0]] + [swapped(found[k], "dp", k) for k in range(1, parts_dp)]
     gate_grad, grad_long_out = call(
         grad_long_kernel, "grad_long", [plane] * 2, 1, me_dp, query, *found
     )
     grad_long = to_channels(grad_long_out)
-
-    filter_b = long_filter.astype(BF16)
-    freqs = seq_len if seq_len <= 1024 else 256
-    if freqs == seq_len:
-        terms = long_terms(0, freqs, filter_b, product, grad_long)
+    product_f, grad_long_f = (product.astype(F32), grad_long.astype(F32))
+
+    def finished(total, direct):
+        return (total * inverse + skip_gain[None, :] * direct).astype(BF16)
+
+    if straight:
+        product_spec = dot(waves, ordered(product, grad_long_out), 1, 0)
+        out_sum = dot(waves, spectral_product(filter_spec, product_spec, False), 0, 0)
+        long_chan = finished(out_sum, product_f)
+        grad_spec = dot(waves, ordered(grad_long, long_chan), 1, 0)
+        back_sum = dot(waves, spectral_product(filter_spec, grad_spec, True), 0, 0)
+        back_chan = finished(back_sum, grad_long_f)
+        late_spec = ordered(grad_spec, back_chan)
+        lag_sum = dot(spectral_product(product_spec, late_spec, True), waves, 0, 0)
     else:
+        freqs = 256
 
         def step(carry, first):
-            new = long_terms(first, freqs, filter_b, product, grad_long)
+            new = transforms(table(first, freqs, seq_len), filter_b, product, grad_long)
             return (tuple(a + b for a, b in zip(carry, new)), None)
 
         zero = jnp.zeros((seq_len, blk), F32)
         start = (zero, zero, jnp.zeros((blk, seq_len), F32))
         terms, _ = lax.scan(step, start, jnp.arange(0, seq_len, freqs))
-    out_sum, back_sum, lag_sum = terms
-    inverse = 1.0 / seq_len
-    product_f, grad_long_f = (product.astype(F32), grad_long.astype(F32))
-    long_chan = (out_sum * inverse + skip_gain[None, :] * product_f).astype(BF16)
+        out_sum, back_sum, lag_sum = terms
+        long_chan = finished(out_sum, product_f)
+        back_chan = finished(back_sum, grad_long_f)
     long_out = to_positions(long_chan.reshape(parts, rows, blk))
-    back_chan = (back_sum * inverse + skip_gain[None, :] * grad_long_f).astype(BF16)
     back_blocks = back_chan.reshape(parts, rows, blk)
     next_heads = jnp.concatenate([back_blocks[1:, :2], jnp.zeros((1, 2, blk), BF16)], 0)
     grad_product = to_positions(jnp.concatenate([back_blocks, next_heads], 1))
+
+    grad_filter = summed_blocks(lag_sum, "dp", 1) * (scale_factor * inverse)
+    skip_sum = jnp.sum(grad_long_f * product_f, 0, keepdims=True)
+    grad_skip = all_sum(skip_sum, "dp", bits_of(parts_dp)) * scale_factor
 
     piece = jax.ShapeDtypeStruct((rows, chans // parts_dp), BF16)
     gates = call(gate_kernel, "gate", [piece] * parts_dp, 1, me_dp, query, long_out)
     gates = [gates[0]] + [swapped(gates[k], "dp", k) for k in range(1, parts_dp)]
     proj_sum = dot(jnp.concatenate(gates, 0), jnp.concatenate(cots, 0), 0, 0)
-    grad_proj = own_share(proj_sum, parts) * scale_factor
+    pair, share = own_share(proj_sum, parts)
+    grad_proj = share * scale_factor
+    grad_product = ordered(grad_product, pair, grad_filter, grad_skip)
 
     query_heads = gate_grad[:, :2].astype(F32) * long_out[:, :2].astype(F32)
     query_after = passed_along(query_heads, "context", -1)
@@ -271,7 +313,7 @@
         "stream_grads",
         [
             jax.ShapeDtypeStruct((rows, width), BF16),
-            jax.ShapeDtypeStruct((parts, 9, blk), F32),
+            jax.ShapeDtypeStruct((3, width), F32),
         ],
         0,
         projected,
@@ -286,21 +328,10 @@
         pair_after,
     )
 
-    grad_filter = summed_blocks(lag_sum, "dp", 1) * (scale_factor * inverse)
-    skip_sum = jnp.sum(grad_long_f * product_f, 0, keepdims=True)
-    grad_skip = skip_sum
-    for k in range(1, parts_dp):
-        grad_skip = grad_skip + swapped(skip_sum, "dp", k)
-
-    shares = lax.all_to_all(tap_sums, "context", split_axis=0, concat_axis=0, tiled=True)
-    share = jnp.sum(shares, 0)
-    total = share
-    for k in range(1, parts_dp):
-        total = total + swapped(share, "dp", k)
-    every = jnp.broadcast_to((total * scale_factor)[None], (parts, 9, blk))
-    taps_out = lax.all_to_all(every, "context", split_axis=0, concat_axis=0, tiled=True)
-    grad_taps = taps_out.reshape(parts, 3, 3, blk).transpose(2, 1, 0, 3).reshape(3, width)
-    return (grad_inputs, grad_taps, grad_filter, grad_skip[0] * scale_factor, grad_proj)
+    tap_sums = tap_sums + swapped(tap_sums, "context", 1)
+    tap_sums = all_sum(tap_sums, "dp", bits_of(parts_dp))
+    grad_taps = all_sum(tap_sums, "context", bits_of(parts, 2)) * scale_factor
+    return (grad_inputs, grad_taps, grad_filter, grad_skip[0], grad_proj)
 
 
 def solution(mesh):

time: 187 us -> 175 us (0.936)
  blocking collectives: 9.16 us -> 0 us
  starting transfers between devices: 51.3 us -> 57 us
  other arithmetic: 20.9 us -> 15.7 us
  local copies, waits for them, and re-layouts: 13.2 us -> 17.7 us
  matrix products: 31.7 us -> 27.7 us
  waiting for transfers between devices: 49.9 us -> 46.8 us
    ppermute x19 -> x26, waiting for transfers between devices: 14.5 us -> 38.2 us  [swapped(): lax.ppermute(value, axis, [(i, i ^ mask) for i in range(lax.axis_size(axi...]
    all_to_all x2, waiting for transfers between devices: 18.5 us -> 2.87 us  [to_positions(): lax.all_to_all(blocks, 'context', split_axis=0, concat_axis=0, tiled=True)]
    ppermute x19 -> x26, starting transfers between devices: 22.2 us -> 34.7 us  [swapped(): lax.ppermute(value, axis, [(i, i ^ mask) for i in range(lax.axis_size(axi...]
    all_to_all x2 -> x0, waiting for transfers between devices: 10.7 us -> none  [the longest x1 7.16 us: own_share(): lax.all_to_all(pair, 'context', split_axis=0, concat_axis=0, tiled=True,...]
    all_to_all x1 -> x0, blocking collectives: 9.16 us -> none  [body(): lax.all_to_all(tap_sums, 'context', split_axis=0, concat_axis=0, tiled=True)]
    all_to_all x2 -> x0, starting transfers between devices: 6.89 us -> none  [the longest x1 3.52 us: own_share(): lax.all_to_all(pair, 'context', split_axis=0, concat_axis=0, tiled=True,...]
    unnamed x43 -> x54, local copies, waits for them, and re-layouts: 9.43 us -> 14.6 us
    dot_general x11, matrix products: 31.7 us -> 27.7 us  [dot(): lax.dot_general(left, right, (((left_dim,), (right_dim,)), ((), ())), pre...]
  transfers between devices with their start and end apart: 28 -> 33, of which waited for: 13 -> 15; matrix products, arithmetic and copies ran while one was open for 26% -> 26% of each run, Pallas kernels for 4% -> 2%
where the time goes in v4:
time: 175 us; the launch traced here: 174 us
  starting transfers between devices  57 us (33%)
  waiting for transfers between devices  46.8 us (27%)
  matrix products  27.7 us (16%)
  local copies, waits for them, and re-layouts  17.7 us (10%)
  other arithmetic  15.7 us (9%)
  Pallas kernels  7.73 us (4%)
    ppermute x26, waiting for transfers between devices, swapped(): lax.ppermute(value, axis, [(i, i ^ mask) for i in range(lax.axis_size(axi...  38.2 us
    ppermute x26, starting transfers between devices, swapped(): lax.ppermute(value, axis, [(i, i ^ mask) for i in range(lax.axis_size(axi...  34.7 us
    dot_general x11, matrix products, dot(): lax.dot_general(left, right, (((left_dim,), (right_dim,)), ((), ())), pre...  27.7 us
    unnamed x54, local copies, waits for them, and re-layouts  14.6 us
    all_to_all x2, starting transfers between devices, to_channels(): lax.all_to_all(blocks, 'context', split_axis=0, concat_axis=0, tiled=True)  11.2 us
    pallas_call x4, Pallas kernels, call(): pl.pallas_call(kernel, out_shape=outs, in_specs=[SMEM] * smem + [VMEM] *...  7.73 us
    all_to_all x2, starting transfers between devices, to_positions(): lax.all_to_all(blocks, 'context', split_axis=0, concat_axis=0, tiled=True)  7.03 us
    another operation x4, other arithmetic  5.83 us
  transfers between devices with their start and end apart: 33, of which 15 were waited for; matrix products, arithmetic and copies ran while one was open for 26% of the time, Pallas kernels for 2%

profile of v4, /device:TPU:0, one launch (start us, length us, event | category | flops | bytes accessed | tf_op | source)
XLA Modules:
  0.0 173.8 jit_solution(11622365487118282760)
XLA Ops:
  0.6 3.0 %collective-permute-start.3 = (bf16[128,2048]{1,0:T(8,128)(2,1)}, bf16[128,2048]{1,0:T(8,128)(2,1)}, u32[]{:S(2)}, u32[]{:S(2)}) collective-permute-start(bf16[128,2048]{1,0:T(8,128)(2,1)} %param.11), channel_id=1, source_target_pairs={{0,16},{8,24},{16,0},{24,8},{1,17},{9,25},{17,1},{25,9},{2,18},{10... | collective-permute-start | bytes 1572872 | tf_op jit(solution)/shard_map/ppermute | solution.py:21
  3.7 1.5 collective-permute-start.1
  5.2 0.9 slice.46
  6.1 1.3 collective-permute-start
  7.5 1.1 fusion.55
  8.6 1.5 subtract_convert_fusion
  11.3 2.7 %fusion.40 = f32[2048,256]{1,0:T(8,128)} fusion(bf16[2048,1024]{1,0:T(8,128)(2,1)S(1)} %bitcast.56, f32[256,1024]{1,0:T(8,128)S(1)} %copy-done.21), kind=kOutput, calls=%fused_computation.60 | convolution fusion | flops 1074003968 | bytes 7340032 | tf_op jit(solution)/shard_map/dot_general | solution.py:149
  14.1 1.2 short_convs.1
  16.9 6.2 %all-to-all-start = ((bf16[8,128,256]{2,1,0:T(8,128)(2,1)}), bf16[8,128,256]{2,1,0:T(8,128)(2,1)}, u32[]{:S(2)}, u32[]{:S(2)}) async-start(bf16[8,128,256]{2,1,0:T(8,128)(2,1)} %copy-done.9), calls=%async_computation | async-start | bytes 1048576 | tf_op jit(solution)/shard_map/all_to_all | solution.py:224
  23.9 1.3 collective-permute-start.18
  25.2 2.5 %fusion.14 = bf16[128,512]{1,0:T(8,128)(2,1)} fusion(bf16[512,2048]{1,0:T(8,128)(2,1)S(1)} %copy-done, bf16[128,2048]{1,0:T(8,128)(2,1)} %collective-permute-done.1), kind=kOutput, calls=%fused_computation.25 | convolution fusion | flops 268500992 | bytes 2752512 | tf_op jit(solution)/shard_map/dot_general | solution.py:149
  27.8 1.5 collective-permute-start.2
  29.3 2.5 %fusion.15 = bf16[128,512]{1,0:T(8,128)(2,1)} fusion(bf16[512,2048]{1,0:T(8,128)(2,1)S(1)} %copy-done, bf16[128,2048]{1,0:T(8,128)(2,1)} %collective-permute-done.3), kind=kOutput, calls=%fused_computation.26 | convolution fusion | flops 268500992 | bytes 2752512 | tf_op jit(solution)/shard_map/dot_general | solution.py:149
  31.8 1.5 collective-permute-start.4
  33.3 1.9 %fusion.16 = bf16[128,512]{1,0:T(8,128)(2,1)S(1)} fusion(bf16[512,2048]{1,0:T(8,128)(2,1)S(1)} %copy-done, bf16[128,2048]{1,0:T(8,128)(2,1)} %collective-permute-done.5), kind=kOutput, calls=%fused_computation.27 | convolution fusion | flops 268500992 | bytes 2752512 | tf_op jit(solution)/shard_map/dot_general | solution.py:149
  36.7 1.8 %collective-permute-done.4.refs_2_ = bf16[128,512]{1,0:T(8,128)(2,1)} collective-permute-done((bf16[128,512]{1,0:T(8,128)(2,1)}, bf16[128,512]{1,0:T(8,128)(2,1)}, u32[]{:S(2)}, u32[]{:S(2)}) %collective-permute-start.4) | collective-permute-done | bytes 131104 | tf_op jit(solution)/shard_map/ppermute | solution.py:21
  38.5 3.8 %collective-permute-done.6.refs_3_ = bf16[128,512]{1,0:T(8,128)(2,1)S(1)} collective-permute-done((bf16[128,512]{1,0:T(8,128)(2,1)S(1)}, bf16[128,512]{1,0:T(8,128)(2,1)S(1)}, u32[]{:S(2)}, u32[]{:S(2)}) %collective-permute-start.6) | collective-permute-done | bytes 131104 | tf_op jit(solution)/shard_map/ppermute | solution.py:21
  42.3 1.8 %grad_long.1 = (bf16[8,128,256]{2,1,0:T(8,128)(2,1)S(1)}, bf16[8,128,256]{2,1,0:T(8,128)(2,1)}) custom-call(s32[1]{0:T(128)} %bitcast.me_ref, bf16[8,128,256]{2,1,0:T(8,128)(2,1)S(1)} %get-tuple-element.22.query_ref, bf16[128,512]{1,0:T(8,128)(2,1)S(1)} %fusion.13.refs_0_, bf16[128,512]{1,0:T(8,128)(2,1)S(1)} %collective-permute-done.2.refs_1_, ...), custom_call_target="tpu_custom_call" | custom-call | flops 8388640 | bytes 2097160 | tf_op jit(solution)/shard_map/grad_long/pallas_call | solution.py:47
  44.9 5.0 %all-to-all-start.2 = ((bf16[8,128,256]{2,1,0:T(8,128)(2,1)}), bf16[8,128,256]{2,1,0:T(8,128)(2,1)S(1)}, u32[]{:S(2)}, u32[]{:S(2)}) async-start(bf16[8,128,256]{2,1,0:T(8,128)(2,1)} %get-tuple-element.26), calls=%async_computation.2 | async-start | bytes 1048576 | tf_op jit(solution)/shard_map/all_to_all | solution.py:224
  50.0 3.8 %fusion.62 = f32[2048,256]{1,0:T(8,128)S(1)} fusion(bf16[2048,1024]{1,0:T(8,128)(2,1)} %bitcast.57, bf16[1024,256]{1,0:T(8,128)(2,1)} %bitcast.6), kind=kOutput, calls=%fused_computation.104 | convolution fusion | flops 1073741824 | bytes 6815744 | tf_op jit(solution)/shard_map/dot_general | solution.py:149
  54.2 0.9 copy-done.17
  55.1 1.6 copy-done.14
  56.7 3.1 %fusion.12 = bf16[1024,256]{1,0:T(8,128)(2,1)} fusion(bf16[2048,1024]{1,0:T(8,128)(2,1)S(1)} %bitcast.59, bf16[1024,256]{1,0:T(8,128)(2,1)S(1)} %get-tuple-element.44, bf16[1024,256]{1,0:T(8,128)(2,1)S(1)} %get-tuple-element.43, bf16[1024,256]{1,0:T(8,128)(2,1)} %bitcast.6, f32[256]{0:T(256)S(1)} %copy-done.26), kind=kOutput, calls=%fused_computation.19 | convolution fusion | flops 1077149696 | bytes 6292480 | tf_op jit(solution)/shard_map/dot_general | solution.py:149
  59.8 5.5 %all-to-all-done.2 = bf16[8,128,256]{2,1,0:T(8,128)(2,1)S(1)} async-done(((bf16[8,128,256]{2,1,0:T(8,128)(2,1)}), bf16[8,128,256]{2,1,0:T(8,128)(2,1)S(1)}, u32[]{:S(2)}, u32[]{:S(2)}) %all-to-all-start.2) | async-done | bytes 524320 | tf_op jit(solution)/shard_map/all_to_all | solution.py:224
  66.1 3.5 %all-to-all-start.1 = ((bf16[8,128,256]{2,1,0:T(8,128)(2,1)}), bf16[8,128,256]{2,1,0:T(8,128)(2,1)S(1)}, u32[]{:S(2)}, u32[]{:S(2)}) async-start(bf16[8,128,256]{2,1,0:T(8,128)(2,1)} %bitcast.68), calls=%async_computation.1 | async-start | bytes 1048576 | tf_op jit(solution)/shard_map/all_to_all | solution.py:229
  69.6 1.4 multiply_reduce_fusion
  71.6 1.5 collective-permute-start.15
  73.1 3.8 %fusion.63 = f32[2048,256]{1,0:T(8,128)S(1)} fusion(bf16[2048,1024]{1,0:T(8,128)(2,1)} %bitcast.58, bf16[1024,256]{1,0:T(8,128)(2,1)} %bitcast.64), kind=kOutput, calls=%fused_computation.105 | convolution fusion | flops 1073741824 | bytes 6815744 | tf_op jit(solution)/shard_map/dot_general | solution.py:149
  77.3 0.9 copy-done.18
  78.3 1.6 copy-done.15
  79.9 2.1 %fusion.11 = bf16[1024,256]{1,0:T(8,128)(2,1)} fusion(bf16[2048,1024]{1,0:T(8,128)(2,1)S(1)} %bitcast.60, bf16[1024,256]{1,0:T(8,128)(2,1)S(1)} %get-tuple-element.42, bf16[1024,256]{1,0:T(8,128)(2,1)S(1)} %get-tuple-element.41, bf16[1024,256]{1,0:T(8,128)(2,1)S(1)} %bitcast.65, f32[256]{0:T(256)S(1)} %copy-done.26), kind=kOutput, calls=%fused_computation.18 | convolution fusion | flops 1077149696 | bytes 6292480 | tf_op jit(solution)/shard_map/dot_general | solution.py:149
  82.0 2.9 %all-to-all-done.1.long_ref.refs_4_ = bf16[8,128,256]{2,1,0:T(8,128)(2,1)S(1)} async-done(((bf16[8,128,256]{2,1,0:T(8,128)(2,1)}), bf16[8,128,256]{2,1,0:T(8,128)(2,1)S(1)}, u32[]{:S(2)}, u32[]{:S(2)}) %all-to-all-start.1) | async-done | bytes 524320 | tf_op jit(solution)/shard_map/all_to_all | solution.py:229
  86.7 2.4 %collective-permute-start.9 = (bf16[128,512]{1,0:T(8,128)(2,1)}, bf16[128,512]{1,0:T(8,128)(2,1)}, u32[]{:S(2)}, u32[]{:S(2)}) collective-permute-start(bf16[128,512]{1,0:T(8,128)(2,1)} %get-tuple-element.32), channel_id=1, source_target_pairs={{0,24},{8,16},{16,8},{24,0},{1,25},{9,17},{17,9},{25,1},{2,26},{10... | collective-permute-start | bytes 393224 | tf_op jit(solution)/shard_map/ppermute | solution.py:21
  89.2 3.5 %add_convert_fusion = (bf16[1024,256]{1,0:T(8,128)(2,1)}, bf16[1024,256]{1,0:T(8,128)(2,1)}) fusion(f32[2048,256]{1,0:T(8,128)} %copy-done.18, f32[2048,256]{1,0:T(8,128)} %copy-done.17), kind=kLoop, calls=%fused_computation.43 | loop fusion | flops 2097152 | bytes 5242880 | tf_op jit(solution)/shard_map/convert.1
  92.7 0.8 fusion.29
  93.6 3.5 %all-to-all-start.3 = ((bf16[8,130,256]{2,1,0:T(8,128)(2,1)}), bf16[8,130,256]{2,1,0:T(8,128)(2,1)S(1)}, u32[]{:S(2)}, u32[]{:S(2)}) async-start(bf16[8,130,256]{2,1,0:T(8,128)(2,1)} %fusion.29), calls=%async_computation.3 | async-start | bytes 1114112 | tf_op jit(solution)/shard_map/all_to_all | solution.py:229
  97.7 3.1 %fusion = f32[512,2048]{1,0:T(8,128)S(1)} fusion(bf16[128,2048]{1,0:T(8,128)(2,1)} %collective-permute-done.5, bf16[128,2048]{1,0:T(8,128)(2,1)} %collective-permute-done.3, bf16[128,2048]{1,0:T(8,128)(2,1)} %collective-permute-done.1, bf16[128,2048]{1,0:T(8,128)(2,1)} %param.11, bf16[128,512]{1,0:T(8,128)(2,1)} %collective-permute-done.9, ...), kind=kOutput, calls=%fused_computation.3 | convolution fusion | flops 1084227584 | bytes 6815744 | tf_op jit(solution)/shard_map/dot_general | solution.py:149
  102.1 1.3 fusion.25
  103.4 1.6 collective-permute-start.11
  105.5 1.5 collective-permute-start.12
  107.6 2.3 %collective-permute-done.11 = bf16[256,256]{1,0:T(8,128)(2,1)S(1)} collective-permute-done((bf16[256,256]{1,0:T(8,128)(2,1)S(1)}, bf16[256,256]{1,0:T(8,128)(2,1)S(1)}, u32[]{:S(2)}, u32[]{:S(2)}) %collective-permute-start.11) | collective-permute-done | bytes 131104 | tf_op jit(solution)/shard_map/ppermute | solution.py:21
  109.8 2.0 %collective-permute-done.13 = bf16[256,256]{1,0:T(8,128)(2,1)S(1)} collective-permute-done((bf16[256,256]{1,0:T(8,128)(2,1)S(1)}, bf16[256,256]{1,0:T(8,128)(2,1)S(1)}, u32[]{:S(2)}, u32[]{:S(2)}) %collective-permute-start.13) | collective-permute-done | bytes 131104 | tf_op jit(solution)/shard_map/ppermute | solution.py:21
  111.8 1.4 collective-permute-done.12
  114.7 1.5 collective-permute-start.17
  116.2 1.3 fusion.8
  117.8 1.4 copy-done.2
  119.2 1.0 copy-done.4
  120.2 1.0 copy-done.6
  121.3 1.0 copy-done.8
  122.3 3.9 %stream_grads.1 = (bf16[128,6144]{1,0:T(8,128)(2,1)}, f32[3,6144]{1,0:T(4,128)S(1)}) custom-call(bf16[128,6144]{1,0:T(8,128)(2,1)S(1)} %copy-done.2, f32[2,6144]{1,0:T(2,128)S(1)} %convert_element_type.133.prev_ref.refs_1_, f32[3,6144]{1,0:T(4,128)S(1)} %copy-done.10, bf16[8,128,256]{2,1,0:T(8,128)(2,1)S(1)} %copy-done.8, ...), custom_call_target="tpu_custom_call" | custom-call | flops 34996224 | bytes 8749056 | tf_op jit(solution)/shard_map/stream_grads/pallas_call | solution.py:47
  126.2 2.0 %collective-permute-start.19 = (f32[3,6144]{1,0:T(4,128)S(1)}, f32[3,6144]{1,0:T(4,128)S(1)}, u32[]{:S(2)}, u32[]{:S(2)}) collective-permute-start(f32[3,6144]{1,0:T(4,128)S(1)} %get-tuple-element.38), channel_id=1, source_target_pairs={{0,1},{1,0},{2,3},{3,2},{4,5},{5,4},{6,7},{7,6},{8,9},{9,8},{10,11... | collective-permute-start | bytes 221192 | tf_op jit(solution)/shard_map/ppermute | solution.py:21
  128.3 0.9 collective-permute-done.19
  129.2 2.5 %collective-permute-start.22 = (f32[3,6144]{1,0:T(4,128)S(1)}, f32[3,6144]{1,0:T(4,128)S(1)}, u32[]{:S(2)}, u32[]{:S(2)}) collective-permute-start(f32[3,6144]{1,0:T(4,128)S(1)} %add.180), channel_id=1, source_target_pairs={{0,24},{8,16},{16,8},{24,0},{1,25},{9,17},{17,9},{25,1},{2,26},{10... | collective-permute-start | bytes 221192 | tf_op jit(solution)/shard_map/ppermute | solution.py:21
  132.8 2.5 %collective-permute-done.22 = f32[3,6144]{1,0:T(4,128)S(1)} collective-permute-done((f32[3,6144]{1,0:T(4,128)S(1)}, f32[3,6144]{1,0:T(4,128)S(1)}, u32[]{:S(2)}, u32[]{:S(2)}) %collective-permute-start.22) | collective-permute-done | bytes 73760 | tf_op jit(solution)/shard_map/ppermute | solution.py:21
  135.3 2.0 %collective-permute-done.21 = f32[3,6144]{1,0:T(4,128)S(1)} collective-permute-done((f32[3,6144]{1,0:T(4,128)S(1)}, f32[3,6144]{1,0:T(4,128)S(1)}, u32[]{:S(2)}, u32[]{:S(2)}) %collective-permute-start.21) | collective-permute-done | bytes 73760 | tf_op jit(solution)/shard_map/ppermute | solution.py:21
  137.5 2.5 %collective-permute-start.25 = (f32[3,6144]{1,0:T(4,128)S(1)}, f32[3,6144]{1,0:T(4,128)S(1)}, u32[]{:S(2)}, u32[]{:S(2)}) collective-permute-start(f32[3,6144]{1,0:T(4,128)S(1)} %add_add_fusion), channel_id=1, source_target_pairs={{0,6},{1,7},{2,4},{3,5},{4,2},{5,3},{6,0},{7,1},{8,14},{9,15},{10,... | collective-permute-start | bytes 221192 | tf_op jit(solution)/shard_map/ppermute | solution.py:21
  140.5 1.4 collective-permute-start.23
  141.9 1.2 dynamic-slice_bitcast_fusion.2
  143.7 2.4 %collective-permute-start.28 = (bf16[64,2048]{1,0:T(8,128)(2,1)S(1)}, bf16[64,2048]{1,0:T(8,128)(2,1)S(1)}, u32[]{:S(2)}, u32[]{:S(2)}) collective-permute-start(bf16[64,2048]{1,0:T(8,128)(2,1)S(1)} %get-tuple-element.46), channel_id=1, source_target_pairs={{0,6},{1,7},{2,4},{3,5},{4,2},{5,3},{6,0},{7,1},{8,14},{9,15},{10,... | collective-permute-start | bytes 786440 | tf_op jit(solution)/shard_map/ppermute | solution.py:21
  146.1 3.7 %collective-permute-start.27 = (bf16[64,2048]{1,0:T(8,128)(2,1)S(1)}, bf16[64,2048]{1,0:T(8,128)(2,1)S(1)}, u32[]{:S(2)}, u32[]{:S(2)}) collective-permute-start(bf16[64,2048]{1,0:T(8,128)(2,1)S(1)} %get-tuple-element.47), channel_id=1, source_target_pairs={{0,4},{1,5},{2,6},{3,7},{4,0},{5,1},{6,2},{7,3},{8,12},{9,13},{10,... | collective-permute-start | bytes 786440 | tf_op jit(solution)/shard_map/ppermute | solution.py:21
  151.1 3.8 %collective-permute-done.26 = bf16[64,2048]{1,0:T(8,128)(2,1)S(1)} collective-permute-done((bf16[64,2048]{1,0:T(8,128)(2,1)S(1)}, bf16[64,2048]{1,0:T(8,128)(2,1)S(1)}, u32[]{:S(2)}, u32[]{:S(2)}) %collective-permute-start.26) | collective-permute-done | bytes 262176 | tf_op jit(solution)/shard_map/ppermute | solution.py:21
  154.9 5.7 %collective-permute-done.28 = bf16[64,2048]{1,0:T(8,128)(2,1)S(1)} collective-permute-done((bf16[64,2048]{1,0:T(8,128)(2,1)S(1)}, bf16[64,2048]{1,0:T(8,128)(2,1)S(1)}, u32[]{:S(2)}, u32[]{:S(2)}) %collective-permute-start.28) | collective-permute-done | bytes 262176 | tf_op jit(solution)/shard_map/ppermute | solution.py:21
  160.5 11.4 %collective-permute-done.27 = bf16[64,2048]{1,0:T(8,128)(2,1)S(1)} collective-permute-done((bf16[64,2048]{1,0:T(8,128)(2,1)S(1)}, bf16[64,2048]{1,0:T(8,128)(2,1)S(1)}, u32[]{:S(2)}, u32[]{:S(2)}) %collective-permute-start.27) | collective-permute-done | bytes 262176 | tf_op jit(solution)/shard_map/ppermute | solution.py:21
  171.9 1.9 %fusion.39 = f32[64,2048]{1,0:T(8,128)} fusion(bf16[64,2048]{1,0:T(8,128)(2,1)S(1)} %collective-permute-done.28, bf16[64,2048]{1,0:T(8,128)(2,1)S(1)} %collective-permute-done.27, bf16[64,2048]{1,0:T(8,128)(2,1)S(1)} %collective-permute-done.26, bf16[4,64,2048]{2,1,0:T(8,128)(2,1)} %fusion.8, s32[]{:T(128)S(6)} %select_n.81), kind=kLoop, calls=%fused_computation.59 | loop fusion | flops 1048576 | bytes 1572868 | tf_op jit(solution)/shard_map/mul | solution.py:306
  (98 shorter events, 18.4 us)
Async XLA Ops:
  0.6 24.6 %copy-start = (bf16[512,2048]{1,0:T(8,128)(2,1)S(1)}, bf16[512,2048]{1,0:T(8,128)(2,1)}, u32[]{:S(2)}) copy-start(bf16[512,2048]{1,0:T(8,128)(2,1)} %param.10) | copy-start | bytes 6291460
  0.6 28.6 %collective-permute-start.3 = (bf16[128,2048]{1,0:T(8,128)(2,1)}, bf16[128,2048]{1,0:T(8,128)(2,1)}, u32[]{:S(2)}, u32[]{:S(2)}) collective-permute-start(bf16[128,2048]{1,0:T(8,128)(2,1)} %param.11), channel_id=1, source_target_pairs={{0,16},{8,24},{16,0},{24,8},{1,17},{9,25},{17,1},{25,9},{2,18},{10... | collective-permute-start | bytes 1572872 | tf_op jit(solution)/shard_map/ppermute | solution.py:21
  3.7 21.6 %collective-permute-start.1 = (bf16[128,2048]{1,0:T(8,128)(2,1)}, bf16[128,2048]{1,0:T(8,128)(2,1)}, u32[]{:S(2)}, u32[]{:S(2)}) collective-permute-start(bf16[128,2048]{1,0:T(8,128)(2,1)} %param.11), channel_id=1, source_target_pairs={{0,8},{8,0},{16,24},{24,16},{1,9},{9,1},{17,25},{25,17},{2,10},{10... | collective-permute-start | bytes 1572872 | tf_op jit(solution)/shard_map/ppermute | solution.py:21
  5.2 28.2 %collective-permute-start.5 = (bf16[128,2048]{1,0:T(8,128)(2,1)}, bf16[128,2048]{1,0:T(8,128)(2,1)}, u32[]{:S(2)}, u32[]{:S(2)}) collective-permute-start(bf16[128,2048]{1,0:T(8,128)(2,1)} %param.11), channel_id=1, source_target_pairs={{0,24},{8,16},{16,8},{24,0},{1,25},{9,17},{17,9},{25,1},{2,26},{10... | collective-permute-start | bytes 1572872 | tf_op jit(solution)/shard_map/ppermute | solution.py:21
  6.1 7.9 %collective-permute-start = (bf16[2,6144]{1,0:T(2,128)(2,1)S(1)}, bf16[2,6144]{1,0:T(2,128)(2,1)S(1)}, u32[]{:S(2)}, u32[]{:S(2)}) collective-permute-start(bf16[2,6144]{1,0:T(2,128)(2,1)S(1)} %slice.46), channel_id=1, source_target_pairs={{0,1},{1,2},{2,3},{3,4},{4,5},{5,6},{6,7},{8,9},{9,10},{10,11},{11... | collective-permute-start | bytes 73736 | tf_op jit(solution)/shard_map/ppermute | solution.py:17
  10.1 1.2 copy-start.21
  10.5 3.6 %copy-start.13 = (bf16[2,32,32,1024]{3,2,1,0:T(8,128)(2,1)}, bf16[2,32,32,1024]{3,2,1,0:T(8,128)(2,1)S(1)}, u32[]{:S(2)}) copy-start(bf16[2,32,32,1024]{3,2,1,0:T(8,128)(2,1)S(1)} %pad_maximum_fusion) | copy-start | bytes 12582916
  11.3 2.8 %copy-start.1 = (bf16[128,6144]{1,0:T(8,128)(2,1)S(1)}, bf16[128,6144]{1,0:T(8,128)(2,1)}, u32[]{:S(2)}) copy-start(bf16[128,6144]{1,0:T(8,128)(2,1)} %refs_0_.1) | copy-start | bytes 4718596
  11.3 2.8 %copy-start.10 = (f32[3,6144]{1,0:T(4,128)S(1)}, f32[3,6144]{1,0:T(4,128)}, u32[]{:S(2)}) copy-start(f32[3,6144]{1,0:T(4,128)} %refs_2_.1) | copy-start | bytes 221188
  15.3 0.8 copy-start.5
  16.1 0.8 copy-start.9
  16.9 14.9 %copy-start.3 = (bf16[8,128,256]{2,1,0:T(8,128)(2,1)}, bf16[8,128,256]{2,1,0:T(8,128)(2,1)S(1)}, u32[]{:S(2)}) copy-start(bf16[8,128,256]{2,1,0:T(8,128)(2,1)S(1)} %get-tuple-element.35.refs_6_) | copy-start | bytes 1572868
  16.9 28.0 %all-to-all-start = ((bf16[8,128,256]{2,1,0:T(8,128)(2,1)}), bf16[8,128,256]{2,1,0:T(8,128)(2,1)}, u32[]{:S(2)}, u32[]{:S(2)}) async-start(bf16[8,128,256]{2,1,0:T(8,128)(2,1)} %copy-done.9), calls=%async_computation | async-start | bytes 1048576 | tf_op jit(solution)/shard_map/all_to_all | solution.py:224
  23.9 12.7 %collective-permute-start.18 = (bf16[2,8,2,256]{3,2,1,0:T(2,128)(2,1)S(1)}, bf16[2,8,2,256]{3,2,1,0:T(2,128)(2,1)S(1)}, u32[]{:S(2)}, u32[]{:S(2)}) collective-permute-start(bf16[2,8,2,256]{3,2,1,0:T(2,128)(2,1)S(1)} %pad_maximum_fusion.1), channel_id=1, source_target_pairs={{1,0},{2,1},{3,2},{4,3},{5,4},{6,5},{7,6},{9,8},{10,9},{11,10},{12... | collective-permute-start | bytes 49160 | tf_op jit(solution)/shard_map/ppermute | solution.py:17
  27.8 8.0 %copy-start.25 = (bf16[128,2048]{1,0:T(8,128)(2,1)S(1)}, bf16[128,2048]{1,0:T(8,128)(2,1)}, u32[]{:S(2)}) copy-start(bf16[128,2048]{1,0:T(8,128)(2,1)} %param.11) | copy-start | bytes 1572868
  27.8 8.9 %collective-permute-start.2 = (bf16[128,512]{1,0:T(8,128)(2,1)}, bf16[128,512]{1,0:T(8,128)(2,1)S(1)}, u32[]{:S(2)}, u32[]{:S(2)}) collective-permute-start(bf16[128,512]{1,0:T(8,128)(2,1)} %fusion.14), channel_id=1, source_target_pairs={{0,8},{8,0},{16,24},{24,16},{1,9},{9,1},{17,25},{25,17},{2,10},{10... | collective-permute-start | bytes 393224 | tf_op jit(solution)/shard_map/ppermute | solution.py:21
  31.8 6.7 %collective-permute-start.4 = (bf16[128,512]{1,0:T(8,128)(2,1)}, bf16[128,512]{1,0:T(8,128)(2,1)}, u32[]{:S(2)}, u32[]{:S(2)}) collective-permute-start(bf16[128,512]{1,0:T(8,128)(2,1)} %fusion.15), channel_id=1, source_target_pairs={{0,16},{8,24},{16,0},{24,8},{1,17},{9,25},{17,1},{25,9},{2,18},{10... | collective-permute-start | bytes 393224 | tf_op jit(solution)/shard_map/ppermute | solution.py:21
  35.2 7.1 %collective-permute-start.6 = (bf16[128,512]{1,0:T(8,128)(2,1)S(1)}, bf16[128,512]{1,0:T(8,128)(2,1)S(1)}, u32[]{:S(2)}, u32[]{:S(2)}) collective-permute-start(bf16[128,512]{1,0:T(8,128)(2,1)S(1)} %fusion.16), channel_id=1, source_target_pairs={{0,24},{8,16},{16,8},{24,0},{1,25},{9,17},{17,9},{25,1},{2,26},{10... | collective-permute-start | bytes 393224 | tf_op jit(solution)/shard_map/ppermute | solution.py:21
  44.1 0.8 copy-start.7
  44.9 20.4 %all-to-all-start.2 = ((bf16[8,128,256]{2,1,0:T(8,128)(2,1)}), bf16[8,128,256]{2,1,0:T(8,128)(2,1)S(1)}, u32[]{:S(2)}, u32[]{:S(2)}) async-start(bf16[8,128,256]{2,1,0:T(8,128)(2,1)} %get-tuple-element.26), calls=%async_computation.2 | async-start | bytes 1048576 | tf_op jit(solution)/shard_map/all_to_all | solution.py:224
  50.0 3.8 %copy-start.11 = (f32[2048,256]{1,0:T(8,128)S(1)}, f32[2048,256]{1,0:T(8,128)}, u32[]{:S(2)}) copy-start(f32[2048,256]{1,0:T(8,128)} %fusion.40) | copy-start | bytes 6291460
  53.8 1.3 copy-start.17
  53.8 2.9 %copy-start.14 = (bf16[2,32,32,1024]{3,2,1,0:T(8,128)(2,1)S(1)}, bf16[2,32,32,1024]{3,2,1,0:T(8,128)(2,1)}, u32[]{:S(2)}) copy-start(bf16[2,32,32,1024]{3,2,1,0:T(8,128)(2,1)} %copy-done.13) | copy-start | bytes 12582916
  53.8 2.9 %copy-start.26 = (f32[256]{0:T(256)S(1)}, f32[256]{0:T(256)}, u32[]{:S(2)}) copy-start(f32[256]{0:T(256)} %param.9) | copy-start | bytes 3076
  65.3 0.8 copy-start.19
  66.1 18.8 %all-to-all-start.1 = ((bf16[8,128,256]{2,1,0:T(8,128)(2,1)}), bf16[8,128,256]{2,1,0:T(8,128)(2,1)S(1)}, u32[]{:S(2)}, u32[]{:S(2)}) async-start(bf16[8,128,256]{2,1,0:T(8,128)(2,1)} %bitcast.68), calls=%async_computation.1 | async-start | bytes 1048576 | tf_op jit(solution)/shard_map/all_to_all | solution.py:229
  71.0 33.9 %collective-permute-start.16 = (f32[1,256]{1,0:T(1,128)S(1)}, f32[1,256]{1,0:T(1,128)S(1)}, u32[]{:S(2)}, u32[]{:S(2)}) collective-permute-start(f32[1,256]{1,0:T(1,128)S(1)} %bitcast.69), channel_id=1, source_target_pairs={{0,24},{8,16},{16,8},{24,0},{1,25},{9,17},{17,9},{25,1},{2,26},{10... | collective-permute-start | bytes 3080 | tf_op jit(solution)/shard_map/ppermute | solution.py:21
  71.6 33.9 %collective-permute-start.15 = (f32[1,256]{1,0:T(1,128)S(1)}, f32[1,256]{1,0:T(1,128)S(1)}, u32[]{:S(2)}, u32[]{:S(2)}) collective-permute-start(f32[1,256]{1,0:T(1,128)S(1)} %bitcast.70), channel_id=1, source_target_pairs={{0,16},{8,24},{16,0},{24,8},{1,17},{9,25},{17,1},{25,9},{2,18},{10... | collective-permute-start | bytes 3080 | tf_op jit(solution)/shard_map/ppermute | solution.py:21
  73.1 3.8 %copy-start.12 = (f32[2048,256]{1,0:T(8,128)S(1)}, f32[2048,256]{1,0:T(8,128)}, u32[]{:S(2)}) copy-start(f32[2048,256]{1,0:T(8,128)} %fusion.40) | copy-start | bytes 6291460
  76.9 1.4 copy-start.18
  76.9 2.9 %copy-start.15 = (bf16[2,32,32,1024]{3,2,1,0:T(8,128)(2,1)S(1)}, bf16[2,32,32,1024]{3,2,1,0:T(8,128)(2,1)}, u32[]{:S(2)}) copy-start(bf16[2,32,32,1024]{3,2,1,0:T(8,128)(2,1)} %copy-done.13) | copy-start | bytes 12582916
  76.9 3.1 %copy-start.20 = (bf16[8,128,256]{2,1,0:T(8,128)(2,1)S(1)}, bf16[8,128,256]{2,1,0:T(8,128)(2,1)}, u32[]{:S(2)}) copy-start(bf16[8,128,256]{2,1,0:T(8,128)(2,1)} %copy-done.19) | copy-start | bytes 1572868
  85.7 11.4 %collective-permute-start.7 = (bf16[128,512]{1,0:T(8,128)(2,1)}, bf16[128,512]{1,0:T(8,128)(2,1)}, u32[]{:S(2)}, u32[]{:S(2)}) collective-permute-start(bf16[128,512]{1,0:T(8,128)(2,1)} %get-tuple-element.30), channel_id=1, source_target_pairs={{0,8},{8,0},{16,24},{24,16},{1,9},{9,1},{17,25},{25,17},{2,10},{10... | collective-permute-start | bytes 393224 | tf_op jit(solution)/shard_map/ppermute | solution.py:21
  86.2 11.5 %collective-permute-start.8 = (bf16[128,512]{1,0:T(8,128)(2,1)}, bf16[128,512]{1,0:T(8,128)(2,1)}, u32[]{:S(2)}, u32[]{:S(2)}) collective-permute-start(bf16[128,512]{1,0:T(8,128)(2,1)} %get-tuple-element.31), channel_id=1, source_target_pairs={{0,16},{8,24},{16,0},{24,8},{1,17},{9,25},{17,1},{25,9},{2,18},{10... | collective-permute-start | bytes 393224 | tf_op jit(solution)/shard_map/ppermute | solution.py:21
  86.7 6.0 %copy-start.22 = (bf16[1024,256]{1,0:T(8,128)(2,1)S(1)}, bf16[1024,256]{1,0:T(8,128)(2,1)}, u32[]{:S(2)}) copy-start(bf16[1024,256]{1,0:T(8,128)(2,1)} %fusion.11) | copy-start | bytes 1572868
  86.7 11.0 %collective-permute-start.9 = (bf16[128,512]{1,0:T(8,128)(2,1)}, bf16[128,512]{1,0:T(8,128)(2,1)}, u32[]{:S(2)}, u32[]{:S(2)}) collective-permute-start(bf16[128,512]{1,0:T(8,128)(2,1)} %get-tuple-element.32), channel_id=1, source_target_pairs={{0,24},{8,16},{16,8},{24,0},{1,25},{9,17},{17,9},{25,1},{2,26},{10... | collective-permute-start | bytes 393224 | tf_op jit(solution)/shard_map/ppermute | solution.py:21
  93.6 24.0 %all-to-all-start.3 = ((bf16[8,130,256]{2,1,0:T(8,128)(2,1)}), bf16[8,130,256]{2,1,0:T(8,128)(2,1)S(1)}, u32[]{:S(2)}, u32[]{:S(2)}) async-start(bf16[8,130,256]{2,1,0:T(8,128)(2,1)} %fusion.29), calls=%async_computation.3 | async-start | bytes 1114112 | tf_op jit(solution)/shard_map/all_to_all | solution.py:229
  97.1 9.9 %collective-permute-start.14 = (f32[1,256]{1,0:T(1,128)S(1)}, f32[1,256]{1,0:T(1,128)S(1)}, u32[]{:S(2)}, u32[]{:S(2)}) collective-permute-start(f32[1,256]{1,0:T(1,128)S(1)} %bitcast.71), channel_id=1, source_target_pairs={{0,8},{8,0},{16,24},{24,16},{1,9},{9,1},{17,25},{25,17},{2,10},{10... | collective-permute-start | bytes 3080 | tf_op jit(solution)/shard_map/ppermute | solution.py:21
  97.7 3.4 %copy-start.16 = (bf16[2,32,32,1024]{3,2,1,0:T(8,128)(2,1)S(1)}, bf16[2,32,32,1024]{3,2,1,0:T(8,128)(2,1)}, u32[]{:S(2)}) copy-start(bf16[2,32,32,1024]{3,2,1,0:T(8,128)(2,1)} %copy-done.13) | copy-start | bytes 12582916
  100.9 1.0 copy-start.23
  100.9 1.2 copy-start.24
  101.0 15.2 %collective-permute-start.10 = (bf16[4,64,2048]{2,1,0:T(8,128)(2,1)S(1)}, bf16[4,64,2048]{2,1,0:T(8,128)(2,1)S(1)}, u32[]{:S(2)}, u32[]{:S(2)}) collective-permute-start(bf16[4,64,2048]{2,1,0:T(8,128)(2,1)S(1)} %fusion.18), channel_id=1, source_target_pairs={{0,1},{1,0},{2,3},{3,2},{4,5},{5,4},{6,7},{7,6},{8,9},{9,8},{10,11... | collective-permute-start | bytes 3145736 | tf_op jit(solution)/shard_map/ppermute | solution.py:21
  103.4 6.4 %collective-permute-start.11 = (bf16[256,256]{1,0:T(8,128)(2,1)S(1)}, bf16[256,256]{1,0:T(8,128)(2,1)S(1)}, u32[]{:S(2)}, u32[]{:S(2)}) collective-permute-start(bf16[256,256]{1,0:T(8,128)(2,1)S(1)} %get-tuple-element.48), channel_id=1, source_target_pairs={{0,8},{8,0},{16,24},{24,16},{1,9},{9,1},{17,25},{25,17},{2,10},{10... | collective-permute-start | bytes 393224 | tf_op jit(solution)/shard_map/ppermute | solution.py:21
  105.0 6.8 %collective-permute-start.13 = (bf16[256,256]{1,0:T(8,128)(2,1)S(1)}, bf16[256,256]{1,0:T(8,128)(2,1)S(1)}, u32[]{:S(2)}, u32[]{:S(2)}) collective-permute-start(bf16[256,256]{1,0:T(8,128)(2,1)S(1)} %get-tuple-element.49), channel_id=1, source_target_pairs={{0,24},{8,16},{16,8},{24,0},{1,25},{9,17},{17,9},{25,1},{2,26},{10... | collective-permute-start | bytes 393224 | tf_op jit(solution)/shard_map/ppermute | solution.py:21
  105.5 7.7 %collective-permute-start.12 = (bf16[256,256]{1,0:T(8,128)(2,1)S(1)}, bf16[256,256]{1,0:T(8,128)(2,1)S(1)}, u32[]{:S(2)}, u32[]{:S(2)}) collective-permute-start(bf16[256,256]{1,0:T(8,128)(2,1)S(1)} %get-tuple-element.50), channel_id=1, source_target_pairs={{0,16},{8,24},{16,0},{24,8},{1,17},{9,25},{17,1},{25,9},{2,18},{10... | collective-permute-start | bytes 393224 | tf_op jit(solution)/shard_map/ppermute | solution.py:21
  114.7 3.1 %collective-permute-start.17 = (f32[8,2,256]{2,1,0:T(2,128)S(1)}, f32[8,2,256]{2,1,0:T(2,128)S(1)}, u32[]{:S(2)}, u32[]{:S(2)}) collective-permute-start(f32[8,2,256]{2,1,0:T(2,128)S(1)} %convert_multiply_fusion), channel_id=1, source_target_pairs={{1,0},{2,1},{3,2},{4,3},{5,4},{6,5},{7,6},{9,8},{10,9},{11,10},{12... | collective-permute-start | bytes 49160 | tf_op jit(solution)/shard_map/ppermute | solution.py:17
  117.8 1.4 copy-start.2
  119.2 1.0 copy-start.4
  120.2 1.0 copy-start.6
  121.3 1.0 copy-start.8
  126.2 3.0 %collective-permute-start.19 = (f32[3,6144]{1,0:T(4,128)S(1)}, f32[3,6144]{1,0:T(4,128)S(1)}, u32[]{:S(2)}, u32[]{:S(2)}) collective-permute-start(f32[3,6144]{1,0:T(4,128)S(1)} %get-tuple-element.38), channel_id=1, source_target_pairs={{0,1},{1,0},{2,3},{3,2},{4,5},{5,4},{6,7},{7,6},{8,9},{9,8},{10,11... | collective-permute-start | bytes 221192 | tf_op jit(solution)/shard_map/ppermute | solution.py:21
  129.2 6.1 %collective-permute-start.22 = (f32[3,6144]{1,0:T(4,128)S(1)}, f32[3,6144]{1,0:T(4,128)S(1)}, u32[]{:S(2)}, u32[]{:S(2)}) collective-permute-start(f32[3,6144]{1,0:T(4,128)S(1)} %add.180), channel_id=1, source_target_pairs={{0,24},{8,16},{16,8},{24,0},{1,25},{9,17},{17,9},{25,1},{2,26},{10... | collective-permute-start | bytes 221192 | tf_op jit(solution)/shard_map/ppermute | solution.py:21
  131.8 5.6 %collective-permute-start.21 = (f32[3,6144]{1,0:T(4,128)S(1)}, f32[3,6144]{1,0:T(4,128)S(1)}, u32[]{:S(2)}, u32[]{:S(2)}) collective-permute-start(f32[3,6144]{1,0:T(4,128)S(1)} %add.180), channel_id=1, source_target_pairs={{0,16},{8,24},{16,0},{24,8},{1,17},{9,25},{17,1},{25,9},{2,18},{10... | collective-permute-start | bytes 221192 | tf_op jit(solution)/shard_map/ppermute | solution.py:21
  132.3 5.1 %collective-permute-start.20 = (f32[3,6144]{1,0:T(4,128)S(1)}, f32[3,6144]{1,0:T(4,128)S(1)}, u32[]{:S(2)}, u32[]{:S(2)}) collective-permute-start(f32[3,6144]{1,0:T(4,128)S(1)} %add.180), channel_id=1, source_target_pairs={{0,8},{8,0},{16,24},{24,16},{1,9},{9,1},{17,25},{25,17},{2,10},{10... | collective-permute-start | bytes 221192 | tf_op jit(solution)/shard_map/ppermute | solution.py:21
  137.5 8.7 %collective-permute-start.25 = (f32[3,6144]{1,0:T(4,128)S(1)}, f32[3,6144]{1,0:T(4,128)S(1)}, u32[]{:S(2)}, u32[]{:S(2)}) collective-permute-start(f32[3,6144]{1,0:T(4,128)S(1)} %add_add_fusion), channel_id=1, source_target_pairs={{0,6},{1,7},{2,4},{3,5},{4,2},{5,3},{6,0},{7,1},{8,14},{9,15},{10,... | collective-permute-start | bytes 221192 | tf_op jit(solution)/shard_map/ppermute | solution.py:21
  139.9 10.5 %collective-permute-start.24 = (f32[3,6144]{1,0:T(4,128)S(1)}, f32[3,6144]{1,0:T(4,128)S(1)}, u32[]{:S(2)}, u32[]{:S(2)}) collective-permute-start(f32[3,6144]{1,0:T(4,128)S(1)} %add_add_fusion), channel_id=1, source_target_pairs={{0,4},{1,5},{2,6},{3,7},{4,0},{5,1},{6,2},{7,3},{8,12},{9,13},{10,... | collective-permute-start | bytes 221192 | tf_op jit(solution)/shard_map/ppermute | solution.py:21
  140.5 9.9 %collective-permute-start.23 = (f32[3,6144]{1,0:T(4,128)S(1)}, f32[3,6144]{1,0:T(4,128)S(1)}, u32[]{:S(2)}, u32[]{:S(2)}) collective-permute-start(f32[3,6144]{1,0:T(4,128)S(1)} %add_add_fusion), channel_id=1, source_target_pairs={{0,2},{1,3},{2,0},{3,1},{4,6},{5,7},{6,4},{7,5},{8,10},{9,11},{10,... | collective-permute-start | bytes 221192 | tf_op jit(solution)/shard_map/ppermute | solution.py:21
  143.1 11.8 %collective-permute-start.26 = (bf16[64,2048]{1,0:T(8,128)(2,1)S(1)}, bf16[64,2048]{1,0:T(8,128)(2,1)S(1)}, u32[]{:S(2)}, u32[]{:S(2)}) collective-permute-start(bf16[64,2048]{1,0:T(8,128)(2,1)S(1)} %get-tuple-element.45), channel_id=1, source_target_pairs={{0,2},{1,3},{2,0},{3,1},{4,6},{5,7},{6,4},{7,5},{8,10},{9,11},{10,... | collective-permute-start | bytes 786440 | tf_op jit(solution)/shard_map/ppermute | solution.py:21
  143.7 16.8 %collective-permute-start.28 = (bf16[64,2048]{1,0:T(8,128)(2,1)S(1)}, bf16[64,2048]{1,0:T(8,128)(2,1)S(1)}, u32[]{:S(2)}, u32[]{:S(2)}) collective-permute-start(bf16[64,2048]{1,0:T(8,128)(2,1)S(1)} %get-tuple-element.46), channel_id=1, source_target_pairs={{0,6},{1,7},{2,4},{3,5},{4,2},{5,3},{6,0},{7,1},{8,14},{9,15},{10,... | collective-permute-start | bytes 786440 | tf_op jit(solution)/shard_map/ppermute | solution.py:21
  146.1 25.8 %collective-permute-start.27 = (bf16[64,2048]{1,0:T(8,128)(2,1)S(1)}, bf16[64,2048]{1,0:T(8,128)(2,1)S(1)}, u32[]{:S(2)}, u32[]{:S(2)}) collective-permute-start(bf16[64,2048]{1,0:T(8,128)(2,1)S(1)} %get-tuple-element.47), channel_id=1, source_target_pairs={{0,4},{1,5},{2,6},{3,7},{4,0},{5,1},{6,2},{7,3},{8,12},{9,13},{10,... | collective-permute-start | bytes 786440 | tf_op jit(solution)/shard_map/ppermute | solution.py:21

commit v5 on v4

--- a/solution.py
+++ b/solution.py
@@ -90,6 +90,12 @@
             grad_long_ref[b] = (values.astype(F32) * query_ref[b].astype(F32)).astype(BF16)
 
 
+def place_kernel(me_ref, *refs):
+    pieces, out_ref = refs[:-1], refs[-1]
+    for k, piece in enumerate(pieces):
+        out_ref[me_ref[0] ^ k] = piece[...]
+
+
 def gate_kernel(me_ref, query_ref, long_ref, *pieces):
     parts, _, blk = query_ref.shape
     ratio = parts // len(pieces)
@@ -102,8 +108,10 @@
 
 def final_kernel(*refs):
     proj_ref, prev_ref, taps_ref, gate_grad_ref, long_ref, back_ref, keyed_ref, valued_ref = refs[:8]
-    query_after_ref, pair_after_ref, out_ref, sums_ref = refs[8:]
+    query_after_ref, pair_after_ref, skip_ref, out_ref, sums_ref = refs[8:]
     parts, rows, blk = long_ref.shape
+    sums_ref[3:4, :] = jnp.zeros((1, sums_ref.shape[1]), F32)
+    sums_ref[3:4, 0:blk] = skip_ref[...]
     for b in range(parts):
         back = back_ref[b, 0:rows].astype(F32)
         back_after = back_ref[b, rows : rows + 2].astype(F32)
@@ -213,11 +221,11 @@
     other = lax.dynamic_index_in_dim(blocks, 1 - core, 1, False).astype(BF16)
     pair = (mine + swapped(other, "context", 1).astype(F32)).astype(BF16)
     row = lax.axis_index("context") // 2
-    total = lax.dynamic_index_in_dim(pair, row, 0, False).astype(F32)
+    shares = [lax.dynamic_index_in_dim(pair, row, 0, False)]
     for k in range(1, parts // 2):
         sent = lax.dynamic_index_in_dim(pair, row ^ k, 0, False)
-        total = total + swapped(sent, "context", 2 * k).astype(F32)
-    return (pair, total)
+        shares.append(swapped(sent, "context", 2 * k))
+    return (other, shares)
 
 
 def to_channels(blocks):
@@ -236,6 +244,7 @@
     blk = chans // parts
     seq_len = rows * parts
     scale_factor = 1.0 / math.sqrt(seq_len * parts_dp)
+    me = lax.axis_index("context").astype(jnp.int32)
     me_dp = lax.axis_index("dp").astype(jnp.int32)[None]
     plane = jax.ShapeDtypeStruct((parts, rows, blk), BF16)
 
@@ -244,8 +253,6 @@
     query, keyed, valued, product_out = call(
         short_kernel, "short_convs", [plane] * 4, 0, projected, prev_rows, short_taps
     )
-    heads = jnp.stack([keyed[:, :2], valued[:, :2]])
-    pair_after = passed_along(heads, "context", -1).astype(F32)
     product = to_channels(product_out)
 
     filter_b = long_filter.astype(BF16)
@@ -262,6 +269,8 @@
         grad_long_kernel, "grad_long", [plane] * 2, 1, me_dp, query, *found
     )
     grad_long = to_channels(grad_long_out)
+    heads = ordered(jnp.stack([keyed[:, :2], valued[:, :2]]), grad_long_out)
+    pair_after = passed_along(heads, "context", -1).astype(F32)
     product_f, grad_long_f = (product.astype(F32), grad_long.astype(F32))
 
     def finished(total, direct):
@@ -289,31 +298,36 @@
         out_sum, back_sum, lag_sum = terms
         long_chan = finished(out_sum, product_f)
         back_chan = finished(back_sum, grad_long_f)
-    long_out = to_positions(long_chan.reshape(parts, rows, blk))
+    long_blocks = long_chan.reshape(parts, rows, blk)
+    long_sent = [lax.dynamic_index_in_dim(long_blocks, me ^ k, 0, False) for k in range(parts)]
+    long_came = [long_sent[0]] + [swapped(long_sent[k], "context", k) for k in range(1, parts)]
     back_blocks = back_chan.reshape(parts, rows, blk)
     next_heads = jnp.concatenate([back_blocks[1:, :2], jnp.zeros((1, 2, blk), BF16)], 0)
-    grad_product = to_positions(jnp.concatenate([back_blocks, next_heads], 1))
+    back_sent = jnp.concatenate([back_blocks, next_heads], 1)
+    grad_product = to_positions(back_sent)
+    long_came = lax.optimization_barrier((*long_came, back_sent))[:parts]
+    (long_out,) = call(place_kernel, "long_out", [plane], 1, me[None], *long_came)
 
     grad_filter = summed_blocks(lag_sum, "dp", 1) * (scale_factor * inverse)
     skip_sum = jnp.sum(grad_long_f * product_f, 0, keepdims=True)
-    grad_skip = all_sum(skip_sum, "dp", bits_of(parts_dp)) * scale_factor
 
     piece = jax.ShapeDtypeStruct((rows, chans // parts_dp), BF16)
     gates = call(gate_kernel, "gate", [piece] * parts_dp, 1, me_dp, query, long_out)
     gates = [gates[0]] + [swapped(gates[k], "dp", k) for k in range(1, parts_dp)]
-    proj_sum = dot(jnp.concatenate(gates, 0), jnp.concatenate(cots, 0), 0, 0)
-    pair, share = own_share(proj_sum, parts)
-    grad_proj = share * scale_factor
-    grad_product = ordered(grad_product, pair, grad_filter, grad_skip)
-
     query_heads = gate_grad[:, :2].astype(F32) * long_out[:, :2].astype(F32)
     query_after = passed_along(query_heads, "context", -1)
+    early = (grad_product, grad_filter, skip_sum, pair_after, query_after)
+    gate_all = ordered(jnp.concatenate(gates, 0), *early)
+    proj_sum = dot(gate_all, jnp.concatenate(cots, 0), 0, 0)
+    other, shares = own_share(proj_sum, parts)
+    grad_product = ordered(grad_product, other)
+
     grad_inputs, tap_sums = call(
         final_kernel,
         "stream_grads",
         [
             jax.ShapeDtypeStruct((rows, width), BF16),
-            jax.ShapeDtypeStruct((3, width), F32),
+            jax.ShapeDtypeStruct((4, width), F32),
         ],
         0,
         projected,
@@ -326,12 +340,17 @@
         valued,
         query_after,
         pair_after,
-    )
-
+        skip_sum,
+    )
+
+    tap_sums = all_sum(tap_sums, "dp", bits_of(parts_dp))
+    grad_skip = tap_sums[3, :blk] * scale_factor
+    tap_sums = ordered(tap_sums[:3], shares[1])
     tap_sums = tap_sums + swapped(tap_sums, "context", 1)
-    tap_sums = all_sum(tap_sums, "dp", bits_of(parts_dp))
+    tap_sums = ordered(tap_sums, *shares[2:])
     grad_taps = all_sum(tap_sums, "context", bits_of(parts, 2)) * scale_factor
-    return (grad_inputs, grad_taps, grad_filter, grad_skip[0], grad_proj)
+    grad_proj = sum(share.astype(F32) for share in shares) * scale_factor
+    return (grad_inputs, grad_taps, grad_filter, grad_skip, grad_proj)
 
 
 def solution(mesh):

time: 175 us -> 174 us (level)
  local copies, waits for them, and re-layouts: 17.7 us -> 27.9 us
  waiting for transfers between devices: 46.8 us -> 40.4 us
  other arithmetic: 15.7 us -> 13.5 us
    unnamed x54 -> x82, local copies, waits for them, and re-layouts: 14.6 us -> 24.2 us
    all_to_all x2, waiting for transfers between devices: 5.49 us -> 0.01 us  [to_channels(): lax.all_to_all(blocks, 'context', split_axis=0, concat_axis=0, tiled=True)]
    all_to_all x2 -> x1, waiting for transfers between devices: 2.87 us -> 0.01 us  [to_positions(): lax.all_to_all(blocks, 'context', split_axis=0, concat_axis=0, tiled=True)]
    all_to_all x2 -> x1, starting transfers between devices: 7.03 us -> 4.86 us  [to_positions(): lax.all_to_all(blocks, 'context', split_axis=0, concat_axis=0, tiled=True)]
    another operation x5, other arithmetic: 5.86 us -> 3.7 us
    pallas_call x4 -> x5, Pallas kernels: 7.73 us -> 6.22 us  [call(): pl.pallas_call(kernel, out_shape=outs, in_specs=[SMEM] * smem + [VMEM] *...]
    ppermute x26 -> x30, starting transfers between devices: 34.7 us -> 36.2 us  [swapped(): lax.ppermute(value, axis, [(i, i ^ mask) for i in range(lax.axis_size(axi...]
    ppermute x26 -> x30, waiting for transfers between devices: 38.2 us -> 38.6 us  [swapped(): lax.ppermute(value, axis, [(i, i ^ mask) for i in range(lax.axis_size(axi...]
  transfers between devices with their start and end apart: 33 -> 36, of which waited for: 15 -> 11; matrix products, arithmetic and copies ran while one was open for 26% -> 23% of each run, Pallas kernels for 2% -> 4%
where the time goes in v5:
time: 174 us; the launch traced here: 172 us
  starting transfers between devices  56.5 us (32%)
  waiting for transfers between devices  40.4 us (23%)
  local copies, waits for them, and re-layouts  27.9 us (16%)
  matrix products  26.7 us (15%)
  other arithmetic  13.5 us (8%)
  Pallas kernels  6.22 us (4%)
    ppermute x30, waiting for transfers between devices, swapped(): lax.ppermute(value, axis, [(i, i ^ mask) for i in range(lax.axis_size(axi...  38.6 us
    ppermute x30, starting transfers between devices, swapped(): lax.ppermute(value, axis, [(i, i ^ mask) for i in range(lax.axis_size(axi...  36.2 us
    dot_general x11, matrix products, dot(): lax.dot_general(left, right, (((left_dim,), (right_dim,)), ((), ())), pre...  26.7 us
    unnamed x82, local copies, waits for them, and re-layouts  24.2 us
    all_to_all x2, starting transfers between devices, to_channels(): lax.all_to_all(blocks, 'context', split_axis=0, concat_axis=0, tiled=True)  11.3 us
    pallas_call x5, Pallas kernels, call(): pl.pallas_call(kernel, out_shape=outs, in_specs=[SMEM] * smem + [VMEM] *...  6.22 us
    all_to_all x1, starting transfers between devices, to_positions(): lax.all_to_all(blocks, 'context', split_axis=0, concat_axis=0, tiled=True)  4.86 us
    ppermute x3, starting transfers between devices, passed_along(): lax.ppermute(value, axis, [(source, source + steps) for source in range(i...  4.08 us
  transfers between devices with their start and end apart: 36, of which 11 were waited for; matrix products, arithmetic and copies ran while one was open for 23% of the time, Pallas kernels for 4%

profile of v5, /device:TPU:0, one launch (start us, length us, event | category | flops | bytes accessed | tf_op | source)
XLA Modules:
  0.0 172.3 jit_solution(9326813844062653492)
XLA Ops:
  0.6 3.0 %collective-permute-start.3 = (bf16[128,2048]{1,0:T(8,128)(2,1)}, bf16[128,2048]{1,0:T(8,128)(2,1)}, u32[]{:S(2)}, u32[]{:S(2)}) collective-permute-start(bf16[128,2048]{1,0:T(8,128)(2,1)} %param.11), channel_id=1, source_target_pairs={{0,16},{8,24},{16,0},{24,8},{1,17},{9,25},{17,1},{25,9},{2,18},{10... | collective-permute-start | bytes 1572872 | tf_op jit(solution)/shard_map/ppermute | solution.py:21
  3.7 1.5 collective-permute-start.1
  5.2 0.9 slice.52
  6.1 1.3 collective-permute-start
  7.5 1.1 fusion.48
  8.6 1.5 subtract_convert_fusion
  11.3 2.7 %fusion.33 = f32[2048,256]{1,0:T(8,128)} fusion(bf16[2048,1024]{1,0:T(8,128)(2,1)S(1)} %bitcast.76, f32[256,1024]{1,0:T(8,128)S(1)} %copy-done.34), kind=kOutput, calls=%fused_computation.54 | convolution fusion | flops 1074003968 | bytes 7340032 | tf_op jit(solution)/shard_map/dot_general | solution.py:157
  14.9 1.4 copy-done.1
  16.3 1.2 short_convs.1
  19.1 6.2 %all-to-all-start = ((bf16[8,128,256]{2,1,0:T(8,128)(2,1)}), bf16[8,128,256]{2,1,0:T(8,128)(2,1)}, u32[]{:S(2)}, u32[]{:S(2)}) async-start(bf16[8,128,256]{2,1,0:T(8,128)(2,1)} %copy-done.11), calls=%async_computation | async-start | bytes 1048576 | tf_op jit(solution)/shard_map/all_to_all | solution.py:232
  25.3 1.9 %fusion.14 = bf16[128,512]{1,0:T(8,128)(2,1)S(1)} fusion(bf16[512,2048]{1,0:T(8,128)(2,1)S(1)} %copy-done, bf16[128,2048]{1,0:T(8,128)(2,1)} %collective-permute-done.1), kind=kOutput, calls=%fused_computation.25 | convolution fusion | flops 268500992 | bytes 2752512 | tf_op jit(solution)/shard_map/dot_general | solution.py:157
  27.2 1.6 collective-permute-start.2
  28.8 1.9 %fusion.15 = bf16[128,512]{1,0:T(8,128)(2,1)S(1)} fusion(bf16[512,2048]{1,0:T(8,128)(2,1)S(1)} %copy-done, bf16[128,2048]{1,0:T(8,128)(2,1)} %collective-permute-done.3), kind=kOutput, calls=%fused_computation.26 | convolution fusion | flops 268500992 | bytes 2752512 | tf_op jit(solution)/shard_map/dot_general | solution.py:157
  30.6 1.6 collective-permute-start.4
  32.2 1.9 %fusion.16 = bf16[128,512]{1,0:T(8,128)(2,1)S(1)} fusion(bf16[512,2048]{1,0:T(8,128)(2,1)S(1)} %copy-done, bf16[128,2048]{1,0:T(8,128)(2,1)} %collective-permute-done.5), kind=kOutput, calls=%fused_computation.27 | convolution fusion | flops 268500992 | bytes 2752512 | tf_op jit(solution)/shard_map/dot_general | solution.py:157
  35.5 1.0 collective-permute-done.4.refs_2_
  36.5 4.1 %collective-permute-done.6.refs_3_ = bf16[128,512]{1,0:T(8,128)(2,1)S(1)} collective-permute-done((bf16[128,512]{1,0:T(8,128)(2,1)S(1)}, bf16[128,512]{1,0:T(8,128)(2,1)S(1)}, u32[]{:S(2)}, u32[]{:S(2)}) %collective-permute-start.6) | collective-permute-done | bytes 131104 | tf_op jit(solution)/shard_map/ppermute | solution.py:21
  40.6 0.9 grad_long.1
  42.3 1.3 collective-permute-start.20
  43.7 1.7 collective-permute-done.20
  45.4 5.1 %all-to-all-start.1 = ((bf16[8,128,256]{2,1,0:T(8,128)(2,1)}), bf16[8,128,256]{2,1,0:T(8,128)(2,1)S(1)}, u32[]{:S(2)}, u32[]{:S(2)}) async-start(bf16[8,128,256]{2,1,0:T(8,128)(2,1)} %get-tuple-element.38), calls=%async_computation.1 | async-start | bytes 1048576 | tf_op jit(solution)/shard_map/all_to_all | solution.py:232
  50.5 3.8 %fusion.55 = f32[2048,256]{1,0:T(8,128)S(1)} fusion(bf16[2048,1024]{1,0:T(8,128)(2,1)} %bitcast.77, bf16[1024,256]{1,0:T(8,128)(2,1)} %bitcast.7), kind=kOutput, calls=%fused_computation.106 | convolution fusion | flops 1073741824 | bytes 6815744 | tf_op jit(solution)/shard_map/dot_general | solution.py:157
  54.7 1.0 copy-done.28
  55.7 1.5 copy-done.26
  57.3 2.3 %fusion.12 = bf16[1024,256]{1,0:T(8,128)(2,1)S(1)} fusion(bf16[2048,1024]{1,0:T(8,128)(2,1)S(1)} %bitcast.80, bf16[1024,256]{1,0:T(8,128)(2,1)S(1)} %get-tuple-element.68, bf16[1024,256]{1,0:T(8,128)(2,1)S(1)} %get-tuple-element.67, bf16[1024,256]{1,0:T(8,128)(2,1)} %bitcast.7, f32[256]{0:T(256)S(1)} %copy-done.40), kind=kOutput, calls=%fused_computation.19 | convolution fusion | flops 1077149696 | bytes 6292480 | tf_op jit(solution)/shard_map/dot_general | solution.py:157
  60.4 3.6 %collective-permute-start.13 = (bf16[128,256]{1,0:T(8,128)(2,1)}, bf16[128,256]{1,0:T(8,128)(2,1)S(1)}, u32[]{:S(2)}, u32[]{:S(2)}) collective-permute-start(bf16[128,256]{1,0:T(8,128)(2,1)} %get-tuple-element.75), channel_id=1, source_target_pairs={{0,7},{1,6},{2,5},{3,4},{4,3},{5,2},{6,1},{7,0},{8,15},{9,14},{10,... | collective-permute-start | bytes 196616 | tf_op jit(solution)/shard_map/ppermute | solution.py:21
  64.8 2.1 %collective-permute-start.10 = (bf16[128,256]{1,0:T(8,128)(2,1)}, bf16[128,256]{1,0:T(8,128)(2,1)S(1)}, u32[]{:S(2)}, u32[]{:S(2)}) collective-permute-start(bf16[128,256]{1,0:T(8,128)(2,1)} %get-tuple-element.78), channel_id=1, source_target_pairs={{0,4},{1,5},{2,6},{3,7},{4,0},{5,1},{6,2},{7,3},{8,12},{9,13},{10,... | collective-permute-start | bytes 196616 | tf_op jit(solution)/shard_map/ppermute | solution.py:21
  66.9 1.2 collective-permute-start.9
  68.1 3.7 %fusion.56 = f32[2048,256]{1,0:T(8,128)S(1)} fusion(bf16[2048,1024]{1,0:T(8,128)(2,1)} %bitcast.78, bf16[1024,256]{1,0:T(8,128)(2,1)S(1)} %bitcast.84), kind=kOutput, calls=%fused_computation.107 | convolution fusion | flops 1073741824 | bytes 6815744 | tf_op jit(solution)/shard_map/dot_general | solution.py:157
  72.3 1.8 %copy-done.27 = bf16[2,32,32,1024]{3,2,1,0:T(8,128)(2,1)S(1)} copy-done((bf16[2,32,32,1024]{3,2,1,0:T(8,128)(2,1)S(1)}, bf16[2,32,32,1024]{3,2,1,0:T(8,128)(2,1)}, u32[]{:S(2)}) %copy-start.27) | copy-done | bytes 4194328
  74.0 1.3 fusion.11
  75.6 1.4 add_convert_fusion
  77.8 0.8 fusion.29
  78.6 4.9 %all-to-all-start.2 = ((bf16[8,130,256]{2,1,0:T(8,128)(2,1)}), bf16[8,130,256]{2,1,0:T(8,128)(2,1)S(1)}, u32[]{:S(2)}, u32[]{:S(2)}) async-start(bf16[8,130,256]{2,1,0:T(8,128)(2,1)} %fusion.29), calls=%async_computation.2 | async-start | bytes 1114112 | tf_op jit(solution)/shard_map/all_to_all | solution.py:237
  86.6 0.8 copy-done.14
  87.5 0.8 copy-done.16
  90.9 1.1 copy-done.4
  92.9 1.5 collective-permute-start.21
  95.0 3.5 %fusion.25 = f32[256,1024]{1,0:T(8,128)S(1)} fusion(bf16[2048,1024]{1,0:T(8,128)(2,1)} %bitcast.79, bf16[1024,256]{1,0:T(8,128)(2,1)S(1)} %copy-done.36, bf16[1024,256]{1,0:T(8,128)(2,1)S(1)} %copy-done.35), kind=kOutput, calls=%fused_computation.37 | convolution fusion | flops 1075838976 | bytes 6291456 | tf_op jit(solution)/shard_map/dot_general | solution.py:157
  98.6 1.6 collective-permute-start.17
  100.7 1.5 collective-permute-start.18
  102.2 1.2 multiply_reduce_fusion
  103.4 1.6 collective-permute-done.17
  105.6 2.2 %collective-permute-done.19 = bf16[256,256]{1,0:T(8,128)(2,1)S(1)} collective-permute-done((bf16[256,256]{1,0:T(8,128)(2,1)S(1)}, bf16[256,256]{1,0:T(8,128)(2,1)S(1)}, u32[]{:S(2)}, u32[]{:S(2)}) %collective-permute-start.19) | collective-permute-done | bytes 131104 | tf_op jit(solution)/shard_map/ppermute | solution.py:21
  107.8 2.4 %collective-permute-start.16 = (bf16[128,512]{1,0:T(8,128)(2,1)S(1)}, bf16[128,512]{1,0:T(8,128)(2,1)S(1)}, u32[]{:S(2)}, u32[]{:S(2)}) collective-permute-start(bf16[128,512]{1,0:T(8,128)(2,1)S(1)} %get-tuple-element.52), channel_id=1, source_target_pairs={{0,24},{8,16},{16,8},{24,0},{1,25},{9,17},{17,9},{25,1},{2,26},{10... | collective-permute-start | bytes 393224 | tf_op jit(solution)/shard_map/ppermute | solution.py:21
  111.0 3.8 %collective-permute-done.15 = bf16[128,512]{1,0:T(8,128)(2,1)S(1)} collective-permute-done((bf16[128,512]{1,0:T(8,128)(2,1)S(1)}, bf16[128,512]{1,0:T(8,128)(2,1)S(1)}, u32[]{:S(2)}, u32[]{:S(2)}) %collective-permute-start.15) | collective-permute-done | bytes 131104 | tf_op jit(solution)/shard_map/ppermute | solution.py:21
  115.6 3.0 %fusion = f32[512,2048]{1,0:T(8,128)S(1)} fusion(bf16[512,512]{1,0:T(8,128)(2,1)} %pad_maximum_fusion.1, bf16[128,2048]{1,0:T(8,128)(2,1)} %collective-permute-done.5, bf16[128,2048]{1,0:T(8,128)(2,1)} %collective-permute-done.3, bf16[128,2048]{1,0:T(8,128)(2,1)} %collective-permute-done.1, bf16[128,2048]{1,0:T(8,128)(2,1)} %param.11), kind=kOutput, calls=%fused_computation.3 | convolution fusion | flops 1082130432 | bytes 6815744 | tf_op jit(solution)/shard_map/dot_general | solution.py:157
  118.6 2.0 %copy-done.30 = f32[512,2048]{1,0:T(8,128)} copy-done((f32[512,2048]{1,0:T(8,128)}, f32[512,2048]{1,0:T(8,128)S(1)}, u32[]{:S(2)}) %copy-start.30) | copy-done | bytes 4194328
  120.6 1.1 fusion.18
  121.7 1.4 copy-done.2
  123.1 1.0 copy-done.6
  124.2 1.0 copy-done.8
  125.2 1.0 copy-done.10
  126.3 3.9 %stream_grads.1 = (bf16[128,6144]{1,0:T(8,128)(2,1)}, f32[4,6144]{1,0:T(4,128)S(1)}) custom-call(bf16[128,6144]{1,0:T(8,128)(2,1)S(1)} %copy-done.2, f32[2,6144]{1,0:T(2,128)S(1)} %convert_element_type.133.prev_ref.refs_1_, f32[3,6144]{1,0:T(4,128)S(1)} %copy-done.12, bf16[8,128,256]{2,1,0:T(8,128)(2,1)S(1)} %copy-done.10, ...), custom_call_target="tpu_custom_call" | custom-call | flops 35004416 | bytes 8751104 | tf_op jit(solution)/shard_map/stream_grads/pallas_call | solution.py:47
  130.2 2.4 %collective-permute-start.24 = (f32[4,6144]{1,0:T(4,128)S(1)}, f32[4,6144]{1,0:T(4,128)S(1)}, u32[]{:S(2)}, u32[]{:S(2)}) collective-permute-start(f32[4,6144]{1,0:T(4,128)S(1)} %get-tuple-element.60), channel_id=1, source_target_pairs={{0,24},{8,16},{16,8},{24,0},{1,25},{9,17},{17,9},{25,1},{2,26},{10... | collective-permute-start | bytes 294920 | tf_op jit(solution)/shard_map/ppermute | solution.py:21
  133.7 1.5 fusion.8
  135.2 3.9 %collective-permute-start.29 = (bf16[64,2048]{1,0:T(8,128)(2,1)S(1)}, bf16[64,2048]{1,0:T(8,128)(2,1)S(1)}, u32[]{:S(2)}, u32[]{:S(2)}) collective-permute-start(bf16[64,2048]{1,0:T(8,128)(2,1)S(1)} %get-tuple-element.69), channel_id=1, source_target_pairs={{0,6},{1,7},{2,4},{3,5},{4,2},{5,3},{6,0},{7,1},{8,14},{9,15},{10,... | collective-permute-start | bytes 786440 | tf_op jit(solution)/shard_map/ppermute | solution.py:21
  139.8 16.0 %collective-permute-done.26 = bf16[64,2048]{1,0:T(8,128)(2,1)S(1)} collective-permute-done((bf16[64,2048]{1,0:T(8,128)(2,1)S(1)}, bf16[64,2048]{1,0:T(8,128)(2,1)S(1)}, u32[]{:S(2)}, u32[]{:S(2)}) %collective-permute-start.26) | collective-permute-done | bytes 262176 | tf_op jit(solution)/shard_map/ppermute | solution.py:21
  157.2 4.3 %collective-permute-done.28 = bf16[64,2048]{1,0:T(8,128)(2,1)S(1)} collective-permute-done((bf16[64,2048]{1,0:T(8,128)(2,1)S(1)}, bf16[64,2048]{1,0:T(8,128)(2,1)S(1)}, u32[]{:S(2)}, u32[]{:S(2)}) %collective-permute-start.28) | collective-permute-done | bytes 262176 | tf_op jit(solution)/shard_map/ppermute | solution.py:21
  161.5 2.3 %collective-permute-start.32 = (f32[3,6144]{1,0:T(4,128)S(1)}, f32[3,6144]{1,0:T(4,128)S(1)}, u32[]{:S(2)}, u32[]{:S(2)}) collective-permute-start(f32[3,6144]{1,0:T(4,128)S(1)} %add.205), channel_id=1, source_target_pairs={{0,6},{1,7},{2,4},{3,5},{4,2},{5,3},{6,0},{7,1},{8,14},{9,15},{10,... | collective-permute-start | bytes 221192 | tf_op jit(solution)/shard_map/ppermute | solution.py:21
  163.9 2.1 %collective-permute-start.30 = (f32[3,6144]{1,0:T(4,128)S(1)}, f32[3,6144]{1,0:T(4,128)S(1)}, u32[]{:S(2)}, u32[]{:S(2)}) collective-permute-start(f32[3,6144]{1,0:T(4,128)S(1)} %add.205), channel_id=1, source_target_pairs={{0,2},{1,3},{2,0},{3,1},{4,6},{5,7},{6,4},{7,5},{8,10},{9,11},{10,... | collective-permute-start | bytes 221192 | tf_op jit(solution)/shard_map/ppermute | solution.py:21
  165.9 0.9 fusion.32
  166.9 2.3 %collective-permute-done.32 = f32[3,6144]{1,0:T(4,128)S(1)} collective-permute-done((f32[3,6144]{1,0:T(4,128)S(1)}, f32[3,6144]{1,0:T(4,128)S(1)}, u32[]{:S(2)}, u32[]{:S(2)}) %collective-permute-start.32) | collective-permute-done | bytes 73760 | tf_op jit(solution)/shard_map/ppermute | solution.py:21
  169.2 2.5 %collective-permute-done.31 = f32[3,6144]{1,0:T(4,128)S(1)} collective-permute-done((f32[3,6144]{1,0:T(4,128)S(1)}, f32[3,6144]{1,0:T(4,128)S(1)}, u32[]{:S(2)}, u32[]{:S(2)}) %collective-permute-start.31) | collective-permute-done | bytes 73760 | tf_op jit(solution)/shard_map/ppermute | solution.py:21
  (135 shorter events, 23.1 us)
Async XLA Ops:
  0.6 13.3 %copy-start = (bf16[512,2048]{1,0:T(8,128)(2,1)S(1)}, bf16[512,2048]{1,0:T(8,128)(2,1)}, u32[]{:S(2)}) copy-start(bf16[512,2048]{1,0:T(8,128)(2,1)} %param.10) | copy-start | bytes 6291460
  0.6 28.1 %collective-permute-start.3 = (bf16[128,2048]{1,0:T(8,128)(2,1)}, bf16[128,2048]{1,0:T(8,128)(2,1)}, u32[]{:S(2)}, u32[]{:S(2)}) collective-permute-start(bf16[128,2048]{1,0:T(8,128)(2,1)} %param.11), channel_id=1, source_target_pairs={{0,16},{8,24},{16,0},{24,8},{1,17},{9,25},{17,1},{25,9},{2,18},{10... | collective-permute-start | bytes 1572872 | tf_op jit(solution)/shard_map/ppermute | solution.py:21
  3.7 21.6 %collective-permute-start.1 = (bf16[128,2048]{1,0:T(8,128)(2,1)}, bf16[128,2048]{1,0:T(8,128)(2,1)}, u32[]{:S(2)}, u32[]{:S(2)}) collective-permute-start(bf16[128,2048]{1,0:T(8,128)(2,1)} %param.11), channel_id=1, source_target_pairs={{0,8},{8,0},{16,24},{24,16},{1,9},{9,1},{17,25},{25,17},{2,10},{10... | collective-permute-start | bytes 1572872 | tf_op jit(solution)/shard_map/ppermute | solution.py:21
  5.2 27.1 %collective-permute-start.5 = (bf16[128,2048]{1,0:T(8,128)(2,1)}, bf16[128,2048]{1,0:T(8,128)(2,1)}, u32[]{:S(2)}, u32[]{:S(2)}) collective-permute-start(bf16[128,2048]{1,0:T(8,128)(2,1)} %param.11), channel_id=1, source_target_pairs={{0,24},{8,16},{16,8},{24,0},{1,25},{9,17},{17,9},{25,1},{2,26},{10... | collective-permute-start | bytes 1572872 | tf_op jit(solution)/shard_map/ppermute | solution.py:21
  6.1 8.7 %collective-permute-start = (bf16[2,6144]{1,0:T(2,128)(2,1)S(1)}, bf16[2,6144]{1,0:T(2,128)(2,1)S(1)}, u32[]{:S(2)}, u32[]{:S(2)}) collective-permute-start(bf16[2,6144]{1,0:T(2,128)(2,1)S(1)} %slice.52), channel_id=1, source_target_pairs={{0,1},{1,2},{2,3},{3,4},{4,5},{5,6},{6,7},{8,9},{9,10},{10,11},{11... | collective-permute-start | bytes 73736 | tf_op jit(solution)/shard_map/ppermute | solution.py:17
  10.1 1.2 copy-start.34
  10.5 3.5 %copy-start.25 = (bf16[2,32,32,1024]{3,2,1,0:T(8,128)(2,1)}, bf16[2,32,32,1024]{3,2,1,0:T(8,128)(2,1)S(1)}, u32[]{:S(2)}) copy-start(bf16[2,32,32,1024]{3,2,1,0:T(8,128)(2,1)S(1)} %pad_maximum_fusion) | copy-start | bytes 12582916
  11.3 2.7 %copy-start.37 = (bf16[128,2048]{1,0:T(8,128)(2,1)S(1)}, bf16[128,2048]{1,0:T(8,128)(2,1)}, u32[]{:S(2)}) copy-start(bf16[128,2048]{1,0:T(8,128)(2,1)} %param.11) | copy-start | bytes 1572868
  14.0 0.9 copy-start.12
  14.9 1.4 copy-start.1
  19.1 15.6 %copy-start.5 = (bf16[8,128,256]{2,1,0:T(8,128)(2,1)}, bf16[8,128,256]{2,1,0:T(8,128)(2,1)S(1)}, u32[]{:S(2)}) copy-start(bf16[8,128,256]{2,1,0:T(8,128)(2,1)S(1)} %get-tuple-element.54.refs_6_) | copy-start | bytes 1572868
  19.1 21.5 %copy-start.3 = (bf16[8,128,256]{2,1,0:T(8,128)(2,1)}, bf16[8,128,256]{2,1,0:T(8,128)(2,1)S(1)}, u32[]{:S(2)}) copy-start(bf16[8,128,256]{2,1,0:T(8,128)(2,1)S(1)} %get-tuple-element.34.query_ref) | copy-start | bytes 1572868
  19.1 26.3 %all-to-all-start = ((bf16[8,128,256]{2,1,0:T(8,128)(2,1)}), bf16[8,128,256]{2,1,0:T(8,128)(2,1)}, u32[]{:S(2)}, u32[]{:S(2)}) async-start(bf16[8,128,256]{2,1,0:T(8,128)(2,1)} %copy-done.11), calls=%async_computation | async-start | bytes 1048576 | tf_op jit(solution)/shard_map/all_to_all | solution.py:232
  27.2 8.3 %collective-permute-start.2 = (bf16[128,512]{1,0:T(8,128)(2,1)S(1)}, bf16[128,512]{1,0:T(8,128)(2,1)S(1)}, u32[]{:S(2)}, u32[]{:S(2)}) collective-permute-start(bf16[128,512]{1,0:T(8,128)(2,1)S(1)} %fusion.14), channel_id=1, source_target_pairs={{0,8},{8,0},{16,24},{24,16},{1,9},{9,1},{17,25},{25,17},{2,10},{10... | collective-permute-start | bytes 393224 | tf_op jit(solution)/shard_map/ppermute | solution.py:21
  30.6 5.8 %collective-permute-start.4 = (bf16[128,512]{1,0:T(8,128)(2,1)S(1)}, bf16[128,512]{1,0:T(8,128)(2,1)S(1)}, u32[]{:S(2)}, u32[]{:S(2)}) collective-permute-start(bf16[128,512]{1,0:T(8,128)(2,1)S(1)} %fusion.15), channel_id=1, source_target_pairs={{0,16},{8,24},{16,0},{24,8},{1,17},{9,25},{17,1},{25,9},{2,18},{10... | collective-permute-start | bytes 393224 | tf_op jit(solution)/shard_map/ppermute | solution.py:21
  34.1 6.4 %collective-permute-start.6 = (bf16[128,512]{1,0:T(8,128)(2,1)S(1)}, bf16[128,512]{1,0:T(8,128)(2,1)S(1)}, u32[]{:S(2)}, u32[]{:S(2)}) collective-permute-start(bf16[128,512]{1,0:T(8,128)(2,1)S(1)} %fusion.16), channel_id=1, source_target_pairs={{0,24},{8,16},{16,8},{24,0},{1,25},{9,17},{17,9},{25,1},{2,26},{10... | collective-permute-start | bytes 393224 | tf_op jit(solution)/shard_map/ppermute | solution.py:21
  42.3 3.1 %collective-permute-start.20 = (bf16[2,8,2,256]{3,2,1,0:T(2,128)(2,1)S(1)}, bf16[2,8,2,256]{3,2,1,0:T(2,128)(2,1)S(1)}, u32[]{:S(2)}, u32[]{:S(2)}) collective-permute-start(bf16[2,8,2,256]{3,2,1,0:T(2,128)(2,1)S(1)} %pad_maximum_fusion.2), channel_id=1, source_target_pairs={{1,0},{2,1},{3,2},{4,3},{5,4},{6,5},{7,6},{9,8},{10,9},{11,10},{12... | collective-permute-start | bytes 49160 | tf_op jit(solution)/shard_map/ppermute | solution.py:17
  45.4 22.7 %all-to-all-start.1 = ((bf16[8,128,256]{2,1,0:T(8,128)(2,1)}), bf16[8,128,256]{2,1,0:T(8,128)(2,1)S(1)}, u32[]{:S(2)}, u32[]{:S(2)}) async-start(bf16[8,128,256]{2,1,0:T(8,128)(2,1)} %get-tuple-element.38), calls=%async_computation.1 | async-start | bytes 1048576 | tf_op jit(solution)/shard_map/all_to_all | solution.py:232
  50.5 3.8 %copy-start.23 = (f32[2048,256]{1,0:T(8,128)S(1)}, f32[2048,256]{1,0:T(8,128)}, u32[]{:S(2)}) copy-start(f32[2048,256]{1,0:T(8,128)} %fusion.33) | copy-start | bytes 6291460
  54.3 1.4 copy-start.28
  54.3 2.9 %copy-start.26 = (bf16[2,32,32,1024]{3,2,1,0:T(8,128)(2,1)S(1)}, bf16[2,32,32,1024]{3,2,1,0:T(8,128)(2,1)}, u32[]{:S(2)}) copy-start(bf16[2,32,32,1024]{3,2,1,0:T(8,128)(2,1)} %copy-done.25) | copy-start | bytes 12582916
  54.3 2.9 %copy-start.40 = (f32[256]{0:T(256)S(1)}, f32[256]{0:T(256)}, u32[]{:S(2)}) copy-start(f32[256]{0:T(256)} %param.9) | copy-start | bytes 3076
  60.4 16.6 %collective-permute-start.13 = (bf16[128,256]{1,0:T(8,128)(2,1)}, bf16[128,256]{1,0:T(8,128)(2,1)S(1)}, u32[]{:S(2)}, u32[]{:S(2)}) collective-permute-start(bf16[128,256]{1,0:T(8,128)(2,1)} %get-tuple-element.75), channel_id=1, source_target_pairs={{0,7},{1,6},{2,5},{3,4},{4,3},{5,2},{6,1},{7,0},{8,15},{9,14},{10,... | collective-permute-start | bytes 196616 | tf_op jit(solution)/shard_map/ppermute | solution.py:21
  64.0 13.8 %collective-permute-start.12 = (bf16[128,256]{1,0:T(8,128)(2,1)}, bf16[128,256]{1,0:T(8,128)(2,1)S(1)}, u32[]{:S(2)}, u32[]{:S(2)}) collective-permute-start(bf16[128,256]{1,0:T(8,128)(2,1)} %get-tuple-element.76), channel_id=1, source_target_pairs={{0,6},{1,7},{2,4},{3,5},{4,2},{5,3},{6,0},{7,1},{8,14},{9,15},{10,... | collective-permute-start | bytes 196616 | tf_op jit(solution)/shard_map/ppermute | solution.py:21
  64.3 19.1 %collective-permute-start.11 = (bf16[128,256]{1,0:T(8,128)(2,1)}, bf16[128,256]{1,0:T(8,128)(2,1)S(1)}, u32[]{:S(2)}, u32[]{:S(2)}) collective-permute-start(bf16[128,256]{1,0:T(8,128)(2,1)} %get-tuple-element.77), channel_id=1, source_target_pairs={{0,5},{1,4},{2,7},{3,6},{4,1},{5,0},{6,3},{7,2},{8,13},{9,12},{10,... | collective-permute-start | bytes 196616 | tf_op jit(solution)/shard_map/ppermute | solution.py:21
  64.8 19.3 %collective-permute-start.10 = (bf16[128,256]{1,0:T(8,128)(2,1)}, bf16[128,256]{1,0:T(8,128)(2,1)S(1)}, u32[]{:S(2)}, u32[]{:S(2)}) collective-permute-start(bf16[128,256]{1,0:T(8,128)(2,1)} %get-tuple-element.78), channel_id=1, source_target_pairs={{0,4},{1,5},{2,6},{3,7},{4,0},{5,1},{6,2},{7,3},{8,12},{9,13},{10,... | collective-permute-start | bytes 196616 | tf_op jit(solution)/shard_map/ppermute | solution.py:21
  66.9 17.9 %collective-permute-start.9 = (bf16[128,256]{1,0:T(8,128)(2,1)}, bf16[128,256]{1,0:T(8,128)(2,1)S(1)}, u32[]{:S(2)}, u32[]{:S(2)}) collective-permute-start(bf16[128,256]{1,0:T(8,128)(2,1)} %get-tuple-element.79), channel_id=1, source_target_pairs={{0,3},{1,2},{2,1},{3,0},{4,7},{5,6},{6,5},{7,4},{8,11},{9,10},{10,... | collective-permute-start | bytes 196616 | tf_op jit(solution)/shard_map/ppermute | solution.py:21
  68.1 4.2 %copy-start.32 = (bf16[8,128,256]{2,1,0:T(8,128)(2,1)}, bf16[8,128,256]{2,1,0:T(8,128)(2,1)S(1)}, u32[]{:S(2)}) copy-start(bf16[8,128,256]{2,1,0:T(8,128)(2,1)S(1)} %all-to-all-done.1) | copy-start | bytes 1572868
  68.1 3.8 %copy-start.24 = (f32[2048,256]{1,0:T(8,128)S(1)}, f32[2048,256]{1,0:T(8,128)}, u32[]{:S(2)}) copy-start(f32[2048,256]{1,0:T(8,128)} %fusion.33) | copy-start | bytes 6291460
  71.8 2.2 %copy-start.27 = (bf16[2,32,32,1024]{3,2,1,0:T(8,128)(2,1)S(1)}, bf16[2,32,32,1024]{3,2,1,0:T(8,128)(2,1)}, u32[]{:S(2)}) copy-start(bf16[2,32,32,1024]{3,2,1,0:T(8,128)(2,1)} %copy-done.25) | copy-start | bytes 12582916
  74.0 1.6 copy-start.29
  75.6 1.4 copy-start.39
  75.6 2.1 %copy-start.38 = (bf16[128,256]{1,0:T(8,128)(2,1)S(1)}, bf16[128,256]{1,0:T(8,128)(2,1)}, u32[]{:S(2)}) copy-start(bf16[128,256]{1,0:T(8,128)(2,1)} %get-tuple-element.81) | copy-start | bytes 196612
  77.0 8.3 %collective-permute-start.8 = (bf16[128,256]{1,0:T(8,128)(2,1)S(1)}, bf16[128,256]{1,0:T(8,128)(2,1)S(1)}, u32[]{:S(2)}, u32[]{:S(2)}) collective-permute-start(bf16[128,256]{1,0:T(8,128)(2,1)S(1)} %copy-done.39), channel_id=1, source_target_pairs={{0,2},{1,3},{2,0},{3,1},{4,6},{5,7},{6,4},{7,5},{8,10},{9,11},{10,... | collective-permute-start | bytes 196616 | tf_op jit(solution)/shard_map/ppermute | solution.py:21
  77.7 8.2 %collective-permute-start.7 = (bf16[128,256]{1,0:T(8,128)(2,1)S(1)}, bf16[128,256]{1,0:T(8,128)(2,1)S(1)}, u32[]{:S(2)}, u32[]{:S(2)}) collective-permute-start(bf16[128,256]{1,0:T(8,128)(2,1)S(1)} %copy-done.38), channel_id=1, source_target_pairs={{0,1},{1,0},{2,3},{3,2},{4,5},{5,4},{6,7},{7,6},{8,9},{9,8},{10,11... | collective-permute-start | bytes 196616 | tf_op jit(solution)/shard_map/ppermute | solution.py:21
  78.6 37.0 %all-to-all-start.2 = ((bf16[8,130,256]{2,1,0:T(8,128)(2,1)}), bf16[8,130,256]{2,1,0:T(8,128)(2,1)S(1)}, u32[]{:S(2)}, u32[]{:S(2)}) async-start(bf16[8,130,256]{2,1,0:T(8,128)(2,1)} %fusion.29), calls=%async_computation.2 | async-start | bytes 1114112 | tf_op jit(solution)/shard_map/all_to_all | solution.py:237
  90.8 4.2 %copy-start.35 = (bf16[1024,256]{1,0:T(8,128)(2,1)S(1)}, bf16[1024,256]{1,0:T(8,128)(2,1)}, u32[]{:S(2)}) copy-start(bf16[1024,256]{1,0:T(8,128)(2,1)} %get-tuple-element.63) | copy-start | bytes 1572868
  90.8 4.2 %copy-start.36 = (bf16[1024,256]{1,0:T(8,128)(2,1)S(1)}, bf16[1024,256]{1,0:T(8,128)(2,1)}, u32[]{:S(2)}) copy-start(bf16[1024,256]{1,0:T(8,128)(2,1)} %get-tuple-element.64) | copy-start | bytes 1572868
  90.9 1.1 copy-start.4
  92.9 22.7 %collective-permute-start.21 = (f32[8,2,256]{2,1,0:T(2,128)S(1)}, f32[8,2,256]{2,1,0:T(2,128)S(1)}, u32[]{:S(2)}, u32[]{:S(2)}) collective-permute-start(f32[8,2,256]{2,1,0:T(2,128)S(1)} %convert_multiply_fusion), channel_id=1, source_target_pairs={{1,0},{2,1},{3,2},{4,3},{5,4},{6,5},{7,6},{9,8},{10,9},{11,10},{12... | collective-permute-start | bytes 49160 | tf_op jit(solution)/shard_map/ppermute | solution.py:17
  94.4 16.6 %collective-permute-start.14 = (bf16[128,512]{1,0:T(8,128)(2,1)S(1)}, bf16[128,512]{1,0:T(8,128)(2,1)S(1)}, u32[]{:S(2)}, u32[]{:S(2)}) collective-permute-start(bf16[128,512]{1,0:T(8,128)(2,1)S(1)} %get-tuple-element.50), channel_id=1, source_target_pairs={{0,8},{8,0},{16,24},{24,16},{1,9},{9,1},{17,25},{25,17},{2,10},{10... | collective-permute-start | bytes 393224 | tf_op jit(solution)/shard_map/ppermute | solution.py:21
  95.0 7.2 %copy-start.33 = (bf16[8,128,256]{2,1,0:T(8,128)(2,1)S(1)}, bf16[8,128,256]{2,1,0:T(8,128)(2,1)}, u32[]{:S(2)}) copy-start(bf16[8,128,256]{2,1,0:T(8,128)(2,1)} %copy-done.32) | copy-start | bytes 1572868
  98.6 6.4 %collective-permute-start.17 = (bf16[256,256]{1,0:T(8,128)(2,1)S(1)}, bf16[256,256]{1,0:T(8,128)(2,1)S(1)}, u32[]{:S(2)}, u32[]{:S(2)}) collective-permute-start(bf16[256,256]{1,0:T(8,128)(2,1)S(1)} %get-tuple-element.72), channel_id=1, source_target_pairs={{0,8},{8,0},{16,24},{24,16},{1,9},{9,1},{17,25},{25,17},{2,10},{10... | collective-permute-start | bytes 393224 | tf_op jit(solution)/shard_map/ppermute | solution.py:21
  100.2 7.6 %collective-permute-start.19 = (bf16[256,256]{1,0:T(8,128)(2,1)S(1)}, bf16[256,256]{1,0:T(8,128)(2,1)S(1)}, u32[]{:S(2)}, u32[]{:S(2)}) collective-permute-start(bf16[256,256]{1,0:T(8,128)(2,1)S(1)} %get-tuple-element.73), channel_id=1, source_target_pairs={{0,24},{8,16},{16,8},{24,0},{1,25},{9,17},{17,9},{25,1},{2,26},{10... | collective-permute-start | bytes 393224 | tf_op jit(solution)/shard_map/ppermute | solution.py:21
  100.7 9.6 %collective-permute-start.18 = (bf16[256,256]{1,0:T(8,128)(2,1)S(1)}, bf16[256,256]{1,0:T(8,128)(2,1)S(1)}, u32[]{:S(2)}, u32[]{:S(2)}) collective-permute-start(bf16[256,256]{1,0:T(8,128)(2,1)S(1)} %get-tuple-element.74), channel_id=1, source_target_pairs={{0,16},{8,24},{16,0},{24,8},{1,17},{9,25},{17,1},{25,9},{2,18},{10... | collective-permute-start | bytes 393224 | tf_op jit(solution)/shard_map/ppermute | solution.py:21
  105.1 9.7 %collective-permute-start.15 = (bf16[128,512]{1,0:T(8,128)(2,1)S(1)}, bf16[128,512]{1,0:T(8,128)(2,1)S(1)}, u32[]{:S(2)}, u32[]{:S(2)}) collective-permute-start(bf16[128,512]{1,0:T(8,128)(2,1)S(1)} %get-tuple-element.51), channel_id=1, source_target_pairs={{0,16},{8,24},{16,0},{24,8},{1,17},{9,25},{17,1},{25,9},{2,18},{10... | collective-permute-start | bytes 393224 | tf_op jit(solution)/shard_map/ppermute | solution.py:21
  107.8 7.0 %collective-permute-start.16 = (bf16[128,512]{1,0:T(8,128)(2,1)S(1)}, bf16[128,512]{1,0:T(8,128)(2,1)S(1)}, u32[]{:S(2)}, u32[]{:S(2)}) collective-permute-start(bf16[128,512]{1,0:T(8,128)(2,1)S(1)} %get-tuple-element.52), channel_id=1, source_target_pairs={{0,24},{8,16},{16,8},{24,0},{1,25},{9,17},{17,9},{25,1},{2,26},{10... | collective-permute-start | bytes 393224 | tf_op jit(solution)/shard_map/ppermute | solution.py:21
  118.6 2.0 %copy-start.30 = (f32[512,2048]{1,0:T(8,128)}, f32[512,2048]{1,0:T(8,128)S(1)}, u32[]{:S(2)}) copy-start(f32[512,2048]{1,0:T(8,128)S(1)} %fusion) | copy-start | bytes 12582916
  121.7 11.9 %collective-permute-start.25 = (bf16[4,64,2048]{2,1,0:T(8,128)(2,1)}, bf16[4,64,2048]{2,1,0:T(8,128)(2,1)}, u32[]{:S(2)}, u32[]{:S(2)}) collective-permute-start(bf16[4,64,2048]{2,1,0:T(8,128)(2,1)} %fusion.18), channel_id=1, source_target_pairs={{0,1},{1,0},{2,3},{3,2},{4,5},{5,4},{6,7},{7,6},{8,9},{9,8},{10,11... | collective-permute-start | bytes 3145736 | tf_op jit(solution)/shard_map/ppermute | solution.py:21
  121.7 1.4 copy-start.2
  123.1 1.0 copy-start.6
  124.2 1.0 copy-start.8
  125.2 1.0 copy-start.10
  126.3 7.4 %copy-start.31 = (f32[512,2048]{1,0:T(8,128)S(1)}, f32[512,2048]{1,0:T(8,128)}, u32[]{:S(2)}) copy-start(f32[512,2048]{1,0:T(8,128)} %copy-done.30) | copy-start | bytes 12582916
  130.2 9.0 %collective-permute-start.24 = (f32[4,6144]{1,0:T(4,128)S(1)}, f32[4,6144]{1,0:T(4,128)S(1)}, u32[]{:S(2)}, u32[]{:S(2)}) collective-permute-start(f32[4,6144]{1,0:T(4,128)S(1)} %get-tuple-element.60), channel_id=1, source_target_pairs={{0,24},{8,16},{16,8},{24,0},{1,25},{9,17},{17,9},{25,1},{2,26},{10... | collective-permute-start | bytes 294920 | tf_op jit(solution)/shard_map/ppermute | solution.py:21
  132.6 7.2 %collective-permute-start.23 = (f32[4,6144]{1,0:T(4,128)S(1)}, f32[4,6144]{1,0:T(4,128)S(1)}, u32[]{:S(2)}, u32[]{:S(2)}) collective-permute-start(f32[4,6144]{1,0:T(4,128)S(1)} %get-tuple-element.60), channel_id=1, source_target_pairs={{0,16},{8,24},{16,0},{24,8},{1,17},{9,25},{17,1},{25,9},{2,18},{10... | collective-permute-start | bytes 294920 | tf_op jit(solution)/shard_map/ppermute | solution.py:21
  133.1 6.7 %collective-permute-start.22 = (f32[4,6144]{1,0:T(4,128)S(1)}, f32[4,6144]{1,0:T(4,128)S(1)}, u32[]{:S(2)}, u32[]{:S(2)}) collective-permute-start(f32[4,6144]{1,0:T(4,128)S(1)} %get-tuple-element.60), channel_id=1, source_target_pairs={{0,8},{8,0},{16,24},{24,16},{1,9},{9,1},{17,25},{25,17},{2,10},{10... | collective-permute-start | bytes 294920 | tf_op jit(solution)/shard_map/ppermute | solution.py:21
  135.2 21.9 %collective-permute-start.29 = (bf16[64,2048]{1,0:T(8,128)(2,1)S(1)}, bf16[64,2048]{1,0:T(8,128)(2,1)S(1)}, u32[]{:S(2)}, u32[]{:S(2)}) collective-permute-start(bf16[64,2048]{1,0:T(8,128)(2,1)S(1)} %get-tuple-element.69), channel_id=1, source_target_pairs={{0,6},{1,7},{2,4},{3,5},{4,2},{5,3},{6,0},{7,1},{8,14},{9,15},{10,... | collective-permute-start | bytes 786440 | tf_op jit(solution)/shard_map/ppermute | solution.py:21
  139.1 22.4 %collective-permute-start.28 = (bf16[64,2048]{1,0:T(8,128)(2,1)S(1)}, bf16[64,2048]{1,0:T(8,128)(2,1)S(1)}, u32[]{:S(2)}, u32[]{:S(2)}) collective-permute-start(bf16[64,2048]{1,0:T(8,128)(2,1)S(1)} %get-tuple-element.70), channel_id=1, source_target_pairs={{0,4},{1,5},{2,6},{3,7},{4,0},{5,1},{6,2},{7,3},{8,12},{9,13},{10,... | collective-permute-start | bytes 786440 | tf_op jit(solution)/shard_map/ppermute | solution.py:21
  139.1 16.7 %collective-permute-start.26 = (bf16[64,2048]{1,0:T(8,128)(2,1)S(1)}, bf16[64,2048]{1,0:T(8,128)(2,1)S(1)}, u32[]{:S(2)}, u32[]{:S(2)}) collective-permute-start(bf16[64,2048]{1,0:T(8,128)(2,1)S(1)} %get-tuple-element.71), channel_id=1, source_target_pairs={{0,2},{1,3},{2,0},{3,1},{4,6},{5,7},{6,4},{7,5},{8,10},{9,11},{10,... | collective-permute-start | bytes 786440 | tf_op jit(solution)/shard_map/ppermute | solution.py:21
  155.9 1.3 collective-permute-start.27
  161.5 7.6 %collective-permute-start.32 = (f32[3,6144]{1,0:T(4,128)S(1)}, f32[3,6144]{1,0:T(4,128)S(1)}, u32[]{:S(2)}, u32[]{:S(2)}) collective-permute-start(f32[3,6144]{1,0:T(4,128)S(1)} %add.205), channel_id=1, source_target_pairs={{0,6},{1,7},{2,4},{3,5},{4,2},{5,3},{6,0},{7,1},{8,14},{9,15},{10,... | collective-permute-start | bytes 221192 | tf_op jit(solution)/shard_map/ppermute | solution.py:21
  163.9 7.8 %collective-permute-start.31 = (f32[3,6144]{1,0:T(4,128)S(1)}, f32[3,6144]{1,0:T(4,128)S(1)}, u32[]{:S(2)}, u32[]{:S(2)}) collective-permute-start(f32[3,6144]{1,0:T(4,128)S(1)} %add.205), channel_id=1, source_target_pairs={{0,4},{1,5},{2,6},{3,7},{4,0},{5,1},{6,2},{7,3},{8,12},{9,13},{10,... | collective-permute-start | bytes 221192 | tf_op jit(solution)/shard_map/ppermute | solution.py:21
  163.9 7.8 %collective-permute-start.30 = (f32[3,6144]{1,0:T(4,128)S(1)}, f32[3,6144]{1,0:T(4,128)S(1)}, u32[]{:S(2)}, u32[]{:S(2)}) collective-permute-start(f32[3,6144]{1,0:T(4,128)S(1)} %add.205), channel_id=1, source_target_pairs={{0,2},{1,3},{2,0},{3,1},{4,6},{5,7},{6,4},{7,5},{8,10},{9,11},{10,... | collective-permute-start | bytes 221192 | tf_op jit(solution)/shard_map/ppermute | solution.py:21
  (13 other events, 9.7 us)

commit v6 on v5

--- a/solution.py
+++ b/solution.py
@@ -21,7 +21,6 @@
     return lax.ppermute(value, axis, [(i, i ^ mask) for i in range(lax.axis_size(axis))])
 
 
-VMEM = pl.BlockSpec(memory_space=pltpu.VMEM)
 SMEM = pl.BlockSpec(memory_space=pltpu.SMEM)
 
 
@@ -42,15 +41,37 @@
     return jnp.where(row == count - 1, after[1:2], jnp.where(row == count - 2, after[0:1], moved))
 
 
-def call(kernel, name, outs, smem, *args):
-    moved = sum(math.prod(a.shape) * a.dtype.itemsize for a in args)
+def call(kernel, name, outs, smem, limit, *args):
+    arrays = args[smem:]
+    count, given = (len(arrays), len(outs))
+
+    def run(*refs):
+        ends = refs[smem : smem + count + given]
+        *buffers, sems = refs[smem + count + given :]
+        copies = []
+        for i, (end, buffer) in enumerate(zip(ends, buffers)):
+            pair = (end, buffer) if i < count else (buffer, end)
+            copies.append(pltpu.make_async_copy(*pair, sems.at[i]))
+        for copy in copies[:count]:
+            copy.start()
+        for copy in copies[:count]:
+            copy.wait()
+        kernel(*refs[:smem], *buffers)
+        for copy in copies[count:]:
+            copy.start()
+        for copy in copies[count:]:
+            copy.wait()
+
+    anywhere = pl.BlockSpec(memory_space=pl.ANY)
     return pl.pallas_call(
-        kernel,
+        run,
         out_shape=outs,
-        in_specs=[SMEM] * smem + [VMEM] * (len(args) - smem),
-        out_specs=[VMEM] * len(outs),
-        compiler_params=pltpu.CompilerParams(vmem_limit_bytes=40 * 2**20),
-        cost_estimate=pl.CostEstimate(flops=8 * moved, transcendentals=0, bytes_accessed=2 * moved),
+        in_specs=[SMEM] * smem + [anywhere] * count,
+        out_specs=[anywhere] * given,
+        scratch_shapes=[pltpu.VMEM(a.shape, a.dtype) for a in (*arrays, *outs)]
+        + [pltpu.SemaphoreType.DMA((count + given,))],
+        compiler_params=pltpu.CompilerParams(vmem_limit_bytes=limit * 2**20),
+        cost_estimate=pl.CostEstimate(flops=0, transcendentals=0, bytes_accessed=0),
         name=name,
     )(*args)
 
@@ -90,18 +111,15 @@
             grad_long_ref[b] = (values.astype(F32) * query_ref[b].astype(F32)).astype(BF16)
 
 
-def place_kernel(me_ref, *refs):
-    pieces, out_ref = refs[:-1], refs[-1]
-    for k, piece in enumerate(pieces):
-        out_ref[me_ref[0] ^ k] = piece[...]
-
-
-def gate_kernel(me_ref, query_ref, long_ref, *pieces):
+def gate_kernel(me_ref, me_dp_ref, query_ref, *refs):
     parts, _, blk = query_ref.shape
+    came, long_ref, pieces = refs[:parts], refs[parts], refs[parts + 1 :]
     ratio = parts // len(pieces)
+    for k, piece in enumerate(came):
+        long_ref[me_ref[0] ^ k] = piece[...]
     for k, piece in enumerate(pieces):
         for i in range(ratio):
-            b = (me_ref[0] ^ k) * ratio + i
+            b = (me_dp_ref[0] ^ k) * ratio + i
             gate = query_ref[b].astype(F32) * long_ref[b].astype(F32)
             piece[:, columns(i, blk)] = gate.astype(BF16)
 
@@ -203,17 +221,6 @@
     return [1 << i for i in range(count.bit_length() - 1) if 1 << i >= first]
 
 
-def summed_blocks(value, axis, dim):
-    count = lax.axis_size(axis)
-    size = value.shape[dim] // count
-    me = lax.axis_index(axis)
-    total = lax.dynamic_slice_in_dim(value, me * size, size, dim)
-    for k in range(1, count):
-        sent = lax.dynamic_slice_in_dim(value, (me ^ k) * size, size, dim).astype(BF16)
-        total = total + swapped(sent, axis, k).astype(F32)
-    return total
-
-
 def own_share(partial, parts):
     blocks = partial.reshape(parts // 2, 2, -1, partial.shape[-1])
     core = lax.axis_index("context") % 2
@@ -225,7 +232,7 @@
     for k in range(1, parts // 2):
         sent = lax.dynamic_index_in_dim(pair, row ^ k, 0, False)
         shares.append(swapped(sent, "context", 2 * k))
-    return (other, shares)
+    return (pair, shares)
 
 
 def to_channels(blocks):
@@ -251,7 +258,7 @@
     prev_rows = passed_along(projected[rows - 2 :], "context", 1).astype(F32)
     cots = [cotangent] + [swapped(cotangent, "dp", k) for k in range(1, parts_dp)]
     query, keyed, valued, product_out = call(
-        short_kernel, "short_convs", [plane] * 4, 0, projected, prev_rows, short_taps
+        short_kernel, "short_convs", [plane] * 4, 0, 60, projected, prev_rows, short_taps
     )
     product = to_channels(product_out)
 
@@ -266,11 +273,9 @@
     found = [dot(cot, weights, 1, 1).astype(BF16) for cot in cots]
     found = [found[0]] + [swapped(found[k], "dp", k) for k in range(1, parts_dp)]
     gate_grad, grad_long_out = call(
-        grad_long_kernel, "grad_long", [plane] * 2, 1, me_dp, query, *found
+        grad_long_kernel, "grad_long", [plane] * 2, 1, 12, me_dp, query, *found
     )
     grad_long = to_channels(grad_long_out)
-    heads = ordered(jnp.stack([keyed[:, :2], valued[:, :2]]), grad_long_out)
-    pair_after = passed_along(heads, "context", -1).astype(F32)
     product_f, grad_long_f = (product.astype(F32), grad_long.astype(F32))
 
     def finished(total, direct):
@@ -305,22 +310,26 @@
     next_heads = jnp.concatenate([back_blocks[1:, :2], jnp.zeros((1, 2, blk), BF16)], 0)
     back_sent = jnp.concatenate([back_blocks, next_heads], 1)
     grad_product = to_positions(back_sent)
+    heads = ordered(jnp.stack([keyed[:, :2], valued[:, :2]]), back_sent)
+    pair_after = passed_along(heads, "context", -1).astype(F32)
     long_came = lax.optimization_barrier((*long_came, back_sent))[:parts]
-    (long_out,) = call(place_kernel, "long_out", [plane], 1, me[None], *long_came)
-
-    grad_filter = summed_blocks(lag_sum, "dp", 1) * (scale_factor * inverse)
+
+    grad_filter = lax.psum_scatter(lag_sum, "dp", scatter_dimension=1, tiled=True)
+    grad_filter = grad_filter * (scale_factor * inverse)
     skip_sum = jnp.sum(grad_long_f * product_f, 0, keepdims=True)
 
     piece = jax.ShapeDtypeStruct((rows, chans // parts_dp), BF16)
-    gates = call(gate_kernel, "gate", [piece] * parts_dp, 1, me_dp, query, long_out)
+    long_out, *gates = call(
+        gate_kernel, "gate", [plane] + [piece] * parts_dp, 2, 12, me[None], me_dp, query, *long_came
+    )
     gates = [gates[0]] + [swapped(gates[k], "dp", k) for k in range(1, parts_dp)]
     query_heads = gate_grad[:, :2].astype(F32) * long_out[:, :2].astype(F32)
     query_after = passed_along(query_heads, "context", -1)
-    early = (grad_product, grad_filter, skip_sum, pair_after, query_after)
+    early = (grad_product, lag_sum, skip_sum, pair_after, query_after)
     gate_all = ordered(jnp.concatenate(gates, 0), *early)
     proj_sum = dot(gate_all, jnp.concatenate(cots, 0), 0, 0)
-    other, shares = own_share(proj_sum, parts)
-    grad_product = ordered(grad_product, other)
+    pair, shares = own_share(proj_sum, parts)
+    grad_product = ordered(grad_product, pair)
 
     grad_inputs, tap_sums = call(
         final_kernel,
@@ -330,6 +339,7 @@
             jax.ShapeDtypeStruct((4, width), F32),
         ],
         0,
+        60,
         projected,
         prev_rows,
         short_taps,
@@ -343,11 +353,10 @@
         skip_sum,
     )
 
-    tap_sums = all_sum(tap_sums, "dp", bits_of(parts_dp))
+    tap_sums = all_sum(ordered(tap_sums, grad_filter), "dp", bits_of(parts_dp))
     grad_skip = tap_sums[3, :blk] * scale_factor
-    tap_sums = ordered(tap_sums[:3], shares[1])
-    tap_sums = tap_sums + swapped(tap_sums, "context", 1)
-    tap_sums = ordered(tap_sums, *shares[2:])
+    tap_sums = tap_sums[:3] + swapped(tap_sums[:3], "context", 1)
+    tap_sums = ordered(tap_sums, *shares[1:])
     grad_taps = all_sum(tap_sums, "context", bits_of(parts, 2)) * scale_factor
     grad_proj = sum(share.astype(F32) for share in shares) * scale_factor
     return (grad_inputs, grad_taps, grad_filter, grad_skip, grad_proj)

time: 174 us -> 181 us (1.040)
  local copies, waits for them, and re-layouts: 27.9 us -> 12.2 us
  between operations: 1.17 us -> 14.6 us
  Pallas kernels: 6.22 us -> 12.3 us
  other arithmetic: 13.5 us -> 15.5 us
    unnamed x82 -> x42, local copies, waits for them, and re-layouts: 24.2 us -> 9.55 us
    pallas_call x5 -> x4, Pallas kernels: 6.22 us -> 12.3 us  [call(): pl.pallas_call(run, out_shape=outs, in_specs=[SMEM] * smem + [anywhere] *...]
    ppermute x30 -> x27, waiting for transfers between devices: 38.6 us -> 41.1 us  [swapped(): lax.ppermute(value, axis, [(i, i ^ mask) for i in range(lax.axis_size(axi...]
    ppermute x30 -> x27, starting transfers between devices: 36.2 us -> 37.1 us  [swapped(): lax.ppermute(value, axis, [(i, i ^ mask) for i in range(lax.axis_size(axi...]
  transfers between devices with their start and end apart: 36 -> 34, of which waited for: 11 -> 10; matrix products, arithmetic and copies ran while one was open for 23% -> 24% of each run, Pallas kernels for 4% -> 7%
where the time goes in v6:
time: 181 us; the launch traced here: 180 us
  starting transfers between devices  56.3 us (31%)
  waiting for transfers between devices  41.2 us (23%)
  matrix products  27.9 us (15%)
  other arithmetic  15.5 us (9%)
  between operations  14.6 us (8%)
  Pallas kernels  12.3 us (7%)
  local copies, waits for them, and re-layouts  12.2 us (7%)
    ppermute x27, waiting for transfers between devices, swapped(): lax.ppermute(value, axis, [(i, i ^ mask) for i in range(lax.axis_size(axi...  41.1 us
    ppermute x27, starting transfers between devices, swapped(): lax.ppermute(value, axis, [(i, i ^ mask) for i in range(lax.axis_size(axi...  37.1 us
    dot_general x11, matrix products, dot(): lax.dot_general(left, right, (((left_dim,), (right_dim,)), ((), ())), pre...  27.9 us
    pallas_call x4, Pallas kernels, call(): pl.pallas_call(run, out_shape=outs, in_specs=[SMEM] * smem + [anywhere] *...  12.3 us
    all_to_all x2, starting transfers between devices, to_channels(): lax.all_to_all(blocks, 'context', split_axis=0, concat_axis=0, tiled=True)  10.8 us
    unnamed x42, local copies, waits for them, and re-layouts  9.55 us
    ppermute x3, starting transfers between devices, passed_along(): lax.ppermute(value, axis, [(source, source + steps) for source in range(i...  4.22 us
    all_to_all x1, starting transfers between devices, to_positions(): lax.all_to_all(blocks, 'context', split_axis=0, concat_axis=0, tiled=True)  4.19 us
  transfers between devices with their start and end apart: 34, of which 10 were waited for; matrix products, arithmetic and copies ran while one was open for 24% of the time, Pallas kernels for 7%

profile of v6, /device:TPU:0, one launch (start us, length us, event | category | flops | bytes accessed | tf_op | source)
XLA Modules:
  0.0 180.1 jit_solution(9025706615088248735)
XLA Ops:
  7.2 3.0 %collective-permute-start.3 = (bf16[128,2048]{1,0:T(8,128)(2,1)}, bf16[128,2048]{1,0:T(8,128)(2,1)S(1)}, u32[]{:S(2)}, u32[]{:S(2)}) collective-permute-start(bf16[128,2048]{1,0:T(8,128)(2,1)} %param.11), channel_id=1, source_target_pairs={{0,16},{8,24},{16,0},{24,8},{1,17},{9,25},{17,1},{25,9},{2,18},{10... | collective-permute-start | bytes 1572872 | tf_op jit(solution)/shard_map/ppermute | solution.py:21
  10.2 1.5 collective-permute-start.1
  11.8 0.9 slice.53
  12.7 1.3 collective-permute-start
  14.0 1.1 fusion.48
  15.1 1.5 subtract_convert_fusion
  17.0 0.8 copy-done.13
  17.8 2.7 %fusion.33 = f32[2048,256]{1,0:T(8,128)} fusion(bf16[2048,1024]{1,0:T(8,128)(2,1)S(1)} %bitcast.75, f32[256,1024]{1,0:T(8,128)S(1)} %copy-done.13), kind=kOutput, calls=%fused_computation.54 | convolution fusion | flops 1074003968 | bytes 7340032 | tf_op jit(solution)/shard_map/dot_general | solution.py:175
  20.5 0.8 fusion.13.refs_2_
  22.1 3.6 %short_convs.1 = (bf16[8,128,256]{2,1,0:T(8,128)(2,1)}, bf16[8,128,256]{2,1,0:T(8,128)(2,1)}, bf16[8,128,256]{2,1,0:T(8,128)(2,1)}, bf16[8,128,256]{2,1,0:T(8,128)(2,1)}) custom-call(bf16[128,6144]{1,0:T(8,128)(2,1)} %refs_0_.3, f32[2,6144]{1,0:T(2,128)} %convert_element_type.115.refs_1_, f32[3,6144]{1,0:T(4,128)} %refs_2_.3), custom_call_target="tpu_custom_call" | custom-call | tf_op jit(solution)/shard_map/short_convs/pallas_call | solution.py:66
  25.7 6.2 %all-to-all-start = ((bf16[8,128,256]{2,1,0:T(8,128)(2,1)}), bf16[8,128,256]{2,1,0:T(8,128)(2,1)}, u32[]{:S(2)}, u32[]{:S(2)}) async-start(bf16[8,128,256]{2,1,0:T(8,128)(2,1)} %get-tuple-element.38), calls=%async_computation | async-start | bytes 1048576 | tf_op jit(solution)/shard_map/all_to_all | solution.py:239
  31.9 1.9 %fusion.14 = bf16[128,512]{1,0:T(8,128)(2,1)S(1)} fusion(bf16[512,2048]{1,0:T(8,128)(2,1)S(1)} %copy-done, bf16[128,2048]{1,0:T(8,128)(2,1)} %collective-permute-done.1), kind=kOutput, calls=%fused_computation.25 | convolution fusion | flops 268500992 | bytes 2752512 | tf_op jit(solution)/shard_map/dot_general | solution.py:175
  33.8 1.6 collective-permute-start.2
  35.3 0.8 copy-done.16
  36.1 0.8 fusion.15
  37.0 1.6 collective-permute-start.4
  38.6 1.9 %fusion.16 = bf16[128,512]{1,0:T(8,128)(2,1)S(1)} fusion(bf16[512,2048]{1,0:T(8,128)(2,1)S(1)} %copy-done, bf16[128,2048]{1,0:T(8,128)(2,1)} %collective-permute-done.5), kind=kOutput, calls=%fused_computation.27 | convolution fusion | flops 268500992 | bytes 2752512 | tf_op jit(solution)/shard_map/dot_general | solution.py:175
  41.0 0.8 slice_bitcast_fusion
  41.8 1.0 collective-permute-done.4.refs_4_
  42.8 4.1 %collective-permute-done.6.refs_5_ = bf16[128,512]{1,0:T(8,128)(2,1)S(1)} collective-permute-done((bf16[128,512]{1,0:T(8,128)(2,1)S(1)}, bf16[128,512]{1,0:T(8,128)(2,1)S(1)}, u32[]{:S(2)}, u32[]{:S(2)}) %collective-permute-start.6) | collective-permute-done | bytes 131104 | tf_op jit(solution)/shard_map/ppermute | solution.py:21
  46.9 1.0 grad_long.1
  47.9 0.8 copy-done.4
  48.7 4.6 %all-to-all-start.1 = ((bf16[8,128,256]{2,1,0:T(8,128)(2,1)}), bf16[8,128,256]{2,1,0:T(8,128)(2,1)}, u32[]{:S(2)}, u32[]{:S(2)}) async-start(bf16[8,128,256]{2,1,0:T(8,128)(2,1)} %copy-done.4), calls=%async_computation.1 | async-start | bytes 1048576 | tf_op jit(solution)/shard_map/all_to_all | solution.py:239
  53.3 3.8 %fusion.55 = f32[2048,256]{1,0:T(8,128)S(1)} fusion(bf16[2048,1024]{1,0:T(8,128)(2,1)} %bitcast.76, bf16[1024,256]{1,0:T(8,128)(2,1)} %bitcast.7), kind=kOutput, calls=%fused_computation.104 | convolution fusion | flops 1073741824 | bytes 6815744 | tf_op jit(solution)/shard_map/dot_general | solution.py:175
  57.5 0.9 copy-done.10
  58.5 1.6 copy-done.8
  60.1 2.3 %fusion.12 = bf16[1024,256]{1,0:T(8,128)(2,1)S(1)} fusion(bf16[2048,1024]{1,0:T(8,128)(2,1)S(1)} %bitcast.79, bf16[1024,256]{1,0:T(8,128)(2,1)S(1)} %get-tuple-element.70, bf16[1024,256]{1,0:T(8,128)(2,1)S(1)} %get-tuple-element.69, bf16[1024,256]{1,0:T(8,128)(2,1)} %bitcast.7, f32[256]{0:T(256)S(1)} %copy-done.19), kind=kOutput, calls=%fused_computation.19 | convolution fusion | flops 1077149696 | bytes 6292480 | tf_op jit(solution)/shard_map/dot_general | solution.py:175
  62.4 0.8 dynamic-slice_bitcast_fusion.3
  63.2 3.6 %collective-permute-start.13 = (bf16[128,256]{1,0:T(8,128)(2,1)}, bf16[128,256]{1,0:T(8,128)(2,1)S(1)}, u32[]{:S(2)}, u32[]{:S(2)}) collective-permute-start(bf16[128,256]{1,0:T(8,128)(2,1)} %get-tuple-element.74), channel_id=1, source_target_pairs={{0,7},{1,6},{2,5},{3,4},{4,3},{5,2},{6,1},{7,0},{8,15},{9,14},{10,... | collective-permute-start | bytes 196616 | tf_op jit(solution)/shard_map/ppermute | solution.py:21
  67.6 2.1 %collective-permute-start.10 = (bf16[128,256]{1,0:T(8,128)(2,1)}, bf16[128,256]{1,0:T(8,128)(2,1)S(1)}, u32[]{:S(2)}, u32[]{:S(2)}) collective-permute-start(bf16[128,256]{1,0:T(8,128)(2,1)} %get-tuple-element.77), channel_id=1, source_target_pairs={{0,4},{1,5},{2,6},{3,7},{4,0},{5,1},{6,2},{7,3},{8,12},{9,13},{10,... | collective-permute-start | bytes 196616 | tf_op jit(solution)/shard_map/ppermute | solution.py:21
  69.7 1.2 collective-permute-start.9
  70.9 3.8 %fusion.56 = f32[2048,256]{1,0:T(8,128)S(1)} fusion(bf16[2048,1024]{1,0:T(8,128)(2,1)} %bitcast.77, bf16[1024,256]{1,0:T(8,128)(2,1)} %bitcast.17), kind=kOutput, calls=%fused_computation.105 | convolution fusion | flops 1073741824 | bytes 6815744 | tf_op jit(solution)/shard_map/dot_general | solution.py:175
  75.1 1.8 copy-done.9
  76.9 2.5 %fusion.11 = bf16[1024,256]{1,0:T(8,128)(2,1)S(1)} fusion(bf16[2048,1024]{1,0:T(8,128)(2,1)S(1)} %bitcast.80, bf16[1024,256]{1,0:T(8,128)(2,1)S(1)} %get-tuple-element.68, bf16[1024,256]{1,0:T(8,128)(2,1)S(1)} %get-tuple-element.67, bf16[1024,256]{1,0:T(8,128)(2,1)} %bitcast.17, f32[256]{0:T(256)S(1)} %copy-done.20), kind=kOutput, calls=%fused_computation.18 | convolution fusion | flops 1077149696 | bytes 6292480 | tf_op jit(solution)/shard_map/dot_general | solution.py:175
  79.4 1.4 add_convert_fusion
  80.8 0.8 fusion.29
  81.6 4.2 %all-to-all-start.2 = ((bf16[8,130,256]{2,1,0:T(8,128)(2,1)}), bf16[8,130,256]{2,1,0:T(8,128)(2,1)}, u32[]{:S(2)}, u32[]{:S(2)}) async-start(bf16[8,130,256]{2,1,0:T(8,128)(2,1)} %fusion.29), calls=%async_computation.2 | async-start | bytes 1114112 | tf_op jit(solution)/shard_map/all_to_all | solution.py:244
  85.9 1.9 %collective-permute-start.8 = (bf16[128,256]{1,0:T(8,128)(2,1)}, bf16[128,256]{1,0:T(8,128)(2,1)}, u32[]{:S(2)}, u32[]{:S(2)}) collective-permute-start(bf16[128,256]{1,0:T(8,128)(2,1)} %get-tuple-element.79), channel_id=1, source_target_pairs={{0,2},{1,3},{2,0},{3,1},{4,6},{5,7},{6,4},{7,5},{8,10},{9,11},{10,... | collective-permute-start | bytes 196616 | tf_op jit(solution)/shard_map/ppermute | solution.py:21
  87.8 4.8 %fusion.25 = f32[256,1024]{1,0:T(8,128)} fusion(bf16[2048,1024]{1,0:T(8,128)(2,1)} %bitcast.78, bf16[1024,256]{1,0:T(8,128)(2,1)} %get-tuple-element.66, bf16[1024,256]{1,0:T(8,128)(2,1)} %get-tuple-element.65), kind=kOutput, calls=%fused_computation.37 | convolution fusion | flops 1075838976 | bytes 6291456 | tf_op jit(solution)/shard_map/dot_general | solution.py:175
  92.7 4.7 %collective-permute-done.8.refs_5_ = bf16[128,256]{1,0:T(8,128)(2,1)} collective-permute-done((bf16[128,256]{1,0:T(8,128)(2,1)}, bf16[128,256]{1,0:T(8,128)(2,1)}, u32[]{:S(2)}, u32[]{:S(2)}) %collective-permute-start.8) | collective-permute-done | bytes 65568 | tf_op jit(solution)/shard_map/ppermute | solution.py:21
  97.3 2.0 %gate.1 = (bf16[8,128,256]{2,1,0:T(8,128)(2,1)S(1)}, bf16[128,512]{1,0:T(8,128)(2,1)S(1)}, bf16[128,512]{1,0:T(8,128)(2,1)S(1)}, bf16[128,512]{1,0:T(8,128)(2,1)S(1)}, bf16[128,512]{1,0:T(8,128)(2,1)S(1)}) custom-call(s32[1]{0:T(128)} %bitcast.6.refs_0_, s32[1]{0:T(128)} %bitcast.refs_0_.refs_1_, bf16[8,128,256]{2,1,0:T(8,128)(2,1)S(1)} %copy-done.1, ...), custom_call_target="tpu_custom_call" | custom-call | tf_op jit(solution)/shard_map/gate/pallas_call | solution.py:66
  99.4 0.8 copy-done.3
  100.2 1.4 collective-permute-start.18
  101.6 1.5 collective-permute-start.17
  104.4 2.3 %collective-permute-start.16 = (bf16[128,512]{1,0:T(8,128)(2,1)S(1)}, bf16[128,512]{1,0:T(8,128)(2,1)S(1)}, u32[]{:S(2)}, u32[]{:S(2)}) collective-permute-start(bf16[128,512]{1,0:T(8,128)(2,1)S(1)} %get-tuple-element.54), channel_id=1, source_target_pairs={{0,24},{8,16},{16,8},{24,0},{1,25},{9,17},{17,9},{25,1},{2,26},{10... | collective-permute-start | bytes 393224 | tf_op jit(solution)/shard_map/ppermute | solution.py:21
  106.6 2.0 %multiply_reduce_fusion = f32[256]{0:T(256)} fusion(bf16[8,128,256]{2,1,0:T(8,128)(2,1)} %all-to-all-done, bf16[8,128,256]{2,1,0:T(8,128)(2,1)} %all-to-all-done.1), kind=kLoop, calls=%fused_computation.41 | loop fusion | flops 1048320 | bytes 1049600 | tf_op jit(solution)/shard_map/reduce_sum | solution.py:319
  109.3 3.2 %collective-permute-done.15 = bf16[128,512]{1,0:T(8,128)(2,1)S(1)} collective-permute-done((bf16[128,512]{1,0:T(8,128)(2,1)S(1)}, bf16[128,512]{1,0:T(8,128)(2,1)S(1)}, u32[]{:S(2)}, u32[]{:S(2)}) %collective-permute-start.15) | collective-permute-done | bytes 131104 | tf_op jit(solution)/shard_map/ppermute | solution.py:21
  112.5 2.7 %fusion = f32[512,2048]{1,0:T(8,128)S(1)} fusion(bf16[512,512]{1,0:T(8,128)(2,1)S(1)} %pad_maximum_fusion.1, bf16[128,2048]{1,0:T(8,128)(2,1)} %collective-permute-done.5, bf16[128,2048]{1,0:T(8,128)(2,1)} %copy-done.16, bf16[128,2048]{1,0:T(8,128)(2,1)} %collective-permute-done.1, bf16[128,2048]{1,0:T(8,128)(2,1)S(1)} %copy-done.15), kind=kOutput, calls=%fused_computation.3 | convolution fusion | flops 1082130432 | bytes 6815744 | tf_op jit(solution)/shard_map/dot_general | solution.py:175
  115.2 2.0 %copy-done.12 = f32[512,2048]{1,0:T(8,128)} copy-done((f32[512,2048]{1,0:T(8,128)}, f32[512,2048]{1,0:T(8,128)S(1)}, u32[]{:S(2)}) %copy-start.12) | copy-done | bytes 4194328
  117.7 2.5 %collective-permute-done.19 = bf16[4,64,2048]{2,1,0:T(8,128)(2,1)} collective-permute-done((bf16[4,64,2048]{2,1,0:T(8,128)(2,1)S(1)}, bf16[4,64,2048]{2,1,0:T(8,128)(2,1)}, u32[]{:S(2)}, u32[]{:S(2)}) %collective-permute-start.19) | collective-permute-done | bytes 1048608 | tf_op jit(solution)/shard_map/ppermute | solution.py:21
  120.2 2.2 %fusion.8 = bf16[4,64,2048]{2,1,0:T(8,128)(2,1)S(1)} fusion(bf16[4,64,2048]{2,1,0:T(8,128)(2,1)} %collective-permute-done.19, f32[4,2,64,2048]{3,2,1,0:T(8,128)} %bitcast.82, s32[]{:T(128)S(6)} %select_n.95), kind=kLoop, calls=%fused_computation.13 | loop fusion | flops 1572864 | bytes 4194308 | tf_op jit(solution)/shard_map/convert_element_type | solution.py:229
  122.4 5.7 %stream_grads.1 = (bf16[128,6144]{1,0:T(8,128)(2,1)}, f32[4,6144]{1,0:T(4,128)}) custom-call(bf16[128,6144]{1,0:T(8,128)(2,1)} %refs_0_.3, f32[2,6144]{1,0:T(2,128)} %convert_element_type.115.refs_1_, f32[3,6144]{1,0:T(4,128)} %refs_2_.3, bf16[8,128,256]{2,1,0:T(8,128)(2,1)} %copy-done.2, bf16[8,128,256]{2,1,0:T(8,128)(2,1)} %copy-done.3, ...), custom_call_target="tpu_custom_call" | custom-call | tf_op jit(solution)/shard_map/stream_grads/pallas_call | solution.py:66
  128.2 1.7 broadcast_multiply_fusion
  129.9 1.3 collective-permute-start.22
  131.2 1.7 collective-permute-start.21
  133.5 6.7 %collective-permute-start.26 = (bf16[64,2048]{1,0:T(8,128)(2,1)S(1)}, bf16[64,2048]{1,0:T(8,128)(2,1)S(1)}, u32[]{:S(2)}, u32[]{:S(2)}) collective-permute-start(bf16[64,2048]{1,0:T(8,128)(2,1)S(1)} %get-tuple-element.71), channel_id=1, source_target_pairs={{0,6},{1,7},{2,4},{3,5},{4,2},{5,3},{6,0},{7,1},{8,14},{9,15},{10,... | collective-permute-start | bytes 786440 | tf_op jit(solution)/shard_map/ppermute | solution.py:21
  141.5 0.7 collective-permute-done.23
  142.3 5.2 %collective-permute-done.26 = bf16[64,2048]{1,0:T(8,128)(2,1)S(1)} collective-permute-done((bf16[64,2048]{1,0:T(8,128)(2,1)S(1)}, bf16[64,2048]{1,0:T(8,128)(2,1)S(1)}, u32[]{:S(2)}, u32[]{:S(2)}) %collective-permute-start.26) | collective-permute-done | bytes 262176 | tf_op jit(solution)/shard_map/ppermute | solution.py:21
  147.5 14.8 %collective-permute-done.25 = bf16[64,2048]{1,0:T(8,128)(2,1)S(1)} collective-permute-done((bf16[64,2048]{1,0:T(8,128)(2,1)S(1)}, bf16[64,2048]{1,0:T(8,128)(2,1)S(1)}, u32[]{:S(2)}, u32[]{:S(2)}) %collective-permute-start.25) | collective-permute-done | bytes 262176 | tf_op jit(solution)/shard_map/ppermute | solution.py:21
  162.3 2.7 %collective-permute-start.29 = (f32[3,6144]{1,0:T(4,128)S(1)}, f32[3,6144]{1,0:T(4,128)S(1)}, u32[]{:S(2)}, u32[]{:S(2)}) collective-permute-start(f32[3,6144]{1,0:T(4,128)S(1)} %slice_add_fusion), channel_id=1, source_target_pairs={{0,6},{1,7},{2,4},{3,5},{4,2},{5,3},{6,0},{7,1},{8,14},{9,15},{10,... | collective-permute-start | bytes 221192 | tf_op jit(solution)/shard_map/ppermute | solution.py:21
  165.0 1.7 collective-permute-start.27
  166.7 0.9 fusion.32
  167.6 2.3 %collective-permute-done.29 = f32[3,6144]{1,0:T(4,128)S(1)} collective-permute-done((f32[3,6144]{1,0:T(4,128)S(1)}, f32[3,6144]{1,0:T(4,128)S(1)}, u32[]{:S(2)}, u32[]{:S(2)}) %collective-permute-start.29) | collective-permute-done | bytes 73760 | tf_op jit(solution)/shard_map/ppermute | solution.py:21
  169.9 2.6 %collective-permute-done.28 = f32[3,6144]{1,0:T(4,128)S(1)} collective-permute-done((f32[3,6144]{1,0:T(4,128)S(1)}, f32[3,6144]{1,0:T(4,128)S(1)}, u32[]{:S(2)}, u32[]{:S(2)}) %collective-permute-start.28) | collective-permute-done | bytes 73760 | tf_op jit(solution)/shard_map/ppermute | solution.py:21
  (90 shorter events, 8.4 us)
Async XLA Ops:
  7.2 13.4 %copy-start = (bf16[512,2048]{1,0:T(8,128)(2,1)S(1)}, bf16[512,2048]{1,0:T(8,128)(2,1)}, u32[]{:S(2)}) copy-start(bf16[512,2048]{1,0:T(8,128)(2,1)} %param.10) | copy-start | bytes 6291460
  7.2 28.1 %collective-permute-start.3 = (bf16[128,2048]{1,0:T(8,128)(2,1)}, bf16[128,2048]{1,0:T(8,128)(2,1)S(1)}, u32[]{:S(2)}, u32[]{:S(2)}) collective-permute-start(bf16[128,2048]{1,0:T(8,128)(2,1)} %param.11), channel_id=1, source_target_pairs={{0,16},{8,24},{16,0},{24,8},{1,17},{9,25},{17,1},{25,9},{2,18},{10... | collective-permute-start | bytes 1572872 | tf_op jit(solution)/shard_map/ppermute | solution.py:21
  10.2 21.7 %collective-permute-start.1 = (bf16[128,2048]{1,0:T(8,128)(2,1)}, bf16[128,2048]{1,0:T(8,128)(2,1)}, u32[]{:S(2)}, u32[]{:S(2)}) collective-permute-start(bf16[128,2048]{1,0:T(8,128)(2,1)} %param.11), channel_id=1, source_target_pairs={{0,8},{8,0},{16,24},{24,16},{1,9},{9,1},{17,25},{25,17},{2,10},{10... | collective-permute-start | bytes 1572872 | tf_op jit(solution)/shard_map/ppermute | solution.py:21
  11.7 26.9 %collective-permute-start.5 = (bf16[128,2048]{1,0:T(8,128)(2,1)}, bf16[128,2048]{1,0:T(8,128)(2,1)}, u32[]{:S(2)}, u32[]{:S(2)}) collective-permute-start(bf16[128,2048]{1,0:T(8,128)(2,1)} %param.11), channel_id=1, source_target_pairs={{0,24},{8,16},{16,8},{24,0},{1,25},{9,17},{17,9},{25,1},{2,26},{10... | collective-permute-start | bytes 1572872 | tf_op jit(solution)/shard_map/ppermute | solution.py:21
  12.7 8.7 %collective-permute-start = (bf16[2,6144]{1,0:T(2,128)(2,1)S(1)}, bf16[2,6144]{1,0:T(2,128)(2,1)S(1)}, u32[]{:S(2)}, u32[]{:S(2)}) collective-permute-start(bf16[2,6144]{1,0:T(2,128)(2,1)S(1)} %slice.53), channel_id=1, source_target_pairs={{0,1},{1,2},{2,3},{3,4},{4,5},{5,6},{6,7},{8,9},{9,10},{10,11},{11... | collective-permute-start | bytes 73736 | tf_op jit(solution)/shard_map/ppermute | solution.py:17
  16.6 1.2 copy-start.13
  17.0 3.5 %copy-start.7 = (bf16[2,32,32,1024]{3,2,1,0:T(8,128)(2,1)}, bf16[2,32,32,1024]{3,2,1,0:T(8,128)(2,1)S(1)}, u32[]{:S(2)}) copy-start(bf16[2,32,32,1024]{3,2,1,0:T(8,128)(2,1)S(1)} %pad_maximum_fusion) | copy-start | bytes 12582916
  17.8 2.7 %copy-start.14 = (bf16[128,2048]{1,0:T(8,128)(2,1)S(1)}, bf16[128,2048]{1,0:T(8,128)(2,1)}, u32[]{:S(2)}) copy-start(bf16[128,2048]{1,0:T(8,128)(2,1)} %param.11) | copy-start | bytes 1572868
  25.7 23.1 %all-to-all-start = ((bf16[8,128,256]{2,1,0:T(8,128)(2,1)}), bf16[8,128,256]{2,1,0:T(8,128)(2,1)}, u32[]{:S(2)}, u32[]{:S(2)}) async-start(bf16[8,128,256]{2,1,0:T(8,128)(2,1)} %get-tuple-element.38), calls=%async_computation | async-start | bytes 1048576 | tf_op jit(solution)/shard_map/all_to_all | solution.py:239
  33.8 8.1 %collective-permute-start.2 = (bf16[128,512]{1,0:T(8,128)(2,1)S(1)}, bf16[128,512]{1,0:T(8,128)(2,1)S(1)}, u32[]{:S(2)}, u32[]{:S(2)}) collective-permute-start(bf16[128,512]{1,0:T(8,128)(2,1)S(1)} %fusion.14), channel_id=1, source_target_pairs={{0,8},{8,0},{16,24},{24,16},{1,9},{9,1},{17,25},{25,17},{2,10},{10... | collective-permute-start | bytes 393224 | tf_op jit(solution)/shard_map/ppermute | solution.py:21
  35.3 0.8 copy-start.16
  37.0 9.9 %copy-start.1 = (bf16[8,128,256]{2,1,0:T(8,128)(2,1)S(1)}, bf16[8,128,256]{2,1,0:T(8,128)(2,1)}, u32[]{:S(2)}) copy-start(bf16[8,128,256]{2,1,0:T(8,128)(2,1)} %get-tuple-element.35.refs_1_.refs_2_) | copy-start | bytes 1572868
  37.0 5.8 %collective-permute-start.4 = (bf16[128,512]{1,0:T(8,128)(2,1)S(1)}, bf16[128,512]{1,0:T(8,128)(2,1)S(1)}, u32[]{:S(2)}, u32[]{:S(2)}) collective-permute-start(bf16[128,512]{1,0:T(8,128)(2,1)S(1)} %fusion.15), channel_id=1, source_target_pairs={{0,16},{8,24},{16,0},{24,8},{1,17},{9,25},{17,1},{25,9},{2,18},{10... | collective-permute-start | bytes 393224 | tf_op jit(solution)/shard_map/ppermute | solution.py:21
  40.5 6.4 %collective-permute-start.6 = (bf16[128,512]{1,0:T(8,128)(2,1)S(1)}, bf16[128,512]{1,0:T(8,128)(2,1)S(1)}, u32[]{:S(2)}, u32[]{:S(2)}) collective-permute-start(bf16[128,512]{1,0:T(8,128)(2,1)S(1)} %fusion.16), channel_id=1, source_target_pairs={{0,24},{8,16},{16,8},{24,0},{1,25},{9,17},{17,9},{25,1},{2,26},{10... | collective-permute-start | bytes 393224 | tf_op jit(solution)/shard_map/ppermute | solution.py:21
  47.9 0.8 copy-start.4
  48.7 50.6 %copy-start.2 = (bf16[8,128,256]{2,1,0:T(8,128)(2,1)}, bf16[8,128,256]{2,1,0:T(8,128)(2,1)S(1)}, u32[]{:S(2)}) copy-start(bf16[8,128,256]{2,1,0:T(8,128)(2,1)S(1)} %get-tuple-element.37.refs_3_) | copy-start | bytes 1572868
  48.7 22.2 %all-to-all-start.1 = ((bf16[8,128,256]{2,1,0:T(8,128)(2,1)}), bf16[8,128,256]{2,1,0:T(8,128)(2,1)}, u32[]{:S(2)}, u32[]{:S(2)}) async-start(bf16[8,128,256]{2,1,0:T(8,128)(2,1)} %copy-done.4), calls=%async_computation.1 | async-start | bytes 1048576 | tf_op jit(solution)/shard_map/all_to_all | solution.py:239
  53.3 3.8 %copy-start.5 = (f32[2048,256]{1,0:T(8,128)S(1)}, f32[2048,256]{1,0:T(8,128)}, u32[]{:S(2)}) copy-start(f32[2048,256]{1,0:T(8,128)} %fusion.33) | copy-start | bytes 6291460
  57.1 1.4 copy-start.10
  57.1 2.9 %copy-start.8 = (bf16[2,32,32,1024]{3,2,1,0:T(8,128)(2,1)S(1)}, bf16[2,32,32,1024]{3,2,1,0:T(8,128)(2,1)}, u32[]{:S(2)}) copy-start(bf16[2,32,32,1024]{3,2,1,0:T(8,128)(2,1)} %copy-done.7) | copy-start | bytes 12582916
  57.1 2.9 %copy-start.19 = (f32[256]{0:T(256)S(1)}, f32[256]{0:T(256)}, u32[]{:S(2)}) copy-start(f32[256]{0:T(256)} %param.9) | copy-start | bytes 3076
  63.2 22.7 %collective-permute-start.13 = (bf16[128,256]{1,0:T(8,128)(2,1)}, bf16[128,256]{1,0:T(8,128)(2,1)S(1)}, u32[]{:S(2)}, u32[]{:S(2)}) collective-permute-start(bf16[128,256]{1,0:T(8,128)(2,1)} %get-tuple-element.74), channel_id=1, source_target_pairs={{0,7},{1,6},{2,5},{3,4},{4,3},{5,2},{6,1},{7,0},{8,15},{9,14},{10,... | collective-permute-start | bytes 196616 | tf_op jit(solution)/shard_map/ppermute | solution.py:21
  66.8 21.0 %collective-permute-start.12 = (bf16[128,256]{1,0:T(8,128)(2,1)}, bf16[128,256]{1,0:T(8,128)(2,1)S(1)}, u32[]{:S(2)}, u32[]{:S(2)}) collective-permute-start(bf16[128,256]{1,0:T(8,128)(2,1)} %get-tuple-element.75), channel_id=1, source_target_pairs={{0,6},{1,7},{2,4},{3,5},{4,2},{5,3},{6,0},{7,1},{8,14},{9,15},{10,... | collective-permute-start | bytes 196616 | tf_op jit(solution)/shard_map/ppermute | solution.py:21
  67.1 25.5 %collective-permute-start.11 = (bf16[128,256]{1,0:T(8,128)(2,1)}, bf16[128,256]{1,0:T(8,128)(2,1)S(1)}, u32[]{:S(2)}, u32[]{:S(2)}) collective-permute-start(bf16[128,256]{1,0:T(8,128)(2,1)} %get-tuple-element.76), channel_id=1, source_target_pairs={{0,5},{1,4},{2,7},{3,6},{4,1},{5,0},{6,3},{7,2},{8,13},{9,12},{10,... | collective-permute-start | bytes 196616 | tf_op jit(solution)/shard_map/ppermute | solution.py:21
  67.6 25.1 %collective-permute-start.10 = (bf16[128,256]{1,0:T(8,128)(2,1)}, bf16[128,256]{1,0:T(8,128)(2,1)S(1)}, u32[]{:S(2)}, u32[]{:S(2)}) collective-permute-start(bf16[128,256]{1,0:T(8,128)(2,1)} %get-tuple-element.77), channel_id=1, source_target_pairs={{0,4},{1,5},{2,6},{3,7},{4,0},{5,1},{6,2},{7,3},{8,12},{9,13},{10,... | collective-permute-start | bytes 196616 | tf_op jit(solution)/shard_map/ppermute | solution.py:21
  69.7 23.0 %collective-permute-start.9 = (bf16[128,256]{1,0:T(8,128)(2,1)}, bf16[128,256]{1,0:T(8,128)(2,1)S(1)}, u32[]{:S(2)}, u32[]{:S(2)}) collective-permute-start(bf16[128,256]{1,0:T(8,128)(2,1)} %get-tuple-element.78), channel_id=1, source_target_pairs={{0,3},{1,2},{2,1},{3,0},{4,7},{5,6},{6,5},{7,4},{8,11},{9,10},{10,... | collective-permute-start | bytes 196616 | tf_op jit(solution)/shard_map/ppermute | solution.py:21
  70.9 3.8 %copy-start.6 = (f32[2048,256]{1,0:T(8,128)S(1)}, f32[2048,256]{1,0:T(8,128)}, u32[]{:S(2)}) copy-start(f32[2048,256]{1,0:T(8,128)} %fusion.33) | copy-start | bytes 6291460
  74.7 2.2 %copy-start.9 = (bf16[2,32,32,1024]{3,2,1,0:T(8,128)(2,1)S(1)}, bf16[2,32,32,1024]{3,2,1,0:T(8,128)(2,1)}, u32[]{:S(2)}) copy-start(bf16[2,32,32,1024]{3,2,1,0:T(8,128)(2,1)} %copy-done.7) | copy-start | bytes 12582916
  74.7 2.2 %copy-start.20 = (f32[256]{0:T(256)S(1)}, f32[256]{0:T(256)}, u32[]{:S(2)}) copy-start(f32[256]{0:T(256)} %param.9) | copy-start | bytes 3076
  76.9 2.5 %copy-start.11 = (f32[2048,256]{1,0:T(8,128)S(1)}, f32[2048,256]{1,0:T(8,128)}, u32[]{:S(2)}) copy-start(f32[2048,256]{1,0:T(8,128)} %copy-done.10) | copy-start | bytes 6291460
  81.6 30.9 %all-to-all-start.2 = ((bf16[8,130,256]{2,1,0:T(8,128)(2,1)}), bf16[8,130,256]{2,1,0:T(8,128)(2,1)}, u32[]{:S(2)}, u32[]{:S(2)}) async-start(bf16[8,130,256]{2,1,0:T(8,128)(2,1)} %fusion.29), calls=%async_computation.2 | async-start | bytes 1114112 | tf_op jit(solution)/shard_map/all_to_all | solution.py:244
  85.8 42.4 %reduce-scatter.2.cloned.1.call-start = ((), (), s32[]{:S(2)}) async-start(), calls=%async_computation.4 | async-start | bytes 1310720 | tf_op jit(solution)/shard_map/reduce_scatter | solution.py:317
  85.9 11.4 %collective-permute-start.8 = (bf16[128,256]{1,0:T(8,128)(2,1)}, bf16[128,256]{1,0:T(8,128)(2,1)}, u32[]{:S(2)}, u32[]{:S(2)}) collective-permute-start(bf16[128,256]{1,0:T(8,128)(2,1)} %get-tuple-element.79), channel_id=1, source_target_pairs={{0,2},{1,3},{2,0},{3,1},{4,6},{5,7},{6,4},{7,5},{8,10},{9,11},{10,... | collective-permute-start | bytes 196616 | tf_op jit(solution)/shard_map/ppermute | solution.py:21
  87.8 9.5 %collective-permute-start.7 = (bf16[128,256]{1,0:T(8,128)(2,1)}, bf16[128,256]{1,0:T(8,128)(2,1)}, u32[]{:S(2)}, u32[]{:S(2)}) collective-permute-start(bf16[128,256]{1,0:T(8,128)(2,1)} %get-tuple-element.80), channel_id=1, source_target_pairs={{0,1},{1,0},{2,3},{3,2},{4,5},{5,4},{6,7},{7,6},{8,9},{9,8},{10,11... | collective-permute-start | bytes 196616 | tf_op jit(solution)/shard_map/ppermute | solution.py:21
  99.3 0.8 copy-start.3
  100.2 12.4 %copy-start.15 = (bf16[128,2048]{1,0:T(8,128)(2,1)S(1)}, bf16[128,2048]{1,0:T(8,128)(2,1)}, u32[]{:S(2)}) copy-start(bf16[128,2048]{1,0:T(8,128)(2,1)} %param.11) | copy-start | bytes 1572868
  100.2 12.3 %collective-permute-start.18 = (f32[8,2,256]{2,1,0:T(2,128)S(1)}, f32[8,2,256]{2,1,0:T(2,128)S(1)}, u32[]{:S(2)}, u32[]{:S(2)}) collective-permute-start(f32[8,2,256]{2,1,0:T(2,128)S(1)} %convert_multiply_fusion), channel_id=1, source_target_pairs={{1,0},{2,1},{3,2},{4,3},{5,4},{6,5},{7,6},{9,8},{10,9},{11,10},{12... | collective-permute-start | bytes 49160 | tf_op jit(solution)/shard_map/ppermute | solution.py:17
  101.6 7.1 %collective-permute-start.17 = (bf16[2,8,2,256]{3,2,1,0:T(2,128)(2,1)S(1)}, bf16[2,8,2,256]{3,2,1,0:T(2,128)(2,1)S(1)}, u32[]{:S(2)}, u32[]{:S(2)}) collective-permute-start(bf16[2,8,2,256]{3,2,1,0:T(2,128)(2,1)S(1)} %pad_maximum_fusion.2), channel_id=1, source_target_pairs={{1,0},{2,1},{3,2},{4,3},{5,4},{6,5},{7,6},{9,8},{10,9},{11,10},{12... | collective-permute-start | bytes 49160 | tf_op jit(solution)/shard_map/ppermute | solution.py:17
  103.1 6.2 %collective-permute-start.14 = (bf16[128,512]{1,0:T(8,128)(2,1)S(1)}, bf16[128,512]{1,0:T(8,128)(2,1)S(1)}, u32[]{:S(2)}, u32[]{:S(2)}) collective-permute-start(bf16[128,512]{1,0:T(8,128)(2,1)S(1)} %get-tuple-element.52), channel_id=1, source_target_pairs={{0,8},{8,0},{16,24},{24,16},{1,9},{9,1},{17,25},{25,17},{2,10},{10... | collective-permute-start | bytes 393224 | tf_op jit(solution)/shard_map/ppermute | solution.py:21
  103.7 8.7 %collective-permute-start.15 = (bf16[128,512]{1,0:T(8,128)(2,1)S(1)}, bf16[128,512]{1,0:T(8,128)(2,1)S(1)}, u32[]{:S(2)}, u32[]{:S(2)}) collective-permute-start(bf16[128,512]{1,0:T(8,128)(2,1)S(1)} %get-tuple-element.53), channel_id=1, source_target_pairs={{0,16},{8,24},{16,0},{24,8},{1,17},{9,25},{17,1},{25,9},{2,18},{10... | collective-permute-start | bytes 393224 | tf_op jit(solution)/shard_map/ppermute | solution.py:21
  104.4 8.1 %collective-permute-start.16 = (bf16[128,512]{1,0:T(8,128)(2,1)S(1)}, bf16[128,512]{1,0:T(8,128)(2,1)S(1)}, u32[]{:S(2)}, u32[]{:S(2)}) collective-permute-start(bf16[128,512]{1,0:T(8,128)(2,1)S(1)} %get-tuple-element.54), channel_id=1, source_target_pairs={{0,24},{8,16},{16,8},{24,0},{1,25},{9,17},{17,9},{25,1},{2,26},{10... | collective-permute-start | bytes 393224 | tf_op jit(solution)/shard_map/ppermute | solution.py:21
  112.5 2.7 %copy-start.18 = (f32[8,2,256]{2,1,0:T(2,128)}, f32[8,2,256]{2,1,0:T(2,128)S(1)}, u32[]{:S(2)}) copy-start(f32[8,2,256]{2,1,0:T(2,128)S(1)} %collective-permute-done.18.refs_8_) | copy-start | bytes 49156
  115.2 2.0 %copy-start.12 = (f32[512,2048]{1,0:T(8,128)}, f32[512,2048]{1,0:T(8,128)S(1)}, u32[]{:S(2)}) copy-start(f32[512,2048]{1,0:T(8,128)S(1)} %fusion) | copy-start | bytes 12582916
  117.3 2.9 %collective-permute-start.19 = (bf16[4,64,2048]{2,1,0:T(8,128)(2,1)S(1)}, bf16[4,64,2048]{2,1,0:T(8,128)(2,1)}, u32[]{:S(2)}, u32[]{:S(2)}) collective-permute-start(bf16[4,64,2048]{2,1,0:T(8,128)(2,1)S(1)} %fusion.18), channel_id=1, source_target_pairs={{0,1},{1,0},{2,3},{3,2},{4,5},{5,4},{6,7},{7,6},{8,9},{9,8},{10,11... | collective-permute-start | bytes 3145736 | tf_op jit(solution)/shard_map/ppermute | solution.py:21
  128.2 12.6 %copy-start.17 = (f32[4,6144]{1,0:T(4,128)S(1)}, f32[4,6144]{1,0:T(4,128)}, u32[]{:S(2)}) copy-start(f32[4,6144]{1,0:T(4,128)} %get-tuple-element.63) | copy-start | bytes 294916
  129.9 10.3 %collective-permute-start.22 = (f32[4,6144]{1,0:T(4,128)}, f32[4,6144]{1,0:T(4,128)S(1)}, u32[]{:S(2)}, u32[]{:S(2)}) collective-permute-start(f32[4,6144]{1,0:T(4,128)} %get-tuple-element.63), channel_id=1, source_target_pairs={{0,24},{8,16},{16,8},{24,0},{1,25},{9,17},{17,9},{25,1},{2,26},{10... | collective-permute-start | bytes 294920 | tf_op jit(solution)/shard_map/ppermute | solution.py:21
  131.2 9.6 %collective-permute-start.21 = (f32[4,6144]{1,0:T(4,128)}, f32[4,6144]{1,0:T(4,128)S(1)}, u32[]{:S(2)}, u32[]{:S(2)}) collective-permute-start(f32[4,6144]{1,0:T(4,128)} %get-tuple-element.63), channel_id=1, source_target_pairs={{0,16},{8,24},{16,0},{24,8},{1,17},{9,25},{17,1},{25,9},{2,18},{10... | collective-permute-start | bytes 294920 | tf_op jit(solution)/shard_map/ppermute | solution.py:21
  133.0 7.8 %collective-permute-start.20 = (f32[4,6144]{1,0:T(4,128)}, f32[4,6144]{1,0:T(4,128)S(1)}, u32[]{:S(2)}, u32[]{:S(2)}) collective-permute-start(f32[4,6144]{1,0:T(4,128)} %get-tuple-element.63), channel_id=1, source_target_pairs={{0,8},{8,0},{16,24},{24,16},{1,9},{9,1},{17,25},{25,17},{2,10},{10... | collective-permute-start | bytes 294920 | tf_op jit(solution)/shard_map/ppermute | solution.py:21
  133.5 14.0 %collective-permute-start.26 = (bf16[64,2048]{1,0:T(8,128)(2,1)S(1)}, bf16[64,2048]{1,0:T(8,128)(2,1)S(1)}, u32[]{:S(2)}, u32[]{:S(2)}) collective-permute-start(bf16[64,2048]{1,0:T(8,128)(2,1)S(1)} %get-tuple-element.71), channel_id=1, source_target_pairs={{0,6},{1,7},{2,4},{3,5},{4,2},{5,3},{6,0},{7,1},{8,14},{9,15},{10,... | collective-permute-start | bytes 786440 | tf_op jit(solution)/shard_map/ppermute | solution.py:21
  140.2 22.1 %collective-permute-start.25 = (bf16[64,2048]{1,0:T(8,128)(2,1)S(1)}, bf16[64,2048]{1,0:T(8,128)(2,1)S(1)}, u32[]{:S(2)}, u32[]{:S(2)}) collective-permute-start(bf16[64,2048]{1,0:T(8,128)(2,1)S(1)} %get-tuple-element.72), channel_id=1, source_target_pairs={{0,4},{1,5},{2,6},{3,7},{4,0},{5,1},{6,2},{7,3},{8,12},{9,13},{10,... | collective-permute-start | bytes 786440 | tf_op jit(solution)/shard_map/ppermute | solution.py:21
  140.2 22.1 %collective-permute-start.24 = (bf16[64,2048]{1,0:T(8,128)(2,1)S(1)}, bf16[64,2048]{1,0:T(8,128)(2,1)S(1)}, u32[]{:S(2)}, u32[]{:S(2)}) collective-permute-start(bf16[64,2048]{1,0:T(8,128)(2,1)S(1)} %get-tuple-element.73), channel_id=1, source_target_pairs={{0,2},{1,3},{2,0},{3,1},{4,6},{5,7},{6,4},{7,5},{8,10},{9,11},{10,... | collective-permute-start | bytes 786440 | tf_op jit(solution)/shard_map/ppermute | solution.py:21
  140.9 1.4 collective-permute-start.23
  162.3 7.6 %collective-permute-start.29 = (f32[3,6144]{1,0:T(4,128)S(1)}, f32[3,6144]{1,0:T(4,128)S(1)}, u32[]{:S(2)}, u32[]{:S(2)}) collective-permute-start(f32[3,6144]{1,0:T(4,128)S(1)} %slice_add_fusion), channel_id=1, source_target_pairs={{0,6},{1,7},{2,4},{3,5},{4,2},{5,3},{6,0},{7,1},{8,14},{9,15},{10,... | collective-permute-start | bytes 221192 | tf_op jit(solution)/shard_map/ppermute | solution.py:21
  165.0 7.6 %collective-permute-start.28 = (f32[3,6144]{1,0:T(4,128)S(1)}, f32[3,6144]{1,0:T(4,128)S(1)}, u32[]{:S(2)}, u32[]{:S(2)}) collective-permute-start(f32[3,6144]{1,0:T(4,128)S(1)} %slice_add_fusion), channel_id=1, source_target_pairs={{0,4},{1,5},{2,6},{3,7},{4,0},{5,1},{6,2},{7,3},{8,12},{9,13},{10,... | collective-permute-start | bytes 221192 | tf_op jit(solution)/shard_map/ppermute | solution.py:21
  165.0 7.6 %collective-permute-start.27 = (f32[3,6144]{1,0:T(4,128)S(1)}, f32[3,6144]{1,0:T(4,128)S(1)}, u32[]{:S(2)}, u32[]{:S(2)}) collective-permute-start(f32[3,6144]{1,0:T(4,128)S(1)} %slice_add_fusion), channel_id=1, source_target_pairs={{0,2},{1,3},{2,0},{3,1},{4,6},{5,7},{6,4},{7,5},{8,10},{9,11},{10,... | collective-permute-start | bytes 221192 | tf_op jit(solution)/shard_map/ppermute | solution.py:21
Sparse Core Ops, SparseCore 0:
  92.7 26.1 reduce-scatter.1

commit v7 on v6

--- a/solution.py
+++ b/solution.py
@@ -113,15 +113,20 @@
 
 def gate_kernel(me_ref, me_dp_ref, query_ref, *refs):
     parts, _, blk = query_ref.shape
-    came, long_ref, pieces = refs[:parts], refs[parts], refs[parts + 1 :]
+    came, long_ref, pieces = refs[: parts // 2], refs[parts // 2], refs[parts // 2 + 1 :]
     ratio = parts // len(pieces)
+    size = blk * ratio // parts
     for k, piece in enumerate(came):
-        long_ref[me_ref[0] ^ k] = piece[...]
+        b = me_ref[0] ^ (2 * k)
+        long_ref[b] = piece[0]
+        long_ref[b ^ 1] = piece[1]
     for k, piece in enumerate(pieces):
         for i in range(ratio):
             b = (me_dp_ref[0] ^ k) * ratio + i
-            gate = query_ref[b].astype(F32) * long_ref[b].astype(F32)
-            piece[:, columns(i, blk)] = gate.astype(BF16)
+            gate = (query_ref[b].astype(F32) * long_ref[b].astype(F32)).astype(BF16)
+            for q in range(blk // size):
+                c = i * (blk // size) + q
+                piece[:, columns(c % 2 * (parts // 2) + c // 2, size)] = gate[:, columns(q, size)]
 
 
 def final_kernel(*refs):
@@ -221,18 +226,32 @@
     return [1 << i for i in range(count.bit_length() - 1) if 1 << i >= first]
 
 
-def own_share(partial, parts):
-    blocks = partial.reshape(parts // 2, 2, -1, partial.shape[-1])
+def own_share(gate_all, cot_all, parts):
     core = lax.axis_index("context") % 2
-    mine = lax.dynamic_index_in_dim(blocks, core, 1, False)
-    other = lax.dynamic_index_in_dim(blocks, 1 - core, 1, False).astype(BF16)
-    pair = (mine + swapped(other, "context", 1).astype(F32)).astype(BF16)
+    width = gate_all.shape[1] // 2
+    other = dot(lax.dynamic_slice_in_dim(gate_all, (1 - core) * width, width, 1), cot_all, 0, 0)
+    other = other.astype(BF16)
+    own_gate = ordered(lax.dynamic_slice_in_dim(gate_all, core * width, width, 1), other)
+    own = dot(own_gate, cot_all, 0, 0)
+    pair = (own + swapped(other, "context", 1).astype(F32)).astype(BF16)
+    pair = pair.reshape(parts // 2, -1, pair.shape[-1])
     row = lax.axis_index("context") // 2
     shares = [lax.dynamic_index_in_dim(pair, row, 0, False)]
     for k in range(1, parts // 2):
         sent = lax.dynamic_index_in_dim(pair, row ^ k, 0, False)
         shares.append(swapped(sent, "context", 2 * k))
     return (pair, shares)
+
+
+def summed_blocks(value, axis, dim):
+    count = lax.axis_size(axis)
+    size = value.shape[dim] // count
+    me = lax.axis_index(axis)
+    total = lax.dynamic_slice_in_dim(value, me * size, size, dim)
+    for k in range(1, count):
+        sent = lax.dynamic_slice_in_dim(value, (me ^ k) * size, size, dim).astype(BF16)
+        total = total + swapped(sent, axis, k).astype(F32)
+    return total
 
 
 def to_channels(blocks):
@@ -288,8 +307,6 @@
         grad_spec = dot(waves, ordered(grad_long, long_chan), 1, 0)
         back_sum = dot(waves, spectral_product(filter_spec, grad_spec, True), 0, 0)
         back_chan = finished(back_sum, grad_long_f)
-        late_spec = ordered(grad_spec, back_chan)
-        lag_sum = dot(spectral_product(product_spec, late_spec, True), waves, 0, 0)
     else:
         freqs = 256
 
@@ -303,19 +320,23 @@
         out_sum, back_sum, lag_sum = terms
         long_chan = finished(out_sum, product_f)
         back_chan = finished(back_sum, grad_long_f)
-    long_blocks = long_chan.reshape(parts, rows, blk)
-    long_sent = [lax.dynamic_index_in_dim(long_blocks, me ^ k, 0, False) for k in range(parts)]
-    long_came = [long_sent[0]] + [swapped(long_sent[k], "context", k) for k in range(1, parts)]
+    by_core = long_chan.reshape(parts // 2, 2, rows, blk)
+    core, row = (me % 2, me // 2)
+    mine = lax.dynamic_index_in_dim(by_core, core, 1, False)
+    near = swapped(lax.dynamic_index_in_dim(by_core, 1 - core, 1, False), "context", 1)
+    long_came = []
+    for k in range(parts // 2):
+        halves = [lax.dynamic_index_in_dim(part, row ^ k, 0, True) for part in (mine, near)]
+        both = jnp.concatenate(halves, 0)
+        long_came.append(swapped(both, "context", 2 * k) if k else both)
     back_blocks = back_chan.reshape(parts, rows, blk)
     next_heads = jnp.concatenate([back_blocks[1:, :2], jnp.zeros((1, 2, blk), BF16)], 0)
     back_sent = jnp.concatenate([back_blocks, next_heads], 1)
     grad_product = to_positions(back_sent)
-    heads = ordered(jnp.stack([keyed[:, :2], valued[:, :2]]), back_sent)
+    heads = ordered(jnp.stack([keyed[:, :2], valued[:, :2]]), grad_long_out)
     pair_after = passed_along(heads, "context", -1).astype(F32)
-    long_came = lax.optimization_barrier((*long_came, back_sent))[:parts]
-
-    grad_filter = lax.psum_scatter(lag_sum, "dp", scatter_dimension=1, tiled=True)
-    grad_filter = grad_filter * (scale_factor * inverse)
+    long_came = lax.optimization_barrier((*long_came, back_sent, pair_after))[: parts // 2]
+
     skip_sum = jnp.sum(grad_long_f * product_f, 0, keepdims=True)
 
     piece = jax.ShapeDtypeStruct((rows, chans // parts_dp), BF16)
@@ -325,10 +346,13 @@
     gates = [gates[0]] + [swapped(gates[k], "dp", k) for k in range(1, parts_dp)]
     query_heads = gate_grad[:, :2].astype(F32) * long_out[:, :2].astype(F32)
     query_after = passed_along(query_heads, "context", -1)
-    early = (grad_product, lag_sum, skip_sum, pair_after, query_after)
+    if straight:
+        late_spec = ordered(grad_spec, long_out)
+        lag_sum = dot(spectral_product(product_spec, late_spec, True), waves, 0, 0)
+    early = (grad_product, skip_sum, query_after, lag_sum)
     gate_all = ordered(jnp.concatenate(gates, 0), *early)
-    proj_sum = dot(gate_all, jnp.concatenate(cots, 0), 0, 0)
-    pair, shares = own_share(proj_sum, parts)
+    cot_all = jnp.concatenate(cots, 0)
+    pair, shares = own_share(gate_all, cot_all, parts)
     grad_product = ordered(grad_product, pair)
 
     grad_inputs, tap_sums = call(
@@ -353,7 +377,9 @@
         skip_sum,
     )
 
-    tap_sums = all_sum(ordered(tap_sums, grad_filter), "dp", bits_of(parts_dp))
+    tap_sums = all_sum(tap_sums, "dp", bits_of(parts_dp))
+    lag_sum = ordered(lag_sum, tap_sums)
+    grad_filter = summed_blocks(lag_sum, "dp", 1) * (scale_factor * inverse)
     grad_skip = tap_sums[3, :blk] * scale_factor
     tap_sums = tap_sums[:3] + swapped(tap_sums[:3], "context", 1)
     tap_sums = ordered(tap_sums, *shares[1:])

time: 181 us -> 156 us (0.86)
  between operations: 14.6 us -> 1.17 us
  waiting for transfers between devices: 41.2 us -> 28.3 us
  starting transfers between devices: 56.3 us -> 52.4 us
  local copies, waits for them, and re-layouts: 12.2 us -> 15.6 us
    ppermute x27, waiting for transfers between devices: 41.1 us -> 27.4 us  [swapped(): lax.ppermute(value, axis, [(i, i ^ mask) for i in range(lax.axis_size(axi...]
    ppermute x27, starting transfers between devices: 37.1 us -> 32 us  [swapped(): lax.ppermute(value, axis, [(i, i ^ mask) for i in range(lax.axis_size(axi...]
    unnamed x42 -> x43, local copies, waits for them, and re-layouts: 9.55 us -> 11.8 us
    convert_element_type x1 -> x0, other arithmetic: 2.21 us -> none  [own_share(): pair = (mine + swapped(other, 'context', 1).astype(F32)).astype(BF16)]
    concatenate x0 -> x4, other arithmetic: none -> 2.01 us  [body(): both = jnp.concatenate(halves, 0)]
    concatenate x0 -> x1, local copies, waits for them, and re-layouts: none -> 1.89 us  [body(): cot_all = jnp.concatenate(cots, 0)]
    dot_general x11 -> x12, matrix products: 27.9 us -> 28.5 us  [dot(): lax.dot_general(left, right, (((left_dim,), (right_dim,)), ((), ())), pre...]
  transfers between devices with their start and end apart: 34 -> 33, of which waited for: 10 -> 10; matrix products, arithmetic and copies ran while one was open for 24% -> 29% of each run, Pallas kernels for 7% -> 5%
where the time goes in v7:
time: 156 us; the launch traced here: 155 us
  starting transfers between devices  52.4 us (34%)
  matrix products  28.5 us (18%)
  waiting for transfers between devices  28.3 us (18%)
  other arithmetic  16.4 us (11%)
  local copies, waits for them, and re-layouts  15.6 us (10%)
  Pallas kernels  12.9 us (8%)
    ppermute x27, starting transfers between devices, swapped(): lax.ppermute(value, axis, [(i, i ^ mask) for i in range(lax.axis_size(axi...  32 us
    dot_general x12, matrix products, dot(): lax.dot_general(left, right, (((left_dim,), (right_dim,)), ((), ())), pre...  28.5 us
    ppermute x27, waiting for transfers between devices, swapped(): lax.ppermute(value, axis, [(i, i ^ mask) for i in range(lax.axis_size(axi...  27.4 us
    pallas_call x4, Pallas kernels, call(): pl.pallas_call(run, out_shape=outs, in_specs=[SMEM] * smem + [anywhere] *...  12.9 us
    unnamed x43, local copies, waits for them, and re-layouts  11.8 us
    all_to_all x2, starting transfers between devices, to_channels(): lax.all_to_all(blocks, 'context', split_axis=0, concat_axis=0, tiled=True)  11.6 us
    another operation x4, other arithmetic  4.78 us
    all_to_all x1, starting transfers between devices, to_positions(): lax.all_to_all(blocks, 'context', split_axis=0, concat_axis=0, tiled=True)  4.75 us
  transfers between devices with their start and end apart: 33, of which 10 were waited for; matrix products, arithmetic and copies ran while one was open for 29% of the time, Pallas kernels for 5%

profile of v7, /device:TPU:0, one launch (start us, length us, event | category | flops | bytes accessed | tf_op | source)
XLA Modules:
  0.0 155.2 jit_solution(2239839825516919498)
XLA Ops:
  0.6 3.0 %collective-permute-start.3 = (bf16[128,2048]{1,0:T(8,128)(2,1)}, bf16[128,2048]{1,0:T(8,128)(2,1)S(1)}, u32[]{:S(2)}, u32[]{:S(2)}) collective-permute-start(bf16[128,2048]{1,0:T(8,128)(2,1)} %param.11), channel_id=1, source_target_pairs={{0,16},{8,24},{16,0},{24,8},{1,17},{9,25},{17,1},{25,9},{2,18},{10... | collective-permute-start | bytes 1572872 | tf_op jit(solution)/shard_map/ppermute | solution.py:21
  3.7 1.5 collective-permute-start.1
  5.2 0.9 slice.53
  6.1 1.3 collective-permute-start
  7.5 1.1 fusion.40
  8.6 1.5 subtract_convert_fusion
  10.5 0.8 copy-done.16
  11.3 2.7 %fusion.24 = f32[2048,256]{1,0:T(8,128)} fusion(bf16[2048,1024]{1,0:T(8,128)(2,1)S(1)} %bitcast.61, f32[256,1024]{1,0:T(8,128)S(1)} %copy-done.16), kind=kOutput, calls=%fused_computation.45 | convolution fusion | flops 1074003968 | bytes 7340032 | tf_op jit(solution)/shard_map/dot_general | solution.py:180
  14.0 0.8 fusion.5.refs_2_
  14.8 0.8 constant_dynamic-update-slice_fusion.3
  16.3 3.6 %short_convs.1 = (bf16[8,128,256]{2,1,0:T(8,128)(2,1)}, bf16[8,128,256]{2,1,0:T(8,128)(2,1)}, bf16[8,128,256]{2,1,0:T(8,128)(2,1)}, bf16[8,128,256]{2,1,0:T(8,128)(2,1)}) custom-call(bf16[128,6144]{1,0:T(8,128)(2,1)} %refs_0_.3, f32[2,6144]{1,0:T(2,128)} %convert_element_type.130.refs_1_, f32[3,6144]{1,0:T(4,128)} %refs_2_.3), custom_call_target="tpu_custom_call" | custom-call | tf_op jit(solution)/shard_map/short_convs/pallas_call | solution.py:66
  19.9 6.2 %all-to-all-start = ((bf16[8,128,256]{2,1,0:T(8,128)(2,1)}), bf16[8,128,256]{2,1,0:T(8,128)(2,1)}, u32[]{:S(2)}, u32[]{:S(2)}) async-start(bf16[8,128,256]{2,1,0:T(8,128)(2,1)} %get-tuple-element.35), calls=%async_computation | async-start | bytes 1048576 | tf_op jit(solution)/shard_map/all_to_all | solution.py:258
  26.1 0.8 slice_bitcast_fusion
  26.9 1.9 %fusion.6 = bf16[128,512]{1,0:T(8,128)(2,1)S(1)} fusion(bf16[512,2048]{1,0:T(8,128)(2,1)S(1)} %copy-done, bf16[128,2048]{1,0:T(8,128)(2,1)} %collective-permute-done.1), kind=kOutput, calls=%fused_computation.17 | convolution fusion | flops 268500992 | bytes 2752512 | tf_op jit(solution)/shard_map/dot_general | solution.py:180
  28.8 1.6 %collective-permute-start.2 = (bf16[128,512]{1,0:T(8,128)(2,1)S(1)}, bf16[128,512]{1,0:T(8,128)(2,1)S(1)}, u32[]{:S(2)}, u32[]{:S(2)}) collective-permute-start(bf16[128,512]{1,0:T(8,128)(2,1)S(1)} %fusion.6), channel_id=1, source_target_pairs={{0,8},{8,0},{16,24},{24,16},{1,9},{9,1},{17,25},{25,17},{2,10},{10... | collective-permute-start | bytes 393224 | tf_op jit(solution)/shard_map/ppermute | solution.py:21
  30.4 0.8 copy-done.14
  31.2 0.8 fusion.7
  32.1 1.6 %collective-permute-start.4 = (bf16[128,512]{1,0:T(8,128)(2,1)S(1)}, bf16[128,512]{1,0:T(8,128)(2,1)S(1)}, u32[]{:S(2)}, u32[]{:S(2)}) collective-permute-start(bf16[128,512]{1,0:T(8,128)(2,1)S(1)} %fusion.7), channel_id=1, source_target_pairs={{0,16},{8,24},{16,0},{24,8},{1,17},{9,25},{17,1},{25,9},{2,18},{10... | collective-permute-start | bytes 393224 | tf_op jit(solution)/shard_map/ppermute | solution.py:21
  33.7 1.9 %fusion.8 = bf16[128,512]{1,0:T(8,128)(2,1)S(1)} fusion(bf16[512,2048]{1,0:T(8,128)(2,1)S(1)} %copy-done, bf16[128,2048]{1,0:T(8,128)(2,1)} %collective-permute-done.5), kind=kOutput, calls=%fused_computation.19 | convolution fusion | flops 268500992 | bytes 2752512 | tf_op jit(solution)/shard_map/dot_general | solution.py:180
  36.1 1.9 %constant_dynamic-update-slice_fusion.2 = bf16[512,2048]{1,0:T(8,128)(2,1)} fusion(bf16[512,2048]{1,0:T(8,128)(2,1)} %constant_dynamic-update-slice_fusion.3, bf16[128,2048]{1,0:T(8,128)(2,1)} %collective-permute-done.1), kind=kLoop, calls=%fused_computation.92 | loop fusion | bytes 1048576
  37.9 0.9 constant_dynamic-update-slice_fusion.1
  38.8 3.2 %collective-permute-done.6.refs_5_ = bf16[128,512]{1,0:T(8,128)(2,1)S(1)} collective-permute-done((bf16[128,512]{1,0:T(8,128)(2,1)S(1)}, bf16[128,512]{1,0:T(8,128)(2,1)S(1)}, u32[]{:S(2)}, u32[]{:S(2)}) %collective-permute-start.6) | collective-permute-done | bytes 131104 | tf_op jit(solution)/shard_map/ppermute | solution.py:21
  42.0 1.0 grad_long.1
  43.8 1.3 collective-permute-start.11
  45.1 5.4 %all-to-all-start.1 = ((bf16[8,128,256]{2,1,0:T(8,128)(2,1)}), bf16[8,128,256]{2,1,0:T(8,128)(2,1)}, u32[]{:S(2)}, u32[]{:S(2)}) async-start(bf16[8,128,256]{2,1,0:T(8,128)(2,1)} %copy-done.4), calls=%async_computation.1 | async-start | bytes 1048576 | tf_op jit(solution)/shard_map/all_to_all | solution.py:258
  50.4 3.8 %fusion.47 = f32[2048,256]{1,0:T(8,128)S(1)} fusion(bf16[2048,1024]{1,0:T(8,128)(2,1)} %bitcast.62, bf16[1024,256]{1,0:T(8,128)(2,1)} %bitcast.7), kind=kOutput, calls=%fused_computation.109 | convolution fusion | flops 1073741824 | bytes 6815744 | tf_op jit(solution)/shard_map/dot_general | solution.py:180
  54.6 0.9 copy-done.11
  55.6 1.6 %copy-done.8 = bf16[2,32,32,1024]{3,2,1,0:T(8,128)(2,1)S(1)} copy-done((bf16[2,32,32,1024]{3,2,1,0:T(8,128)(2,1)S(1)}, bf16[2,32,32,1024]{3,2,1,0:T(8,128)(2,1)}, u32[]{:S(2)}) %copy-start.8) | copy-done | bytes 4194328
  57.1 2.3 %fusion.4 = bf16[1024,256]{1,0:T(8,128)(2,1)S(1)} fusion(bf16[2048,1024]{1,0:T(8,128)(2,1)S(1)} %bitcast.64, bf16[1024,256]{1,0:T(8,128)(2,1)S(1)} %get-tuple-element.64, bf16[1024,256]{1,0:T(8,128)(2,1)S(1)} %get-tuple-element.63, bf16[1024,256]{1,0:T(8,128)(2,1)} %bitcast.7, f32[256]{0:T(256)S(1)} %copy-done.19), kind=kOutput, calls=%fused_computation.11 | convolution fusion | flops 1077149696 | bytes 6292480 | tf_op jit(solution)/shard_map/dot_general | solution.py:180
  60.1 1.9 %constant_dynamic-update-slice_fusion = bf16[512,2048]{1,0:T(8,128)(2,1)} fusion(bf16[512,2048]{1,0:T(8,128)(2,1)} %constant_dynamic-update-slice_fusion.1, bf16[128,2048]{1,0:T(8,128)(2,1)} %collective-permute-done.5), kind=kLoop, calls=%fused_computation.90 | loop fusion | bytes 1048576 | tf_op jit(solution)/shard_map/concatenate | solution.py:354
  63.4 1.7 %collective-permute-start.8 = (bf16[2,128,256]{2,1,0:T(8,128)(2,1)}, bf16[2,128,256]{2,1,0:T(8,128)(2,1)S(1)}, u32[]{:S(2)}, u32[]{:S(2)}) collective-permute-start(bf16[2,128,256]{2,1,0:T(8,128)(2,1)} %pad_maximum_fusion.3), channel_id=1, source_target_pairs={{0,2},{1,3},{2,0},{3,1},{4,6},{5,7},{6,4},{7,5},{8,10},{9,11},{10,... | collective-permute-start | bytes 393224 | tf_op jit(solution)/shard_map/ppermute | solution.py:21
  65.7 2.4 %collective-permute-start.9 = (bf16[2,128,256]{2,1,0:T(8,128)(2,1)}, bf16[2,128,256]{2,1,0:T(8,128)(2,1)S(1)}, u32[]{:S(2)}, u32[]{:S(2)}) collective-permute-start(bf16[2,128,256]{2,1,0:T(8,128)(2,1)} %pad_maximum_fusion.4), channel_id=1, source_target_pairs={{0,4},{1,5},{2,6},{3,7},{4,0},{5,1},{6,2},{7,3},{8,12},{9,13},{10,... | collective-permute-start | bytes 393224 | tf_op jit(solution)/shard_map/ppermute | solution.py:21
  69.1 3.8 %fusion.48 = f32[2048,256]{1,0:T(8,128)S(1)} fusion(bf16[2048,1024]{1,0:T(8,128)(2,1)} %bitcast.63, bf16[1024,256]{1,0:T(8,128)(2,1)} %bitcast.14), kind=kOutput, calls=%fused_computation.110 | convolution fusion | flops 1073741824 | bytes 6815744 | tf_op jit(solution)/shard_map/dot_general | solution.py:180
  73.3 0.9 copy-done.12
  74.2 1.6 %copy-done.9 = bf16[2,32,32,1024]{3,2,1,0:T(8,128)(2,1)S(1)} copy-done((bf16[2,32,32,1024]{3,2,1,0:T(8,128)(2,1)S(1)}, bf16[2,32,32,1024]{3,2,1,0:T(8,128)(2,1)}, u32[]{:S(2)}) %copy-start.9) | copy-done | bytes 4194328
  75.8 2.3 %fusion.3 = bf16[1024,256]{1,0:T(8,128)(2,1)S(1)} fusion(bf16[2048,1024]{1,0:T(8,128)(2,1)S(1)} %bitcast.65, bf16[1024,256]{1,0:T(8,128)(2,1)S(1)} %get-tuple-element.62, bf16[1024,256]{1,0:T(8,128)(2,1)S(1)} %get-tuple-element.61, bf16[1024,256]{1,0:T(8,128)(2,1)} %bitcast.14, f32[256]{0:T(256)S(1)} %copy-done.19), kind=kOutput, calls=%fused_computation.10 | convolution fusion | flops 1077149696 | bytes 6292480 | tf_op jit(solution)/shard_map/dot_general | solution.py:180
  78.2 0.8 fusion.20
  79.1 4.8 %all-to-all-start.2 = ((bf16[8,130,256]{2,1,0:T(8,128)(2,1)}), bf16[8,130,256]{2,1,0:T(8,128)(2,1)}, u32[]{:S(2)}, u32[]{:S(2)}) async-start(bf16[8,130,256]{2,1,0:T(8,128)(2,1)} %fusion.20), calls=%async_computation.2 | async-start | bytes 1114112 | tf_op jit(solution)/shard_map/all_to_all | solution.py:263
  83.8 2.6 %gate.1 = (bf16[8,128,256]{2,1,0:T(8,128)(2,1)S(1)}, bf16[128,512]{1,0:T(8,128)(2,1)S(1)}, bf16[128,512]{1,0:T(8,128)(2,1)S(1)}, bf16[128,512]{1,0:T(8,128)(2,1)S(1)}, bf16[128,512]{1,0:T(8,128)(2,1)S(1)}) custom-call(s32[1]{0:T(128)} %bitcast.6.refs_0_, s32[1]{0:T(128)} %bitcast.refs_0_.refs_1_, bf16[8,128,256]{2,1,0:T(8,128)(2,1)S(1)} %copy-done.1, ...), custom_call_target="tpu_custom_call" | custom-call | tf_op jit(solution)/shard_map/gate/pallas_call | solution.py:66
  87.3 1.5 collective-permute-start.15
  89.9 2.4 %collective-permute-start.14 = (bf16[128,512]{1,0:T(8,128)(2,1)S(1)}, bf16[128,512]{1,0:T(8,128)(2,1)S(1)}, u32[]{:S(2)}, u32[]{:S(2)}) collective-permute-start(bf16[128,512]{1,0:T(8,128)(2,1)S(1)} %get-tuple-element.50), channel_id=1, source_target_pairs={{0,24},{8,16},{16,8},{24,0},{1,25},{9,17},{17,9},{25,1},{2,26},{10... | collective-permute-start | bytes 393224 | tf_op jit(solution)/shard_map/ppermute | solution.py:21
  92.3 2.5 %add_convert_fusion = (bf16[1024,256]{1,0:T(8,128)(2,1)S(1)}, bf16[1024,256]{1,0:T(8,128)(2,1)S(1)}) fusion(f32[2048,256]{1,0:T(8,128)} %copy-done.12, f32[2048,256]{1,0:T(8,128)} %copy-done.11), kind=kLoop, calls=%fused_computation.33 | loop fusion | flops 2097152 | bytes 5242880 | tf_op jit(solution)/shard_map/convert.1
  94.8 2.3 %fusion.16 = f32[256,1024]{1,0:T(8,128)} fusion(bf16[2048,1024]{1,0:T(8,128)(2,1)S(1)} %bitcast.66, bf16[1024,256]{1,0:T(8,128)(2,1)S(1)} %get-tuple-element.60, bf16[1024,256]{1,0:T(8,128)(2,1)S(1)} %get-tuple-element.59), kind=kOutput, calls=%fused_computation.28 | convolution fusion | flops 1075838976 | bytes 6291456 | tf_op jit(solution)/shard_map/dot_general | solution.py:180
  97.1 2.0 %multiply_reduce_fusion = f32[256]{0:T(256)} fusion(bf16[8,128,256]{2,1,0:T(8,128)(2,1)} %all-to-all-done, bf16[8,128,256]{2,1,0:T(8,128)(2,1)} %all-to-all-done.1), kind=kLoop, calls=%fused_computation.34 | loop fusion | flops 1048320 | bytes 1049600 | tf_op jit(solution)/shard_map/reduce_sum | solution.py:340
  99.2 0.8 all-to-all-done.2.refs_5_
  100.0 3.3 %convolution_convert_fusion = bf16[256,2048]{1,0:T(8,128)(2,1)} fusion(bf16[512,2048]{1,0:T(8,128)(2,1)} %constant_dynamic-update-slice_fusion, bf16[512,512]{1,0:T(8,128)(2,1)S(1)} %pad_maximum_fusion.1, s32[]{:T(128)S(6)} %select_n.115), kind=kOutput, calls=%fused_computation.5 | convolution fusion | flops 537395200 | bytes 3407876 | tf_op jit(solution)/shard_map/dot_general | solution.py:180
  103.3 3.0 %collective-permute-done.16 = bf16[256,2048]{1,0:T(8,128)(2,1)} collective-permute-done((bf16[256,2048]{1,0:T(8,128)(2,1)}, bf16[256,2048]{1,0:T(8,128)(2,1)}, u32[]{:S(2)}, u32[]{:S(2)}) %collective-permute-start.16) | collective-permute-done | bytes 1048608 | tf_op jit(solution)/shard_map/ppermute | solution.py:21
  106.3 2.6 %fusion = bf16[256,2048]{1,0:T(8,128)(2,1)S(1)} fusion(bf16[512,256]{1,0:T(8,128)(2,1)S(1)} %constant_dynamic-slice_fusion, bf16[512,2048]{1,0:T(8,128)(2,1)} %constant_dynamic-update-slice_fusion, bf16[256,2048]{1,0:T(8,128)(2,1)} %collective-permute-done.16), kind=kOutput, calls=%fused_computation.4 | convolution fusion | flops 538443776 | bytes 4456448 | tf_op jit(solution)/shard_map/dot_general | solution.py:180
  108.9 5.7 %stream_grads.1 = (bf16[128,6144]{1,0:T(8,128)(2,1)}, f32[4,6144]{1,0:T(4,128)}) custom-call(bf16[128,6144]{1,0:T(8,128)(2,1)} %refs_0_.3, f32[2,6144]{1,0:T(2,128)} %convert_element_type.130.refs_1_, f32[3,6144]{1,0:T(4,128)} %refs_2_.3, bf16[8,128,256]{2,1,0:T(8,128)(2,1)} %copy-done.2, bf16[8,128,256]{2,1,0:T(8,128)(2,1)} %copy-done.3, ...), custom_call_target="tpu_custom_call" | custom-call | tf_op jit(solution)/shard_map/stream_grads/pallas_call | solution.py:66
  115.2 1.5 collective-permute-start.18
  116.7 1.5 collective-permute-start.17
  118.3 4.0 %collective-permute-start.23 = (bf16[64,2048]{1,0:T(8,128)(2,1)S(1)}, bf16[64,2048]{1,0:T(8,128)(2,1)S(1)}, u32[]{:S(2)}, u32[]{:S(2)}) collective-permute-start(bf16[64,2048]{1,0:T(8,128)(2,1)S(1)} %get-tuple-element.68), channel_id=1, source_target_pairs={{0,6},{1,7},{2,4},{3,5},{4,2},{5,3},{6,0},{7,1},{8,14},{9,15},{10,... | collective-permute-start | bytes 786440 | tf_op jit(solution)/shard_map/ppermute | solution.py:21
  122.3 1.2 collective-permute-start.21
  123.5 0.9 add_add_fusion
  125.8 1.2 collective-permute-start.29
  127.0 3.9 %collective-permute-done.27 = bf16[256,256]{1,0:T(8,128)(2,1)S(1)} collective-permute-done((bf16[256,256]{1,0:T(8,128)(2,1)S(1)}, bf16[256,256]{1,0:T(8,128)(2,1)S(1)}, u32[]{:S(2)}, u32[]{:S(2)}) %collective-permute-start.27) | collective-permute-done | bytes 131104 | tf_op jit(solution)/shard_map/ppermute | solution.py:21
  131.3 1.8 %collective-permute-done.29 = bf16[256,256]{1,0:T(8,128)(2,1)S(1)} collective-permute-done((bf16[256,256]{1,0:T(8,128)(2,1)S(1)}, bf16[256,256]{1,0:T(8,128)(2,1)S(1)}, u32[]{:S(2)}, u32[]{:S(2)}) %collective-permute-start.29) | collective-permute-done | bytes 131104 | tf_op jit(solution)/shard_map/ppermute | solution.py:21
  133.1 2.8 %collective-permute-done.28 = bf16[256,256]{1,0:T(8,128)(2,1)S(1)} collective-permute-done((bf16[256,256]{1,0:T(8,128)(2,1)S(1)}, bf16[256,256]{1,0:T(8,128)(2,1)S(1)}, u32[]{:S(2)}, u32[]{:S(2)}) %collective-permute-start.28) | collective-permute-done | bytes 131104 | tf_op jit(solution)/shard_map/ppermute | solution.py:21
  136.7 7.4 %collective-permute-done.22 = bf16[64,2048]{1,0:T(8,128)(2,1)S(1)} collective-permute-done((bf16[64,2048]{1,0:T(8,128)(2,1)S(1)}, bf16[64,2048]{1,0:T(8,128)(2,1)S(1)}, u32[]{:S(2)}, u32[]{:S(2)}) %collective-permute-start.22) | collective-permute-done | bytes 262176 | tf_op jit(solution)/shard_map/ppermute | solution.py:21
  144.1 2.9 %collective-permute-start.26 = (f32[3,6144]{1,0:T(4,128)S(1)}, f32[3,6144]{1,0:T(4,128)S(1)}, u32[]{:S(2)}, u32[]{:S(2)}) collective-permute-start(f32[3,6144]{1,0:T(4,128)S(1)} %slice_add_fusion), channel_id=1, source_target_pairs={{0,6},{1,7},{2,4},{3,5},{4,2},{5,3},{6,0},{7,1},{8,14},{9,15},{10,... | collective-permute-start | bytes 221192 | tf_op jit(solution)/shard_map/ppermute | solution.py:21
  147.0 1.5 collective-permute-start.24
  148.5 0.9 fusion.23
  149.4 2.2 %collective-permute-done.26 = f32[3,6144]{1,0:T(4,128)S(1)} collective-permute-done((f32[3,6144]{1,0:T(4,128)S(1)}, f32[3,6144]{1,0:T(4,128)S(1)}, u32[]{:S(2)}, u32[]{:S(2)}) %collective-permute-start.26) | collective-permute-done | bytes 73760 | tf_op jit(solution)/shard_map/ppermute | solution.py:21
  151.6 2.9 %collective-permute-done.25 = f32[3,6144]{1,0:T(4,128)S(1)} collective-permute-done((f32[3,6144]{1,0:T(4,128)S(1)}, f32[3,6144]{1,0:T(4,128)S(1)}, u32[]{:S(2)}, u32[]{:S(2)}) %collective-permute-start.25) | collective-permute-done | bytes 73760 | tf_op jit(solution)/shard_map/ppermute | solution.py:21
  (96 shorter events, 12.7 us)
Async XLA Ops:
  0.6 13.4 %copy-start = (bf16[512,2048]{1,0:T(8,128)(2,1)S(1)}, bf16[512,2048]{1,0:T(8,128)(2,1)}, u32[]{:S(2)}) copy-start(bf16[512,2048]{1,0:T(8,128)(2,1)} %param.10) | copy-start | bytes 6291460
  0.6 29.7 %collective-permute-start.3 = (bf16[128,2048]{1,0:T(8,128)(2,1)}, bf16[128,2048]{1,0:T(8,128)(2,1)S(1)}, u32[]{:S(2)}, u32[]{:S(2)}) collective-permute-start(bf16[128,2048]{1,0:T(8,128)(2,1)} %param.11), channel_id=1, source_target_pairs={{0,16},{8,24},{16,0},{24,8},{1,17},{9,25},{17,1},{25,9},{2,18},{10... | collective-permute-start | bytes 1572872 | tf_op jit(solution)/shard_map/ppermute | solution.py:21
  3.7 23.2 %collective-permute-start.1 = (bf16[128,2048]{1,0:T(8,128)(2,1)}, bf16[128,2048]{1,0:T(8,128)(2,1)}, u32[]{:S(2)}, u32[]{:S(2)}) collective-permute-start(bf16[128,2048]{1,0:T(8,128)(2,1)} %param.11), channel_id=1, source_target_pairs={{0,8},{8,0},{16,24},{24,16},{1,9},{9,1},{17,25},{25,17},{2,10},{10... | collective-permute-start | bytes 1572872 | tf_op jit(solution)/shard_map/ppermute | solution.py:21
  5.2 28.5 %collective-permute-start.5 = (bf16[128,2048]{1,0:T(8,128)(2,1)}, bf16[128,2048]{1,0:T(8,128)(2,1)}, u32[]{:S(2)}, u32[]{:S(2)}) collective-permute-start(bf16[128,2048]{1,0:T(8,128)(2,1)} %param.11), channel_id=1, source_target_pairs={{0,24},{8,16},{16,8},{24,0},{1,25},{9,17},{17,9},{25,1},{2,26},{10... | collective-permute-start | bytes 1572872 | tf_op jit(solution)/shard_map/ppermute | solution.py:21
  6.1 9.5 %collective-permute-start = (bf16[2,6144]{1,0:T(2,128)(2,1)S(1)}, bf16[2,6144]{1,0:T(2,128)(2,1)S(1)}, u32[]{:S(2)}, u32[]{:S(2)}) collective-permute-start(bf16[2,6144]{1,0:T(2,128)(2,1)S(1)} %slice.53), channel_id=1, source_target_pairs={{0,1},{1,2},{2,3},{3,4},{4,5},{5,6},{6,7},{8,9},{9,10},{10,11},{11... | collective-permute-start | bytes 73736 | tf_op jit(solution)/shard_map/ppermute | solution.py:17
  10.1 1.2 copy-start.16
  10.5 3.5 %copy-start.7 = (bf16[2,32,32,1024]{3,2,1,0:T(8,128)(2,1)}, bf16[2,32,32,1024]{3,2,1,0:T(8,128)(2,1)S(1)}, u32[]{:S(2)}) copy-start(bf16[2,32,32,1024]{3,2,1,0:T(8,128)(2,1)S(1)} %pad_maximum_fusion) | copy-start | bytes 12582916
  11.3 2.7 %copy-start.13 = (bf16[128,2048]{1,0:T(8,128)(2,1)S(1)}, bf16[128,2048]{1,0:T(8,128)(2,1)}, u32[]{:S(2)}) copy-start(bf16[128,2048]{1,0:T(8,128)(2,1)} %param.11) | copy-start | bytes 1572868
  19.9 25.2 %all-to-all-start = ((bf16[8,128,256]{2,1,0:T(8,128)(2,1)}), bf16[8,128,256]{2,1,0:T(8,128)(2,1)}, u32[]{:S(2)}, u32[]{:S(2)}) async-start(bf16[8,128,256]{2,1,0:T(8,128)(2,1)} %get-tuple-element.35), calls=%async_computation | async-start | bytes 1048576 | tf_op jit(solution)/shard_map/all_to_all | solution.py:258
  28.8 10.0 %collective-permute-start.2 = (bf16[128,512]{1,0:T(8,128)(2,1)S(1)}, bf16[128,512]{1,0:T(8,128)(2,1)S(1)}, u32[]{:S(2)}, u32[]{:S(2)}) collective-permute-start(bf16[128,512]{1,0:T(8,128)(2,1)S(1)} %fusion.6), channel_id=1, source_target_pairs={{0,8},{8,0},{16,24},{24,16},{1,9},{9,1},{17,25},{25,17},{2,10},{10... | collective-permute-start | bytes 393224 | tf_op jit(solution)/shard_map/ppermute | solution.py:21
  30.4 0.8 copy-start.14
  32.1 5.9 %copy-start.15 = (bf16[128,2048]{1,0:T(8,128)(2,1)S(1)}, bf16[128,2048]{1,0:T(8,128)(2,1)}, u32[]{:S(2)}) copy-start(bf16[128,2048]{1,0:T(8,128)(2,1)} %copy-done.14) | copy-start | bytes 1572868
  32.1 9.9 %copy-start.1 = (bf16[8,128,256]{2,1,0:T(8,128)(2,1)S(1)}, bf16[8,128,256]{2,1,0:T(8,128)(2,1)}, u32[]{:S(2)}) copy-start(bf16[8,128,256]{2,1,0:T(8,128)(2,1)} %get-tuple-element.32.refs_1_.refs_2_) | copy-start | bytes 1572868
  32.1 6.7 %collective-permute-start.4 = (bf16[128,512]{1,0:T(8,128)(2,1)S(1)}, bf16[128,512]{1,0:T(8,128)(2,1)S(1)}, u32[]{:S(2)}, u32[]{:S(2)}) collective-permute-start(bf16[128,512]{1,0:T(8,128)(2,1)S(1)} %fusion.7), channel_id=1, source_target_pairs={{0,16},{8,24},{16,0},{24,8},{1,17},{9,25},{17,1},{25,9},{2,18},{10... | collective-permute-start | bytes 393224 | tf_op jit(solution)/shard_map/ppermute | solution.py:21
  35.5 6.4 %collective-permute-start.6 = (bf16[128,512]{1,0:T(8,128)(2,1)S(1)}, bf16[128,512]{1,0:T(8,128)(2,1)S(1)}, u32[]{:S(2)}, u32[]{:S(2)}) collective-permute-start(bf16[128,512]{1,0:T(8,128)(2,1)S(1)} %fusion.8), channel_id=1, source_target_pairs={{0,24},{8,16},{16,8},{24,0},{1,25},{9,17},{17,9},{25,1},{2,26},{10... | collective-permute-start | bytes 393224 | tf_op jit(solution)/shard_map/ppermute | solution.py:21
  43.0 0.8 copy-start.4
  43.8 42.7 %copy-start.2 = (bf16[8,128,256]{2,1,0:T(8,128)(2,1)}, bf16[8,128,256]{2,1,0:T(8,128)(2,1)S(1)}, u32[]{:S(2)}) copy-start(bf16[8,128,256]{2,1,0:T(8,128)(2,1)S(1)} %get-tuple-element.34.refs_3_) | copy-start | bytes 1572868
  43.8 18.2 %collective-permute-start.11 = (bf16[2,8,2,256]{3,2,1,0:T(2,128)(2,1)S(1)}, bf16[2,8,2,256]{3,2,1,0:T(2,128)(2,1)S(1)}, u32[]{:S(2)}, u32[]{:S(2)}) collective-permute-start(bf16[2,8,2,256]{3,2,1,0:T(2,128)(2,1)S(1)} %pad_maximum_fusion.6), channel_id=1, source_target_pairs={{1,0},{2,1},{3,2},{4,3},{5,4},{6,5},{7,6},{9,8},{10,9},{11,10},{12... | collective-permute-start | bytes 49160 | tf_op jit(solution)/shard_map/ppermute | solution.py:17
  45.1 24.0 %all-to-all-start.1 = ((bf16[8,128,256]{2,1,0:T(8,128)(2,1)}), bf16[8,128,256]{2,1,0:T(8,128)(2,1)}, u32[]{:S(2)}, u32[]{:S(2)}) async-start(bf16[8,128,256]{2,1,0:T(8,128)(2,1)} %copy-done.4), calls=%async_computation.1 | async-start | bytes 1048576 | tf_op jit(solution)/shard_map/all_to_all | solution.py:258
  50.4 3.8 %copy-start.5 = (f32[2048,256]{1,0:T(8,128)S(1)}, f32[2048,256]{1,0:T(8,128)}, u32[]{:S(2)}) copy-start(f32[2048,256]{1,0:T(8,128)} %fusion.24) | copy-start | bytes 6291460
  54.2 1.4 copy-start.11
  54.2 2.9 %copy-start.8 = (bf16[2,32,32,1024]{3,2,1,0:T(8,128)(2,1)S(1)}, bf16[2,32,32,1024]{3,2,1,0:T(8,128)(2,1)}, u32[]{:S(2)}) copy-start(bf16[2,32,32,1024]{3,2,1,0:T(8,128)(2,1)} %copy-done.7) | copy-start | bytes 12582916
  54.2 2.9 %copy-start.19 = (f32[256]{0:T(256)S(1)}, f32[256]{0:T(256)}, u32[]{:S(2)}) copy-start(f32[256]{0:T(256)} %param.9) | copy-start | bytes 3076
  59.5 3.1 %collective-permute-start.7 = (bf16[4,128,256]{2,1,0:T(8,128)(2,1)S(1)}, bf16[4,128,256]{2,1,0:T(8,128)(2,1)S(1)}, u32[]{:S(2)}, u32[]{:S(2)}) collective-permute-start(bf16[4,128,256]{2,1,0:T(8,128)(2,1)S(1)} %dynamic-slice_bitcast_fusion.3), channel_id=1, source_target_pairs={{0,1},{1,0},{2,3},{3,2},{4,5},{5,4},{6,7},{7,6},{8,9},{9,8},{10,11... | collective-permute-start | bytes 786440 | tf_op jit(solution)/shard_map/ppermute | solution.py:21
  63.4 20.5 %collective-permute-start.8 = (bf16[2,128,256]{2,1,0:T(8,128)(2,1)}, bf16[2,128,256]{2,1,0:T(8,128)(2,1)S(1)}, u32[]{:S(2)}, u32[]{:S(2)}) collective-permute-start(bf16[2,128,256]{2,1,0:T(8,128)(2,1)} %pad_maximum_fusion.3), channel_id=1, source_target_pairs={{0,2},{1,3},{2,0},{3,1},{4,6},{5,7},{6,4},{7,5},{8,10},{9,11},{10,... | collective-permute-start | bytes 393224 | tf_op jit(solution)/shard_map/ppermute | solution.py:21
  65.7 18.1 %collective-permute-start.9 = (bf16[2,128,256]{2,1,0:T(8,128)(2,1)}, bf16[2,128,256]{2,1,0:T(8,128)(2,1)S(1)}, u32[]{:S(2)}, u32[]{:S(2)}) collective-permute-start(bf16[2,128,256]{2,1,0:T(8,128)(2,1)} %pad_maximum_fusion.4), channel_id=1, source_target_pairs={{0,4},{1,5},{2,6},{3,7},{4,0},{5,1},{6,2},{7,3},{8,12},{9,13},{10,... | collective-permute-start | bytes 393224 | tf_op jit(solution)/shard_map/ppermute | solution.py:21
  68.7 15.1 %collective-permute-start.10 = (bf16[2,128,256]{2,1,0:T(8,128)(2,1)}, bf16[2,128,256]{2,1,0:T(8,128)(2,1)}, u32[]{:S(2)}, u32[]{:S(2)}) collective-permute-start(bf16[2,128,256]{2,1,0:T(8,128)(2,1)} %pad_maximum_fusion.5), channel_id=1, source_target_pairs={{0,6},{1,7},{2,4},{3,5},{4,2},{5,3},{6,0},{7,1},{8,14},{9,15},{10,... | collective-permute-start | bytes 393224 | tf_op jit(solution)/shard_map/ppermute | solution.py:21
  69.1 3.8 %copy-start.6 = (f32[2048,256]{1,0:T(8,128)S(1)}, f32[2048,256]{1,0:T(8,128)}, u32[]{:S(2)}) copy-start(f32[2048,256]{1,0:T(8,128)} %fusion.24) | copy-start | bytes 6291460
  72.9 1.4 copy-start.12
  72.9 2.9 %copy-start.9 = (bf16[2,32,32,1024]{3,2,1,0:T(8,128)(2,1)S(1)}, bf16[2,32,32,1024]{3,2,1,0:T(8,128)(2,1)}, u32[]{:S(2)}) copy-start(bf16[2,32,32,1024]{3,2,1,0:T(8,128)(2,1)} %copy-done.7) | copy-start | bytes 12582916
  79.1 20.9 %all-to-all-start.2 = ((bf16[8,130,256]{2,1,0:T(8,128)(2,1)}), bf16[8,130,256]{2,1,0:T(8,128)(2,1)}, u32[]{:S(2)}, u32[]{:S(2)}) async-start(bf16[8,130,256]{2,1,0:T(8,128)(2,1)} %fusion.20), calls=%async_computation.2 | async-start | bytes 1114112 | tf_op jit(solution)/shard_map/all_to_all | solution.py:263
  86.5 0.8 copy-start.3
  87.3 11.9 %collective-permute-start.15 = (f32[8,2,256]{2,1,0:T(2,128)S(1)}, f32[8,2,256]{2,1,0:T(2,128)S(1)}, u32[]{:S(2)}, u32[]{:S(2)}) collective-permute-start(f32[8,2,256]{2,1,0:T(2,128)S(1)} %convert_multiply_fusion), channel_id=1, source_target_pairs={{1,0},{2,1},{3,2},{4,3},{5,4},{6,5},{7,6},{9,8},{10,9},{11,10},{12... | collective-permute-start | bytes 49160 | tf_op jit(solution)/shard_map/ppermute | solution.py:17
  88.8 10.3 %collective-permute-start.12 = (bf16[128,512]{1,0:T(8,128)(2,1)S(1)}, bf16[128,512]{1,0:T(8,128)(2,1)S(1)}, u32[]{:S(2)}, u32[]{:S(2)}) collective-permute-start(bf16[128,512]{1,0:T(8,128)(2,1)S(1)} %get-tuple-element.48), channel_id=1, source_target_pairs={{0,8},{8,0},{16,24},{24,16},{1,9},{9,1},{17,25},{25,17},{2,10},{10... | collective-permute-start | bytes 393224 | tf_op jit(solution)/shard_map/ppermute | solution.py:21
  89.4 9.7 %collective-permute-start.13 = (bf16[128,512]{1,0:T(8,128)(2,1)S(1)}, bf16[128,512]{1,0:T(8,128)(2,1)S(1)}, u32[]{:S(2)}, u32[]{:S(2)}) collective-permute-start(bf16[128,512]{1,0:T(8,128)(2,1)S(1)} %get-tuple-element.49), channel_id=1, source_target_pairs={{0,16},{8,24},{16,0},{24,8},{1,17},{9,25},{17,1},{25,9},{2,18},{10... | collective-permute-start | bytes 393224 | tf_op jit(solution)/shard_map/ppermute | solution.py:21
  89.9 4.9 %copy-start.10 = (bf16[2,32,32,1024]{3,2,1,0:T(8,128)(2,1)S(1)}, bf16[2,32,32,1024]{3,2,1,0:T(8,128)(2,1)}, u32[]{:S(2)}) copy-start(bf16[2,32,32,1024]{3,2,1,0:T(8,128)(2,1)} %copy-done.7) | copy-start | bytes 12582916
  89.9 9.2 %collective-permute-start.14 = (bf16[128,512]{1,0:T(8,128)(2,1)S(1)}, bf16[128,512]{1,0:T(8,128)(2,1)S(1)}, u32[]{:S(2)}, u32[]{:S(2)}) collective-permute-start(bf16[128,512]{1,0:T(8,128)(2,1)S(1)} %get-tuple-element.50), channel_id=1, source_target_pairs={{0,24},{8,16},{16,8},{24,0},{1,25},{9,17},{17,9},{25,1},{2,26},{10... | collective-permute-start | bytes 393224 | tf_op jit(solution)/shard_map/ppermute | solution.py:21
  99.1 9.7 %copy-start.18 = (f32[8,2,256]{2,1,0:T(2,128)}, f32[8,2,256]{2,1,0:T(2,128)S(1)}, u32[]{:S(2)}) copy-start(f32[8,2,256]{2,1,0:T(2,128)S(1)} %collective-permute-done.15.refs_8_) | copy-start | bytes 49156
  103.3 3.0 %collective-permute-start.16 = (bf16[256,2048]{1,0:T(8,128)(2,1)}, bf16[256,2048]{1,0:T(8,128)(2,1)}, u32[]{:S(2)}, u32[]{:S(2)}) collective-permute-start(bf16[256,2048]{1,0:T(8,128)(2,1)} %convolution_convert_fusion), channel_id=1, source_target_pairs={{0,1},{1,0},{2,3},{3,2},{4,5},{5,4},{6,7},{7,6},{8,9},{9,8},{10,11... | collective-permute-start | bytes 3145736 | tf_op jit(solution)/shard_map/ppermute | solution.py:21
  114.6 9.8 %copy-start.17 = (f32[256,1024]{1,0:T(8,128)S(1)}, f32[256,1024]{1,0:T(8,128)}, u32[]{:S(2)}) copy-start(f32[256,1024]{1,0:T(8,128)} %fusion.16) | copy-start | bytes 3145732
  114.7 7.6 %collective-permute-start.19 = (f32[4,6144]{1,0:T(4,128)}, f32[4,6144]{1,0:T(4,128)S(1)}, u32[]{:S(2)}, u32[]{:S(2)}) collective-permute-start(f32[4,6144]{1,0:T(4,128)} %get-tuple-element.56), channel_id=1, source_target_pairs={{0,24},{8,16},{16,8},{24,0},{1,25},{9,17},{17,9},{25,1},{2,26},{10... | collective-permute-start | bytes 294920 | tf_op jit(solution)/shard_map/ppermute | solution.py:21
  115.2 8.3 %collective-permute-start.18 = (f32[4,6144]{1,0:T(4,128)}, f32[4,6144]{1,0:T(4,128)S(1)}, u32[]{:S(2)}, u32[]{:S(2)}) collective-permute-start(f32[4,6144]{1,0:T(4,128)} %get-tuple-element.56), channel_id=1, source_target_pairs={{0,16},{8,24},{16,0},{24,8},{1,17},{9,25},{17,1},{25,9},{2,18},{10... | collective-permute-start | bytes 294920 | tf_op jit(solution)/shard_map/ppermute | solution.py:21
  116.7 6.7 %collective-permute-start.17 = (f32[4,6144]{1,0:T(4,128)}, f32[4,6144]{1,0:T(4,128)S(1)}, u32[]{:S(2)}, u32[]{:S(2)}) collective-permute-start(f32[4,6144]{1,0:T(4,128)} %get-tuple-element.56), channel_id=1, source_target_pairs={{0,8},{8,0},{16,24},{24,16},{1,9},{9,1},{17,25},{25,17},{2,10},{10... | collective-permute-start | bytes 294920 | tf_op jit(solution)/shard_map/ppermute | solution.py:21
  118.3 18.4 %collective-permute-start.23 = (bf16[64,2048]{1,0:T(8,128)(2,1)S(1)}, bf16[64,2048]{1,0:T(8,128)(2,1)S(1)}, u32[]{:S(2)}, u32[]{:S(2)}) collective-permute-start(bf16[64,2048]{1,0:T(8,128)(2,1)S(1)} %get-tuple-element.68), channel_id=1, source_target_pairs={{0,6},{1,7},{2,4},{3,5},{4,2},{5,3},{6,0},{7,1},{8,14},{9,15},{10,... | collective-permute-start | bytes 786440 | tf_op jit(solution)/shard_map/ppermute | solution.py:21
  122.3 21.8 %collective-permute-start.22 = (bf16[64,2048]{1,0:T(8,128)(2,1)S(1)}, bf16[64,2048]{1,0:T(8,128)(2,1)S(1)}, u32[]{:S(2)}, u32[]{:S(2)}) collective-permute-start(bf16[64,2048]{1,0:T(8,128)(2,1)S(1)} %get-tuple-element.69), channel_id=1, source_target_pairs={{0,4},{1,5},{2,6},{3,7},{4,0},{5,1},{6,2},{7,3},{8,12},{9,13},{10,... | collective-permute-start | bytes 786440 | tf_op jit(solution)/shard_map/ppermute | solution.py:21
  122.3 21.8 %collective-permute-start.21 = (bf16[64,2048]{1,0:T(8,128)(2,1)S(1)}, bf16[64,2048]{1,0:T(8,128)(2,1)S(1)}, u32[]{:S(2)}, u32[]{:S(2)}) collective-permute-start(bf16[64,2048]{1,0:T(8,128)(2,1)S(1)} %get-tuple-element.70), channel_id=1, source_target_pairs={{0,2},{1,3},{2,0},{3,1},{4,6},{5,7},{6,4},{7,5},{8,10},{9,11},{10,... | collective-permute-start | bytes 786440 | tf_op jit(solution)/shard_map/ppermute | solution.py:21
  124.4 1.4 collective-permute-start.20
  124.6 6.4 %collective-permute-start.27 = (bf16[256,256]{1,0:T(8,128)(2,1)S(1)}, bf16[256,256]{1,0:T(8,128)(2,1)S(1)}, u32[]{:S(2)}, u32[]{:S(2)}) collective-permute-start(bf16[256,256]{1,0:T(8,128)(2,1)S(1)} %get-tuple-element.65), channel_id=1, source_target_pairs={{0,8},{8,0},{16,24},{24,16},{1,9},{9,1},{17,25},{25,17},{2,10},{10... | collective-permute-start | bytes 393224 | tf_op jit(solution)/shard_map/ppermute | solution.py:21
  125.8 7.3 %collective-permute-start.29 = (bf16[256,256]{1,0:T(8,128)(2,1)S(1)}, bf16[256,256]{1,0:T(8,128)(2,1)S(1)}, u32[]{:S(2)}, u32[]{:S(2)}) collective-permute-start(bf16[256,256]{1,0:T(8,128)(2,1)S(1)} %get-tuple-element.66), channel_id=1, source_target_pairs={{0,24},{8,16},{16,8},{24,0},{1,25},{9,17},{17,9},{25,1},{2,26},{10... | collective-permute-start | bytes 393224 | tf_op jit(solution)/shard_map/ppermute | solution.py:21
  130.9 5.0 %collective-permute-start.28 = (bf16[256,256]{1,0:T(8,128)(2,1)S(1)}, bf16[256,256]{1,0:T(8,128)(2,1)S(1)}, u32[]{:S(2)}, u32[]{:S(2)}) collective-permute-start(bf16[256,256]{1,0:T(8,128)(2,1)S(1)} %get-tuple-element.67), channel_id=1, source_target_pairs={{0,16},{8,24},{16,0},{24,8},{1,17},{9,25},{17,1},{25,9},{2,18},{10... | collective-permute-start | bytes 393224 | tf_op jit(solution)/shard_map/ppermute | solution.py:21
  144.1 7.5 %collective-permute-start.26 = (f32[3,6144]{1,0:T(4,128)S(1)}, f32[3,6144]{1,0:T(4,128)S(1)}, u32[]{:S(2)}, u32[]{:S(2)}) collective-permute-start(f32[3,6144]{1,0:T(4,128)S(1)} %slice_add_fusion), channel_id=1, source_target_pairs={{0,6},{1,7},{2,4},{3,5},{4,2},{5,3},{6,0},{7,1},{8,14},{9,15},{10,... | collective-permute-start | bytes 221192 | tf_op jit(solution)/shard_map/ppermute | solution.py:21
  147.0 7.6 %collective-permute-start.25 = (f32[3,6144]{1,0:T(4,128)S(1)}, f32[3,6144]{1,0:T(4,128)S(1)}, u32[]{:S(2)}, u32[]{:S(2)}) collective-permute-start(f32[3,6144]{1,0:T(4,128)S(1)} %slice_add_fusion), channel_id=1, source_target_pairs={{0,4},{1,5},{2,6},{3,7},{4,0},{5,1},{6,2},{7,3},{8,12},{9,13},{10,... | collective-permute-start | bytes 221192 | tf_op jit(solution)/shard_map/ppermute | solution.py:21
  147.0 7.6 %collective-permute-start.24 = (f32[3,6144]{1,0:T(4,128)S(1)}, f32[3,6144]{1,0:T(4,128)S(1)}, u32[]{:S(2)}, u32[]{:S(2)}) collective-permute-start(f32[3,6144]{1,0:T(4,128)S(1)} %slice_add_fusion), channel_id=1, source_target_pairs={{0,2},{1,3},{2,0},{3,1},{4,6},{5,7},{6,4},{7,5},{8,10},{9,11},{10,... | collective-permute-start | bytes 221192 | tf_op jit(solution)/shard_map/ppermute | solution.py:21

commit v8 on v7

--- a/solution.py
+++ b/solution.py
@@ -2,6 +2,7 @@
 
 import jax
 import jax.numpy as jnp
+import numpy as np
 from jax import lax
 from jax.experimental import pallas as pl
 from jax.experimental.pallas import tpu as pltpu
@@ -176,6 +177,12 @@
     return both.astype(BF16).reshape(2 * freqs, seq_len)
 
 
+def constant_table(seq_len):
+    odd = 2 * np.arange(seq_len)[:, None] + 1
+    angles = odd * np.arange(seq_len)[None, :] % (4 * seq_len) * (math.pi / (2 * seq_len))
+    return np.stack([np.cos(angles), -np.sin(angles)]).astype(np.float32).astype(BF16)
+
+
 def dot(left, right, left_dim, right_dim):
     return lax.dot_general(
         left, right, (((left_dim,), (right_dim,)), ((), ())), preferred_element_type=F32
@@ -193,6 +200,91 @@
         real = left_re * right_re - left_im * right_im
         imag = left_re * right_im + left_im * right_re
     return jnp.concatenate([real, imag], 0).astype(BF16)
+
+
+def filter_kernel(waves_ref, filter_ref, spec_ref):
+    for i in range(2):
+        spec_ref[i] = dot(filter_ref[...], waves_ref[i], 1, 1)
+
+
+def out_kernel(waves_ref, filter_spec_ref, product_ref, skip_ref, spec_ref, long_ref, turned, total):
+    step = pl.program_id(0)
+
+    @pl.when(step == 0)
+    def _():
+        turned[...] = product_ref[...].astype(F32).T.astype(BF16)
+        total[...] = jnp.zeros_like(total)
+
+    spec_re, spec_im = (dot(turned[...], waves_ref[i], 1, 1) for i in range(2))
+    spec_ref[0], spec_ref[1] = (spec_re, spec_im)
+    filter_re, filter_im = (filter_spec_ref[0], filter_spec_ref[1])
+    real = (filter_re * spec_re - filter_im * spec_im).astype(BF16)
+    imag = (filter_re * spec_im + filter_im * spec_re).astype(BF16)
+    total[...] += dot(real, waves_ref[0], 1, 0) + dot(imag, waves_ref[1], 1, 0)
+
+    @pl.when(step == pl.num_programs(0) - 1)
+    def _():
+        inverse = 1.0 / total.shape[1]
+        direct = skip_ref[...] * product_ref[...].astype(F32)
+        long_ref[...] = (total[...].T * inverse + direct).astype(BF16)
+
+
+def back_kernel(
+    waves_ref, filter_spec_ref, spec_ref, grad_ref, product_ref, skip_ref,
+    back_ref, lag_ref, sum_ref, turned, total,
+):
+    step = pl.program_id(0)
+
+    @pl.when(step == 0)
+    def _():
+        turned[...] = grad_ref[...].astype(F32).T.astype(BF16)
+        total[...] = jnp.zeros_like(total)
+        lag_ref[...] = jnp.zeros_like(lag_ref)
+
+    grad_re, grad_im = (dot(turned[...], waves_ref[i], 1, 1) for i in range(2))
+    for ref, sums in ((filter_spec_ref, total), (spec_ref, lag_ref)):
+        left_re, left_im = (ref[0], ref[1])
+        real = (left_re * grad_re + left_im * grad_im).astype(BF16)
+        imag = (left_re * grad_im - left_im * grad_re).astype(BF16)
+        sums[...] += dot(real, waves_ref[0], 1, 0) + dot(imag, waves_ref[1], 1, 0)
+
+    @pl.when(step == pl.num_programs(0) - 1)
+    def _():
+        inverse = 1.0 / total.shape[1]
+        parts, rows = (back_ref.shape[0], back_ref.shape[1] - 2)
+        grad = grad_ref[...].astype(F32)
+        back = (total[...].T * inverse + skip_ref[...] * grad).astype(BF16)
+        for b in range(parts):
+            back_ref[b, 0:rows] = back[b * rows : (b + 1) * rows]
+            if b < parts - 1:
+                back_ref[b, rows : rows + 2] = back[(b + 1) * rows : (b + 1) * rows + 2]
+            else:
+                back_ref[b, rows : rows + 2] = jnp.zeros((2, back.shape[1]), BF16)
+        sum_ref[...] = jnp.sum(grad * product_ref[...].astype(F32), 0, keepdims=True)
+
+
+def chunked(kernel, name, waves, specs, planes, outs, spec_out, scratch):
+    freqs, seq_len = waves.shape[1:]
+    size = min(256, freqs)
+    blk = (specs + spec_out)[0].shape[1]
+    chunk = pl.BlockSpec((2, blk, size), lambda i: (0, 0, i))
+
+    def whole(array):
+        return pl.BlockSpec(array.shape, lambda i: (0,) * len(array.shape))
+
+    return pl.pallas_call(
+        kernel,
+        out_shape=spec_out + outs,
+        grid=(freqs // size,),
+        in_specs=[pl.BlockSpec((2, size, seq_len), lambda i: (0, i, 0))]
+        + [chunk] * len(specs)
+        + [whole(a) for a in planes],
+        out_specs=[chunk] * len(spec_out) + [whole(a) for a in outs],
+        scratch_shapes=scratch,
+        compiler_params=pltpu.CompilerParams(vmem_limit_bytes=60 * 2**20),
+        cost_estimate=pl.CostEstimate(flops=0, transcendentals=0, bytes_accessed=0),
+        name=name,
+    )(waves, *specs, *planes)
 
 
 def ordered(value, *first):
@@ -286,8 +378,13 @@
     straight = seq_len <= 1024
     weights = out_proj
     if straight:
-        waves = table(0, seq_len, seq_len)
-        filter_spec = dot(waves, filter_b, 1, 1)
+        waves = jnp.asarray(constant_table(seq_len))
+        spec = jax.ShapeDtypeStruct((2, blk, seq_len), F32)
+        scratch = [pltpu.VMEM((blk, seq_len), BF16), pltpu.VMEM((blk, seq_len), F32)]
+        skip_row = skip_gain[None, :]
+        (filter_spec,) = chunked(
+            filter_kernel, "filter_spectrum", waves, [], [filter_b], [], [spec], []
+        )
         weights = ordered(out_proj, filter_spec)
     found = [dot(cot, weights, 1, 1).astype(BF16) for cot in cots]
     found = [found[0]] + [swapped(found[k], "dp", k) for k in range(1, parts_dp)]
@@ -300,13 +397,45 @@
     def finished(total, direct):
         return (total * inverse + skip_gain[None, :] * direct).astype(BF16)
 
+    def crossed(values):
+        by_core = values.reshape(parts // 2, 2, rows, blk)
+        core, row = (me % 2, me // 2)
+        mine = lax.dynamic_index_in_dim(by_core, core, 1, False)
+        near = swapped(lax.dynamic_index_in_dim(by_core, 1 - core, 1, False), "context", 1)
+        stacked = jnp.stack([mine, near], 1)
+        came = [lax.dynamic_index_in_dim(stacked, row, 0, False)]
+        for k in range(1, parts // 2):
+            sent = lax.dynamic_index_in_dim(stacked, row ^ k, 0, False)
+            came.append(swapped(sent, "context", 2 * k))
+        return came
+
     if straight:
-        product_spec = dot(waves, ordered(product, grad_long_out), 1, 0)
-        out_sum = dot(waves, spectral_product(filter_spec, product_spec, False), 0, 0)
-        long_chan = finished(out_sum, product_f)
-        grad_spec = dot(waves, ordered(grad_long, long_chan), 1, 0)
-        back_sum = dot(waves, spectral_product(filter_spec, grad_spec, True), 0, 0)
-        back_chan = finished(back_sum, grad_long_f)
+        late_product = ordered(product, grad_long_out)
+        product_spec, long_chan = chunked(
+            out_kernel,
+            "long_out",
+            waves,
+            [filter_spec],
+            [late_product, skip_row],
+            [jax.ShapeDtypeStruct((seq_len, blk), BF16)],
+            [spec],
+            scratch,
+        )
+        long_came = crossed(long_chan)
+        back_sent, lag_sum, skip_sum = chunked(
+            back_kernel,
+            "grad_product",
+            waves,
+            [filter_spec, product_spec],
+            [ordered(grad_long, *long_came[1:]), product, skip_row],
+            [
+                jax.ShapeDtypeStruct((parts, rows + 2, blk), BF16),
+                jax.ShapeDtypeStruct((blk, seq_len), F32),
+                jax.ShapeDtypeStruct((1, blk), F32),
+            ],
+            [],
+            scratch,
+        )
     else:
         freqs = 256
 
@@ -318,27 +447,16 @@
         start = (zero, zero, jnp.zeros((blk, seq_len), F32))
         terms, _ = lax.scan(step, start, jnp.arange(0, seq_len, freqs))
         out_sum, back_sum, lag_sum = terms
-        long_chan = finished(out_sum, product_f)
-        back_chan = finished(back_sum, grad_long_f)
-    by_core = long_chan.reshape(parts // 2, 2, rows, blk)
-    core, row = (me % 2, me // 2)
-    mine = lax.dynamic_index_in_dim(by_core, core, 1, False)
-    near = swapped(lax.dynamic_index_in_dim(by_core, 1 - core, 1, False), "context", 1)
-    long_came = []
-    for k in range(parts // 2):
-        halves = [lax.dynamic_index_in_dim(part, row ^ k, 0, True) for part in (mine, near)]
-        both = jnp.concatenate(halves, 0)
-        long_came.append(swapped(both, "context", 2 * k) if k else both)
-    back_blocks = back_chan.reshape(parts, rows, blk)
-    next_heads = jnp.concatenate([back_blocks[1:, :2], jnp.zeros((1, 2, blk), BF16)], 0)
-    back_sent = jnp.concatenate([back_blocks, next_heads], 1)
+        long_came = crossed(finished(out_sum, product_f))
+        back_blocks = finished(back_sum, grad_long_f).reshape(parts, rows, blk)
+        next_heads = jnp.concatenate([back_blocks[1:, :2], jnp.zeros((1, 2, blk), BF16)], 0)
+        back_sent = jnp.concatenate([back_blocks, next_heads], 1)
+        skip_sum = jnp.sum(grad_long_f * product_f, 0, keepdims=True)
     grad_product = to_positions(back_sent)
     heads = ordered(jnp.stack([keyed[:, :2], valued[:, :2]]), grad_long_out)
     pair_after = passed_along(heads, "context", -1).astype(F32)
     long_came = lax.optimization_barrier((*long_came, back_sent, pair_after))[: parts // 2]
 
-    skip_sum = jnp.sum(grad_long_f * product_f, 0, keepdims=True)
-
     piece = jax.ShapeDtypeStruct((rows, chans // parts_dp), BF16)
     long_out, *gates = call(
         gate_kernel, "gate", [plane] + [piece] * parts_dp, 2, 12, me[None], me_dp, query, *long_came
@@ -346,10 +464,7 @@
     gates = [gates[0]] + [swapped(gates[k], "dp", k) for k in range(1, parts_dp)]
     query_heads = gate_grad[:, :2].astype(F32) * long_out[:, :2].astype(F32)
     query_after = passed_along(query_heads, "context", -1)
-    if straight:
-        late_spec = ordered(grad_spec, long_out)
-        lag_sum = dot(spectral_product(product_spec, late_spec, True), waves, 0, 0)
-    early = (grad_product, skip_sum, query_after, lag_sum)
+    early = (grad_product, query_after)
     gate_all = ordered(jnp.concatenate(gates, 0), *early)
     cot_all = jnp.concatenate(cots, 0)
     pair, shares = own_share(gate_all, cot_all, parts)

time: 156 us -> 171 us (1.096)
  Pallas kernels: 12.9 us -> 33.6 us
  matrix products: 28.5 us -> 12.3 us
  waiting for transfers between devices: 28.3 us -> 39.8 us
  other arithmetic: 16.4 us -> 8.33 us
  starting transfers between devices: 52.4 us -> 60.2 us
    pallas_call x0 -> x3, Pallas kernels: none -> 21.4 us  [chunked(): pl.pallas_call(kernel, out_shape=spec_out + outs, grid=(freqs // size,),...]
    dot_general x12 -> x6, matrix products: 28.5 us -> 12.3 us  [dot(): lax.dot_general(left, right, (((left_dim,), (right_dim,)), ((), ())), pre...]
    ppermute x27, waiting for transfers between devices: 27.4 us -> 39.8 us  [swapped(): lax.ppermute(value, axis, [(i, i ^ mask) for i in range(lax.axis_size(axi...]
    ppermute x27, starting transfers between devices: 32 us -> 41.1 us  [swapped(): lax.ppermute(value, axis, [(i, i ^ mask) for i in range(lax.axis_size(axi...]
    another operation x5 -> x0, other arithmetic: 5.17 us -> none
    unnamed x43 -> x31, local copies, waits for them, and re-layouts: 11.8 us -> 8.76 us
    concatenate x5 -> x0, other arithmetic: 2.86 us -> none  [the longest x4 2.01 us: body(): both = jnp.concatenate(halves, 0)]
    convert_element_type x0 -> x1, other arithmetic: none -> 2.09 us  [body(): filter_b = long_filter.astype(BF16)]
  transfers between devices with their start and end apart: 33 -> 33, of which waited for: 10 -> 16; matrix products, arithmetic and copies ran while one was open for 29% -> 15% of each run, Pallas kernels for 5% -> 11%
where the time goes in v8:
time: 171 us; the launch traced here: 169 us
  starting transfers between devices  60.2 us (35%)
  waiting for transfers between devices  39.8 us (23%)
  Pallas kernels  33.6 us (20%)
  local copies, waits for them, and re-layouts  14.3 us (8%)
  matrix products  12.3 us (7%)
  other arithmetic  8.33 us (5%)
    ppermute x27, starting transfers between devices, swapped(): lax.ppermute(value, axis, [(i, i ^ mask) for i in range(lax.axis_size(axi...  41.1 us
    ppermute x27, waiting for transfers between devices, swapped(): lax.ppermute(value, axis, [(i, i ^ mask) for i in range(lax.axis_size(axi...  39.8 us
    pallas_call x3, Pallas kernels, chunked(): pl.pallas_call(kernel, out_shape=spec_out + outs, grid=(freqs // size,),...  21.4 us
    dot_general x6, matrix products, dot(): lax.dot_general(left, right, (((left_dim,), (right_dim,)), ((), ())), pre...  12.3 us
    pallas_call x4, Pallas kernels, call(): pl.pallas_call(run, out_shape=outs, in_specs=[SMEM] * smem + [anywhere] *...  12.2 us
    all_to_all x2, starting transfers between devices, to_channels(): lax.all_to_all(blocks, 'context', split_axis=0, concat_axis=0, tiled=True)  10.4 us
    unnamed x31, local copies, waits for them, and re-layouts  8.76 us
    all_to_all x1, starting transfers between devices, to_positions(): lax.all_to_all(blocks, 'context', split_axis=0, concat_axis=0, tiled=True)  4.67 us
  transfers between devices with their start and end apart: 33, of which 16 were waited for; matrix products, arithmetic and copies ran while one was open for 15% of the time, Pallas kernels for 11%

profile of v8, /device:TPU:0, one launch (start us, length us, event | category | flops | bytes accessed | tf_op | source)
XLA Modules:
  0.0 169.4 jit_solution(7634364971290384096)
XLA Ops:
  0.6 3.0 %collective-permute-start.1 = (bf16[128,2048]{1,0:T(8,128)(2,1)}, bf16[128,2048]{1,0:T(8,128)(2,1)S(1)}, u32[]{:S(2)}, u32[]{:S(2)}) collective-permute-start(bf16[128,2048]{1,0:T(8,128)(2,1)} %param.12), channel_id=1, source_target_pairs={{0,8},{8,0},{16,24},{24,16},{1,9},{9,1},{17,25},{25,17},{2,10},{10... | collective-permute-start | bytes 1572872 | tf_op jit(solution)/shard_map/ppermute | solution.py:22
  3.6 1.5 collective-permute-start.3
  5.2 0.9 slice.22
  6.1 1.3 collective-permute-start
  7.8 2.1 %convert_element_type.81.filter_ref = bf16[256,1024]{1,0:T(8,128)(2,1)} convert(f32[256,1024]{1,0:T(8,128)} %param.9) | non-fusion elementwise | flops 262144 | bytes 1572864 | tf_op jit(solution)/shard_map/convert_element_type | solution.py:376
  9.9 5.3 %filter_spectrum.1.filter_spec_ref = f32[2,256,1024]{2,1,0:T(8,128)} custom-call(bf16[2,1024,1024]{2,1,0:T(8,128)(2,1)} %constant.82.clone.waves_ref, bf16[256,1024]{1,0:T(8,128)(2,1)} %convert_element_type.81.filter_ref), custom_call_target="tpu_custom_call" | custom-call | tf_op jit(solution)/shard_map/filter_spectrum/pallas_call | solution.py:275
  15.8 3.6 %short_convs.1 = (bf16[8,128,256]{2,1,0:T(8,128)(2,1)}, bf16[8,128,256]{2,1,0:T(8,128)(2,1)}, bf16[8,128,256]{2,1,0:T(8,128)(2,1)}, bf16[8,128,256]{2,1,0:T(8,128)(2,1)}) custom-call(bf16[128,6144]{1,0:T(8,128)(2,1)} %refs_0_.3, f32[2,6144]{1,0:T(2,128)} %convert_element_type.80.refs_1_, f32[3,6144]{1,0:T(4,128)} %refs_2_.3), custom_call_target="tpu_custom_call" | custom-call | tf_op jit(solution)/shard_map/short_convs/pallas_call | solution.py:67
  19.4 5.6 %all-to-all-start = ((bf16[8,128,256]{2,1,0:T(8,128)(2,1)}), bf16[8,128,256]{2,1,0:T(8,128)(2,1)}, u32[]{:S(2)}, u32[]{:S(2)}) async-start(bf16[8,128,256]{2,1,0:T(8,128)(2,1)} %get-tuple-element.39), calls=%async_computation | async-start | bytes 1048576 | tf_op jit(solution)/shard_map/all_to_all | solution.py:350
  25.1 1.5 fusion.2
  26.6 1.5 collective-permute-start.2
  28.5 1.5 fusion.3
  30.0 1.5 collective-permute-start.4
  31.5 2.5 %fusion.4 = bf16[128,512]{1,0:T(8,128)(2,1)} fusion(bf16[512,2048]{1,0:T(8,128)(2,1)S(1)} %copy-done, bf16[128,2048]{1,0:T(8,128)(2,1)} %collective-permute-done.5), kind=kOutput, calls=%fused_computation.10 | convolution fusion | flops 268500992 | bytes 2752512 | tf_op jit(solution)/shard_map/dot_general | solution.py:187
  34.2 0.8 fusion.1.refs_2_
  35.5 4.7 %collective-permute-done.6.refs_5_ = bf16[128,512]{1,0:T(8,128)(2,1)S(1)} collective-permute-done((bf16[128,512]{1,0:T(8,128)(2,1)}, bf16[128,512]{1,0:T(8,128)(2,1)S(1)}, u32[]{:S(2)}, u32[]{:S(2)}) %collective-permute-start.6) | collective-permute-done | bytes 131104 | tf_op jit(solution)/shard_map/ppermute | solution.py:22
  40.9 0.9 copy-done.8
  41.8 1.0 grad_long.1
  42.8 0.8 copy-done.4
  43.6 4.8 %all-to-all-start.1 = ((bf16[8,128,256]{2,1,0:T(8,128)(2,1)}), bf16[8,128,256]{2,1,0:T(8,128)(2,1)}, u32[]{:S(2)}, u32[]{:S(2)}) async-start(bf16[8,128,256]{2,1,0:T(8,128)(2,1)} %copy-done.4), calls=%async_computation.1 | async-start | bytes 1048576 | tf_op jit(solution)/shard_map/all_to_all | solution.py:350
  48.4 7.4 %long_out.1 = (f32[2,256,1024]{2,1,0:T(8,128)}, bf16[1024,256]{1,0:T(8,128)(2,1)}) custom-call(bf16[2,1024,1024]{2,1,0:T(8,128)(2,1)} %constant.82.clone.waves_ref, f32[2,256,1024]{2,1,0:T(8,128)} %filter_spectrum.1.filter_spec_ref, bf16[1024,256]{1,0:T(8,128)(2,1)} %bitcast.6.product_ref, f32[1,256]{1,0:T(1,128)} %bitcast.56), custom_call_target="tpu_custom_call" | custom-call | tf_op jit(solution)/shard_map/long_out/pallas_call | solution.py:275
  55.7 1.8 %dynamic-slice_bitcast_fusion.3 = (bf16[4,128,256]{2,1,0:T(8,128)(2,1)}, bf16[4,1,128,256]{3,2,1,0:T(8,128)(2,1)S(1)}) fusion(bf16[4,2,128,256]{3,2,1,0:T(8,128)(2,1)} %bitcast.54, s32[]{:T(128)S(6)} %select_n.59, s32[]{:T(128)S(6)} %select_n.58), kind=kLoop, calls=%fused_computation.32 | loop fusion | bytes 1048584 | tf_op jit(solution)/shard_map/jit(dynamic_index_in_dim)/squeeze | solution.py:404
  58.0 1.9 %constant_dynamic-update-slice_fusion.3 = bf16[512,2048]{1,0:T(8,128)(2,1)} fusion(bf16[128,2048]{1,0:T(8,128)(2,1)} %param.12), kind=kLoop, calls=%fused_computation.48 | loop fusion | bytes 1048576
  59.9 1.0 fusion.10
  60.9 1.7 %collective-permute-start.8 = (bf16[2,128,256]{2,1,0:T(8,128)(2,1)S(1)}, bf16[2,128,256]{2,1,0:T(8,128)(2,1)S(1)}, u32[]{:S(2)}, u32[]{:S(2)}) collective-permute-start(bf16[2,128,256]{2,1,0:T(8,128)(2,1)S(1)} %get-tuple-element.75), channel_id=1, source_target_pairs={{0,2},{1,3},{2,0},{3,1},{4,6},{5,7},{6,4},{7,5},{8,10},{9,11},{10,... | collective-permute-start | bytes 393224 | tf_op jit(solution)/shard_map/ppermute | solution.py:22
  62.6 2.4 %collective-permute-start.9 = (bf16[2,128,256]{2,1,0:T(8,128)(2,1)S(1)}, bf16[2,128,256]{2,1,0:T(8,128)(2,1)S(1)}, u32[]{:S(2)}, u32[]{:S(2)}) collective-permute-start(bf16[2,128,256]{2,1,0:T(8,128)(2,1)S(1)} %get-tuple-element.76), channel_id=1, source_target_pairs={{0,4},{1,5},{2,6},{3,7},{4,0},{5,1},{6,2},{7,3},{8,12},{9,13},{10,... | collective-permute-start | bytes 393224 | tf_op jit(solution)/shard_map/ppermute | solution.py:22
  65.3 0.8 slice_bitcast_fusion
  66.2 2.5 %collective-permute-done.8.refs_4_ = bf16[2,128,256]{2,1,0:T(8,128)(2,1)S(1)} collective-permute-done((bf16[2,128,256]{2,1,0:T(8,128)(2,1)S(1)}, bf16[2,128,256]{2,1,0:T(8,128)(2,1)S(1)}, u32[]{:S(2)}, u32[]{:S(2)}) %collective-permute-start.8) | collective-permute-done | bytes 131104 | tf_op jit(solution)/shard_map/ppermute | solution.py:22
  68.7 6.8 %collective-permute-done.9.refs_5_ = bf16[2,128,256]{2,1,0:T(8,128)(2,1)S(1)} collective-permute-done((bf16[2,128,256]{2,1,0:T(8,128)(2,1)S(1)}, bf16[2,128,256]{2,1,0:T(8,128)(2,1)S(1)}, u32[]{:S(2)}, u32[]{:S(2)}) %collective-permute-start.9) | collective-permute-done | bytes 131104 | tf_op jit(solution)/shard_map/ppermute | solution.py:22
  75.5 0.7 copy-done.5
  76.2 8.8 %grad_product.1 = (bf16[8,130,256]{2,1,0:T(8,128)(2,1)}, f32[256,1024]{1,0:T(8,128)}, f32[1,256]{1,0:T(1,128)}) custom-call(bf16[2,1024,1024]{2,1,0:T(8,128)(2,1)} %constant.82.clone.waves_ref, f32[2,256,1024]{2,1,0:T(8,128)} %filter_spectrum.1.filter_spec_ref, f32[2,256,1024]{2,1,0:T(8,128)} %get-tuple-element.43.spec_ref, ...), custom_call_target="tpu_custom_call" | custom-call | tf_op jit(solution)/shard_map/grad_product/pallas_call | solution.py:275
  85.0 4.7 %all-to-all-start.2 = ((bf16[8,130,256]{2,1,0:T(8,128)(2,1)}), bf16[8,130,256]{2,1,0:T(8,128)(2,1)}, u32[]{:S(2)}, u32[]{:S(2)}) async-start(bf16[8,130,256]{2,1,0:T(8,128)(2,1)} %get-tuple-element.45), calls=%async_computation.2 | async-start | bytes 1114112 | tf_op jit(solution)/shard_map/all_to_all | solution.py:355
  89.6 1.9 %constant_dynamic-update-slice_fusion.2 = bf16[512,2048]{1,0:T(8,128)(2,1)} fusion(bf16[512,2048]{1,0:T(8,128)(2,1)} %constant_dynamic-update-slice_fusion.3, bf16[128,2048]{1,0:T(8,128)(2,1)} %copy-done.10), kind=kLoop, calls=%fused_computation.47 | loop fusion | bytes 1048576
  91.6 1.9 %constant_dynamic-update-slice_fusion.1 = bf16[512,2048]{1,0:T(8,128)(2,1)} fusion(bf16[512,2048]{1,0:T(8,128)(2,1)} %constant_dynamic-update-slice_fusion.2, bf16[128,2048]{1,0:T(8,128)(2,1)} %copy-done.11), kind=kLoop, calls=%fused_computation.46 | loop fusion | bytes 1048576
  93.4 1.3 collective-permute-start.11
  94.7 1.9 %constant_dynamic-update-slice_fusion = bf16[512,2048]{1,0:T(8,128)(2,1)} fusion(bf16[512,2048]{1,0:T(8,128)(2,1)} %constant_dynamic-update-slice_fusion.1, bf16[128,2048]{1,0:T(8,128)(2,1)} %collective-permute-done.5), kind=kLoop, calls=%fused_computation.45 | loop fusion | bytes 1048576 | tf_op jit(solution)/shard_map/concatenate | solution.py:469
  97.3 1.9 %gate.1 = (bf16[8,128,256]{2,1,0:T(8,128)(2,1)S(1)}, bf16[128,512]{1,0:T(8,128)(2,1)S(1)}, bf16[128,512]{1,0:T(8,128)(2,1)S(1)}, bf16[128,512]{1,0:T(8,128)(2,1)S(1)}, bf16[128,512]{1,0:T(8,128)(2,1)S(1)}) custom-call(s32[1]{0:T(128)} %bitcast.5.refs_0_, s32[1]{0:T(128)} %bitcast.refs_0_.refs_1_, bf16[8,128,256]{2,1,0:T(8,128)(2,1)S(1)} %copy-done.1, ...), custom_call_target="tpu_custom_call" | custom-call | tf_op jit(solution)/shard_map/gate/pallas_call | solution.py:67
  99.5 1.7 collective-permute-start.13
  101.2 1.5 collective-permute-start.12
  102.8 1.5 collective-permute-start.15
  104.2 1.0 collective-permute-done.14
  105.2 2.8 %collective-permute-done.13 = bf16[128,512]{1,0:T(8,128)(2,1)S(1)} collective-permute-done((bf16[128,512]{1,0:T(8,128)(2,1)S(1)}, bf16[128,512]{1,0:T(8,128)(2,1)S(1)}, u32[]{:S(2)}, u32[]{:S(2)}) %collective-permute-start.13) | collective-permute-done | bytes 131104 | tf_op jit(solution)/shard_map/ppermute | solution.py:22
  108.1 3.3 %convolution_convert_fusion = bf16[256,2048]{1,0:T(8,128)(2,1)} fusion(bf16[512,2048]{1,0:T(8,128)(2,1)} %constant_dynamic-update-slice_fusion, bf16[512,512]{1,0:T(8,128)(2,1)S(1)} %pad_maximum_fusion, s32[]{:T(128)S(6)} %select_n.66), kind=kOutput, calls=%fused_computation.2 | convolution fusion | flops 537395200 | bytes 3407876 | tf_op jit(solution)/shard_map/dot_general | solution.py:187
  111.4 1.2 collective-permute-start.16
  112.6 2.6 %collective-permute-done.16 = bf16[256,2048]{1,0:T(8,128)(2,1)} collective-permute-done((bf16[256,2048]{1,0:T(8,128)(2,1)}, bf16[256,2048]{1,0:T(8,128)(2,1)}, u32[]{:S(2)}, u32[]{:S(2)}) %collective-permute-start.16) | collective-permute-done | bytes 1048608 | tf_op jit(solution)/shard_map/ppermute | solution.py:22
  115.3 2.6 %fusion = bf16[256,2048]{1,0:T(8,128)(2,1)S(1)} fusion(bf16[512,256]{1,0:T(8,128)(2,1)S(1)} %constant_dynamic-slice_fusion, bf16[512,2048]{1,0:T(8,128)(2,1)} %constant_dynamic-update-slice_fusion, bf16[256,2048]{1,0:T(8,128)(2,1)} %collective-permute-done.16), kind=kOutput, calls=%fused_computation.1 | convolution fusion | flops 538443776 | bytes 4456448 | tf_op jit(solution)/shard_map/dot_general | solution.py:187
  117.9 5.7 %stream_grads.1 = (bf16[128,6144]{1,0:T(8,128)(2,1)}, f32[4,6144]{1,0:T(4,128)}) custom-call(bf16[128,6144]{1,0:T(8,128)(2,1)} %refs_0_.3, f32[2,6144]{1,0:T(2,128)} %convert_element_type.80.refs_1_, f32[3,6144]{1,0:T(4,128)} %refs_2_.3, bf16[8,128,256]{2,1,0:T(8,128)(2,1)} %copy-done.2, bf16[8,128,256]{2,1,0:T(8,128)(2,1)} %copy-done.3, ...), custom_call_target="tpu_custom_call" | custom-call | tf_op jit(solution)/shard_map/stream_grads/pallas_call | solution.py:67
  123.6 0.9 collective-permute-start.18
  124.5 1.5 collective-permute-start.19
  126.0 1.2 collective-permute-start.17
  127.3 7.6 %collective-permute-start.21 = (bf16[64,2048]{1,0:T(8,128)(2,1)S(1)}, bf16[64,2048]{1,0:T(8,128)(2,1)S(1)}, u32[]{:S(2)}, u32[]{:S(2)}) collective-permute-start(bf16[64,2048]{1,0:T(8,128)(2,1)S(1)} %get-tuple-element.72), channel_id=1, source_target_pairs={{0,2},{1,3},{2,0},{3,1},{4,6},{5,7},{6,4},{7,5},{8,10},{9,11},{10,... | collective-permute-start | bytes 786440 | tf_op jit(solution)/shard_map/ppermute | solution.py:22
  134.9 2.4 %collective-permute-start.23 = (bf16[64,2048]{1,0:T(8,128)(2,1)S(1)}, bf16[64,2048]{1,0:T(8,128)(2,1)S(1)}, u32[]{:S(2)}, u32[]{:S(2)}) collective-permute-start(bf16[64,2048]{1,0:T(8,128)(2,1)S(1)} %get-tuple-element.70), channel_id=1, source_target_pairs={{0,6},{1,7},{2,4},{3,5},{4,2},{5,3},{6,0},{7,1},{8,14},{9,15},{10,... | collective-permute-start | bytes 786440 | tf_op jit(solution)/shard_map/ppermute | solution.py:22
  137.3 0.9 add_add_fusion
  139.7 1.2 collective-permute-start.28
  140.8 4.6 %collective-permute-done.29 = bf16[256,256]{1,0:T(8,128)(2,1)S(1)} collective-permute-done((bf16[256,256]{1,0:T(8,128)(2,1)S(1)}, bf16[256,256]{1,0:T(8,128)(2,1)S(1)}, u32[]{:S(2)}, u32[]{:S(2)}) %collective-permute-start.29) | collective-permute-done | bytes 131104 | tf_op jit(solution)/shard_map/ppermute | solution.py:22
  145.7 2.3 %collective-permute-done.28 = bf16[256,256]{1,0:T(8,128)(2,1)S(1)} collective-permute-done((bf16[256,256]{1,0:T(8,128)(2,1)S(1)}, bf16[256,256]{1,0:T(8,128)(2,1)S(1)}, u32[]{:S(2)}, u32[]{:S(2)}) %collective-permute-start.28) | collective-permute-done | bytes 131104 | tf_op jit(solution)/shard_map/ppermute | solution.py:22
  148.0 2.4 %collective-permute-done.27 = bf16[256,256]{1,0:T(8,128)(2,1)S(1)} collective-permute-done((bf16[256,256]{1,0:T(8,128)(2,1)S(1)}, bf16[256,256]{1,0:T(8,128)(2,1)S(1)}, u32[]{:S(2)}, u32[]{:S(2)}) %collective-permute-start.27) | collective-permute-done | bytes 131104 | tf_op jit(solution)/shard_map/ppermute | solution.py:22
  150.4 0.8 add_multiply_fusion
  151.2 5.1 %collective-permute-done.22 = bf16[64,2048]{1,0:T(8,128)(2,1)S(1)} collective-permute-done((bf16[64,2048]{1,0:T(8,128)(2,1)S(1)}, bf16[64,2048]{1,0:T(8,128)(2,1)S(1)}, u32[]{:S(2)}, u32[]{:S(2)}) %collective-permute-start.22) | collective-permute-done | bytes 262176 | tf_op jit(solution)/shard_map/ppermute | solution.py:22
  156.3 4.3 %collective-permute-start.25 = (f32[3,6144]{1,0:T(4,128)S(1)}, f32[3,6144]{1,0:T(4,128)S(1)}, u32[]{:S(2)}, u32[]{:S(2)}) collective-permute-start(f32[3,6144]{1,0:T(4,128)S(1)} %slice_add_fusion), channel_id=1, source_target_pairs={{0,4},{1,5},{2,6},{3,7},{4,0},{5,1},{6,2},{7,3},{8,12},{9,13},{10,... | collective-permute-start | bytes 221192 | tf_op jit(solution)/shard_map/ppermute | solution.py:22
  160.6 3.4 %collective-permute-start.26 = (f32[3,6144]{1,0:T(4,128)S(1)}, f32[3,6144]{1,0:T(4,128)S(1)}, u32[]{:S(2)}, u32[]{:S(2)}) collective-permute-start(f32[3,6144]{1,0:T(4,128)S(1)} %slice_add_fusion), channel_id=1, source_target_pairs={{0,6},{1,7},{2,4},{3,5},{4,2},{5,3},{6,0},{7,1},{8,14},{9,15},{10,... | collective-permute-start | bytes 221192 | tf_op jit(solution)/shard_map/ppermute | solution.py:22
  164.0 0.9 fusion.7
  165.5 2.2 %collective-permute-done.26 = f32[3,6144]{1,0:T(4,128)S(1)} collective-permute-done((f32[3,6144]{1,0:T(4,128)S(1)}, f32[3,6144]{1,0:T(4,128)S(1)}, u32[]{:S(2)}, u32[]{:S(2)}) %collective-permute-start.26) | collective-permute-done | bytes 73760 | tf_op jit(solution)/shard_map/ppermute | solution.py:22
  167.7 1.0 collective-permute-done.24
  168.8 0.7 add_multiply_fusion.1
  (66 shorter events, 7.1 us)
Async XLA Ops:
  0.6 24.4 %copy-start = (bf16[512,2048]{1,0:T(8,128)(2,1)S(1)}, bf16[512,2048]{1,0:T(8,128)(2,1)}, u32[]{:S(2)}) copy-start(bf16[512,2048]{1,0:T(8,128)(2,1)} %param.11) | copy-start | bytes 6291460
  0.6 24.4 %collective-permute-start.1 = (bf16[128,2048]{1,0:T(8,128)(2,1)}, bf16[128,2048]{1,0:T(8,128)(2,1)S(1)}, u32[]{:S(2)}, u32[]{:S(2)}) collective-permute-start(bf16[128,2048]{1,0:T(8,128)(2,1)} %param.12), channel_id=1, source_target_pairs={{0,8},{8,0},{16,24},{24,16},{1,9},{9,1},{17,25},{25,17},{2,10},{10... | collective-permute-start | bytes 1572872 | tf_op jit(solution)/shard_map/ppermute | solution.py:22
  3.6 24.8 %collective-permute-start.3 = (bf16[128,2048]{1,0:T(8,128)(2,1)}, bf16[128,2048]{1,0:T(8,128)(2,1)S(1)}, u32[]{:S(2)}, u32[]{:S(2)}) collective-permute-start(bf16[128,2048]{1,0:T(8,128)(2,1)} %param.12), channel_id=1, source_target_pairs={{0,16},{8,24},{16,0},{24,8},{1,17},{9,25},{17,1},{25,9},{2,18},{10... | collective-permute-start | bytes 1572872 | tf_op jit(solution)/shard_map/ppermute | solution.py:22
  6.1 9.1 %collective-permute-start = (bf16[2,6144]{1,0:T(2,128)(2,1)S(1)}, bf16[2,6144]{1,0:T(2,128)(2,1)S(1)}, u32[]{:S(2)}, u32[]{:S(2)}) collective-permute-start(bf16[2,6144]{1,0:T(2,128)(2,1)S(1)} %slice.22), channel_id=1, source_target_pairs={{0,1},{1,2},{2,3},{3,4},{4,5},{5,6},{6,7},{8,9},{9,10},{10,11},{11... | collective-permute-start | bytes 73736 | tf_op jit(solution)/shard_map/ppermute | solution.py:18
  7.4 24.1 %collective-permute-start.5 = (bf16[128,2048]{1,0:T(8,128)(2,1)}, bf16[128,2048]{1,0:T(8,128)(2,1)}, u32[]{:S(2)}, u32[]{:S(2)}) collective-permute-start(bf16[128,2048]{1,0:T(8,128)(2,1)} %param.12), channel_id=1, source_target_pairs={{0,24},{8,16},{16,8},{24,0},{1,25},{9,17},{17,9},{25,1},{2,26},{10... | collective-permute-start | bytes 1572872 | tf_op jit(solution)/shard_map/ppermute | solution.py:22
  19.4 24.1 %all-to-all-start = ((bf16[8,128,256]{2,1,0:T(8,128)(2,1)}), bf16[8,128,256]{2,1,0:T(8,128)(2,1)}, u32[]{:S(2)}, u32[]{:S(2)}) async-start(bf16[8,128,256]{2,1,0:T(8,128)(2,1)} %get-tuple-element.39), calls=%async_computation | async-start | bytes 1048576 | tf_op jit(solution)/shard_map/all_to_all | solution.py:350
  25.1 3.4 %copy-start.10 = (bf16[128,2048]{1,0:T(8,128)(2,1)}, bf16[128,2048]{1,0:T(8,128)(2,1)S(1)}, u32[]{:S(2)}) copy-start(bf16[128,2048]{1,0:T(8,128)(2,1)S(1)} %collective-permute-done.1) | copy-start | bytes 1572868
  26.6 7.6 %copy-start.9 = (bf16[128,2048]{1,0:T(8,128)(2,1)S(1)}, bf16[128,2048]{1,0:T(8,128)(2,1)}, u32[]{:S(2)}) copy-start(bf16[128,2048]{1,0:T(8,128)(2,1)} %param.12) | copy-start | bytes 1572868
  26.6 8.4 %collective-permute-start.2 = (bf16[128,512]{1,0:T(8,128)(2,1)}, bf16[128,512]{1,0:T(8,128)(2,1)S(1)}, u32[]{:S(2)}, u32[]{:S(2)}) collective-permute-start(bf16[128,512]{1,0:T(8,128)(2,1)} %fusion.2), channel_id=1, source_target_pairs={{0,8},{8,0},{16,24},{24,16},{1,9},{9,1},{17,25},{25,17},{2,10},{10... | collective-permute-start | bytes 393224 | tf_op jit(solution)/shard_map/ppermute | solution.py:22
  28.5 3.0 %copy-start.11 = (bf16[128,2048]{1,0:T(8,128)(2,1)}, bf16[128,2048]{1,0:T(8,128)(2,1)S(1)}, u32[]{:S(2)}) copy-start(bf16[128,2048]{1,0:T(8,128)(2,1)S(1)} %collective-permute-done.3) | copy-start | bytes 1572868
  30.0 10.9 %copy-start.1 = (bf16[8,128,256]{2,1,0:T(8,128)(2,1)S(1)}, bf16[8,128,256]{2,1,0:T(8,128)(2,1)}, u32[]{:S(2)}) copy-start(bf16[8,128,256]{2,1,0:T(8,128)(2,1)} %get-tuple-element.36.refs_1_.refs_2_) | copy-start | bytes 1572868
  30.0 5.6 %collective-permute-start.4 = (bf16[128,512]{1,0:T(8,128)(2,1)}, bf16[128,512]{1,0:T(8,128)(2,1)S(1)}, u32[]{:S(2)}, u32[]{:S(2)}) collective-permute-start(bf16[128,512]{1,0:T(8,128)(2,1)} %fusion.3), channel_id=1, source_target_pairs={{0,16},{8,24},{16,0},{24,8},{1,17},{9,25},{17,1},{25,9},{2,18},{10... | collective-permute-start | bytes 393224 | tf_op jit(solution)/shard_map/ppermute | solution.py:22
  34.0 6.2 %collective-permute-start.6 = (bf16[128,512]{1,0:T(8,128)(2,1)}, bf16[128,512]{1,0:T(8,128)(2,1)S(1)}, u32[]{:S(2)}, u32[]{:S(2)}) collective-permute-start(bf16[128,512]{1,0:T(8,128)(2,1)} %fusion.4), channel_id=1, source_target_pairs={{0,24},{8,16},{16,8},{24,0},{1,25},{9,17},{17,9},{25,1},{2,26},{10... | collective-permute-start | bytes 393224 | tf_op jit(solution)/shard_map/ppermute | solution.py:22
  40.2 0.7 copy-start.7
  40.9 0.9 copy-start.8
  42.8 0.8 copy-start.4
  43.6 59.2 %copy-start.2 = (bf16[8,128,256]{2,1,0:T(8,128)(2,1)}, bf16[8,128,256]{2,1,0:T(8,128)(2,1)S(1)}, u32[]{:S(2)}) copy-start(bf16[8,128,256]{2,1,0:T(8,128)(2,1)S(1)} %get-tuple-element.38.refs_3_) | copy-start | bytes 1572868
  43.6 32.6 %all-to-all-start.1 = ((bf16[8,128,256]{2,1,0:T(8,128)(2,1)}), bf16[8,128,256]{2,1,0:T(8,128)(2,1)}, u32[]{:S(2)}, u32[]{:S(2)}) async-start(bf16[8,128,256]{2,1,0:T(8,128)(2,1)} %copy-done.4), calls=%async_computation.1 | async-start | bytes 1048576 | tf_op jit(solution)/shard_map/all_to_all | solution.py:350
  57.5 2.4 %collective-permute-start.7 = (bf16[4,128,256]{2,1,0:T(8,128)(2,1)}, bf16[4,128,256]{2,1,0:T(8,128)(2,1)}, u32[]{:S(2)}, u32[]{:S(2)}) collective-permute-start(bf16[4,128,256]{2,1,0:T(8,128)(2,1)} %get-tuple-element.77), channel_id=1, source_target_pairs={{0,1},{1,0},{2,3},{3,2},{4,5},{5,4},{6,7},{7,6},{8,9},{9,8},{10,11... | collective-permute-start | bytes 786440 | tf_op jit(solution)/shard_map/ppermute | solution.py:22
  60.9 7.8 %collective-permute-start.8 = (bf16[2,128,256]{2,1,0:T(8,128)(2,1)S(1)}, bf16[2,128,256]{2,1,0:T(8,128)(2,1)S(1)}, u32[]{:S(2)}, u32[]{:S(2)}) collective-permute-start(bf16[2,128,256]{2,1,0:T(8,128)(2,1)S(1)} %get-tuple-element.75), channel_id=1, source_target_pairs={{0,2},{1,3},{2,0},{3,1},{4,6},{5,7},{6,4},{7,5},{8,10},{9,11},{10,... | collective-permute-start | bytes 393224 | tf_op jit(solution)/shard_map/ppermute | solution.py:22
  62.6 12.9 %collective-permute-start.9 = (bf16[2,128,256]{2,1,0:T(8,128)(2,1)S(1)}, bf16[2,128,256]{2,1,0:T(8,128)(2,1)S(1)}, u32[]{:S(2)}, u32[]{:S(2)}) collective-permute-start(bf16[2,128,256]{2,1,0:T(8,128)(2,1)S(1)} %get-tuple-element.76), channel_id=1, source_target_pairs={{0,4},{1,5},{2,6},{3,7},{4,0},{5,1},{6,2},{7,3},{8,12},{9,13},{10,... | collective-permute-start | bytes 393224 | tf_op jit(solution)/shard_map/ppermute | solution.py:22
  65.0 10.6 %collective-permute-start.10 = (bf16[2,128,256]{2,1,0:T(8,128)(2,1)S(1)}, bf16[2,128,256]{2,1,0:T(8,128)(2,1)S(1)}, u32[]{:S(2)}, u32[]{:S(2)}) collective-permute-start(bf16[2,128,256]{2,1,0:T(8,128)(2,1)S(1)} %get-tuple-element.73), channel_id=1, source_target_pairs={{0,6},{1,7},{2,4},{3,5},{4,2},{5,3},{6,0},{7,1},{8,14},{9,15},{10,... | collective-permute-start | bytes 393224 | tf_op jit(solution)/shard_map/ppermute | solution.py:22
  75.5 0.7 copy-start.5
  85.0 23.1 %all-to-all-start.2 = ((bf16[8,130,256]{2,1,0:T(8,128)(2,1)}), bf16[8,130,256]{2,1,0:T(8,128)(2,1)}, u32[]{:S(2)}, u32[]{:S(2)}) async-start(bf16[8,130,256]{2,1,0:T(8,128)(2,1)} %get-tuple-element.45), calls=%async_computation.2 | async-start | bytes 1114112 | tf_op jit(solution)/shard_map/all_to_all | solution.py:355
  89.6 7.6 %copy-start.6 = (bf16[2,128,256]{2,1,0:T(8,128)(2,1)S(1)}, bf16[2,128,256]{2,1,0:T(8,128)(2,1)}, u32[]{:S(2)}) copy-start(bf16[2,128,256]{2,1,0:T(8,128)(2,1)} %copy-done.5) | copy-start | bytes 393220
  93.4 3.2 %collective-permute-start.11 = (bf16[2,8,2,256]{3,2,1,0:T(2,128)(2,1)S(1)}, bf16[2,8,2,256]{3,2,1,0:T(2,128)(2,1)S(1)}, u32[]{:S(2)}, u32[]{:S(2)}) collective-permute-start(bf16[2,8,2,256]{3,2,1,0:T(2,128)(2,1)S(1)} %pad_maximum_fusion.1), channel_id=1, source_target_pairs={{1,0},{2,1},{3,2},{4,3},{5,4},{6,5},{7,6},{9,8},{10,9},{11,10},{12... | collective-permute-start | bytes 49160 | tf_op jit(solution)/shard_map/ppermute | solution.py:18
  99.2 3.6 %copy-start.3 = (bf16[8,128,256]{2,1,0:T(8,128)(2,1)}, bf16[8,128,256]{2,1,0:T(8,128)(2,1)S(1)}, u32[]{:S(2)}) copy-start(bf16[8,128,256]{2,1,0:T(8,128)(2,1)S(1)} %get-tuple-element.53.refs_4_) | copy-start | bytes 1572868
  99.2 6.1 %collective-permute-start.14 = (bf16[128,512]{1,0:T(8,128)(2,1)S(1)}, bf16[128,512]{1,0:T(8,128)(2,1)S(1)}, u32[]{:S(2)}, u32[]{:S(2)}) collective-permute-start(bf16[128,512]{1,0:T(8,128)(2,1)S(1)} %get-tuple-element.57), channel_id=1, source_target_pairs={{0,24},{8,16},{16,8},{24,0},{1,25},{9,17},{17,9},{25,1},{2,26},{10... | collective-permute-start | bytes 393224 | tf_op jit(solution)/shard_map/ppermute | solution.py:22
  99.5 8.5 %collective-permute-start.13 = (bf16[128,512]{1,0:T(8,128)(2,1)S(1)}, bf16[128,512]{1,0:T(8,128)(2,1)S(1)}, u32[]{:S(2)}, u32[]{:S(2)}) collective-permute-start(bf16[128,512]{1,0:T(8,128)(2,1)S(1)} %get-tuple-element.56), channel_id=1, source_target_pairs={{0,16},{8,24},{16,0},{24,8},{1,17},{9,25},{17,1},{25,9},{2,18},{10... | collective-permute-start | bytes 393224 | tf_op jit(solution)/shard_map/ppermute | solution.py:22
  101.2 6.8 %collective-permute-start.12 = (bf16[128,512]{1,0:T(8,128)(2,1)S(1)}, bf16[128,512]{1,0:T(8,128)(2,1)S(1)}, u32[]{:S(2)}, u32[]{:S(2)}) collective-permute-start(bf16[128,512]{1,0:T(8,128)(2,1)S(1)} %get-tuple-element.55), channel_id=1, source_target_pairs={{0,8},{8,0},{16,24},{24,16},{1,9},{9,1},{17,25},{25,17},{2,10},{10... | collective-permute-start | bytes 393224 | tf_op jit(solution)/shard_map/ppermute | solution.py:22
  102.8 5.3 %collective-permute-start.15 = (f32[8,2,256]{2,1,0:T(2,128)S(1)}, f32[8,2,256]{2,1,0:T(2,128)S(1)}, u32[]{:S(2)}, u32[]{:S(2)}) collective-permute-start(f32[8,2,256]{2,1,0:T(2,128)S(1)} %convert_multiply_fusion), channel_id=1, source_target_pairs={{1,0},{2,1},{3,2},{4,3},{5,4},{6,5},{7,6},{9,8},{10,9},{11,10},{12... | collective-permute-start | bytes 49160 | tf_op jit(solution)/shard_map/ppermute | solution.py:18
  108.1 9.8 %copy-start.13 = (f32[8,2,256]{2,1,0:T(2,128)}, f32[8,2,256]{2,1,0:T(2,128)S(1)}, u32[]{:S(2)}) copy-start(f32[8,2,256]{2,1,0:T(2,128)S(1)} %collective-permute-done.15.refs_8_) | copy-start | bytes 49156
  111.4 3.9 %collective-permute-start.16 = (bf16[256,2048]{1,0:T(8,128)(2,1)}, bf16[256,2048]{1,0:T(8,128)(2,1)}, u32[]{:S(2)}, u32[]{:S(2)}) collective-permute-start(bf16[256,2048]{1,0:T(8,128)(2,1)} %convolution_convert_fusion), channel_id=1, source_target_pairs={{0,1},{1,0},{2,3},{3,2},{4,5},{5,4},{6,7},{7,6},{8,9},{9,8},{10,11... | collective-permute-start | bytes 3145736 | tf_op jit(solution)/shard_map/ppermute | solution.py:22
  123.6 14.8 %copy-start.12 = (f32[256,1024]{1,0:T(8,128)S(1)}, f32[256,1024]{1,0:T(8,128)}, u32[]{:S(2)}) copy-start(f32[256,1024]{1,0:T(8,128)} %get-tuple-element.66) | copy-start | bytes 3145732
  123.6 11.3 %collective-permute-start.18 = (f32[4,6144]{1,0:T(4,128)}, f32[4,6144]{1,0:T(4,128)S(1)}, u32[]{:S(2)}, u32[]{:S(2)}) collective-permute-start(f32[4,6144]{1,0:T(4,128)} %get-tuple-element.63), channel_id=1, source_target_pairs={{0,16},{8,24},{16,0},{24,8},{1,17},{9,25},{17,1},{25,9},{2,18},{10... | collective-permute-start | bytes 294920 | tf_op jit(solution)/shard_map/ppermute | solution.py:22
  124.5 12.8 %collective-permute-start.19 = (f32[4,6144]{1,0:T(4,128)}, f32[4,6144]{1,0:T(4,128)S(1)}, u32[]{:S(2)}, u32[]{:S(2)}) collective-permute-start(f32[4,6144]{1,0:T(4,128)} %get-tuple-element.63), channel_id=1, source_target_pairs={{0,24},{8,16},{16,8},{24,0},{1,25},{9,17},{17,9},{25,1},{2,26},{10... | collective-permute-start | bytes 294920 | tf_op jit(solution)/shard_map/ppermute | solution.py:22
  126.0 11.3 %collective-permute-start.17 = (f32[4,6144]{1,0:T(4,128)}, f32[4,6144]{1,0:T(4,128)S(1)}, u32[]{:S(2)}, u32[]{:S(2)}) collective-permute-start(f32[4,6144]{1,0:T(4,128)} %get-tuple-element.63), channel_id=1, source_target_pairs={{0,8},{8,0},{16,24},{24,16},{1,9},{9,1},{17,25},{25,17},{2,10},{10... | collective-permute-start | bytes 294920 | tf_op jit(solution)/shard_map/ppermute | solution.py:22
  127.3 23.9 %collective-permute-start.21 = (bf16[64,2048]{1,0:T(8,128)(2,1)S(1)}, bf16[64,2048]{1,0:T(8,128)(2,1)S(1)}, u32[]{:S(2)}, u32[]{:S(2)}) collective-permute-start(bf16[64,2048]{1,0:T(8,128)(2,1)S(1)} %get-tuple-element.72), channel_id=1, source_target_pairs={{0,2},{1,3},{2,0},{3,1},{4,6},{5,7},{6,4},{7,5},{8,10},{9,11},{10,... | collective-permute-start | bytes 786440 | tf_op jit(solution)/shard_map/ppermute | solution.py:22
  134.9 21.4 %collective-permute-start.22 = (bf16[64,2048]{1,0:T(8,128)(2,1)S(1)}, bf16[64,2048]{1,0:T(8,128)(2,1)S(1)}, u32[]{:S(2)}, u32[]{:S(2)}) collective-permute-start(bf16[64,2048]{1,0:T(8,128)(2,1)S(1)} %get-tuple-element.71), channel_id=1, source_target_pairs={{0,4},{1,5},{2,6},{3,7},{4,0},{5,1},{6,2},{7,3},{8,12},{9,13},{10,... | collective-permute-start | bytes 786440 | tf_op jit(solution)/shard_map/ppermute | solution.py:22
  134.9 21.4 %collective-permute-start.23 = (bf16[64,2048]{1,0:T(8,128)(2,1)S(1)}, bf16[64,2048]{1,0:T(8,128)(2,1)S(1)}, u32[]{:S(2)}, u32[]{:S(2)}) collective-permute-start(bf16[64,2048]{1,0:T(8,128)(2,1)S(1)} %get-tuple-element.70), channel_id=1, source_target_pairs={{0,6},{1,7},{2,4},{3,5},{4,2},{5,3},{6,0},{7,1},{8,14},{9,15},{10,... | collective-permute-start | bytes 786440 | tf_op jit(solution)/shard_map/ppermute | solution.py:22
  138.3 1.4 collective-permute-start.20
  138.4 6.9 %collective-permute-start.29 = (bf16[256,256]{1,0:T(8,128)(2,1)S(1)}, bf16[256,256]{1,0:T(8,128)(2,1)S(1)}, u32[]{:S(2)}, u32[]{:S(2)}) collective-permute-start(bf16[256,256]{1,0:T(8,128)(2,1)S(1)} %get-tuple-element.68), channel_id=1, source_target_pairs={{0,24},{8,16},{16,8},{24,0},{1,25},{9,17},{17,9},{25,1},{2,26},{10... | collective-permute-start | bytes 393224 | tf_op jit(solution)/shard_map/ppermute | solution.py:22
  139.7 8.4 %collective-permute-start.28 = (bf16[256,256]{1,0:T(8,128)(2,1)S(1)}, bf16[256,256]{1,0:T(8,128)(2,1)S(1)}, u32[]{:S(2)}, u32[]{:S(2)}) collective-permute-start(bf16[256,256]{1,0:T(8,128)(2,1)S(1)} %get-tuple-element.69), channel_id=1, source_target_pairs={{0,16},{8,24},{16,0},{24,8},{1,17},{9,25},{17,1},{25,9},{2,18},{10... | collective-permute-start | bytes 393224 | tf_op jit(solution)/shard_map/ppermute | solution.py:22
  145.4 5.0 %collective-permute-start.27 = (bf16[256,256]{1,0:T(8,128)(2,1)S(1)}, bf16[256,256]{1,0:T(8,128)(2,1)S(1)}, u32[]{:S(2)}, u32[]{:S(2)}) collective-permute-start(bf16[256,256]{1,0:T(8,128)(2,1)S(1)} %get-tuple-element.67), channel_id=1, source_target_pairs={{0,8},{8,0},{16,24},{24,16},{1,9},{9,1},{17,25},{25,17},{2,10},{10... | collective-permute-start | bytes 393224 | tf_op jit(solution)/shard_map/ppermute | solution.py:22
  156.3 9.2 %collective-permute-start.25 = (f32[3,6144]{1,0:T(4,128)S(1)}, f32[3,6144]{1,0:T(4,128)S(1)}, u32[]{:S(2)}, u32[]{:S(2)}) collective-permute-start(f32[3,6144]{1,0:T(4,128)S(1)} %slice_add_fusion), channel_id=1, source_target_pairs={{0,4},{1,5},{2,6},{3,7},{4,0},{5,1},{6,2},{7,3},{8,12},{9,13},{10,... | collective-permute-start | bytes 221192 | tf_op jit(solution)/shard_map/ppermute | solution.py:22
  160.6 7.1 %collective-permute-start.26 = (f32[3,6144]{1,0:T(4,128)S(1)}, f32[3,6144]{1,0:T(4,128)S(1)}, u32[]{:S(2)}, u32[]{:S(2)}) collective-permute-start(f32[3,6144]{1,0:T(4,128)S(1)} %slice_add_fusion), channel_id=1, source_target_pairs={{0,6},{1,7},{2,4},{3,5},{4,2},{5,3},{6,0},{7,1},{8,14},{9,15},{10,... | collective-permute-start | bytes 221192 | tf_op jit(solution)/shard_map/ppermute | solution.py:22
  164.0 4.8 %collective-permute-start.24 = (f32[3,6144]{1,0:T(4,128)S(1)}, f32[3,6144]{1,0:T(4,128)S(1)}, u32[]{:S(2)}, u32[]{:S(2)}) collective-permute-start(f32[3,6144]{1,0:T(4,128)S(1)} %slice_add_fusion), channel_id=1, source_target_pairs={{0,2},{1,3},{2,0},{3,1},{4,6},{5,7},{6,4},{7,5},{8,10},{9,11},{10,... | collective-permute-start | bytes 221192 | tf_op jit(solution)/shard_map/ppermute | solution.py:22

commit v9 on v8

--- a/solution.py
+++ b/solution.py
@@ -180,7 +180,10 @@
 def constant_table(seq_len):
     odd = 2 * np.arange(seq_len)[:, None] + 1
     angles = odd * np.arange(seq_len)[None, :] % (4 * seq_len) * (math.pi / (2 * seq_len))
-    return np.stack([np.cos(angles), -np.sin(angles)]).astype(np.float32).astype(BF16)
+    both = np.stack([np.cos(angles), -np.sin(angles)])
+    size = min(128, seq_len)
+    both = both.reshape(2, seq_len // size, size, seq_len).transpose(1, 0, 2, 3)
+    return both.reshape(-1, 2 * size, seq_len).astype(np.float32).astype(BF16)
 
 
 def dot(left, right, left_dim, right_dim):
@@ -202,9 +205,13 @@
     return jnp.concatenate([real, imag], 0).astype(BF16)
 
 
+def halves(value):
+    half = value.shape[1] // 2
+    return (value[:, :half], value[:, half:])
+
+
 def filter_kernel(waves_ref, filter_ref, spec_ref):
-    for i in range(2):
-        spec_ref[i] = dot(filter_ref[...], waves_ref[i], 1, 1)
+    spec_ref[...] = dot(filter_ref[...].astype(BF16), waves_ref[...], 1, 1)
 
 
 def out_kernel(waves_ref, filter_spec_ref, product_ref, skip_ref, spec_ref, long_ref, turned, total):
@@ -215,12 +222,12 @@
         turned[...] = product_ref[...].astype(F32).T.astype(BF16)
         total[...] = jnp.zeros_like(total)
 
-    spec_re, spec_im = (dot(turned[...], waves_ref[i], 1, 1) for i in range(2))
-    spec_ref[0], spec_ref[1] = (spec_re, spec_im)
-    filter_re, filter_im = (filter_spec_ref[0], filter_spec_ref[1])
-    real = (filter_re * spec_re - filter_im * spec_im).astype(BF16)
-    imag = (filter_re * spec_im + filter_im * spec_re).astype(BF16)
-    total[...] += dot(real, waves_ref[0], 1, 0) + dot(imag, waves_ref[1], 1, 0)
+    spec = dot(turned[...], waves_ref[...], 1, 1)
+    spec_ref[...] = spec
+    real, imag = halves(spec)
+    filter_re, filter_im = halves(filter_spec_ref[...])
+    mixed = [filter_re * real - filter_im * imag, filter_re * imag + filter_im * real]
+    total[...] += dot(jnp.concatenate(mixed, 1).astype(BF16), waves_ref[...], 1, 0)
 
     @pl.when(step == pl.num_programs(0) - 1)
     def _():
@@ -241,12 +248,11 @@
         total[...] = jnp.zeros_like(total)
         lag_ref[...] = jnp.zeros_like(lag_ref)
 
-    grad_re, grad_im = (dot(turned[...], waves_ref[i], 1, 1) for i in range(2))
+    real, imag = halves(dot(turned[...], waves_ref[...], 1, 1))
     for ref, sums in ((filter_spec_ref, total), (spec_ref, lag_ref)):
-        left_re, left_im = (ref[0], ref[1])
-        real = (left_re * grad_re + left_im * grad_im).astype(BF16)
-        imag = (left_re * grad_im - left_im * grad_re).astype(BF16)
-        sums[...] += dot(real, waves_ref[0], 1, 0) + dot(imag, waves_ref[1], 1, 0)
+        left_re, left_im = halves(ref[...])
+        mixed = [left_re * real + left_im * imag, left_re * imag - left_im * real]
+        sums[...] += dot(jnp.concatenate(mixed, 1).astype(BF16), waves_ref[...], 1, 0)
 
     @pl.when(step == pl.num_programs(0) - 1)
     def _():
@@ -264,10 +270,8 @@
 
 
 def chunked(kernel, name, waves, specs, planes, outs, spec_out, scratch):
-    freqs, seq_len = waves.shape[1:]
-    size = min(256, freqs)
-    blk = (specs + spec_out)[0].shape[1]
-    chunk = pl.BlockSpec((2, blk, size), lambda i: (0, 0, i))
+    def chunk(array):
+        return pl.BlockSpec((None, *array.shape[1:]), lambda i: (i, 0, 0))
 
     def whole(array):
         return pl.BlockSpec(array.shape, lambda i: (0,) * len(array.shape))
@@ -275,16 +279,30 @@
     return pl.pallas_call(
         kernel,
         out_shape=spec_out + outs,
-        grid=(freqs // size,),
-        in_specs=[pl.BlockSpec((2, size, seq_len), lambda i: (0, i, 0))]
-        + [chunk] * len(specs)
-        + [whole(a) for a in planes],
-        out_specs=[chunk] * len(spec_out) + [whole(a) for a in outs],
+        grid=(waves.shape[0],),
+        in_specs=[chunk(a) for a in (waves, *specs)] + [whole(a) for a in planes],
+        out_specs=[chunk(a) for a in spec_out] + [whole(a) for a in outs],
         scratch_shapes=scratch,
         compiler_params=pltpu.CompilerParams(vmem_limit_bytes=60 * 2**20),
         cost_estimate=pl.CostEstimate(flops=0, transcendentals=0, bytes_accessed=0),
         name=name,
     )(waves, *specs, *planes)
+
+
+def share_kernel(take, core_ref, *refs):
+    refs, out_ref = refs[:-1], refs[-1]
+    count = len(refs) // 2
+    gates, cots = refs[:count], refs[count : 2 * count]
+    width = out_ref.shape[0]
+    core = core_ref[0] if take else 1 - core_ref[0]
+    cols = pl.ds(pl.multiple_of(core * width, 128), width)
+    turned = [gate[:, cols].astype(F32).T.astype(BF16) for gate in gates]
+    size = min(512, out_ref.shape[1])
+    for n in range(out_ref.shape[1] // size):
+        total = sum(dot(turned[k], cots[k][:, columns(n, size)], 1, 0) for k in range(count))
+        if take:
+            total = total + refs[-1][:, columns(n, size)].astype(F32)
+        out_ref[:, columns(n, size)] = total.astype(BF16)
 
 
 def ordered(value, *first):
@@ -318,19 +336,21 @@
     return [1 << i for i in range(count.bit_length() - 1) if 1 << i >= first]
 
 
-def own_share(gate_all, cot_all, parts):
-    core = lax.axis_index("context") % 2
-    width = gate_all.shape[1] // 2
-    other = dot(lax.dynamic_slice_in_dim(gate_all, (1 - core) * width, width, 1), cot_all, 0, 0)
-    other = other.astype(BF16)
-    own_gate = ordered(lax.dynamic_slice_in_dim(gate_all, core * width, width, 1), other)
-    own = dot(own_gate, cot_all, 0, 0)
-    pair = (own + swapped(other, "context", 1).astype(F32)).astype(BF16)
-    pair = pair.reshape(parts // 2, -1, pair.shape[-1])
+def own_share(gates, cots, parts):
+    core = (lax.axis_index("context") % 2).astype(jnp.int32)[None]
+    half = jax.ShapeDtypeStruct((gates[0].shape[1] // 2, cots[0].shape[1]), BF16)
+
+    def product(take, name, *more):
+        kernel = lambda *refs: share_kernel(take, *refs)
+        return call(kernel, name, [half], 1, 60, core, *gates, *cots, *more)[0]
+
+    other = product(False, "other_share")
+    pair = product(True, "own_share", swapped(other, "context", 1))
+    blocks = pair.reshape(parts // 2, -1, pair.shape[-1])
     row = lax.axis_index("context") // 2
-    shares = [lax.dynamic_index_in_dim(pair, row, 0, False)]
+    shares = [lax.dynamic_index_in_dim(blocks, row, 0, False)]
     for k in range(1, parts // 2):
-        sent = lax.dynamic_index_in_dim(pair, row ^ k, 0, False)
+        sent = lax.dynamic_index_in_dim(blocks, row ^ k, 0, False)
         shares.append(swapped(sent, "context", 2 * k))
     return (pair, shares)
 
@@ -379,11 +399,11 @@
     weights = out_proj
     if straight:
         waves = jnp.asarray(constant_table(seq_len))
-        spec = jax.ShapeDtypeStruct((2, blk, seq_len), F32)
+        spec = jax.ShapeDtypeStruct((waves.shape[0], blk, waves.shape[1]), F32)
         scratch = [pltpu.VMEM((blk, seq_len), BF16), pltpu.VMEM((blk, seq_len), F32)]
         skip_row = skip_gain[None, :]
         (filter_spec,) = chunked(
-            filter_kernel, "filter_spectrum", waves, [], [filter_b], [], [spec], []
+            filter_kernel, "filter_spectrum", waves, [], [long_filter], [], [spec], []
         )
         weights = ordered(out_proj, filter_spec)
     found = [dot(cot, weights, 1, 1).astype(BF16) for cot in cots]
@@ -427,7 +447,7 @@
             "grad_product",
             waves,
             [filter_spec, product_spec],
-            [ordered(grad_long, *long_came[1:]), product, skip_row],
+            [ordered(grad_long, long_came[1]), product, skip_row],
             [
                 jax.ShapeDtypeStruct((parts, rows + 2, blk), BF16),
                 jax.ShapeDtypeStruct((blk, seq_len), F32),
@@ -464,10 +484,10 @@
     gates = [gates[0]] + [swapped(gates[k], "dp", k) for k in range(1, parts_dp)]
     query_heads = gate_grad[:, :2].astype(F32) * long_out[:, :2].astype(F32)
     query_after = passed_along(query_heads, "context", -1)
-    early = (grad_product, query_after)
-    gate_all = ordered(jnp.concatenate(gates, 0), *early)
-    cot_all = jnp.concatenate(cots, 0)
-    pair, shares = own_share(gate_all, cot_all, parts)
+    grad_filter = summed_blocks(lag_sum, "dp", 1) * (scale_factor * inverse)
+    early = (grad_product, query_after, grad_filter)
+    gates[0] = ordered(gates[0], *early)
+    pair, shares = own_share(gates, cots, parts)
     grad_product = ordered(grad_product, pair)
 
     grad_inputs, tap_sums = call(
@@ -493,8 +513,6 @@
     )
 
     tap_sums = all_sum(tap_sums, "dp", bits_of(parts_dp))
-    lag_sum = ordered(lag_sum, tap_sums)
-    grad_filter = summed_blocks(lag_sum, "dp", 1) * (scale_factor * inverse)
     grad_skip = tap_sums[3, :blk] * scale_factor
     tap_sums = tap_sums[:3] + swapped(tap_sums[:3], "context", 1)
     tap_sums = ordered(tap_sums, *shares[1:])

time: 171 us -> 181 us (1.058)
  Pallas kernels: 33.6 us -> 52.1 us
  matrix products: 12.3 us -> 6.33 us
  local copies, waits for them, and re-layouts: 14.3 us -> 10.1 us
    pallas_call x4 -> x6, Pallas kernels: 12.2 us -> 21.8 us  [call(): pl.pallas_call(run, out_shape=outs, in_specs=[SMEM] * smem + [anywhere] *...]
    pallas_call x3, Pallas kernels: 21.4 us -> 30.3 us  [chunked(): pl.pallas_call(kernel, out_shape=spec_out + outs, grid=(waves.shape[0],),...]
    dot_general x6 -> x4, matrix products: 12.3 us -> 6.33 us  [dot(): lax.dot_general(left, right, (((left_dim,), (right_dim,)), ((), ())), pre...]
    unnamed x31 -> x34, local copies, waits for them, and re-layouts: 8.76 us -> 5.43 us
    convert_element_type x1 -> x0, other arithmetic: 2.09 us -> none  [body(): filter_b = long_filter.astype(BF16)]
    ppermute x3, waiting for transfers between devices: 0.01 us -> 1.98 us  [passed_along(): lax.ppermute(value, axis, [(source, source + steps) for source in range(i...]
    concatenate x1 -> x0, local copies, waits for them, and re-layouts: 1.9 us -> none  [body(): cot_all = jnp.concatenate(cots, 0)]
  transfers between devices with their start and end apart: 33 -> 33, of which waited for: 16 -> 14; matrix products, arithmetic and copies ran while one was open for 15% -> 10% of each run, Pallas kernels for 11% -> 21%
where the time goes in v9:
time: 181 us; the launch traced here: 180 us
  starting transfers between devices  61.3 us (34%)
  Pallas kernels  52.1 us (29%)
  waiting for transfers between devices  40.4 us (22%)
  local copies, waits for them, and re-layouts  10.1 us (6%)
  other arithmetic  8.47 us (5%)
  matrix products  6.33 us (3%)
    ppermute x27, starting transfers between devices, swapped(): lax.ppermute(value, axis, [(i, i ^ mask) for i in range(lax.axis_size(axi...  41.8 us
    ppermute x27, waiting for transfers between devices, swapped(): lax.ppermute(value, axis, [(i, i ^ mask) for i in range(lax.axis_size(axi...  38.4 us
    pallas_call x3, Pallas kernels, chunked(): pl.pallas_call(kernel, out_shape=spec_out + outs, grid=(waves.shape[0],),...  30.3 us
    pallas_call x6, Pallas kernels, call(): pl.pallas_call(run, out_shape=outs, in_specs=[SMEM] * smem + [anywhere] *...  21.8 us
    all_to_all x2, starting transfers between devices, to_channels(): lax.all_to_all(blocks, 'context', split_axis=0, concat_axis=0, tiled=True)  10.2 us
    dot_general x4, matrix products, dot(): lax.dot_general(left, right, (((left_dim,), (right_dim,)), ((), ())), pre...  6.33 us
    unnamed x34, local copies, waits for them, and re-layouts  5.43 us
    all_to_all x1, starting transfers between devices, to_positions(): lax.all_to_all(blocks, 'context', split_axis=0, concat_axis=0, tiled=True)  5.18 us
  transfers between devices with their start and end apart: 33, of which 14 were waited for; matrix products, arithmetic and copies ran while one was open for 10% of the time, Pallas kernels for 21%

profile of v9, /device:TPU:0, one launch (start us, length us, event | category | flops | bytes accessed | tf_op | source)
XLA Modules:
  0.0 179.6 jit_solution(824871476300542958)
XLA Ops:
  0.6 3.0 %collective-permute-start.1 = (bf16[128,2048]{1,0:T(8,128)(2,1)}, bf16[128,2048]{1,0:T(8,128)(2,1)S(1)}, u32[]{:S(2)}, u32[]{:S(2)}) collective-permute-start(bf16[128,2048]{1,0:T(8,128)(2,1)} %refs_5_.3), channel_id=1, source_target_pairs={{0,8},{8,0},{16,24},{24,16},{1,9},{9,1},{17,25},{25,17},{2,10},{10... | collective-permute-start | bytes 1572872 | tf_op jit(solution)/shard_map/ppermute | solution.py:22
  3.6 1.5 collective-permute-start.3
  5.2 0.9 slice.22
  6.1 1.3 collective-permute-start
  7.8 7.7 %filter_spectrum.1.filter_spec_ref = f32[8,256,256]{2,1,0:T(8,128)} custom-call(bf16[8,256,1024]{2,1,0:T(8,128)(2,1)} %constant.80.clone.waves_ref, f32[256,1024]{1,0:T(8,128)} %filter_ref.1), custom_call_target="tpu_custom_call" | custom-call | tf_op jit(solution)/shard_map/filter_spectrum/pallas_call | solution.py:279
  15.5 0.6 convert_element_type.68.refs_1_
  16.1 3.6 %short_convs.1 = (bf16[8,128,256]{2,1,0:T(8,128)(2,1)}, bf16[8,128,256]{2,1,0:T(8,128)(2,1)}, bf16[8,128,256]{2,1,0:T(8,128)(2,1)}, bf16[8,128,256]{2,1,0:T(8,128)(2,1)}) custom-call(bf16[128,6144]{1,0:T(8,128)(2,1)} %refs_0_.3, f32[2,6144]{1,0:T(2,128)} %convert_element_type.68.refs_1_, f32[3,6144]{1,0:T(4,128)} %refs_2_.3), custom_call_target="tpu_custom_call" | custom-call | tf_op jit(solution)/shard_map/short_convs/pallas_call | solution.py:67
  19.8 5.6 %all-to-all-start = ((bf16[8,128,256]{2,1,0:T(8,128)(2,1)}), bf16[8,128,256]{2,1,0:T(8,128)(2,1)}, u32[]{:S(2)}, u32[]{:S(2)}) async-start(bf16[8,128,256]{2,1,0:T(8,128)(2,1)} %get-tuple-element.37), calls=%async_computation | async-start | bytes 1048576 | tf_op jit(solution)/shard_map/all_to_all | solution.py:370
  25.4 1.5 fusion.1
  26.9 1.5 collective-permute-start.2
  28.5 1.5 fusion.2
  30.0 1.5 collective-permute-start.4
  31.5 2.5 %fusion.3 = bf16[128,512]{1,0:T(8,128)(2,1)} fusion(bf16[512,2048]{1,0:T(8,128)(2,1)S(1)} %copy-done, bf16[128,2048]{1,0:T(8,128)(2,1)} %collective-permute-done.5.refs_8_), kind=kOutput, calls=%fused_computation.7 | convolution fusion | flops 268500992 | bytes 2752512 | tf_op jit(solution)/shard_map/dot_general | solution.py:190
  34.4 0.8 fusion.refs_2_
  35.8 4.7 %collective-permute-done.6.refs_5_ = bf16[128,512]{1,0:T(8,128)(2,1)S(1)} collective-permute-done((bf16[128,512]{1,0:T(8,128)(2,1)}, bf16[128,512]{1,0:T(8,128)(2,1)S(1)}, u32[]{:S(2)}, u32[]{:S(2)}) %collective-permute-start.6) | collective-permute-done | bytes 131104 | tf_op jit(solution)/shard_map/ppermute | solution.py:22
  40.5 0.7 copy-done.6
  41.2 0.9 copy-done.7
  42.1 1.0 grad_long.1
  43.1 0.8 copy-done.5
  43.9 4.6 %all-to-all-start.1 = ((bf16[8,128,256]{2,1,0:T(8,128)(2,1)}), bf16[8,128,256]{2,1,0:T(8,128)(2,1)}, u32[]{:S(2)}, u32[]{:S(2)}) async-start(bf16[8,128,256]{2,1,0:T(8,128)(2,1)} %copy-done.5), calls=%async_computation.1 | async-start | bytes 1048576 | tf_op jit(solution)/shard_map/all_to_all | solution.py:370
  48.5 10.6 %long_out.1 = (f32[8,256,256]{2,1,0:T(8,128)}, bf16[1024,256]{1,0:T(8,128)(2,1)}) custom-call(bf16[8,256,1024]{2,1,0:T(8,128)(2,1)} %constant.80.clone.waves_ref, f32[8,256,256]{2,1,0:T(8,128)} %filter_spectrum.1.filter_spec_ref, bf16[1024,256]{1,0:T(8,128)(2,1)} %bitcast.6.product_ref, f32[1,256]{1,0:T(1,128)} %bitcast.54), custom_call_target="tpu_custom_call" | custom-call | tf_op jit(solution)/shard_map/long_out/pallas_call | solution.py:279
  59.0 1.8 dynamic-slice_bitcast_fusion.3
  61.3 1.5 collective-permute-done.7
  62.8 1.7 fusion.8
  64.5 1.9 %collective-permute-start.8 = (bf16[2,128,256]{2,1,0:T(8,128)(2,1)S(1)}, bf16[2,128,256]{2,1,0:T(8,128)(2,1)S(1)}, u32[]{:S(2)}, u32[]{:S(2)}) collective-permute-start(bf16[2,128,256]{2,1,0:T(8,128)(2,1)S(1)} %get-tuple-element.71), channel_id=1, source_target_pairs={{0,2},{1,3},{2,0},{3,1},{4,6},{5,7},{6,4},{7,5},{8,10},{9,11},{10,... | collective-permute-start | bytes 393224 | tf_op jit(solution)/shard_map/ppermute | solution.py:22
  66.4 2.4 %collective-permute-start.10 = (bf16[2,128,256]{2,1,0:T(8,128)(2,1)}, bf16[2,128,256]{2,1,0:T(8,128)(2,1)S(1)}, u32[]{:S(2)}, u32[]{:S(2)}) collective-permute-start(bf16[2,128,256]{2,1,0:T(8,128)(2,1)} %get-tuple-element.69), channel_id=1, source_target_pairs={{0,6},{1,7},{2,4},{3,5},{4,2},{5,3},{6,0},{7,1},{8,14},{9,15},{10,... | collective-permute-start | bytes 393224 | tf_op jit(solution)/shard_map/ppermute | solution.py:22
  68.8 1.5 collective-permute-done.8.refs_4_
  70.3 12.1 %grad_product.1 = (bf16[8,130,256]{2,1,0:T(8,128)(2,1)}, f32[256,1024]{1,0:T(8,128)}, f32[1,256]{1,0:T(1,128)}) custom-call(bf16[8,256,1024]{2,1,0:T(8,128)(2,1)} %constant.80.clone.waves_ref, f32[8,256,256]{2,1,0:T(8,128)} %filter_spectrum.1.filter_spec_ref, f32[8,256,256]{2,1,0:T(8,128)} %get-tuple-element.41.spec_ref, ...), custom_call_target="tpu_custom_call" | custom-call | tf_op jit(solution)/shard_map/grad_product/pallas_call | solution.py:279
  82.4 5.2 %all-to-all-start.2 = ((bf16[8,130,256]{2,1,0:T(8,128)(2,1)}), bf16[8,130,256]{2,1,0:T(8,128)(2,1)}, u32[]{:S(2)}, u32[]{:S(2)}) async-start(bf16[8,130,256]{2,1,0:T(8,128)(2,1)} %get-tuple-element.43), calls=%async_computation.2 | async-start | bytes 1114112 | tf_op jit(solution)/shard_map/all_to_all | solution.py:375
  87.6 0.8 slice_bitcast_fusion
  88.3 0.6 pad_maximum_fusion
  89.0 1.3 collective-permute-start.11
  90.3 2.0 %collective-permute-done.11 = bf16[2,8,2,256]{3,2,1,0:T(2,128)(2,1)S(1)} collective-permute-done((bf16[2,8,2,256]{3,2,1,0:T(2,128)(2,1)}, bf16[2,8,2,256]{3,2,1,0:T(2,128)(2,1)S(1)}, u32[]{:S(2)}, u32[]{:S(2)}) %collective-permute-start.11) | collective-permute-done | bytes 16416 | tf_op jit(solution)/shard_map/ppermute | solution.py:18
  92.9 1.2 dynamic-slice_convert_fusion.2
  94.6 1.4 collective-permute-start.15
  96.1 1.5 collective-permute-start.14
  97.6 2.7 %gate.1 = (bf16[8,128,256]{2,1,0:T(8,128)(2,1)S(1)}, bf16[128,512]{1,0:T(8,128)(2,1)S(1)}, bf16[128,512]{1,0:T(8,128)(2,1)}, bf16[128,512]{1,0:T(8,128)(2,1)}, bf16[128,512]{1,0:T(8,128)(2,1)}) custom-call(s32[1]{0:T(128)} %bitcast.5.refs_0_, s32[1]{0:T(128)} %bitcast.refs_0_.refs_1_, bf16[8,128,256]{2,1,0:T(8,128)(2,1)S(1)} %copy-done.1, ...), custom_call_target="tpu_custom_call" | custom-call | tf_op jit(solution)/shard_map/gate/pallas_call | solution.py:67
  100.3 0.6 copy-done.4
  101.0 0.8 copy-done.3
  101.7 1.5 collective-permute-start.12
  104.3 2.5 %collective-permute-start.18 = (bf16[128,512]{1,0:T(8,128)(2,1)}, bf16[128,512]{1,0:T(8,128)(2,1)S(1)}, u32[]{:S(2)}, u32[]{:S(2)}) collective-permute-start(bf16[128,512]{1,0:T(8,128)(2,1)} %get-tuple-element.57), channel_id=1, source_target_pairs={{0,24},{8,16},{16,8},{24,0},{1,25},{9,17},{17,9},{25,1},{2,26},{10... | collective-permute-start | bytes 393224 | tf_op jit(solution)/shard_map/ppermute | solution.py:22
  106.8 1.7 add_multiply_fusion
  108.5 0.9 collective-permute-done.17.refs_3_
  109.4 2.4 %collective-permute-done.18.refs_4_ = bf16[128,512]{1,0:T(8,128)(2,1)S(1)} collective-permute-done((bf16[128,512]{1,0:T(8,128)(2,1)}, bf16[128,512]{1,0:T(8,128)(2,1)S(1)}, u32[]{:S(2)}, u32[]{:S(2)}) %collective-permute-start.18) | collective-permute-done | bytes 131104 | tf_op jit(solution)/shard_map/ppermute | solution.py:22
  112.4 4.1 %other_share.1 = bf16[256,2048]{1,0:T(8,128)(2,1)} custom-call(s32[1]{0:T(128)} %bitcast.18.refs_0_, bf16[128,512]{1,0:T(8,128)(2,1)} %copy-done.4, bf16[128,512]{1,0:T(8,128)(2,1)} %copy-done.13, bf16[128,512]{1,0:T(8,128)(2,1)} %copy-done.14, bf16[128,512]{1,0:T(8,128)(2,1)} %copy-done.15, bf16[128,2048]{1,0:T(8,128)(2,1)} %refs_5_.3, ...), custom_call_target="tpu_custom_call" | custom-call | tf_op jit(solution)/shard_map/other_share/pallas_call | solution.py:67
  116.6 1.4 collective-permute-start.19
  117.9 2.5 %collective-permute-done.19.refs_9_ = bf16[256,2048]{1,0:T(8,128)(2,1)S(1)} collective-permute-done((bf16[256,2048]{1,0:T(8,128)(2,1)}, bf16[256,2048]{1,0:T(8,128)(2,1)S(1)}, u32[]{:S(2)}, u32[]{:S(2)}) %collective-permute-start.19) | collective-permute-done | bytes 1048608 | tf_op jit(solution)/shard_map/ppermute | solution.py:22
  120.4 1.0 copy-done.12
  121.4 4.5 %own_share.1 = bf16[256,2048]{1,0:T(8,128)(2,1)} custom-call(s32[1]{0:T(128)} %bitcast.18.refs_0_, bf16[128,512]{1,0:T(8,128)(2,1)} %copy-done.4, bf16[128,512]{1,0:T(8,128)(2,1)} %copy-done.13, bf16[128,512]{1,0:T(8,128)(2,1)} %copy-done.14, bf16[128,512]{1,0:T(8,128)(2,1)} %copy-done.15, bf16[128,2048]{1,0:T(8,128)(2,1)} %refs_5_.3, ...), custom_call_target="tpu_custom_call" | custom-call | tf_op jit(solution)/shard_map/own_share/pallas_call | solution.py:67
  125.9 5.8 %stream_grads.1 = (bf16[128,6144]{1,0:T(8,128)(2,1)}, f32[4,6144]{1,0:T(4,128)}) custom-call(bf16[128,6144]{1,0:T(8,128)(2,1)} %refs_0_.3, f32[2,6144]{1,0:T(2,128)} %convert_element_type.68.refs_1_, f32[3,6144]{1,0:T(4,128)} %refs_2_.3, bf16[8,128,256]{2,1,0:T(8,128)(2,1)} %copy-done.2, bf16[8,128,256]{2,1,0:T(8,128)(2,1)} %copy-done.3, ...), custom_call_target="tpu_custom_call" | custom-call | tf_op jit(solution)/shard_map/stream_grads/pallas_call | solution.py:67
  131.8 1.5 collective-permute-start.22
  133.3 1.5 collective-permute-start.21
  135.4 9.6 %collective-permute-start.26 = (bf16[64,2048]{1,0:T(8,128)(2,1)S(1)}, bf16[64,2048]{1,0:T(8,128)(2,1)S(1)}, u32[]{:S(2)}, u32[]{:S(2)}) collective-permute-start(bf16[64,2048]{1,0:T(8,128)(2,1)S(1)} %get-tuple-element.63), channel_id=1, source_target_pairs={{0,6},{1,7},{2,4},{3,5},{4,2},{5,3},{6,0},{7,1},{8,14},{9,15},{10,... | collective-permute-start | bytes 786440 | tf_op jit(solution)/shard_map/ppermute | solution.py:22
  145.1 2.1 %collective-permute-start.25 = (bf16[64,2048]{1,0:T(8,128)(2,1)S(1)}, bf16[64,2048]{1,0:T(8,128)(2,1)S(1)}, u32[]{:S(2)}, u32[]{:S(2)}) collective-permute-start(bf16[64,2048]{1,0:T(8,128)(2,1)S(1)} %get-tuple-element.64), channel_id=1, source_target_pairs={{0,4},{1,5},{2,6},{3,7},{4,0},{5,1},{6,2},{7,3},{8,12},{9,13},{10,... | collective-permute-start | bytes 786440 | tf_op jit(solution)/shard_map/ppermute | solution.py:22
  147.6 0.9 add_add_fusion
  149.2 0.7 collective-permute-done.23
  150.0 2.2 %collective-permute-done.26 = bf16[64,2048]{1,0:T(8,128)(2,1)S(1)} collective-permute-done((bf16[64,2048]{1,0:T(8,128)(2,1)S(1)}, bf16[64,2048]{1,0:T(8,128)(2,1)S(1)}, u32[]{:S(2)}, u32[]{:S(2)}) %collective-permute-start.26) | collective-permute-done | bytes 262176 | tf_op jit(solution)/shard_map/ppermute | solution.py:22
  152.1 15.5 %collective-permute-done.25 = bf16[64,2048]{1,0:T(8,128)(2,1)S(1)} collective-permute-done((bf16[64,2048]{1,0:T(8,128)(2,1)S(1)}, bf16[64,2048]{1,0:T(8,128)(2,1)S(1)}, u32[]{:S(2)}, u32[]{:S(2)}) %collective-permute-start.25) | collective-permute-done | bytes 262176 | tf_op jit(solution)/shard_map/ppermute | solution.py:22
  167.7 3.5 %collective-permute-start.29 = (f32[3,6144]{1,0:T(4,128)S(1)}, f32[3,6144]{1,0:T(4,128)S(1)}, u32[]{:S(2)}, u32[]{:S(2)}) collective-permute-start(f32[3,6144]{1,0:T(4,128)S(1)} %slice_add_fusion), channel_id=1, source_target_pairs={{0,6},{1,7},{2,4},{3,5},{4,2},{5,3},{6,0},{7,1},{8,14},{9,15},{10,... | collective-permute-start | bytes 221192 | tf_op jit(solution)/shard_map/ppermute | solution.py:22
  171.2 0.8 collective-permute-start.27
  172.1 0.9 fusion.6
  173.0 2.2 %collective-permute-done.29 = f32[3,6144]{1,0:T(4,128)S(1)} collective-permute-done((f32[3,6144]{1,0:T(4,128)S(1)}, f32[3,6144]{1,0:T(4,128)S(1)}, u32[]{:S(2)}, u32[]{:S(2)}) %collective-permute-start.29) | collective-permute-done | bytes 73760 | tf_op jit(solution)/shard_map/ppermute | solution.py:22
  175.2 3.6 %collective-permute-done.28 = f32[3,6144]{1,0:T(4,128)S(1)} collective-permute-done((f32[3,6144]{1,0:T(4,128)S(1)}, f32[3,6144]{1,0:T(4,128)S(1)}, u32[]{:S(2)}, u32[]{:S(2)}) %collective-permute-start.28) | collective-permute-done | bytes 73760 | tf_op jit(solution)/shard_map/ppermute | solution.py:22
  178.9 0.7 add_multiply_fusion.1
  (65 shorter events, 6.8 us)
Async XLA Ops:
  0.6 24.7 %copy-start = (bf16[512,2048]{1,0:T(8,128)(2,1)S(1)}, bf16[512,2048]{1,0:T(8,128)(2,1)}, u32[]{:S(2)}) copy-start(bf16[512,2048]{1,0:T(8,128)(2,1)} %param.11) | copy-start | bytes 6291460
  0.6 24.7 %collective-permute-start.1 = (bf16[128,2048]{1,0:T(8,128)(2,1)}, bf16[128,2048]{1,0:T(8,128)(2,1)S(1)}, u32[]{:S(2)}, u32[]{:S(2)}) collective-permute-start(bf16[128,2048]{1,0:T(8,128)(2,1)} %refs_5_.3), channel_id=1, source_target_pairs={{0,8},{8,0},{16,24},{24,16},{1,9},{9,1},{17,25},{25,17},{2,10},{10... | collective-permute-start | bytes 1572872 | tf_op jit(solution)/shard_map/ppermute | solution.py:22
  3.6 24.8 %collective-permute-start.3 = (bf16[128,2048]{1,0:T(8,128)(2,1)}, bf16[128,2048]{1,0:T(8,128)(2,1)S(1)}, u32[]{:S(2)}, u32[]{:S(2)}) collective-permute-start(bf16[128,2048]{1,0:T(8,128)(2,1)} %refs_5_.3), channel_id=1, source_target_pairs={{0,16},{8,24},{16,0},{24,8},{1,17},{9,25},{17,1},{25,9},{2,18},{10... | collective-permute-start | bytes 1572872 | tf_op jit(solution)/shard_map/ppermute | solution.py:22
  6.1 9.4 %collective-permute-start = (bf16[2,6144]{1,0:T(2,128)(2,1)S(1)}, bf16[2,6144]{1,0:T(2,128)(2,1)S(1)}, u32[]{:S(2)}, u32[]{:S(2)}) collective-permute-start(bf16[2,6144]{1,0:T(2,128)(2,1)S(1)} %slice.22), channel_id=1, source_target_pairs={{0,1},{1,2},{2,3},{3,4},{4,5},{5,6},{6,7},{8,9},{9,10},{10,11},{11... | collective-permute-start | bytes 73736 | tf_op jit(solution)/shard_map/ppermute | solution.py:18
  7.4 24.1 %collective-permute-start.5 = (bf16[128,2048]{1,0:T(8,128)(2,1)}, bf16[128,2048]{1,0:T(8,128)(2,1)}, u32[]{:S(2)}, u32[]{:S(2)}) collective-permute-start(bf16[128,2048]{1,0:T(8,128)(2,1)} %refs_5_.3), channel_id=1, source_target_pairs={{0,24},{8,16},{16,8},{24,0},{1,25},{9,17},{17,9},{25,1},{2,26},{10... | collective-permute-start | bytes 1572872 | tf_op jit(solution)/shard_map/ppermute | solution.py:22
  19.8 24.1 %all-to-all-start = ((bf16[8,128,256]{2,1,0:T(8,128)(2,1)}), bf16[8,128,256]{2,1,0:T(8,128)(2,1)}, u32[]{:S(2)}, u32[]{:S(2)}) async-start(bf16[8,128,256]{2,1,0:T(8,128)(2,1)} %get-tuple-element.37), calls=%async_computation | async-start | bytes 1048576 | tf_op jit(solution)/shard_map/all_to_all | solution.py:370
  25.4 3.1 %copy-start.9 = (bf16[128,2048]{1,0:T(8,128)(2,1)}, bf16[128,2048]{1,0:T(8,128)(2,1)S(1)}, u32[]{:S(2)}) copy-start(bf16[128,2048]{1,0:T(8,128)(2,1)S(1)} %collective-permute-done.1.refs_6_) | copy-start | bytes 1572868
  26.9 7.5 %copy-start.8 = (bf16[128,2048]{1,0:T(8,128)(2,1)S(1)}, bf16[128,2048]{1,0:T(8,128)(2,1)}, u32[]{:S(2)}) copy-start(bf16[128,2048]{1,0:T(8,128)(2,1)} %refs_5_.3) | copy-start | bytes 1572868
  26.9 8.4 %collective-permute-start.2 = (bf16[128,512]{1,0:T(8,128)(2,1)}, bf16[128,512]{1,0:T(8,128)(2,1)S(1)}, u32[]{:S(2)}, u32[]{:S(2)}) collective-permute-start(bf16[128,512]{1,0:T(8,128)(2,1)} %fusion.1), channel_id=1, source_target_pairs={{0,8},{8,0},{16,24},{24,16},{1,9},{9,1},{17,25},{25,17},{2,10},{10... | collective-permute-start | bytes 393224 | tf_op jit(solution)/shard_map/ppermute | solution.py:22
  28.5 3.0 %copy-start.10 = (bf16[128,2048]{1,0:T(8,128)(2,1)}, bf16[128,2048]{1,0:T(8,128)(2,1)S(1)}, u32[]{:S(2)}) copy-start(bf16[128,2048]{1,0:T(8,128)(2,1)S(1)} %collective-permute-done.3.refs_7_) | copy-start | bytes 1572868
  30.0 11.2 %copy-start.1 = (bf16[8,128,256]{2,1,0:T(8,128)(2,1)S(1)}, bf16[8,128,256]{2,1,0:T(8,128)(2,1)}, u32[]{:S(2)}) copy-start(bf16[8,128,256]{2,1,0:T(8,128)(2,1)} %get-tuple-element.34.refs_1_.refs_2_) | copy-start | bytes 1572868
  30.0 5.9 %collective-permute-start.4 = (bf16[128,512]{1,0:T(8,128)(2,1)}, bf16[128,512]{1,0:T(8,128)(2,1)S(1)}, u32[]{:S(2)}, u32[]{:S(2)}) collective-permute-start(bf16[128,512]{1,0:T(8,128)(2,1)} %fusion.2), channel_id=1, source_target_pairs={{0,16},{8,24},{16,0},{24,8},{1,17},{9,25},{17,1},{25,9},{2,18},{10... | collective-permute-start | bytes 393224 | tf_op jit(solution)/shard_map/ppermute | solution.py:22
  34.0 6.5 %collective-permute-start.6 = (bf16[128,512]{1,0:T(8,128)(2,1)}, bf16[128,512]{1,0:T(8,128)(2,1)S(1)}, u32[]{:S(2)}, u32[]{:S(2)}) collective-permute-start(bf16[128,512]{1,0:T(8,128)(2,1)} %fusion.3), channel_id=1, source_target_pairs={{0,24},{8,16},{16,8},{24,0},{1,25},{9,17},{17,9},{25,1},{2,26},{10... | collective-permute-start | bytes 393224 | tf_op jit(solution)/shard_map/ppermute | solution.py:22
  40.5 0.7 copy-start.6
  41.2 0.9 copy-start.7
  43.1 0.8 copy-start.5
  43.9 57.1 %copy-start.2 = (bf16[8,128,256]{2,1,0:T(8,128)(2,1)}, bf16[8,128,256]{2,1,0:T(8,128)(2,1)S(1)}, u32[]{:S(2)}) copy-start(bf16[8,128,256]{2,1,0:T(8,128)(2,1)S(1)} %get-tuple-element.36.refs_3_) | copy-start | bytes 1572868
  43.9 26.4 %all-to-all-start.1 = ((bf16[8,128,256]{2,1,0:T(8,128)(2,1)}), bf16[8,128,256]{2,1,0:T(8,128)(2,1)}, u32[]{:S(2)}, u32[]{:S(2)}) async-start(bf16[8,128,256]{2,1,0:T(8,128)(2,1)} %copy-done.5), calls=%async_computation.1 | async-start | bytes 1048576 | tf_op jit(solution)/shard_map/all_to_all | solution.py:370
  60.8 2.0 %collective-permute-start.7 = (bf16[4,128,256]{2,1,0:T(8,128)(2,1)}, bf16[4,128,256]{2,1,0:T(8,128)(2,1)}, u32[]{:S(2)}, u32[]{:S(2)}) collective-permute-start(bf16[4,128,256]{2,1,0:T(8,128)(2,1)} %get-tuple-element.73), channel_id=1, source_target_pairs={{0,1},{1,0},{2,3},{3,2},{4,5},{5,4},{6,7},{7,6},{8,9},{9,8},{10,11... | collective-permute-start | bytes 786440 | tf_op jit(solution)/shard_map/ppermute | solution.py:22
  64.5 5.8 %collective-permute-start.8 = (bf16[2,128,256]{2,1,0:T(8,128)(2,1)S(1)}, bf16[2,128,256]{2,1,0:T(8,128)(2,1)S(1)}, u32[]{:S(2)}, u32[]{:S(2)}) collective-permute-start(bf16[2,128,256]{2,1,0:T(8,128)(2,1)S(1)} %get-tuple-element.71), channel_id=1, source_target_pairs={{0,2},{1,3},{2,0},{3,1},{4,6},{5,7},{6,4},{7,5},{8,10},{9,11},{10,... | collective-permute-start | bytes 393224 | tf_op jit(solution)/shard_map/ppermute | solution.py:22
  66.4 26.5 %collective-permute-start.10 = (bf16[2,128,256]{2,1,0:T(8,128)(2,1)}, bf16[2,128,256]{2,1,0:T(8,128)(2,1)S(1)}, u32[]{:S(2)}, u32[]{:S(2)}) collective-permute-start(bf16[2,128,256]{2,1,0:T(8,128)(2,1)} %get-tuple-element.69), channel_id=1, source_target_pairs={{0,6},{1,7},{2,4},{3,5},{4,2},{5,3},{6,0},{7,1},{8,14},{9,15},{10,... | collective-permute-start | bytes 393224 | tf_op jit(solution)/shard_map/ppermute | solution.py:22
  68.8 24.1 %collective-permute-start.9 = (bf16[2,128,256]{2,1,0:T(8,128)(2,1)}, bf16[2,128,256]{2,1,0:T(8,128)(2,1)}, u32[]{:S(2)}, u32[]{:S(2)}) collective-permute-start(bf16[2,128,256]{2,1,0:T(8,128)(2,1)} %get-tuple-element.72), channel_id=1, source_target_pairs={{0,4},{1,5},{2,6},{3,7},{4,0},{5,1},{6,2},{7,3},{8,12},{9,13},{10,... | collective-permute-start | bytes 393224 | tf_op jit(solution)/shard_map/ppermute | solution.py:22
  82.4 26.1 %all-to-all-start.2 = ((bf16[8,130,256]{2,1,0:T(8,128)(2,1)}), bf16[8,130,256]{2,1,0:T(8,128)(2,1)}, u32[]{:S(2)}, u32[]{:S(2)}) async-start(bf16[8,130,256]{2,1,0:T(8,128)(2,1)} %get-tuple-element.43), calls=%async_computation.2 | async-start | bytes 1114112 | tf_op jit(solution)/shard_map/all_to_all | solution.py:375
  89.0 3.3 %collective-permute-start.11 = (bf16[2,8,2,256]{3,2,1,0:T(2,128)(2,1)}, bf16[2,8,2,256]{3,2,1,0:T(2,128)(2,1)S(1)}, u32[]{:S(2)}, u32[]{:S(2)}) collective-permute-start(bf16[2,8,2,256]{3,2,1,0:T(2,128)(2,1)} %pad_maximum_fusion), channel_id=1, source_target_pairs={{1,0},{2,1},{3,2},{4,3},{5,4},{6,5},{7,6},{9,8},{10,9},{11,10},{12... | collective-permute-start | bytes 49160 | tf_op jit(solution)/shard_map/ppermute | solution.py:18
  94.0 9.8 %collective-permute-start.13 = (bf16[256,256]{1,0:T(8,128)(2,1)S(1)}, bf16[256,256]{1,0:T(8,128)(2,1)S(1)}, u32[]{:S(2)}, u32[]{:S(2)}) collective-permute-start(bf16[256,256]{1,0:T(8,128)(2,1)S(1)} %get-tuple-element.66), channel_id=1, source_target_pairs={{0,8},{8,0},{16,24},{24,16},{1,9},{9,1},{17,25},{25,17},{2,10},{10... | collective-permute-start | bytes 393224 | tf_op jit(solution)/shard_map/ppermute | solution.py:22
  94.6 9.7 %collective-permute-start.15 = (bf16[256,256]{1,0:T(8,128)(2,1)S(1)}, bf16[256,256]{1,0:T(8,128)(2,1)S(1)}, u32[]{:S(2)}, u32[]{:S(2)}) collective-permute-start(bf16[256,256]{1,0:T(8,128)(2,1)S(1)} %get-tuple-element.67), channel_id=1, source_target_pairs={{0,24},{8,16},{16,8},{24,0},{1,25},{9,17},{17,9},{25,1},{2,26},{10... | collective-permute-start | bytes 393224 | tf_op jit(solution)/shard_map/ppermute | solution.py:22
  96.1 10.7 %collective-permute-start.14 = (bf16[256,256]{1,0:T(8,128)(2,1)S(1)}, bf16[256,256]{1,0:T(8,128)(2,1)S(1)}, u32[]{:S(2)}, u32[]{:S(2)}) collective-permute-start(bf16[256,256]{1,0:T(8,128)(2,1)S(1)} %get-tuple-element.68), channel_id=1, source_target_pairs={{0,16},{8,24},{16,0},{24,8},{1,17},{9,25},{17,1},{25,9},{2,18},{10... | collective-permute-start | bytes 393224 | tf_op jit(solution)/shard_map/ppermute | solution.py:22
  100.3 0.6 copy-start.4
  100.9 0.8 copy-start.3
  101.7 6.8 %collective-permute-start.12 = (f32[8,2,256]{2,1,0:T(2,128)S(1)}, f32[8,2,256]{2,1,0:T(2,128)S(1)}, u32[]{:S(2)}, u32[]{:S(2)}) collective-permute-start(f32[8,2,256]{2,1,0:T(2,128)S(1)} %convert_multiply_fusion), channel_id=1, source_target_pairs={{1,0},{2,1},{3,2},{4,3},{5,4},{6,5},{7,6},{9,8},{10,9},{11,10},{12... | collective-permute-start | bytes 49160 | tf_op jit(solution)/shard_map/ppermute | solution.py:18
  103.2 5.3 %collective-permute-start.16 = (bf16[128,512]{1,0:T(8,128)(2,1)}, bf16[128,512]{1,0:T(8,128)(2,1)S(1)}, u32[]{:S(2)}, u32[]{:S(2)}) collective-permute-start(bf16[128,512]{1,0:T(8,128)(2,1)} %get-tuple-element.55), channel_id=1, source_target_pairs={{0,8},{8,0},{16,24},{24,16},{1,9},{9,1},{17,25},{25,17},{2,10},{10... | collective-permute-start | bytes 393224 | tf_op jit(solution)/shard_map/ppermute | solution.py:22
  103.8 5.6 %collective-permute-start.17 = (bf16[128,512]{1,0:T(8,128)(2,1)}, bf16[128,512]{1,0:T(8,128)(2,1)S(1)}, u32[]{:S(2)}, u32[]{:S(2)}) collective-permute-start(bf16[128,512]{1,0:T(8,128)(2,1)} %get-tuple-element.56), channel_id=1, source_target_pairs={{0,16},{8,24},{16,0},{24,8},{1,17},{9,25},{17,1},{25,9},{2,18},{10... | collective-permute-start | bytes 393224 | tf_op jit(solution)/shard_map/ppermute | solution.py:22
  104.3 7.5 %collective-permute-start.18 = (bf16[128,512]{1,0:T(8,128)(2,1)}, bf16[128,512]{1,0:T(8,128)(2,1)S(1)}, u32[]{:S(2)}, u32[]{:S(2)}) collective-permute-start(bf16[128,512]{1,0:T(8,128)(2,1)} %get-tuple-element.57), channel_id=1, source_target_pairs={{0,24},{8,16},{16,8},{24,0},{1,25},{9,17},{17,9},{25,1},{2,26},{10... | collective-permute-start | bytes 393224 | tf_op jit(solution)/shard_map/ppermute | solution.py:22
  108.5 17.4 %copy-start.16 = (f32[8,2,256]{2,1,0:T(2,128)}, f32[8,2,256]{2,1,0:T(2,128)S(1)}, u32[]{:S(2)}) copy-start(f32[8,2,256]{2,1,0:T(2,128)S(1)} %collective-permute-done.12.refs_8_) | copy-start | bytes 49156
  108.5 3.3 %copy-start.13 = (bf16[128,512]{1,0:T(8,128)(2,1)}, bf16[128,512]{1,0:T(8,128)(2,1)S(1)}, u32[]{:S(2)}) copy-start(bf16[128,512]{1,0:T(8,128)(2,1)S(1)} %collective-permute-done.16.refs_2_) | copy-start | bytes 393220
  109.4 2.4 %copy-start.14 = (bf16[128,512]{1,0:T(8,128)(2,1)}, bf16[128,512]{1,0:T(8,128)(2,1)S(1)}, u32[]{:S(2)}) copy-start(bf16[128,512]{1,0:T(8,128)(2,1)S(1)} %collective-permute-done.17.refs_3_) | copy-start | bytes 393220
  111.8 0.6 copy-start.15
  116.6 3.9 %collective-permute-start.19 = (bf16[256,2048]{1,0:T(8,128)(2,1)}, bf16[256,2048]{1,0:T(8,128)(2,1)S(1)}, u32[]{:S(2)}, u32[]{:S(2)}) collective-permute-start(bf16[256,2048]{1,0:T(8,128)(2,1)} %other_share.1), channel_id=1, source_target_pairs={{0,1},{1,0},{2,3},{3,2},{4,5},{5,4},{6,7},{7,6},{8,9},{9,8},{10,11... | collective-permute-start | bytes 3145736 | tf_op jit(solution)/shard_map/ppermute | solution.py:22
  120.4 1.0 copy-start.12
  125.9 9.4 %copy-start.11 = (bf16[256,2048]{1,0:T(8,128)(2,1)S(1)}, bf16[256,2048]{1,0:T(8,128)(2,1)}, u32[]{:S(2)}) copy-start(bf16[256,2048]{1,0:T(8,128)(2,1)} %own_share.1) | copy-start | bytes 3145732
  131.8 15.4 %collective-permute-start.22 = (f32[4,6144]{1,0:T(4,128)}, f32[4,6144]{1,0:T(4,128)S(1)}, u32[]{:S(2)}, u32[]{:S(2)}) collective-permute-start(f32[4,6144]{1,0:T(4,128)} %get-tuple-element.61), channel_id=1, source_target_pairs={{0,24},{8,16},{16,8},{24,0},{1,25},{9,17},{17,9},{25,1},{2,26},{10... | collective-permute-start | bytes 294920 | tf_op jit(solution)/shard_map/ppermute | solution.py:22
  133.3 14.3 %collective-permute-start.21 = (f32[4,6144]{1,0:T(4,128)}, f32[4,6144]{1,0:T(4,128)S(1)}, u32[]{:S(2)}, u32[]{:S(2)}) collective-permute-start(f32[4,6144]{1,0:T(4,128)} %get-tuple-element.61), channel_id=1, source_target_pairs={{0,16},{8,24},{16,0},{24,8},{1,17},{9,25},{17,1},{25,9},{2,18},{10... | collective-permute-start | bytes 294920 | tf_op jit(solution)/shard_map/ppermute | solution.py:22
  134.8 12.8 %collective-permute-start.20 = (f32[4,6144]{1,0:T(4,128)}, f32[4,6144]{1,0:T(4,128)S(1)}, u32[]{:S(2)}, u32[]{:S(2)}) collective-permute-start(f32[4,6144]{1,0:T(4,128)} %get-tuple-element.61), channel_id=1, source_target_pairs={{0,8},{8,0},{16,24},{24,16},{1,9},{9,1},{17,25},{25,17},{2,10},{10... | collective-permute-start | bytes 294920 | tf_op jit(solution)/shard_map/ppermute | solution.py:22
  135.4 16.7 %collective-permute-start.26 = (bf16[64,2048]{1,0:T(8,128)(2,1)S(1)}, bf16[64,2048]{1,0:T(8,128)(2,1)S(1)}, u32[]{:S(2)}, u32[]{:S(2)}) collective-permute-start(bf16[64,2048]{1,0:T(8,128)(2,1)S(1)} %get-tuple-element.63), channel_id=1, source_target_pairs={{0,6},{1,7},{2,4},{3,5},{4,2},{5,3},{6,0},{7,1},{8,14},{9,15},{10,... | collective-permute-start | bytes 786440 | tf_op jit(solution)/shard_map/ppermute | solution.py:22
  145.1 22.6 %collective-permute-start.25 = (bf16[64,2048]{1,0:T(8,128)(2,1)S(1)}, bf16[64,2048]{1,0:T(8,128)(2,1)S(1)}, u32[]{:S(2)}, u32[]{:S(2)}) collective-permute-start(bf16[64,2048]{1,0:T(8,128)(2,1)S(1)} %get-tuple-element.64), channel_id=1, source_target_pairs={{0,4},{1,5},{2,6},{3,7},{4,0},{5,1},{6,2},{7,3},{8,12},{9,13},{10,... | collective-permute-start | bytes 786440 | tf_op jit(solution)/shard_map/ppermute | solution.py:22
  147.1 20.5 %collective-permute-start.24 = (bf16[64,2048]{1,0:T(8,128)(2,1)S(1)}, bf16[64,2048]{1,0:T(8,128)(2,1)S(1)}, u32[]{:S(2)}, u32[]{:S(2)}) collective-permute-start(bf16[64,2048]{1,0:T(8,128)(2,1)S(1)} %get-tuple-element.65), channel_id=1, source_target_pairs={{0,2},{1,3},{2,0},{3,1},{4,6},{5,7},{6,4},{7,5},{8,10},{9,11},{10,... | collective-permute-start | bytes 786440 | tf_op jit(solution)/shard_map/ppermute | solution.py:22
  148.6 1.4 collective-permute-start.23
  167.7 7.6 %collective-permute-start.29 = (f32[3,6144]{1,0:T(4,128)S(1)}, f32[3,6144]{1,0:T(4,128)S(1)}, u32[]{:S(2)}, u32[]{:S(2)}) collective-permute-start(f32[3,6144]{1,0:T(4,128)S(1)} %slice_add_fusion), channel_id=1, source_target_pairs={{0,6},{1,7},{2,4},{3,5},{4,2},{5,3},{6,0},{7,1},{8,14},{9,15},{10,... | collective-permute-start | bytes 221192 | tf_op jit(solution)/shard_map/ppermute | solution.py:22
  171.2 7.7 %collective-permute-start.28 = (f32[3,6144]{1,0:T(4,128)S(1)}, f32[3,6144]{1,0:T(4,128)S(1)}, u32[]{:S(2)}, u32[]{:S(2)}) collective-permute-start(f32[3,6144]{1,0:T(4,128)S(1)} %slice_add_fusion), channel_id=1, source_target_pairs={{0,4},{1,5},{2,6},{3,7},{4,0},{5,1},{6,2},{7,3},{8,12},{9,13},{10,... | collective-permute-start | bytes 221192 | tf_op jit(solution)/shard_map/ppermute | solution.py:22
  171.2 7.7 %collective-permute-start.27 = (f32[3,6144]{1,0:T(4,128)S(1)}, f32[3,6144]{1,0:T(4,128)S(1)}, u32[]{:S(2)}, u32[]{:S(2)}) collective-permute-start(f32[3,6144]{1,0:T(4,128)S(1)} %slice_add_fusion), channel_id=1, source_target_pairs={{0,2},{1,3},{2,0},{3,1},{4,6},{5,7},{6,4},{7,5},{8,10},{9,11},{10,... | collective-permute-start | bytes 221192 | tf_op jit(solution)/shard_map/ppermute | solution.py:22

commit v10 on v8

--- a/solution.py
+++ b/solution.py
@@ -77,6 +77,32 @@
     )(*args)
 
 
+def joined(pieces):
+    count, rows = (len(pieces), pieces[0].shape[0])
+
+    def kernel(*refs):
+        ins, out_ref, sems = refs[:count], refs[count], refs[count + 1]
+        copies = [
+            pltpu.make_async_copy(ref, out_ref.at[pl.ds(k * rows, rows)], sems.at[k])
+            for k, ref in enumerate(ins)
+        ]
+        for copy in copies:
+            copy.start()
+        for copy in copies:
+            copy.wait()
+
+    anywhere = pl.BlockSpec(memory_space=pl.ANY)
+    return pl.pallas_call(
+        kernel,
+        out_shape=jax.ShapeDtypeStruct((count * rows, pieces[0].shape[1]), pieces[0].dtype),
+        in_specs=[anywhere] * count,
+        out_specs=anywhere,
+        scratch_shapes=[pltpu.SemaphoreType.DMA((count,))],
+        cost_estimate=pl.CostEstimate(flops=0, transcendentals=0, bytes_accessed=0),
+        name="joined",
+    )(*pieces)
+
+
 def columns(index, size):
     return slice(index * size, (index + 1) * size)
 
@@ -130,12 +156,13 @@
                 piece[:, columns(c % 2 * (parts // 2) + c // 2, size)] = gate[:, columns(q, size)]
 
 
-def final_kernel(*refs):
+def final_kernel(me_ref, *refs):
     proj_ref, prev_ref, taps_ref, gate_grad_ref, long_ref, back_ref, keyed_ref, valued_ref = refs[:8]
     query_after_ref, pair_after_ref, skip_ref, out_ref, sums_ref = refs[8:]
     parts, rows, blk = long_ref.shape
     sums_ref[3:4, :] = jnp.zeros((1, sums_ref.shape[1]), F32)
-    sums_ref[3:4, 0:blk] = skip_ref[...]
+    for b in range(parts):
+        sums_ref[3:4, columns(b, blk)] = jnp.where(me_ref[0] == b, skip_ref[...], 0.0)
     for b in range(parts):
         back = back_ref[b, 0:rows].astype(F32)
         back_after = back_ref[b, rows : rows + 2].astype(F32)
@@ -203,8 +230,9 @@
 
 
 def filter_kernel(waves_ref, filter_ref, spec_ref):
+    values = filter_ref[...].astype(BF16)
     for i in range(2):
-        spec_ref[i] = dot(filter_ref[...], waves_ref[i], 1, 1)
+        spec_ref[i] = dot(values, waves_ref[i], 1, 1)
 
 
 def out_kernel(waves_ref, filter_spec_ref, product_ref, skip_ref, spec_ref, long_ref, turned, total):
@@ -383,11 +411,13 @@
         scratch = [pltpu.VMEM((blk, seq_len), BF16), pltpu.VMEM((blk, seq_len), F32)]
         skip_row = skip_gain[None, :]
         (filter_spec,) = chunked(
-            filter_kernel, "filter_spectrum", waves, [], [filter_b], [], [spec], []
+            filter_kernel, "filter_spectrum", waves, [], [long_filter], [], [spec], []
         )
         weights = ordered(out_proj, filter_spec)
     found = [dot(cot, weights, 1, 1).astype(BF16) for cot in cots]
     found = [found[0]] + [swapped(found[k], "dp", k) for k in range(1, parts_dp)]
+    cot_all = joined(cots)
+    found[0] = ordered(found[0], cot_all)
     gate_grad, grad_long_out = call(
         grad_long_kernel, "grad_long", [plane] * 2, 1, 12, me_dp, query, *found
     )
@@ -427,7 +457,7 @@
             "grad_product",
             waves,
             [filter_spec, product_spec],
-            [ordered(grad_long, *long_came[1:]), product, skip_row],
+            [ordered(grad_long, long_came[1]), product, skip_row],
             [
                 jax.ShapeDtypeStruct((parts, rows + 2, blk), BF16),
                 jax.ShapeDtypeStruct((blk, seq_len), F32),
@@ -464,9 +494,9 @@
     gates = [gates[0]] + [swapped(gates[k], "dp", k) for k in range(1, parts_dp)]
     query_heads = gate_grad[:, :2].astype(F32) * long_out[:, :2].astype(F32)
     query_after = passed_along(query_heads, "context", -1)
-    early = (grad_product, query_after)
+    grad_filter = summed_blocks(lag_sum, "dp", 1) * (scale_factor * inverse)
+    early = (grad_product, query_after, grad_filter)
     gate_all = ordered(jnp.concatenate(gates, 0), *early)
-    cot_all = jnp.concatenate(cots, 0)
     pair, shares = own_share(gate_all, cot_all, parts)
     grad_product = ordered(grad_product, pair)
 
@@ -477,8 +507,9 @@
             jax.ShapeDtypeStruct((rows, width), BF16),
             jax.ShapeDtypeStruct((4, width), F32),
         ],
-        0,
+        1,
         60,
+        me[None],
         projected,
         prev_rows,
         short_taps,
@@ -493,12 +524,11 @@
     )
 
     tap_sums = all_sum(tap_sums, "dp", bits_of(parts_dp))
-    lag_sum = ordered(lag_sum, tap_sums)
-    grad_filter = summed_blocks(lag_sum, "dp", 1) * (scale_factor * inverse)
-    grad_skip = tap_sums[3, :blk] * scale_factor
-    tap_sums = tap_sums[:3] + swapped(tap_sums[:3], "context", 1)
-    tap_sums = ordered(tap_sums, *shares[1:])
-    grad_taps = all_sum(tap_sums, "context", bits_of(parts, 2)) * scale_factor
+    tap_sums = ordered(tap_sums + swapped(tap_sums, "context", 1), *shares[1:])
+    tap_sums = all_sum(tap_sums, "context", bits_of(parts, 2)) * scale_factor
+    grad_taps = tap_sums[:3]
+    skip_blocks = tap_sums[3, :chans].reshape(parts, blk)
+    grad_skip = lax.dynamic_index_in_dim(skip_blocks, me, 0, False)
     grad_proj = sum(share.astype(F32) for share in shares) * scale_factor
     return (grad_inputs, grad_taps, grad_filter, grad_skip, grad_proj)
 

time: 171 us -> 231 us (1.35)
  Pallas kernels: 33.6 us -> 99.1 us
  local copies, waits for them, and re-layouts: 14.3 us -> 9.25 us
    pallas_call x0 -> x1, Pallas kernels: none -> 64.7 us  [joined(): pl.pallas_call(kernel, out_shape=jax.ShapeDtypeStruct((count * rows, piec...]
    unnamed x31 -> x24, local copies, waits for them, and re-layouts: 8.76 us -> 3.15 us
    ppermute x27, waiting for transfers between devices: 39.8 us -> 35.8 us  [swapped(): lax.ppermute(value, axis, [(i, i ^ mask) for i in range(lax.axis_size(axi...]
  transfers between devices with their start and end apart: 33 -> 33, of which waited for: 16 -> 12; matrix products, arithmetic and copies ran while one was open for 15% -> 9% of each run, Pallas kernels for 11% -> 41%
where the time goes in v10:
time: 231 us; the launch traced here: 229 us
  Pallas kernels  99.1 us (43%)
  starting transfers between devices  61.5 us (27%)
  waiting for transfers between devices  37.8 us (16%)
  matrix products  11.6 us (5%)
  other arithmetic  9.29 us (4%)
  local copies, waits for them, and re-layouts  9.25 us (4%)
    pallas_call x1, Pallas kernels, joined(): pl.pallas_call(kernel, out_shape=jax.ShapeDtypeStruct((count * rows, piec...  64.7 us
    ppermute x27, starting transfers between devices, swapped(): lax.ppermute(value, axis, [(i, i ^ mask) for i in range(lax.axis_size(axi...  41.7 us
    ppermute x27, waiting for transfers between devices, swapped(): lax.ppermute(value, axis, [(i, i ^ mask) for i in range(lax.axis_size(axi...  35.8 us
    pallas_call x3, Pallas kernels, chunked(): pl.pallas_call(kernel, out_shape=spec_out + outs, grid=(freqs // size,),...  21.7 us
    pallas_call x4, Pallas kernels, call(): pl.pallas_call(run, out_shape=outs, in_specs=[SMEM] * smem + [anywhere] *...  12.8 us
    dot_general x6, matrix products, dot(): lax.dot_general(left, right, (((left_dim,), (right_dim,)), ((), ())), pre...  11.6 us
    all_to_all x2, starting transfers between devices, to_channels(): lax.all_to_all(blocks, 'context', split_axis=0, concat_axis=0, tiled=True)  10.5 us
    all_to_all x1, starting transfers between devices, to_positions(): lax.all_to_all(blocks, 'context', split_axis=0, concat_axis=0, tiled=True)  5.17 us
  transfers between devices with their start and end apart: 33, of which 12 were waited for; matrix products, arithmetic and copies ran while one was open for 9% of the time, Pallas kernels for 41%

profile of v10, /device:TPU:0, one launch (start us, length us, event | category | flops | bytes accessed | tf_op | source)
XLA Modules:
  0.0 229.5 jit_solution(17578795415661439204)
XLA Ops:
  0.6 3.0 %collective-permute-start.1 = (bf16[128,2048]{1,0:T(8,128)(2,1)}, bf16[128,2048]{1,0:T(8,128)(2,1)S(1)}, u32[]{:S(2)}, u32[]{:S(2)}) collective-permute-start(bf16[128,2048]{1,0:T(8,128)(2,1)} %refs_0_.3), channel_id=1, source_target_pairs={{0,8},{8,0},{16,24},{24,16},{1,9},{9,1},{17,25},{25,17},{2,10},{10... | collective-permute-start | bytes 1572872 | tf_op jit(solution)/shard_map/ppermute | solution.py:22
  3.6 1.5 collective-permute-start.2
  5.2 0.9 slice.21
  6.1 1.3 collective-permute-start
  7.8 5.5 %filter_spectrum.1.filter_spec_ref = f32[2,256,1024]{2,1,0:T(8,128)} custom-call(bf16[2,1024,1024]{2,1,0:T(8,128)(2,1)} %constant.86.clone.waves_ref, f32[256,1024]{1,0:T(8,128)} %filter_ref.1), custom_call_target="tpu_custom_call" | custom-call | tf_op jit(solution)/shard_map/filter_spectrum/pallas_call | solution.py:303
  14.0 3.6 %short_convs.1 = (bf16[8,128,256]{2,1,0:T(8,128)(2,1)}, bf16[8,128,256]{2,1,0:T(8,128)(2,1)}, bf16[8,128,256]{2,1,0:T(8,128)(2,1)}, bf16[8,128,256]{2,1,0:T(8,128)(2,1)}) custom-call(bf16[128,6144]{1,0:T(8,128)(2,1)} %refs_1_.1, f32[2,6144]{1,0:T(2,128)} %convert_element_type.78.refs_1_.refs_2_, f32[3,6144]{1,0:T(4,128)} %refs_3_.1), custom_call_target="tpu_custom_call" | custom-call | tf_op jit(solution)/shard_map/short_convs/pallas_call | solution.py:67
  17.6 5.6 %all-to-all-start = ((bf16[8,128,256]{2,1,0:T(8,128)(2,1)}), bf16[8,128,256]{2,1,0:T(8,128)(2,1)}, u32[]{:S(2)}, u32[]{:S(2)}) async-start(bf16[8,128,256]{2,1,0:T(8,128)(2,1)} %get-tuple-element.40), calls=%async_computation | async-start | bytes 1048576 | tf_op jit(solution)/shard_map/all_to_all | solution.py:378
  23.2 1.5 fusion.2
  24.7 1.5 collective-permute-start.4
  26.2 2.3 collective-permute-done.2.refs_2_
  28.5 1.5 fusion.3
  30.0 1.5 collective-permute-start.5
  31.5 1.9 fusion.4
  33.5 0.8 fusion.1.refs_2_
  34.3 64.7 %joined.1 = bf16[512,2048]{1,0:T(8,128)(2,1)} custom-call(bf16[128,2048]{1,0:T(8,128)(2,1)} %refs_0_.3, bf16[128,2048]{1,0:T(8,128)(2,1)} %copy-done.8, bf16[128,2048]{1,0:T(8,128)(2,1)} %copy-done.9, bf16[128,2048]{1,0:T(8,128)(2,1)} %collective-permute-done.3.refs_3_), custom_call_target="tpu_custom_call" | custom-call | tf_op jit(solution)/shard_map/joined/pallas_call | solution.py:95
  99.1 0.6 copy-done.5
  99.7 0.9 copy-done.6
  100.6 1.0 grad_long.1
  101.6 0.8 copy-done.4
  102.4 4.9 %all-to-all-start.1 = ((bf16[8,128,256]{2,1,0:T(8,128)(2,1)}), bf16[8,128,256]{2,1,0:T(8,128)(2,1)}, u32[]{:S(2)}, u32[]{:S(2)}) async-start(bf16[8,128,256]{2,1,0:T(8,128)(2,1)} %copy-done.4), calls=%async_computation.1 | async-start | bytes 1048576 | tf_op jit(solution)/shard_map/all_to_all | solution.py:378
  107.3 7.4 %long_out.1 = (f32[2,256,1024]{2,1,0:T(8,128)}, bf16[1024,256]{1,0:T(8,128)(2,1)}) custom-call(bf16[2,1024,1024]{2,1,0:T(8,128)(2,1)} %constant.86.clone.waves_ref, f32[2,256,1024]{2,1,0:T(8,128)} %filter_spectrum.1.filter_spec_ref, bf16[1024,256]{1,0:T(8,128)(2,1)} %bitcast.6.product_ref, f32[1,256]{1,0:T(1,128)} %bitcast.56), custom_call_target="tpu_custom_call" | custom-call | tf_op jit(solution)/shard_map/long_out/pallas_call | solution.py:303
  114.6 1.8 dynamic-slice_bitcast_fusion.3
  116.9 1.5 collective-permute-done.7
  118.4 1.7 fusion.10
  120.1 1.9 collective-permute-start.8
  122.0 2.4 %collective-permute-start.10 = (bf16[2,128,256]{2,1,0:T(8,128)(2,1)}, bf16[2,128,256]{2,1,0:T(8,128)(2,1)S(1)}, u32[]{:S(2)}, u32[]{:S(2)}) collective-permute-start(bf16[2,128,256]{2,1,0:T(8,128)(2,1)} %get-tuple-element.73), channel_id=1, source_target_pairs={{0,6},{1,7},{2,4},{3,5},{4,2},{5,3},{6,0},{7,1},{8,14},{9,15},{10,... | collective-permute-start | bytes 393224 | tf_op jit(solution)/shard_map/ppermute | solution.py:22
  124.3 1.5 collective-permute-done.8.refs_4_
  125.9 8.8 %grad_product.1 = (bf16[8,130,256]{2,1,0:T(8,128)(2,1)}, f32[256,1024]{1,0:T(8,128)}, f32[1,256]{1,0:T(1,128)}) custom-call(bf16[2,1024,1024]{2,1,0:T(8,128)(2,1)} %constant.86.clone.waves_ref, f32[2,256,1024]{2,1,0:T(8,128)} %filter_spectrum.1.filter_spec_ref, f32[2,256,1024]{2,1,0:T(8,128)} %get-tuple-element.44.spec_ref, ...), custom_call_target="tpu_custom_call" | custom-call | tf_op jit(solution)/shard_map/grad_product/pallas_call | solution.py:303
  134.6 5.2 %all-to-all-start.2 = ((bf16[8,130,256]{2,1,0:T(8,128)(2,1)}), bf16[8,130,256]{2,1,0:T(8,128)(2,1)}, u32[]{:S(2)}, u32[]{:S(2)}) async-start(bf16[8,130,256]{2,1,0:T(8,128)(2,1)} %get-tuple-element.46), calls=%async_computation.2 | async-start | bytes 1114112 | tf_op jit(solution)/shard_map/all_to_all | solution.py:383
  139.8 0.8 slice_bitcast_fusion
  141.2 1.3 collective-permute-start.11
  142.6 2.0 collective-permute-done.11
  145.2 1.2 dynamic-slice_convert_fusion.2
  146.3 2.0 collective-permute-start.16
  148.3 1.5 collective-permute-start.18
  149.9 2.4 %gate.1 = (bf16[8,128,256]{2,1,0:T(8,128)(2,1)S(1)}, bf16[128,512]{1,0:T(8,128)(2,1)S(1)}, bf16[128,512]{1,0:T(8,128)(2,1)S(1)}, bf16[128,512]{1,0:T(8,128)(2,1)S(1)}, bf16[128,512]{1,0:T(8,128)(2,1)S(1)}) custom-call(s32[1]{0:T(128)} %bitcast.refs_0_, s32[1]{0:T(128)} %bitcast.1.refs_0_.refs_1_, bf16[8,128,256]{2,1,0:T(8,128)(2,1)S(1)} %copy-done.1, ...), custom_call_target="tpu_custom_call" | custom-call | tf_op jit(solution)/shard_map/gate/pallas_call | solution.py:67
  152.4 0.8 copy-done.3
  153.1 1.5 collective-permute-start.15
  154.6 2.0 collective-permute-start.12
  156.6 1.5 collective-permute-start.13
  158.2 1.7 add_multiply_fusion
  159.9 1.9 collective-permute-done.13
  161.8 2.8 %collective-permute-done.14 = bf16[128,512]{1,0:T(8,128)(2,1)S(1)} collective-permute-done((bf16[128,512]{1,0:T(8,128)(2,1)S(1)}, bf16[128,512]{1,0:T(8,128)(2,1)S(1)}, u32[]{:S(2)}, u32[]{:S(2)}) %collective-permute-start.14) | collective-permute-done | bytes 131104 | tf_op jit(solution)/shard_map/ppermute | solution.py:22
  164.7 3.3 %convolution_convert_fusion = bf16[256,2048]{1,0:T(8,128)(2,1)} fusion(bf16[512,2048]{1,0:T(8,128)(2,1)} %joined.1, bf16[512,512]{1,0:T(8,128)(2,1)S(1)} %pad_maximum_fusion, s32[]{:T(128)S(6)} %select_n.74), kind=kOutput, calls=%fused_computation.2 | convolution fusion | flops 537395200 | bytes 3407876 | tf_op jit(solution)/shard_map/dot_general | solution.py:214
  168.0 1.0 collective-permute-start.19
  169.0 2.6 %collective-permute-done.19 = bf16[256,2048]{1,0:T(8,128)(2,1)} collective-permute-done((bf16[256,2048]{1,0:T(8,128)(2,1)}, bf16[256,2048]{1,0:T(8,128)(2,1)}, u32[]{:S(2)}, u32[]{:S(2)}) %collective-permute-start.19) | collective-permute-done | bytes 1048608 | tf_op jit(solution)/shard_map/ppermute | solution.py:22
  171.6 2.6 %fusion = bf16[256,2048]{1,0:T(8,128)(2,1)S(1)} fusion(bf16[512,256]{1,0:T(8,128)(2,1)S(1)} %constant_dynamic-slice_fusion.1, bf16[512,2048]{1,0:T(8,128)(2,1)} %joined.1, bf16[256,2048]{1,0:T(8,128)(2,1)} %collective-permute-done.19), kind=kOutput, calls=%fused_computation.1 | convolution fusion | flops 538443776 | bytes 4456448 | tf_op jit(solution)/shard_map/dot_general | solution.py:214
  174.2 5.8 %stream_grads.1 = (bf16[128,6144]{1,0:T(8,128)(2,1)}, f32[4,6144]{1,0:T(4,128)}) custom-call(s32[1]{0:T(128)} %bitcast.refs_0_, bf16[128,6144]{1,0:T(8,128)(2,1)} %refs_1_.1, f32[2,6144]{1,0:T(2,128)} %convert_element_type.78.refs_1_.refs_2_, f32[3,6144]{1,0:T(4,128)} %refs_3_.1, bf16[8,128,256]{2,1,0:T(8,128)(2,1)} %copy-done.2, ...), custom_call_target="tpu_custom_call" | custom-call | tf_op jit(solution)/shard_map/stream_grads/pallas_call | solution.py:67
  180.0 1.6 collective-permute-start.22
  181.6 1.0 collective-permute-start.21
  182.6 1.0 collective-permute-start.20
  183.6 0.8 dynamic-slice_bitcast_fusion
  184.4 10.2 %collective-permute-start.26 = (bf16[64,2048]{1,0:T(8,128)(2,1)}, bf16[64,2048]{1,0:T(8,128)(2,1)}, u32[]{:S(2)}, u32[]{:S(2)}) collective-permute-start(bf16[64,2048]{1,0:T(8,128)(2,1)} %get-tuple-element.67), channel_id=1, source_target_pairs={{0,6},{1,7},{2,4},{3,5},{4,2},{5,3},{6,0},{7,1},{8,14},{9,15},{10,... | collective-permute-start | bytes 786440 | tf_op jit(solution)/shard_map/ppermute | solution.py:22
  194.6 2.0 collective-permute-start.25
  197.2 0.9 add_add_fusion
  198.2 1.4 collective-permute-done.23
  199.6 0.9 add.116
  200.6 1.5 collective-permute-done.26
  202.1 15.5 %collective-permute-done.25 = bf16[64,2048]{1,0:T(8,128)(2,1)} collective-permute-done((bf16[64,2048]{1,0:T(8,128)(2,1)}, bf16[64,2048]{1,0:T(8,128)(2,1)}, u32[]{:S(2)}, u32[]{:S(2)}) %collective-permute-start.25) | collective-permute-done | bytes 262176 | tf_op jit(solution)/shard_map/ppermute | solution.py:22
  217.6 3.5 %collective-permute-start.29 = (f32[4,6144]{1,0:T(4,128)S(1)}, f32[4,6144]{1,0:T(4,128)S(1)}, u32[]{:S(2)}, u32[]{:S(2)}) collective-permute-start(f32[4,6144]{1,0:T(4,128)S(1)} %add.116), channel_id=1, source_target_pairs={{0,6},{1,7},{2,4},{3,5},{4,2},{5,3},{6,0},{7,1},{8,14},{9,15},{10,... | collective-permute-start | bytes 294920 | tf_op jit(solution)/shard_map/ppermute | solution.py:22
  221.1 0.8 collective-permute-start.27
  222.0 2.0 fusion.7
  224.0 1.1 collective-permute-done.29
  225.1 3.6 %collective-permute-done.28 = f32[4,6144]{1,0:T(4,128)S(1)} collective-permute-done((f32[4,6144]{1,0:T(4,128)S(1)}, f32[4,6144]{1,0:T(4,128)S(1)}, u32[]{:S(2)}, u32[]{:S(2)}) %collective-permute-start.28) | collective-permute-done | bytes 98336 | tf_op jit(solution)/shard_map/ppermute | solution.py:22
  (60 shorter events, 4.5 us)
Async XLA Ops:
  0.6 22.6 %copy-start = (bf16[512,2048]{1,0:T(8,128)(2,1)S(1)}, bf16[512,2048]{1,0:T(8,128)(2,1)}, u32[]{:S(2)}) copy-start(bf16[512,2048]{1,0:T(8,128)(2,1)} %param.11) | copy-start | bytes 6291460
  0.6 22.6 %collective-permute-start.1 = (bf16[128,2048]{1,0:T(8,128)(2,1)}, bf16[128,2048]{1,0:T(8,128)(2,1)S(1)}, u32[]{:S(2)}, u32[]{:S(2)}) collective-permute-start(bf16[128,2048]{1,0:T(8,128)(2,1)} %refs_0_.3), channel_id=1, source_target_pairs={{0,8},{8,0},{16,24},{24,16},{1,9},{9,1},{17,25},{25,17},{2,10},{10... | collective-permute-start | bytes 1572872 | tf_op jit(solution)/shard_map/ppermute | solution.py:22
  3.6 24.8 %collective-permute-start.2 = (bf16[128,2048]{1,0:T(8,128)(2,1)}, bf16[128,2048]{1,0:T(8,128)(2,1)S(1)}, u32[]{:S(2)}, u32[]{:S(2)}) collective-permute-start(bf16[128,2048]{1,0:T(8,128)(2,1)} %refs_0_.3), channel_id=1, source_target_pairs={{0,16},{8,24},{16,0},{24,8},{1,17},{9,25},{17,1},{25,9},{2,18},{10... | collective-permute-start | bytes 1572872 | tf_op jit(solution)/shard_map/ppermute | solution.py:22
  6.1 7.3 %collective-permute-start = (bf16[2,6144]{1,0:T(2,128)(2,1)S(1)}, bf16[2,6144]{1,0:T(2,128)(2,1)S(1)}, u32[]{:S(2)}, u32[]{:S(2)}) collective-permute-start(bf16[2,6144]{1,0:T(2,128)(2,1)S(1)} %slice.21), channel_id=1, source_target_pairs={{0,1},{1,2},{2,3},{3,4},{4,5},{5,6},{6,7},{8,9},{9,10},{10,11},{11... | collective-permute-start | bytes 73736 | tf_op jit(solution)/shard_map/ppermute | solution.py:18
  7.4 24.1 %collective-permute-start.3 = (bf16[128,2048]{1,0:T(8,128)(2,1)}, bf16[128,2048]{1,0:T(8,128)(2,1)}, u32[]{:S(2)}, u32[]{:S(2)}) collective-permute-start(bf16[128,2048]{1,0:T(8,128)(2,1)} %refs_0_.3), channel_id=1, source_target_pairs={{0,24},{8,16},{16,8},{24,0},{1,25},{9,17},{17,9},{25,1},{2,26},{10... | collective-permute-start | bytes 1572872 | tf_op jit(solution)/shard_map/ppermute | solution.py:22
  17.6 84.8 %all-to-all-start = ((bf16[8,128,256]{2,1,0:T(8,128)(2,1)}), bf16[8,128,256]{2,1,0:T(8,128)(2,1)}, u32[]{:S(2)}, u32[]{:S(2)}) async-start(bf16[8,128,256]{2,1,0:T(8,128)(2,1)} %get-tuple-element.40), calls=%async_computation | async-start | bytes 1048576 | tf_op jit(solution)/shard_map/all_to_all | solution.py:378
  23.2 6.8 %copy-start.8 = (bf16[128,2048]{1,0:T(8,128)(2,1)}, bf16[128,2048]{1,0:T(8,128)(2,1)S(1)}, u32[]{:S(2)}) copy-start(bf16[128,2048]{1,0:T(8,128)(2,1)S(1)} %collective-permute-done.1.refs_1_) | copy-start | bytes 1572868
  24.7 8.7 %copy-start.7 = (bf16[128,2048]{1,0:T(8,128)(2,1)S(1)}, bf16[128,2048]{1,0:T(8,128)(2,1)}, u32[]{:S(2)}) copy-start(bf16[128,2048]{1,0:T(8,128)(2,1)} %refs_0_.3) | copy-start | bytes 1572868
  24.7 74.3 %collective-permute-start.4 = (bf16[128,512]{1,0:T(8,128)(2,1)}, bf16[128,512]{1,0:T(8,128)(2,1)S(1)}, u32[]{:S(2)}, u32[]{:S(2)}) collective-permute-start(bf16[128,512]{1,0:T(8,128)(2,1)} %fusion.2), channel_id=1, source_target_pairs={{0,8},{8,0},{16,24},{24,16},{1,9},{9,1},{17,25},{25,17},{2,10},{10... | collective-permute-start | bytes 393224 | tf_op jit(solution)/shard_map/ppermute | solution.py:22
  28.5 3.0 %copy-start.9 = (bf16[128,2048]{1,0:T(8,128)(2,1)}, bf16[128,2048]{1,0:T(8,128)(2,1)S(1)}, u32[]{:S(2)}) copy-start(bf16[128,2048]{1,0:T(8,128)(2,1)S(1)} %collective-permute-done.2.refs_2_) | copy-start | bytes 1572868
  30.0 69.0 %collective-permute-start.5 = (bf16[128,512]{1,0:T(8,128)(2,1)}, bf16[128,512]{1,0:T(8,128)(2,1)S(1)}, u32[]{:S(2)}, u32[]{:S(2)}) collective-permute-start(bf16[128,512]{1,0:T(8,128)(2,1)} %fusion.3), channel_id=1, source_target_pairs={{0,16},{8,24},{16,0},{24,8},{1,17},{9,25},{17,1},{25,9},{2,18},{10... | collective-permute-start | bytes 393224 | tf_op jit(solution)/shard_map/ppermute | solution.py:22
  33.4 65.6 %collective-permute-start.6 = (bf16[128,512]{1,0:T(8,128)(2,1)S(1)}, bf16[128,512]{1,0:T(8,128)(2,1)S(1)}, u32[]{:S(2)}, u32[]{:S(2)}) collective-permute-start(bf16[128,512]{1,0:T(8,128)(2,1)S(1)} %fusion.4), channel_id=1, source_target_pairs={{0,24},{8,16},{16,8},{24,0},{1,25},{9,17},{17,9},{25,1},{2,26},{10... | collective-permute-start | bytes 393224 | tf_op jit(solution)/shard_map/ppermute | solution.py:22
  34.3 65.4 %copy-start.1 = (bf16[8,128,256]{2,1,0:T(8,128)(2,1)S(1)}, bf16[8,128,256]{2,1,0:T(8,128)(2,1)}, u32[]{:S(2)}) copy-start(bf16[8,128,256]{2,1,0:T(8,128)(2,1)} %get-tuple-element.36.refs_1_.refs_2_) | copy-start | bytes 1572868
  99.0 0.7 copy-start.5
  99.7 0.9 copy-start.6
  101.6 0.8 copy-start.4
  102.4 50.0 %copy-start.2 = (bf16[8,128,256]{2,1,0:T(8,128)(2,1)}, bf16[8,128,256]{2,1,0:T(8,128)(2,1)S(1)}, u32[]{:S(2)}) copy-start(bf16[8,128,256]{2,1,0:T(8,128)(2,1)S(1)} %get-tuple-element.39.refs_4_) | copy-start | bytes 1572868
  102.4 23.5 %all-to-all-start.1 = ((bf16[8,128,256]{2,1,0:T(8,128)(2,1)}), bf16[8,128,256]{2,1,0:T(8,128)(2,1)}, u32[]{:S(2)}, u32[]{:S(2)}) async-start(bf16[8,128,256]{2,1,0:T(8,128)(2,1)} %copy-done.4), calls=%async_computation.1 | async-start | bytes 1048576 | tf_op jit(solution)/shard_map/all_to_all | solution.py:378
  116.4 2.0 collective-permute-start.7
  120.1 5.8 %collective-permute-start.8 = (bf16[2,128,256]{2,1,0:T(8,128)(2,1)S(1)}, bf16[2,128,256]{2,1,0:T(8,128)(2,1)S(1)}, u32[]{:S(2)}, u32[]{:S(2)}) collective-permute-start(bf16[2,128,256]{2,1,0:T(8,128)(2,1)S(1)} %get-tuple-element.75), channel_id=1, source_target_pairs={{0,2},{1,3},{2,0},{3,1},{4,6},{5,7},{6,4},{7,5},{8,10},{9,11},{10,... | collective-permute-start | bytes 393224 | tf_op jit(solution)/shard_map/ppermute | solution.py:22
  122.0 23.2 %collective-permute-start.10 = (bf16[2,128,256]{2,1,0:T(8,128)(2,1)}, bf16[2,128,256]{2,1,0:T(8,128)(2,1)S(1)}, u32[]{:S(2)}, u32[]{:S(2)}) collective-permute-start(bf16[2,128,256]{2,1,0:T(8,128)(2,1)} %get-tuple-element.73), channel_id=1, source_target_pairs={{0,6},{1,7},{2,4},{3,5},{4,2},{5,3},{6,0},{7,1},{8,14},{9,15},{10,... | collective-permute-start | bytes 393224 | tf_op jit(solution)/shard_map/ppermute | solution.py:22
  124.3 20.8 %collective-permute-start.9 = (bf16[2,128,256]{2,1,0:T(8,128)(2,1)}, bf16[2,128,256]{2,1,0:T(8,128)(2,1)}, u32[]{:S(2)}, u32[]{:S(2)}) collective-permute-start(bf16[2,128,256]{2,1,0:T(8,128)(2,1)} %get-tuple-element.76), channel_id=1, source_target_pairs={{0,4},{1,5},{2,6},{3,7},{4,0},{5,1},{6,2},{7,3},{8,12},{9,13},{10,... | collective-permute-start | bytes 393224 | tf_op jit(solution)/shard_map/ppermute | solution.py:22
  134.6 30.0 %all-to-all-start.2 = ((bf16[8,130,256]{2,1,0:T(8,128)(2,1)}), bf16[8,130,256]{2,1,0:T(8,128)(2,1)}, u32[]{:S(2)}, u32[]{:S(2)}) async-start(bf16[8,130,256]{2,1,0:T(8,128)(2,1)} %get-tuple-element.46), calls=%async_computation.2 | async-start | bytes 1114112 | tf_op jit(solution)/shard_map/all_to_all | solution.py:383
  141.2 3.3 %collective-permute-start.11 = (bf16[2,8,2,256]{3,2,1,0:T(2,128)(2,1)}, bf16[2,8,2,256]{3,2,1,0:T(2,128)(2,1)S(1)}, u32[]{:S(2)}, u32[]{:S(2)}) collective-permute-start(bf16[2,8,2,256]{3,2,1,0:T(2,128)(2,1)} %pad_maximum_fusion.1), channel_id=1, source_target_pairs={{1,0},{2,1},{3,2},{4,3},{5,4},{6,5},{7,6},{9,8},{10,9},{11,10},{12... | collective-permute-start | bytes 49160 | tf_op jit(solution)/shard_map/ppermute | solution.py:18
  146.3 10.3 %collective-permute-start.16 = (bf16[256,256]{1,0:T(8,128)(2,1)S(1)}, bf16[256,256]{1,0:T(8,128)(2,1)S(1)}, u32[]{:S(2)}, u32[]{:S(2)}) collective-permute-start(bf16[256,256]{1,0:T(8,128)(2,1)S(1)} %get-tuple-element.70), channel_id=1, source_target_pairs={{0,8},{8,0},{16,24},{24,16},{1,9},{9,1},{17,25},{25,17},{2,10},{10... | collective-permute-start | bytes 393224 | tf_op jit(solution)/shard_map/ppermute | solution.py:22
  148.3 9.8 %collective-permute-start.18 = (bf16[256,256]{1,0:T(8,128)(2,1)S(1)}, bf16[256,256]{1,0:T(8,128)(2,1)S(1)}, u32[]{:S(2)}, u32[]{:S(2)}) collective-permute-start(bf16[256,256]{1,0:T(8,128)(2,1)S(1)} %get-tuple-element.71), channel_id=1, source_target_pairs={{0,24},{8,16},{16,8},{24,0},{1,25},{9,17},{17,9},{25,1},{2,26},{10... | collective-permute-start | bytes 393224 | tf_op jit(solution)/shard_map/ppermute | solution.py:22
  149.8 8.4 %collective-permute-start.17 = (bf16[256,256]{1,0:T(8,128)(2,1)S(1)}, bf16[256,256]{1,0:T(8,128)(2,1)S(1)}, u32[]{:S(2)}, u32[]{:S(2)}) collective-permute-start(bf16[256,256]{1,0:T(8,128)(2,1)S(1)} %get-tuple-element.72), channel_id=1, source_target_pairs={{0,16},{8,24},{16,0},{24,8},{1,17},{9,25},{17,1},{25,9},{2,18},{10... | collective-permute-start | bytes 393224 | tf_op jit(solution)/shard_map/ppermute | solution.py:22
  152.3 0.8 copy-start.3
  153.1 11.5 %collective-permute-start.15 = (f32[8,2,256]{2,1,0:T(2,128)S(1)}, f32[8,2,256]{2,1,0:T(2,128)S(1)}, u32[]{:S(2)}, u32[]{:S(2)}) collective-permute-start(f32[8,2,256]{2,1,0:T(2,128)S(1)} %convert_multiply_fusion), channel_id=1, source_target_pairs={{1,0},{2,1},{3,2},{4,3},{5,4},{6,5},{7,6},{9,8},{10,9},{11,10},{12... | collective-permute-start | bytes 49160 | tf_op jit(solution)/shard_map/ppermute | solution.py:18
  154.6 5.3 %collective-permute-start.12 = (bf16[128,512]{1,0:T(8,128)(2,1)S(1)}, bf16[128,512]{1,0:T(8,128)(2,1)S(1)}, u32[]{:S(2)}, u32[]{:S(2)}) collective-permute-start(bf16[128,512]{1,0:T(8,128)(2,1)S(1)} %get-tuple-element.56), channel_id=1, source_target_pairs={{0,8},{8,0},{16,24},{24,16},{1,9},{9,1},{17,25},{25,17},{2,10},{10... | collective-permute-start | bytes 393224 | tf_op jit(solution)/shard_map/ppermute | solution.py:22
  156.6 5.2 %collective-permute-start.13 = (bf16[128,512]{1,0:T(8,128)(2,1)S(1)}, bf16[128,512]{1,0:T(8,128)(2,1)S(1)}, u32[]{:S(2)}, u32[]{:S(2)}) collective-permute-start(bf16[128,512]{1,0:T(8,128)(2,1)S(1)} %get-tuple-element.57), channel_id=1, source_target_pairs={{0,16},{8,24},{16,0},{24,8},{1,17},{9,25},{17,1},{25,9},{2,18},{10... | collective-permute-start | bytes 393224 | tf_op jit(solution)/shard_map/ppermute | solution.py:22
  158.2 6.5 %collective-permute-start.14 = (bf16[128,512]{1,0:T(8,128)(2,1)S(1)}, bf16[128,512]{1,0:T(8,128)(2,1)S(1)}, u32[]{:S(2)}, u32[]{:S(2)}) collective-permute-start(bf16[128,512]{1,0:T(8,128)(2,1)S(1)} %get-tuple-element.58), channel_id=1, source_target_pairs={{0,24},{8,16},{16,8},{24,0},{1,25},{9,17},{17,9},{25,1},{2,26},{10... | collective-permute-start | bytes 393224 | tf_op jit(solution)/shard_map/ppermute | solution.py:22
  164.7 9.5 %copy-start.11 = (f32[8,2,256]{2,1,0:T(2,128)}, f32[8,2,256]{2,1,0:T(2,128)S(1)}, u32[]{:S(2)}) copy-start(f32[8,2,256]{2,1,0:T(2,128)S(1)} %collective-permute-done.15.refs_9_) | copy-start | bytes 49156
  168.0 3.6 %collective-permute-start.19 = (bf16[256,2048]{1,0:T(8,128)(2,1)}, bf16[256,2048]{1,0:T(8,128)(2,1)}, u32[]{:S(2)}, u32[]{:S(2)}) collective-permute-start(bf16[256,2048]{1,0:T(8,128)(2,1)} %convolution_convert_fusion), channel_id=1, source_target_pairs={{0,1},{1,0},{2,3},{3,2},{4,5},{5,4},{6,7},{7,6},{8,9},{9,8},{10,11... | collective-permute-start | bytes 3145736 | tf_op jit(solution)/shard_map/ppermute | solution.py:22
  180.0 16.6 %collective-permute-start.22 = (f32[4,6144]{1,0:T(4,128)}, f32[4,6144]{1,0:T(4,128)S(1)}, u32[]{:S(2)}, u32[]{:S(2)}) collective-permute-start(f32[4,6144]{1,0:T(4,128)} %get-tuple-element.65), channel_id=1, source_target_pairs={{0,24},{8,16},{16,8},{24,0},{1,25},{9,17},{17,9},{25,1},{2,26},{10... | collective-permute-start | bytes 294920 | tf_op jit(solution)/shard_map/ppermute | solution.py:22
  181.6 15.6 %collective-permute-start.21 = (f32[4,6144]{1,0:T(4,128)}, f32[4,6144]{1,0:T(4,128)S(1)}, u32[]{:S(2)}, u32[]{:S(2)}) collective-permute-start(f32[4,6144]{1,0:T(4,128)} %get-tuple-element.65), channel_id=1, source_target_pairs={{0,16},{8,24},{16,0},{24,8},{1,17},{9,25},{17,1},{25,9},{2,18},{10... | collective-permute-start | bytes 294920 | tf_op jit(solution)/shard_map/ppermute | solution.py:22
  182.6 14.6 %collective-permute-start.20 = (f32[4,6144]{1,0:T(4,128)}, f32[4,6144]{1,0:T(4,128)S(1)}, u32[]{:S(2)}, u32[]{:S(2)}) collective-permute-start(f32[4,6144]{1,0:T(4,128)} %get-tuple-element.65), channel_id=1, source_target_pairs={{0,8},{8,0},{16,24},{24,16},{1,9},{9,1},{17,25},{25,17},{2,10},{10... | collective-permute-start | bytes 294920 | tf_op jit(solution)/shard_map/ppermute | solution.py:22
  184.4 17.7 %collective-permute-start.26 = (bf16[64,2048]{1,0:T(8,128)(2,1)}, bf16[64,2048]{1,0:T(8,128)(2,1)}, u32[]{:S(2)}, u32[]{:S(2)}) collective-permute-start(bf16[64,2048]{1,0:T(8,128)(2,1)} %get-tuple-element.67), channel_id=1, source_target_pairs={{0,6},{1,7},{2,4},{3,5},{4,2},{5,3},{6,0},{7,1},{8,14},{9,15},{10,... | collective-permute-start | bytes 786440 | tf_op jit(solution)/shard_map/ppermute | solution.py:22
  194.6 22.9 %collective-permute-start.25 = (bf16[64,2048]{1,0:T(8,128)(2,1)}, bf16[64,2048]{1,0:T(8,128)(2,1)}, u32[]{:S(2)}, u32[]{:S(2)}) collective-permute-start(bf16[64,2048]{1,0:T(8,128)(2,1)} %get-tuple-element.68), channel_id=1, source_target_pairs={{0,4},{1,5},{2,6},{3,7},{4,0},{5,1},{6,2},{7,3},{8,12},{9,13},{10,... | collective-permute-start | bytes 786440 | tf_op jit(solution)/shard_map/ppermute | solution.py:22
  196.6 21.0 %collective-permute-start.24 = (bf16[64,2048]{1,0:T(8,128)(2,1)S(1)}, bf16[64,2048]{1,0:T(8,128)(2,1)}, u32[]{:S(2)}, u32[]{:S(2)}) collective-permute-start(bf16[64,2048]{1,0:T(8,128)(2,1)S(1)} %get-tuple-element.69), channel_id=1, source_target_pairs={{0,2},{1,3},{2,0},{3,1},{4,6},{5,7},{6,4},{7,5},{8,10},{9,11},{10,... | collective-permute-start | bytes 786440 | tf_op jit(solution)/shard_map/ppermute | solution.py:22
  198.1 1.5 collective-permute-start.23
  217.6 7.6 %collective-permute-start.29 = (f32[4,6144]{1,0:T(4,128)S(1)}, f32[4,6144]{1,0:T(4,128)S(1)}, u32[]{:S(2)}, u32[]{:S(2)}) collective-permute-start(f32[4,6144]{1,0:T(4,128)S(1)} %add.116), channel_id=1, source_target_pairs={{0,6},{1,7},{2,4},{3,5},{4,2},{5,3},{6,0},{7,1},{8,14},{9,15},{10,... | collective-permute-start | bytes 294920 | tf_op jit(solution)/shard_map/ppermute | solution.py:22
  221.1 7.7 %collective-permute-start.28 = (f32[4,6144]{1,0:T(4,128)S(1)}, f32[4,6144]{1,0:T(4,128)S(1)}, u32[]{:S(2)}, u32[]{:S(2)}) collective-permute-start(f32[4,6144]{1,0:T(4,128)S(1)} %add.116), channel_id=1, source_target_pairs={{0,4},{1,5},{2,6},{3,7},{4,0},{5,1},{6,2},{7,3},{8,12},{9,13},{10,... | collective-permute-start | bytes 294920 | tf_op jit(solution)/shard_map/ppermute | solution.py:22
  221.1 7.7 %collective-permute-start.27 = (f32[4,6144]{1,0:T(4,128)S(1)}, f32[4,6144]{1,0:T(4,128)S(1)}, u32[]{:S(2)}, u32[]{:S(2)}) collective-permute-start(f32[4,6144]{1,0:T(4,128)S(1)} %add.116), channel_id=1, source_target_pairs={{0,2},{1,3},{2,0},{3,1},{4,6},{5,7},{6,4},{7,5},{8,10},{9,11},{10,... | collective-permute-start | bytes 294920 | tf_op jit(solution)/shard_map/ppermute | solution.py:22
  228.8 0.6 copy-start.10

commit v11 on v8

--- a/solution.py
+++ b/solution.py
@@ -130,12 +130,13 @@
                 piece[:, columns(c % 2 * (parts // 2) + c // 2, size)] = gate[:, columns(q, size)]
 
 
-def final_kernel(*refs):
+def final_kernel(me_ref, *refs):
     proj_ref, prev_ref, taps_ref, gate_grad_ref, long_ref, back_ref, keyed_ref, valued_ref = refs[:8]
     query_after_ref, pair_after_ref, skip_ref, out_ref, sums_ref = refs[8:]
     parts, rows, blk = long_ref.shape
     sums_ref[3:4, :] = jnp.zeros((1, sums_ref.shape[1]), F32)
-    sums_ref[3:4, 0:blk] = skip_ref[...]
+    for b in range(parts):
+        sums_ref[3:4, columns(b, blk)] = jnp.where(me_ref[0] == b, skip_ref[...], 0.0)
     for b in range(parts):
         back = back_ref[b, 0:rows].astype(F32)
         back_after = back_ref[b, rows : rows + 2].astype(F32)
@@ -203,8 +204,9 @@
 
 
 def filter_kernel(waves_ref, filter_ref, spec_ref):
+    values = filter_ref[...].astype(BF16)
     for i in range(2):
-        spec_ref[i] = dot(filter_ref[...], waves_ref[i], 1, 1)
+        spec_ref[i] = dot(values, waves_ref[i], 1, 1)
 
 
 def out_kernel(waves_ref, filter_spec_ref, product_ref, skip_ref, spec_ref, long_ref, turned, total):
@@ -376,17 +378,16 @@
     filter_b = long_filter.astype(BF16)
     inverse = 1.0 / seq_len
     straight = seq_len <= 1024
-    weights = out_proj
+    found = [dot(cot, out_proj, 1, 1).astype(BF16) for cot in cots]
     if straight:
         waves = jnp.asarray(constant_table(seq_len))
         spec = jax.ShapeDtypeStruct((2, blk, seq_len), F32)
         scratch = [pltpu.VMEM((blk, seq_len), BF16), pltpu.VMEM((blk, seq_len), F32)]
         skip_row = skip_gain[None, :]
         (filter_spec,) = chunked(
-            filter_kernel, "filter_spectrum", waves, [], [filter_b], [], [spec], []
+            filter_kernel, "filter_spectrum", waves, [], [ordered(long_filter, *found)], [], [spec], []
         )
-        weights = ordered(out_proj, filter_spec)
-    found = [dot(cot, weights, 1, 1).astype(BF16) for cot in cots]
+        found[0] = ordered(found[0], filter_spec)
     found = [found[0]] + [swapped(found[k], "dp", k) for k in range(1, parts_dp)]
     gate_grad, grad_long_out = call(
         grad_long_kernel, "grad_long", [plane] * 2, 1, 12, me_dp, query, *found
@@ -396,6 +397,9 @@
 
     def finished(total, direct):
         return (total * inverse + skip_gain[None, :] * direct).astype(BF16)
+
+    heads = ordered(jnp.stack([keyed[:, :2], valued[:, :2]]), grad_long_out)
+    pair_after = passed_along(heads, "context", -1).astype(F32)
 
     def crossed(values):
         by_core = values.reshape(parts // 2, 2, rows, blk)
@@ -427,7 +431,7 @@
             "grad_product",
             waves,
             [filter_spec, product_spec],
-            [ordered(grad_long, *long_came[1:]), product, skip_row],
+            [ordered(grad_long, long_came[1], pair_after), product, skip_row],
             [
                 jax.ShapeDtypeStruct((parts, rows + 2, blk), BF16),
                 jax.ShapeDtypeStruct((blk, seq_len), F32),
@@ -453,8 +457,6 @@
         back_sent = jnp.concatenate([back_blocks, next_heads], 1)
         skip_sum = jnp.sum(grad_long_f * product_f, 0, keepdims=True)
     grad_product = to_positions(back_sent)
-    heads = ordered(jnp.stack([keyed[:, :2], valued[:, :2]]), grad_long_out)
-    pair_after = passed_along(heads, "context", -1).astype(F32)
     long_came = lax.optimization_barrier((*long_came, back_sent, pair_after))[: parts // 2]
 
     piece = jax.ShapeDtypeStruct((rows, chans // parts_dp), BF16)
@@ -465,8 +467,8 @@
     query_heads = gate_grad[:, :2].astype(F32) * long_out[:, :2].astype(F32)
     query_after = passed_along(query_heads, "context", -1)
     early = (grad_product, query_after)
+    cot_all = jnp.concatenate(lax.optimization_barrier((*cots, gates[0]))[:parts_dp], 0)
     gate_all = ordered(jnp.concatenate(gates, 0), *early)
-    cot_all = jnp.concatenate(cots, 0)
     pair, shares = own_share(gate_all, cot_all, parts)
     grad_product = ordered(grad_product, pair)
 
@@ -477,8 +479,9 @@
             jax.ShapeDtypeStruct((rows, width), BF16),
             jax.ShapeDtypeStruct((4, width), F32),
         ],
-        0,
+        1,
         60,
+        me[None],
         projected,
         prev_rows,
         short_taps,
@@ -495,10 +498,11 @@
     tap_sums = all_sum(tap_sums, "dp", bits_of(parts_dp))
     lag_sum = ordered(lag_sum, tap_sums)
     grad_filter = summed_blocks(lag_sum, "dp", 1) * (scale_factor * inverse)
-    grad_skip = tap_sums[3, :blk] * scale_factor
-    tap_sums = tap_sums[:3] + swapped(tap_sums[:3], "context", 1)
-    tap_sums = ordered(tap_sums, *shares[1:])
-    grad_taps = all_sum(tap_sums, "context", bits_of(parts, 2)) * scale_factor
+    tap_sums = ordered(tap_sums + swapped(tap_sums, "context", 1), *shares[1:])
+    tap_sums = all_sum(tap_sums, "context", bits_of(parts, 2)) * scale_factor
+    grad_taps = tap_sums[:3]
+    skip_blocks = tap_sums[3, :chans].reshape(parts, blk)
+    grad_skip = lax.dynamic_index_in_dim(skip_blocks, me, 0, False)
     grad_proj = sum(share.astype(F32) for share in shares) * scale_factor
     return (grad_inputs, grad_taps, grad_filter, grad_skip, grad_proj)
 

time: 171 us -> 174 us (1.018)
    ppermute x27, starting transfers between devices: 41.1 us -> 34.3 us  [swapped(): lax.ppermute(value, axis, [(i, i ^ mask) for i in range(lax.axis_size(axi...]
    ppermute x27, waiting for transfers between devices: 39.8 us -> 34.5 us  [swapped(): lax.ppermute(value, axis, [(i, i ^ mask) for i in range(lax.axis_size(axi...]
    all_to_all x1, starting transfers between devices: 4.67 us -> 9.31 us  [to_positions(): lax.all_to_all(blocks, 'context', split_axis=0, concat_axis=0, tiled=True)]
    all_to_all x1, waiting for transfers between devices: 0.01 us -> 3.46 us  [to_positions(): lax.all_to_all(blocks, 'context', split_axis=0, concat_axis=0, tiled=True)]
    unnamed x31 -> x33, local copies, waits for them, and re-layouts: 8.76 us -> 6.09 us
    ppermute x3, waiting for transfers between devices: 0.01 us -> 2.37 us  [passed_along(): lax.ppermute(value, axis, [(source, source + steps) for source in range(i...]
    all_to_all x2, starting transfers between devices: 10.4 us -> 12.6 us  [to_channels(): lax.all_to_all(blocks, 'context', split_axis=0, concat_axis=0, tiled=True)]
    convert_element_type x1 -> x0, other arithmetic: 2.09 us -> none  [body(): filter_b = long_filter.astype(BF16)]
  transfers between devices with their start and end apart: 33 -> 33, of which waited for: 16 -> 15; matrix products, arithmetic and copies ran while one was open for 15% -> 15% of each run, Pallas kernels for 11% -> 17%
where the time goes in v11:
time: 174 us; the launch traced here: 173 us
  starting transfers between devices  60.2 us (35%)
  waiting for transfers between devices  40.4 us (23%)
  Pallas kernels  34.6 us (20%)
  local copies, waits for them, and re-layouts  14 us (8%)
  matrix products  13.3 us (8%)
  other arithmetic  9.49 us (5%)
    ppermute x27, waiting for transfers between devices, swapped(): lax.ppermute(value, axis, [(i, i ^ mask) for i in range(lax.axis_size(axi...  34.5 us
    ppermute x27, starting transfers between devices, swapped(): lax.ppermute(value, axis, [(i, i ^ mask) for i in range(lax.axis_size(axi...  34.3 us
    pallas_call x3, Pallas kernels, chunked(): pl.pallas_call(kernel, out_shape=spec_out + outs, grid=(freqs // size,),...  21.7 us
    dot_general x6, matrix products, dot(): lax.dot_general(left, right, (((left_dim,), (right_dim,)), ((), ())), pre...  13.3 us
    pallas_call x4, Pallas kernels, call(): pl.pallas_call(run, out_shape=outs, in_specs=[SMEM] * smem + [anywhere] *...  12.9 us
    all_to_all x2, starting transfers between devices, to_channels(): lax.all_to_all(blocks, 'context', split_axis=0, concat_axis=0, tiled=True)  12.6 us
    all_to_all x1, starting transfers between devices, to_positions(): lax.all_to_all(blocks, 'context', split_axis=0, concat_axis=0, tiled=True)  9.31 us
    unnamed x33, local copies, waits for them, and re-layouts  6.09 us
  transfers between devices with their start and end apart: 33, of which 15 were waited for; matrix products, arithmetic and copies ran while one was open for 15% of the time, Pallas kernels for 17%

profile of v11, /device:TPU:0, one launch (start us, length us, event | category | flops | bytes accessed | tf_op | source)
XLA Modules:
  0.0 172.9 jit_solution(15422253990008843647)
XLA Ops:
  0.6 3.0 %collective-permute-start.1 = (bf16[128,2048]{1,0:T(8,128)(2,1)}, bf16[128,2048]{1,0:T(8,128)(2,1)S(1)}, u32[]{:S(2)}, u32[]{:S(2)}) collective-permute-start(bf16[128,2048]{1,0:T(8,128)(2,1)} %param.12), channel_id=1, source_target_pairs={{0,8},{8,0},{16,24},{24,16},{1,9},{9,1},{17,25},{25,17},{2,10},{10... | collective-permute-start | bytes 1572872 | tf_op jit(solution)/shard_map/ppermute | solution.py:22
  3.6 1.5 collective-permute-start.2
  5.2 0.9 slice.21
  6.1 1.3 collective-permute-start
  8.9 3.6 %short_convs.1 = (bf16[8,128,256]{2,1,0:T(8,128)(2,1)}, bf16[8,128,256]{2,1,0:T(8,128)(2,1)}, bf16[8,128,256]{2,1,0:T(8,128)(2,1)}, bf16[8,128,256]{2,1,0:T(8,128)(2,1)}) custom-call(bf16[128,6144]{1,0:T(8,128)(2,1)} %refs_1_.1, f32[2,6144]{1,0:T(2,128)} %convert_element_type.66.refs_1_.refs_2_, f32[3,6144]{1,0:T(4,128)} %refs_3_.1), custom_call_target="tpu_custom_call" | custom-call | tf_op jit(solution)/shard_map/short_convs/pallas_call | solution.py:67
  12.5 7.9 %all-to-all-start = ((bf16[8,128,256]{2,1,0:T(8,128)(2,1)}), bf16[8,128,256]{2,1,0:T(8,128)(2,1)}, u32[]{:S(2)}, u32[]{:S(2)}) async-start(bf16[8,128,256]{2,1,0:T(8,128)(2,1)} %get-tuple-element.45), calls=%async_computation | async-start | bytes 1048576 | tf_op jit(solution)/shard_map/all_to_all | solution.py:352
  20.4 0.8 copy-done.9
  21.2 1.5 convolution_convert_fusion.3
  23.2 5.0 %collective-permute-done.2 = bf16[128,2048]{1,0:T(8,128)(2,1)} collective-permute-done((bf16[128,2048]{1,0:T(8,128)(2,1)}, bf16[128,2048]{1,0:T(8,128)(2,1)}, u32[]{:S(2)}, u32[]{:S(2)}) %collective-permute-start.2) | collective-permute-done | bytes 524320 | tf_op jit(solution)/shard_map/ppermute | solution.py:22
  28.2 2.5 %convolution_convert_fusion.2 = bf16[128,512]{1,0:T(8,128)(2,1)} fusion(bf16[128,2048]{1,0:T(8,128)(2,1)} %collective-permute-done.2, bf16[512,2048]{1,0:T(8,128)(2,1)S(1)} %copy-done), kind=kOutput, calls=%fused_computation.4 | convolution fusion | flops 268500992 | bytes 2752512 | tf_op jit(solution)/shard_map/dot_general | solution.py:188
  30.7 2.5 %collective-permute-start.5 = (bf16[128,512]{1,0:T(8,128)(2,1)}, bf16[128,512]{1,0:T(8,128)(2,1)S(1)}, u32[]{:S(2)}, u32[]{:S(2)}) collective-permute-start(bf16[128,512]{1,0:T(8,128)(2,1)} %convolution_convert_fusion.2), channel_id=1, source_target_pairs={{0,16},{8,24},{16,0},{24,8},{1,17},{9,25},{17,1},{25,9},{2,18},{10... | collective-permute-start | bytes 393224 | tf_op jit(solution)/shard_map/ppermute | solution.py:22
  33.2 2.5 %convolution_convert_fusion.1 = bf16[128,512]{1,0:T(8,128)(2,1)} fusion(bf16[128,2048]{1,0:T(8,128)(2,1)} %collective-permute-done.3, bf16[512,2048]{1,0:T(8,128)(2,1)S(1)} %copy-done), kind=kOutput, calls=%fused_computation.3 | convolution fusion | flops 268500992 | bytes 2752512 | tf_op jit(solution)/shard_map/dot_general | solution.py:188
  35.8 0.8 convolution_convert_fusion.4.refs_2_
  36.6 5.5 %filter_spectrum.1.filter_spec_ref = f32[2,256,1024]{2,1,0:T(8,128)} custom-call(bf16[2,1024,1024]{2,1,0:T(8,128)(2,1)} %constant.86.clone.waves_ref, f32[256,1024]{1,0:T(8,128)} %filter_ref), custom_call_target="tpu_custom_call" | custom-call | tf_op jit(solution)/shard_map/filter_spectrum/pallas_call | solution.py:277
  42.2 0.6 copy-done.5
  42.8 0.9 copy-done.6
  43.7 1.0 grad_long.1
  44.7 0.8 copy-done.4
  45.5 4.7 %all-to-all-start.1 = ((bf16[8,128,256]{2,1,0:T(8,128)(2,1)}), bf16[8,128,256]{2,1,0:T(8,128)(2,1)}, u32[]{:S(2)}, u32[]{:S(2)}) async-start(bf16[8,128,256]{2,1,0:T(8,128)(2,1)} %copy-done.4), calls=%async_computation.1 | async-start | bytes 1048576 | tf_op jit(solution)/shard_map/all_to_all | solution.py:352
  50.2 7.4 %long_out.1 = (f32[2,256,1024]{2,1,0:T(8,128)}, bf16[1024,256]{1,0:T(8,128)(2,1)}) custom-call(bf16[2,1024,1024]{2,1,0:T(8,128)(2,1)} %constant.86.clone.waves_ref, f32[2,256,1024]{2,1,0:T(8,128)} %filter_spectrum.1.filter_spec_ref, bf16[1024,256]{1,0:T(8,128)(2,1)} %bitcast.2.product_ref, f32[1,256]{1,0:T(1,128)} %bitcast.48), custom_call_target="tpu_custom_call" | custom-call | tf_op jit(solution)/shard_map/long_out/pallas_call | solution.py:277
  57.6 1.8 %dynamic-slice_bitcast_fusion.3 = (bf16[4,128,256]{2,1,0:T(8,128)(2,1)}, bf16[4,1,128,256]{3,2,1,0:T(8,128)(2,1)S(1)}) fusion(bf16[4,2,128,256]{3,2,1,0:T(8,128)(2,1)} %bitcast.46, s32[]{:T(128)S(6)} %select_n.63, s32[]{:T(128)S(6)} %select_n.62), kind=kLoop, calls=%fused_computation.28 | loop fusion | bytes 1048584 | tf_op jit(solution)/shard_map/jit(dynamic_index_in_dim)/squeeze | solution.py:408
  59.8 1.5 collective-permute-done.7
  61.3 1.7 fusion.6
  63.0 1.9 %collective-permute-start.8 = (bf16[2,128,256]{2,1,0:T(8,128)(2,1)}, bf16[2,128,256]{2,1,0:T(8,128)(2,1)S(1)}, u32[]{:S(2)}, u32[]{:S(2)}) collective-permute-start(bf16[2,128,256]{2,1,0:T(8,128)(2,1)} %get-tuple-element.85), channel_id=1, source_target_pairs={{0,2},{1,3},{2,0},{3,1},{4,6},{5,7},{6,4},{7,5},{8,10},{9,11},{10,... | collective-permute-start | bytes 393224 | tf_op jit(solution)/shard_map/ppermute | solution.py:22
  64.9 2.4 %collective-permute-start.9 = (bf16[2,128,256]{2,1,0:T(8,128)(2,1)}, bf16[2,128,256]{2,1,0:T(8,128)(2,1)S(1)}, u32[]{:S(2)}, u32[]{:S(2)}) collective-permute-start(bf16[2,128,256]{2,1,0:T(8,128)(2,1)} %get-tuple-element.86), channel_id=1, source_target_pairs={{0,4},{1,5},{2,6},{3,7},{4,0},{5,1},{6,2},{7,3},{8,12},{9,13},{10,... | collective-permute-start | bytes 393224 | tf_op jit(solution)/shard_map/ppermute | solution.py:22
  67.4 0.8 slice_bitcast_fusion
  68.8 1.3 collective-permute-start.11
  70.1 2.0 %collective-permute-done.11 = bf16[2,8,2,256]{3,2,1,0:T(2,128)(2,1)S(1)} collective-permute-done((bf16[2,8,2,256]{3,2,1,0:T(2,128)(2,1)}, bf16[2,8,2,256]{3,2,1,0:T(2,128)(2,1)S(1)}, u32[]{:S(2)}, u32[]{:S(2)}) %collective-permute-start.11) | collective-permute-done | bytes 16416 | tf_op jit(solution)/shard_map/ppermute | solution.py:18
  72.7 8.8 %grad_product.1 = (bf16[8,130,256]{2,1,0:T(8,128)(2,1)}, f32[256,1024]{1,0:T(8,128)}, f32[1,256]{1,0:T(1,128)}) custom-call(bf16[2,1024,1024]{2,1,0:T(8,128)(2,1)} %constant.86.clone.waves_ref, f32[2,256,1024]{2,1,0:T(8,128)} %filter_spectrum.1.filter_spec_ref, f32[2,256,1024]{2,1,0:T(8,128)} %get-tuple-element.49.spec_ref, ...), custom_call_target="tpu_custom_call" | custom-call | tf_op jit(solution)/shard_map/grad_product/pallas_call | solution.py:277
  81.5 9.3 %all-to-all-start.2 = ((bf16[8,130,256]{2,1,0:T(8,128)(2,1)}), bf16[8,130,256]{2,1,0:T(8,128)(2,1)}, u32[]{:S(2)}, u32[]{:S(2)}) async-start(bf16[8,130,256]{2,1,0:T(8,128)(2,1)} %get-tuple-element.54), calls=%async_computation.2 | async-start | bytes 1114112 | tf_op jit(solution)/shard_map/all_to_all | solution.py:357
  90.9 2.6 %gate.1 = (bf16[8,128,256]{2,1,0:T(8,128)(2,1)S(1)}, bf16[128,512]{1,0:T(8,128)(2,1)S(1)}, bf16[128,512]{1,0:T(8,128)(2,1)S(1)}, bf16[128,512]{1,0:T(8,128)(2,1)S(1)}, bf16[128,512]{1,0:T(8,128)(2,1)S(1)}) custom-call(s32[1]{0:T(128)} %bitcast.refs_0_, s32[1]{0:T(128)} %bitcast.1.refs_0_.refs_1_, bf16[8,128,256]{2,1,0:T(8,128)(2,1)S(1)} %copy-done.1, ...), custom_call_target="tpu_custom_call" | custom-call | tf_op jit(solution)/shard_map/gate/pallas_call | solution.py:67
  93.5 3.0 %collective-permute-start.14 = (bf16[128,512]{1,0:T(8,128)(2,1)S(1)}, bf16[128,512]{1,0:T(8,128)(2,1)S(1)}, u32[]{:S(2)}, u32[]{:S(2)}) collective-permute-start(bf16[128,512]{1,0:T(8,128)(2,1)S(1)} %get-tuple-element.63), channel_id=1, source_target_pairs={{0,24},{8,16},{16,8},{24,0},{1,25},{9,17},{17,9},{25,1},{2,26},{10... | collective-permute-start | bytes 393224 | tf_op jit(solution)/shard_map/ppermute | solution.py:22
  97.2 1.5 collective-permute-start.15
  98.6 1.1 constant_dynamic-update-slice_fusion.3
  99.8 1.1 constant_dynamic-update-slice_fusion.1
  100.9 1.1 constant_dynamic-update-slice_fusion
  102.0 1.5 collective-permute-done.13
  103.5 3.5 %all-to-all-done.2.refs_6_ = bf16[8,130,256]{2,1,0:T(8,128)(2,1)} async-done(((bf16[8,130,256]{2,1,0:T(8,128)(2,1)}), bf16[8,130,256]{2,1,0:T(8,128)(2,1)}, u32[]{:S(2)}, u32[]{:S(2)}) %all-to-all-start.2) | async-done | bytes 532512 | tf_op jit(solution)/shard_map/all_to_all | solution.py:357
  107.0 3.3 %convolution_convert_fusion = bf16[256,2048]{1,0:T(8,128)(2,1)} fusion(bf16[512,2048]{1,0:T(8,128)(2,1)} %copy-done.7, bf16[512,512]{1,0:T(8,128)(2,1)S(1)} %pad_maximum_fusion, s32[]{:T(128)S(6)} %select_n.70), kind=kOutput, calls=%fused_computation.2 | convolution fusion | flops 537395200 | bytes 3407876 | tf_op jit(solution)/shard_map/dot_general | solution.py:188
  110.3 3.0 %collective-permute-done.16 = bf16[256,2048]{1,0:T(8,128)(2,1)} collective-permute-done((bf16[256,2048]{1,0:T(8,128)(2,1)}, bf16[256,2048]{1,0:T(8,128)(2,1)}, u32[]{:S(2)}, u32[]{:S(2)}) %collective-permute-start.16) | collective-permute-done | bytes 1048608 | tf_op jit(solution)/shard_map/ppermute | solution.py:22
  113.3 2.6 %fusion = bf16[256,2048]{1,0:T(8,128)(2,1)S(1)} fusion(bf16[512,256]{1,0:T(8,128)(2,1)S(1)} %constant_dynamic-slice_fusion.1, bf16[512,2048]{1,0:T(8,128)(2,1)} %copy-done.7, bf16[256,2048]{1,0:T(8,128)(2,1)} %collective-permute-done.16), kind=kOutput, calls=%fused_computation.1 | convolution fusion | flops 538443776 | bytes 4456448 | tf_op jit(solution)/shard_map/dot_general | solution.py:188
  115.9 5.8 %stream_grads.1 = (bf16[128,6144]{1,0:T(8,128)(2,1)}, f32[4,6144]{1,0:T(4,128)}) custom-call(s32[1]{0:T(128)} %bitcast.refs_0_, bf16[128,6144]{1,0:T(8,128)(2,1)} %refs_1_.1, f32[2,6144]{1,0:T(2,128)} %convert_element_type.66.refs_1_.refs_2_, f32[3,6144]{1,0:T(4,128)} %refs_3_.1, bf16[8,128,256]{2,1,0:T(8,128)(2,1)} %copy-done.2, ...), custom_call_target="tpu_custom_call" | custom-call | tf_op jit(solution)/shard_map/stream_grads/pallas_call | solution.py:67
  121.7 0.8 collective-permute-start.18
  122.5 2.3 %collective-permute-start.19 = (f32[4,6144]{1,0:T(4,128)}, f32[4,6144]{1,0:T(4,128)S(1)}, u32[]{:S(2)}, u32[]{:S(2)}) collective-permute-start(f32[4,6144]{1,0:T(4,128)} %get-tuple-element.73), channel_id=1, source_target_pairs={{0,24},{8,16},{16,8},{24,0},{1,25},{9,17},{17,9},{25,1},{2,26},{10... | collective-permute-start | bytes 294920 | tf_op jit(solution)/shard_map/ppermute | solution.py:22
  125.2 3.7 %collective-permute-done.18 = f32[4,6144]{1,0:T(4,128)S(1)} collective-permute-done((f32[4,6144]{1,0:T(4,128)}, f32[4,6144]{1,0:T(4,128)S(1)}, u32[]{:S(2)}, u32[]{:S(2)}) %collective-permute-start.18) | collective-permute-done | bytes 98336 | tf_op jit(solution)/shard_map/ppermute | solution.py:22
  128.9 1.5 collective-permute-done.17
  130.4 0.9 add_add_fusion
  131.4 1.9 %dynamic-slice_convert_fusion.2 = (bf16[256,256]{1,0:T(8,128)(2,1)}, bf16[256,256]{1,0:T(8,128)(2,1)S(1)}, bf16[256,256]{1,0:T(8,128)(2,1)}) fusion(f32[256,1024]{1,0:T(8,128)} %get-tuple-element.76, s32[]{:T(128)S(6)} %select_n.72, s32[]{:T(128)S(6)} %select_n.74, s32[]{:T(128)S(6)} %select_n.73), kind=kLoop, calls=%fused_computation.23 | loop fusion | bytes 786444 | tf_op jit(solution)/shard_map/convert_element_type | solution.py:346
  133.3 2.6 %collective-permute-start.29 = (bf16[256,256]{1,0:T(8,128)(2,1)S(1)}, bf16[256,256]{1,0:T(8,128)(2,1)S(1)}, u32[]{:S(2)}, u32[]{:S(2)}) collective-permute-start(bf16[256,256]{1,0:T(8,128)(2,1)S(1)} %get-tuple-element.78), channel_id=1, source_target_pairs={{0,24},{8,16},{16,8},{24,0},{1,25},{9,17},{17,9},{25,1},{2,26},{10... | collective-permute-start | bytes 393224 | tf_op jit(solution)/shard_map/ppermute | solution.py:22
  136.7 0.9 dynamic-slice_bitcast_fusion
  137.9 1.5 collective-permute-start.22
  139.4 0.7 collective-permute-done.29
  140.2 0.6 copy-done.11
  140.8 1.8 %collective-permute-start.23 = (bf16[64,2048]{1,0:T(8,128)(2,1)S(1)}, bf16[64,2048]{1,0:T(8,128)(2,1)}, u32[]{:S(2)}, u32[]{:S(2)}) collective-permute-start(bf16[64,2048]{1,0:T(8,128)(2,1)S(1)} %get-tuple-element.80), channel_id=1, source_target_pairs={{0,6},{1,7},{2,4},{3,5},{4,2},{5,3},{6,0},{7,1},{8,14},{9,15},{10,... | collective-permute-start | bytes 786440 | tf_op jit(solution)/shard_map/ppermute | solution.py:22
  142.6 0.9 add.109
  143.6 1.9 %add_multiply_fusion = f32[256,256]{1,0:T(8,128)} fusion(bf16[256,256]{1,0:T(8,128)(2,1)} %copy-done.11, bf16[256,256]{1,0:T(8,128)(2,1)} %collective-permute-done.28, bf16[256,256]{1,0:T(8,128)(2,1)} %collective-permute-done.27, f32[256,1024]{1,0:T(8,128)} %get-tuple-element.76, s32[]{:T(128)S(6)} %select_n.71), kind=kLoop, calls=%fused_computation.20 | loop fusion | flops 458752 | bytes 917508 | tf_op jit(solution)/shard_map/mul | solution.py:500
  145.5 4.6 %collective-permute-done.21 = bf16[64,2048]{1,0:T(8,128)(2,1)} collective-permute-done((bf16[64,2048]{1,0:T(8,128)(2,1)}, bf16[64,2048]{1,0:T(8,128)(2,1)}, u32[]{:S(2)}, u32[]{:S(2)}) %collective-permute-start.21) | collective-permute-done | bytes 262176 | tf_op jit(solution)/shard_map/ppermute | solution.py:22
  150.1 9.5 %collective-permute-done.22 = bf16[64,2048]{1,0:T(8,128)(2,1)} collective-permute-done((bf16[64,2048]{1,0:T(8,128)(2,1)}, bf16[64,2048]{1,0:T(8,128)(2,1)}, u32[]{:S(2)}, u32[]{:S(2)}) %collective-permute-start.22) | collective-permute-done | bytes 262176 | tf_op jit(solution)/shard_map/ppermute | solution.py:22
  159.6 4.7 %collective-permute-start.25 = (f32[4,6144]{1,0:T(4,128)S(1)}, f32[4,6144]{1,0:T(4,128)S(1)}, u32[]{:S(2)}, u32[]{:S(2)}) collective-permute-start(f32[4,6144]{1,0:T(4,128)S(1)} %add.109), channel_id=1, source_target_pairs={{0,4},{1,5},{2,6},{3,7},{4,0},{5,1},{6,2},{7,3},{8,12},{9,13},{10,... | collective-permute-start | bytes 294920 | tf_op jit(solution)/shard_map/ppermute | solution.py:22
  164.3 2.2 %collective-permute-start.26 = (f32[4,6144]{1,0:T(4,128)S(1)}, f32[4,6144]{1,0:T(4,128)S(1)}, u32[]{:S(2)}, u32[]{:S(2)}) collective-permute-start(f32[4,6144]{1,0:T(4,128)S(1)} %add.109), channel_id=1, source_target_pairs={{0,6},{1,7},{2,4},{3,5},{4,2},{5,3},{6,0},{7,1},{8,14},{9,15},{10,... | collective-permute-start | bytes 294920 | tf_op jit(solution)/shard_map/ppermute | solution.py:22
  166.6 2.0 %fusion.3 = f32[64,2048]{1,0:T(8,128)} fusion(bf16[64,2048]{1,0:T(8,128)(2,1)} %collective-permute-done.23, bf16[64,2048]{1,0:T(8,128)(2,1)} %collective-permute-done.22, bf16[64,2048]{1,0:T(8,128)(2,1)} %collective-permute-done.21, bf16[4,64,2048]{2,1,0:T(8,128)(2,1)S(1)} %bitcast.45, s32[]{:T(128)S(6)} %select_n.65), kind=kLoop, calls=%fused_computation.19 | loop fusion | flops 1048576 | bytes 1572868 | tf_op jit(solution)/shard_map/mul | solution.py:506
  168.6 1.2 collective-permute-done.25
  169.8 1.4 collective-permute-done.26
  171.3 1.0 collective-permute-done.24
  (69 shorter events, 7.2 us)
Async XLA Ops:
  0.6 20.6 %copy-start = (bf16[512,2048]{1,0:T(8,128)(2,1)S(1)}, bf16[512,2048]{1,0:T(8,128)(2,1)}, u32[]{:S(2)}) copy-start(bf16[512,2048]{1,0:T(8,128)(2,1)} %param.11) | copy-start | bytes 6291460
  0.6 19.7 %collective-permute-start.1 = (bf16[128,2048]{1,0:T(8,128)(2,1)}, bf16[128,2048]{1,0:T(8,128)(2,1)S(1)}, u32[]{:S(2)}, u32[]{:S(2)}) collective-permute-start(bf16[128,2048]{1,0:T(8,128)(2,1)} %param.12), channel_id=1, source_target_pairs={{0,8},{8,0},{16,24},{24,16},{1,9},{9,1},{17,25},{25,17},{2,10},{10... | collective-permute-start | bytes 1572872 | tf_op jit(solution)/shard_map/ppermute | solution.py:22
  3.6 24.6 %collective-permute-start.2 = (bf16[128,2048]{1,0:T(8,128)(2,1)}, bf16[128,2048]{1,0:T(8,128)(2,1)}, u32[]{:S(2)}, u32[]{:S(2)}) collective-permute-start(bf16[128,2048]{1,0:T(8,128)(2,1)} %param.12), channel_id=1, source_target_pairs={{0,16},{8,24},{16,0},{24,8},{1,17},{9,25},{17,1},{25,9},{2,18},{10... | collective-permute-start | bytes 1572872 | tf_op jit(solution)/shard_map/ppermute | solution.py:22
  6.1 2.1 %collective-permute-start = (bf16[2,6144]{1,0:T(2,128)(2,1)S(1)}, bf16[2,6144]{1,0:T(2,128)(2,1)S(1)}, u32[]{:S(2)}, u32[]{:S(2)}) collective-permute-start(bf16[2,6144]{1,0:T(2,128)(2,1)S(1)} %slice.21), channel_id=1, source_target_pairs={{0,1},{1,2},{2,3},{3,4},{4,5},{5,6},{6,7},{8,9},{9,10},{10,11},{11... | collective-permute-start | bytes 73736 | tf_op jit(solution)/shard_map/ppermute | solution.py:18
  7.4 25.8 %collective-permute-start.3 = (bf16[128,2048]{1,0:T(8,128)(2,1)}, bf16[128,2048]{1,0:T(8,128)(2,1)}, u32[]{:S(2)}, u32[]{:S(2)}) collective-permute-start(bf16[128,2048]{1,0:T(8,128)(2,1)} %param.12), channel_id=1, source_target_pairs={{0,24},{8,16},{16,8},{24,0},{1,25},{9,17},{17,9},{25,1},{2,26},{10... | collective-permute-start | bytes 1572872 | tf_op jit(solution)/shard_map/ppermute | solution.py:22
  12.5 33.1 %all-to-all-start = ((bf16[8,128,256]{2,1,0:T(8,128)(2,1)}), bf16[8,128,256]{2,1,0:T(8,128)(2,1)}, u32[]{:S(2)}, u32[]{:S(2)}) async-start(bf16[8,128,256]{2,1,0:T(8,128)(2,1)} %get-tuple-element.45), calls=%async_computation | async-start | bytes 1048576 | tf_op jit(solution)/shard_map/all_to_all | solution.py:352
  20.4 0.9 copy-start.9
  22.7 13.0 %copy-start.8 = (bf16[128,2048]{1,0:T(8,128)(2,1)S(1)}, bf16[128,2048]{1,0:T(8,128)(2,1)}, u32[]{:S(2)}) copy-start(bf16[128,2048]{1,0:T(8,128)(2,1)} %param.12) | copy-start | bytes 1572868
  22.7 19.4 %collective-permute-start.4 = (bf16[128,512]{1,0:T(8,128)(2,1)}, bf16[128,512]{1,0:T(8,128)(2,1)S(1)}, u32[]{:S(2)}, u32[]{:S(2)}) collective-permute-start(bf16[128,512]{1,0:T(8,128)(2,1)} %convolution_convert_fusion.3), channel_id=1, source_target_pairs={{0,8},{8,0},{16,24},{24,16},{1,9},{9,1},{17,25},{25,17},{2,10},{10... | collective-permute-start | bytes 393224 | tf_op jit(solution)/shard_map/ppermute | solution.py:22
  30.7 11.4 %collective-permute-start.5 = (bf16[128,512]{1,0:T(8,128)(2,1)}, bf16[128,512]{1,0:T(8,128)(2,1)S(1)}, u32[]{:S(2)}, u32[]{:S(2)}) collective-permute-start(bf16[128,512]{1,0:T(8,128)(2,1)} %convolution_convert_fusion.2), channel_id=1, source_target_pairs={{0,16},{8,24},{16,0},{24,8},{1,17},{9,25},{17,1},{25,9},{2,18},{10... | collective-permute-start | bytes 393224 | tf_op jit(solution)/shard_map/ppermute | solution.py:22
  35.8 6.4 %collective-permute-start.6 = (bf16[128,512]{1,0:T(8,128)(2,1)}, bf16[128,512]{1,0:T(8,128)(2,1)S(1)}, u32[]{:S(2)}, u32[]{:S(2)}) collective-permute-start(bf16[128,512]{1,0:T(8,128)(2,1)} %convolution_convert_fusion.1), channel_id=1, source_target_pairs={{0,24},{8,16},{16,8},{24,0},{1,25},{9,17},{17,9},{25,1},{2,26},{10... | collective-permute-start | bytes 393224 | tf_op jit(solution)/shard_map/ppermute | solution.py:22
  36.6 6.2 %copy-start.1 = (bf16[8,128,256]{2,1,0:T(8,128)(2,1)S(1)}, bf16[8,128,256]{2,1,0:T(8,128)(2,1)}, u32[]{:S(2)}) copy-start(bf16[8,128,256]{2,1,0:T(8,128)(2,1)} %get-tuple-element.41.refs_1_.refs_2_) | copy-start | bytes 1572868
  42.2 0.7 copy-start.5
  42.8 0.9 copy-start.6
  44.7 0.8 copy-start.4
  45.5 51.6 %copy-start.2 = (bf16[8,128,256]{2,1,0:T(8,128)(2,1)}, bf16[8,128,256]{2,1,0:T(8,128)(2,1)S(1)}, u32[]{:S(2)}) copy-start(bf16[8,128,256]{2,1,0:T(8,128)(2,1)S(1)} %get-tuple-element.44.refs_4_) | copy-start | bytes 1572868
  45.5 27.2 %all-to-all-start.1 = ((bf16[8,128,256]{2,1,0:T(8,128)(2,1)}), bf16[8,128,256]{2,1,0:T(8,128)(2,1)}, u32[]{:S(2)}, u32[]{:S(2)}) async-start(bf16[8,128,256]{2,1,0:T(8,128)(2,1)} %copy-done.4), calls=%async_computation.1 | async-start | bytes 1048576 | tf_op jit(solution)/shard_map/all_to_all | solution.py:352
  59.3 2.0 %collective-permute-start.7 = (bf16[4,128,256]{2,1,0:T(8,128)(2,1)}, bf16[4,128,256]{2,1,0:T(8,128)(2,1)}, u32[]{:S(2)}, u32[]{:S(2)}) collective-permute-start(bf16[4,128,256]{2,1,0:T(8,128)(2,1)} %get-tuple-element.87), channel_id=1, source_target_pairs={{0,1},{1,0},{2,3},{3,2},{4,5},{5,4},{6,7},{7,6},{8,9},{9,8},{10,11... | collective-permute-start | bytes 786440 | tf_op jit(solution)/shard_map/ppermute | solution.py:22
  63.0 9.7 %collective-permute-start.8 = (bf16[2,128,256]{2,1,0:T(8,128)(2,1)}, bf16[2,128,256]{2,1,0:T(8,128)(2,1)S(1)}, u32[]{:S(2)}, u32[]{:S(2)}) collective-permute-start(bf16[2,128,256]{2,1,0:T(8,128)(2,1)} %get-tuple-element.85), channel_id=1, source_target_pairs={{0,2},{1,3},{2,0},{3,1},{4,6},{5,7},{6,4},{7,5},{8,10},{9,11},{10,... | collective-permute-start | bytes 393224 | tf_op jit(solution)/shard_map/ppermute | solution.py:22
  64.9 25.9 %collective-permute-start.9 = (bf16[2,128,256]{2,1,0:T(8,128)(2,1)}, bf16[2,128,256]{2,1,0:T(8,128)(2,1)S(1)}, u32[]{:S(2)}, u32[]{:S(2)}) collective-permute-start(bf16[2,128,256]{2,1,0:T(8,128)(2,1)} %get-tuple-element.86), channel_id=1, source_target_pairs={{0,4},{1,5},{2,6},{3,7},{4,0},{5,1},{6,2},{7,3},{8,12},{9,13},{10,... | collective-permute-start | bytes 393224 | tf_op jit(solution)/shard_map/ppermute | solution.py:22
  67.3 23.6 %collective-permute-start.10 = (bf16[2,128,256]{2,1,0:T(8,128)(2,1)}, bf16[2,128,256]{2,1,0:T(8,128)(2,1)}, u32[]{:S(2)}, u32[]{:S(2)}) collective-permute-start(bf16[2,128,256]{2,1,0:T(8,128)(2,1)} %get-tuple-element.83), channel_id=1, source_target_pairs={{0,6},{1,7},{2,4},{3,5},{4,2},{5,3},{6,0},{7,1},{8,14},{9,15},{10,... | collective-permute-start | bytes 393224 | tf_op jit(solution)/shard_map/ppermute | solution.py:22
  68.8 3.3 %collective-permute-start.11 = (bf16[2,8,2,256]{3,2,1,0:T(2,128)(2,1)}, bf16[2,8,2,256]{3,2,1,0:T(2,128)(2,1)S(1)}, u32[]{:S(2)}, u32[]{:S(2)}) collective-permute-start(bf16[2,8,2,256]{3,2,1,0:T(2,128)(2,1)} %pad_maximum_fusion.1), channel_id=1, source_target_pairs={{1,0},{2,1},{3,2},{4,3},{5,4},{6,5},{7,6},{9,8},{10,9},{11,10},{12... | collective-permute-start | bytes 49160 | tf_op jit(solution)/shard_map/ppermute | solution.py:18
  81.5 25.5 %all-to-all-start.2 = ((bf16[8,130,256]{2,1,0:T(8,128)(2,1)}), bf16[8,130,256]{2,1,0:T(8,128)(2,1)}, u32[]{:S(2)}, u32[]{:S(2)}) async-start(bf16[8,130,256]{2,1,0:T(8,128)(2,1)} %get-tuple-element.54), calls=%async_computation.2 | async-start | bytes 1114112 | tf_op jit(solution)/shard_map/all_to_all | solution.py:357
  90.8 8.9 %copy-start.10 = (bf16[128,2048]{1,0:T(8,128)(2,1)S(1)}, bf16[128,2048]{1,0:T(8,128)(2,1)}, u32[]{:S(2)}) copy-start(bf16[128,2048]{1,0:T(8,128)(2,1)} %copy-done.9) | copy-start | bytes 1572868
  93.5 3.7 %copy-start.3 = (bf16[8,128,256]{2,1,0:T(8,128)(2,1)}, bf16[8,128,256]{2,1,0:T(8,128)(2,1)S(1)}, u32[]{:S(2)}) copy-start(bf16[8,128,256]{2,1,0:T(8,128)(2,1)S(1)} %get-tuple-element.59.refs_5_) | copy-start | bytes 1572868
  93.5 8.5 %collective-permute-start.14 = (bf16[128,512]{1,0:T(8,128)(2,1)S(1)}, bf16[128,512]{1,0:T(8,128)(2,1)S(1)}, u32[]{:S(2)}, u32[]{:S(2)}) collective-permute-start(bf16[128,512]{1,0:T(8,128)(2,1)S(1)} %get-tuple-element.63), channel_id=1, source_target_pairs={{0,24},{8,16},{16,8},{24,0},{1,25},{9,17},{17,9},{25,1},{2,26},{10... | collective-permute-start | bytes 393224 | tf_op jit(solution)/shard_map/ppermute | solution.py:22
  96.5 7.0 %collective-permute-start.13 = (bf16[128,512]{1,0:T(8,128)(2,1)S(1)}, bf16[128,512]{1,0:T(8,128)(2,1)S(1)}, u32[]{:S(2)}, u32[]{:S(2)}) collective-permute-start(bf16[128,512]{1,0:T(8,128)(2,1)S(1)} %get-tuple-element.62), channel_id=1, source_target_pairs={{0,16},{8,24},{16,0},{24,8},{1,17},{9,25},{17,1},{25,9},{2,18},{10... | collective-permute-start | bytes 393224 | tf_op jit(solution)/shard_map/ppermute | solution.py:22
  96.5 7.0 %collective-permute-start.12 = (bf16[128,512]{1,0:T(8,128)(2,1)S(1)}, bf16[128,512]{1,0:T(8,128)(2,1)S(1)}, u32[]{:S(2)}, u32[]{:S(2)}) collective-permute-start(bf16[128,512]{1,0:T(8,128)(2,1)S(1)} %get-tuple-element.61), channel_id=1, source_target_pairs={{0,8},{8,0},{16,24},{24,16},{1,9},{9,1},{17,25},{25,17},{2,10},{10... | collective-permute-start | bytes 393224 | tf_op jit(solution)/shard_map/ppermute | solution.py:22
  97.2 6.4 %collective-permute-start.15 = (f32[8,2,256]{2,1,0:T(2,128)S(1)}, f32[8,2,256]{2,1,0:T(2,128)S(1)}, u32[]{:S(2)}, u32[]{:S(2)}) collective-permute-start(f32[8,2,256]{2,1,0:T(2,128)S(1)} %convert_multiply_fusion), channel_id=1, source_target_pairs={{1,0},{2,1},{3,2},{4,3},{5,4},{6,5},{7,6},{9,8},{10,9},{11,10},{12... | collective-permute-start | bytes 49160 | tf_op jit(solution)/shard_map/ppermute | solution.py:18
  102.0 1.5 copy-start.7
  103.5 12.4 %copy-start.14 = (f32[8,2,256]{2,1,0:T(2,128)}, f32[8,2,256]{2,1,0:T(2,128)S(1)}, u32[]{:S(2)}) copy-start(f32[8,2,256]{2,1,0:T(2,128)S(1)} %collective-permute-done.15.refs_9_) | copy-start | bytes 49156
  110.3 3.0 %collective-permute-start.16 = (bf16[256,2048]{1,0:T(8,128)(2,1)}, bf16[256,2048]{1,0:T(8,128)(2,1)}, u32[]{:S(2)}, u32[]{:S(2)}) collective-permute-start(bf16[256,2048]{1,0:T(8,128)(2,1)} %convolution_convert_fusion), channel_id=1, source_target_pairs={{0,1},{1,0},{2,3},{3,2},{4,5},{5,4},{6,7},{7,6},{8,9},{9,8},{10,11... | collective-permute-start | bytes 3145736 | tf_op jit(solution)/shard_map/ppermute | solution.py:22
  121.7 7.2 %collective-permute-start.18 = (f32[4,6144]{1,0:T(4,128)}, f32[4,6144]{1,0:T(4,128)S(1)}, u32[]{:S(2)}, u32[]{:S(2)}) collective-permute-start(f32[4,6144]{1,0:T(4,128)} %get-tuple-element.73), channel_id=1, source_target_pairs={{0,16},{8,24},{16,0},{24,8},{1,17},{9,25},{17,1},{25,9},{2,18},{10... | collective-permute-start | bytes 294920 | tf_op jit(solution)/shard_map/ppermute | solution.py:22
  122.5 6.4 %collective-permute-start.19 = (f32[4,6144]{1,0:T(4,128)}, f32[4,6144]{1,0:T(4,128)S(1)}, u32[]{:S(2)}, u32[]{:S(2)}) collective-permute-start(f32[4,6144]{1,0:T(4,128)} %get-tuple-element.73), channel_id=1, source_target_pairs={{0,24},{8,16},{16,8},{24,0},{1,25},{9,17},{17,9},{25,1},{2,26},{10... | collective-permute-start | bytes 294920 | tf_op jit(solution)/shard_map/ppermute | solution.py:22
  124.7 5.6 %collective-permute-start.17 = (f32[4,6144]{1,0:T(4,128)}, f32[4,6144]{1,0:T(4,128)S(1)}, u32[]{:S(2)}, u32[]{:S(2)}) collective-permute-start(f32[4,6144]{1,0:T(4,128)} %get-tuple-element.73), channel_id=1, source_target_pairs={{0,8},{8,0},{16,24},{24,16},{1,9},{9,1},{17,25},{25,17},{2,10},{10... | collective-permute-start | bytes 294920 | tf_op jit(solution)/shard_map/ppermute | solution.py:22
  131.3 6.6 %collective-permute-start.20 = (f32[4,6144]{1,0:T(4,128)S(1)}, f32[4,6144]{1,0:T(4,128)S(1)}, u32[]{:S(2)}, u32[]{:S(2)}) collective-permute-start(f32[4,6144]{1,0:T(4,128)S(1)} %add_add_fusion), channel_id=1, source_target_pairs={{0,1},{1,0},{2,3},{3,2},{4,5},{5,4},{6,7},{7,6},{8,9},{9,8},{10,11... | collective-permute-start | bytes 294920 | tf_op jit(solution)/shard_map/ppermute | solution.py:22
  133.3 6.9 %collective-permute-start.29 = (bf16[256,256]{1,0:T(8,128)(2,1)S(1)}, bf16[256,256]{1,0:T(8,128)(2,1)S(1)}, u32[]{:S(2)}, u32[]{:S(2)}) collective-permute-start(bf16[256,256]{1,0:T(8,128)(2,1)S(1)} %get-tuple-element.78), channel_id=1, source_target_pairs={{0,24},{8,16},{16,8},{24,0},{1,25},{9,17},{17,9},{25,1},{2,26},{10... | collective-permute-start | bytes 393224 | tf_op jit(solution)/shard_map/ppermute | solution.py:22
  135.9 7.7 %collective-permute-start.28 = (bf16[256,256]{1,0:T(8,128)(2,1)}, bf16[256,256]{1,0:T(8,128)(2,1)}, u32[]{:S(2)}, u32[]{:S(2)}) collective-permute-start(bf16[256,256]{1,0:T(8,128)(2,1)} %get-tuple-element.79), channel_id=1, source_target_pairs={{0,16},{8,24},{16,0},{24,8},{1,17},{9,25},{17,1},{25,9},{2,18},{10... | collective-permute-start | bytes 393224 | tf_op jit(solution)/shard_map/ppermute | solution.py:22
  136.3 7.3 %collective-permute-start.27 = (bf16[256,256]{1,0:T(8,128)(2,1)}, bf16[256,256]{1,0:T(8,128)(2,1)}, u32[]{:S(2)}, u32[]{:S(2)}) collective-permute-start(bf16[256,256]{1,0:T(8,128)(2,1)} %get-tuple-element.77), channel_id=1, source_target_pairs={{0,8},{8,0},{16,24},{24,16},{1,9},{9,1},{17,25},{25,17},{2,10},{10... | collective-permute-start | bytes 393224 | tf_op jit(solution)/shard_map/ppermute | solution.py:22
  137.6 12.5 %collective-permute-start.21 = (bf16[64,2048]{1,0:T(8,128)(2,1)}, bf16[64,2048]{1,0:T(8,128)(2,1)}, u32[]{:S(2)}, u32[]{:S(2)}) collective-permute-start(bf16[64,2048]{1,0:T(8,128)(2,1)} %get-tuple-element.82), channel_id=1, source_target_pairs={{0,2},{1,3},{2,0},{3,1},{4,6},{5,7},{6,4},{7,5},{8,10},{9,11},{10,... | collective-permute-start | bytes 786440 | tf_op jit(solution)/shard_map/ppermute | solution.py:22
  137.9 2.9 %copy-start.13 = (f32[4,6144]{1,0:T(4,128)}, f32[4,6144]{1,0:T(4,128)S(1)}, u32[]{:S(2)}) copy-start(f32[4,6144]{1,0:T(4,128)S(1)} %collective-permute-done.20) | copy-start | bytes 294916
  137.9 21.7 %collective-permute-start.22 = (bf16[64,2048]{1,0:T(8,128)(2,1)}, bf16[64,2048]{1,0:T(8,128)(2,1)}, u32[]{:S(2)}, u32[]{:S(2)}) collective-permute-start(bf16[64,2048]{1,0:T(8,128)(2,1)} %get-tuple-element.81), channel_id=1, source_target_pairs={{0,4},{1,5},{2,6},{3,7},{4,0},{5,1},{6,2},{7,3},{8,12},{9,13},{10,... | collective-permute-start | bytes 786440 | tf_op jit(solution)/shard_map/ppermute | solution.py:22
  140.2 0.6 copy-start.11
  140.8 18.8 %collective-permute-start.23 = (bf16[64,2048]{1,0:T(8,128)(2,1)S(1)}, bf16[64,2048]{1,0:T(8,128)(2,1)}, u32[]{:S(2)}, u32[]{:S(2)}) collective-permute-start(bf16[64,2048]{1,0:T(8,128)(2,1)S(1)} %get-tuple-element.80), channel_id=1, source_target_pairs={{0,6},{1,7},{2,4},{3,5},{4,2},{5,3},{6,0},{7,1},{8,14},{9,15},{10,... | collective-permute-start | bytes 786440 | tf_op jit(solution)/shard_map/ppermute | solution.py:22
  159.6 10.2 %collective-permute-start.25 = (f32[4,6144]{1,0:T(4,128)S(1)}, f32[4,6144]{1,0:T(4,128)S(1)}, u32[]{:S(2)}, u32[]{:S(2)}) collective-permute-start(f32[4,6144]{1,0:T(4,128)S(1)} %add.109), channel_id=1, source_target_pairs={{0,4},{1,5},{2,6},{3,7},{4,0},{5,1},{6,2},{7,3},{8,12},{9,13},{10,... | collective-permute-start | bytes 294920 | tf_op jit(solution)/shard_map/ppermute | solution.py:22
  164.3 6.9 %collective-permute-start.26 = (f32[4,6144]{1,0:T(4,128)S(1)}, f32[4,6144]{1,0:T(4,128)S(1)}, u32[]{:S(2)}, u32[]{:S(2)}) collective-permute-start(f32[4,6144]{1,0:T(4,128)S(1)} %add.109), channel_id=1, source_target_pairs={{0,6},{1,7},{2,4},{3,5},{4,2},{5,3},{6,0},{7,1},{8,14},{9,15},{10,... | collective-permute-start | bytes 294920 | tf_op jit(solution)/shard_map/ppermute | solution.py:22
  166.6 5.6 %collective-permute-start.24 = (f32[4,6144]{1,0:T(4,128)S(1)}, f32[4,6144]{1,0:T(4,128)S(1)}, u32[]{:S(2)}, u32[]{:S(2)}) collective-permute-start(f32[4,6144]{1,0:T(4,128)S(1)} %add.109), channel_id=1, source_target_pairs={{0,2},{1,3},{2,0},{3,1},{4,6},{5,7},{6,4},{7,5},{8,10},{9,11},{10,... | collective-permute-start | bytes 294920 | tf_op jit(solution)/shard_map/ppermute | solution.py:22
  172.3 0.6 copy-start.12

commit v12 on v8

--- a/solution.py
+++ b/solution.py
@@ -203,8 +203,9 @@
 
 
 def filter_kernel(waves_ref, filter_ref, spec_ref):
+    values = filter_ref[...].astype(BF16)
     for i in range(2):
-        spec_ref[i] = dot(filter_ref[...], waves_ref[i], 1, 1)
+        spec_ref[i] = dot(values, waves_ref[i], 1, 1)
 
 
 def out_kernel(waves_ref, filter_spec_ref, product_ref, skip_ref, spec_ref, long_ref, turned, total):
@@ -383,7 +384,7 @@
         scratch = [pltpu.VMEM((blk, seq_len), BF16), pltpu.VMEM((blk, seq_len), F32)]
         skip_row = skip_gain[None, :]
         (filter_spec,) = chunked(
-            filter_kernel, "filter_spectrum", waves, [], [filter_b], [], [spec], []
+            filter_kernel, "filter_spectrum", waves, [], [long_filter], [], [spec], []
         )
         weights = ordered(out_proj, filter_spec)
     found = [dot(cot, weights, 1, 1).astype(BF16) for cot in cots]
@@ -391,7 +392,9 @@
     gate_grad, grad_long_out = call(
         grad_long_kernel, "grad_long", [plane] * 2, 1, 12, me_dp, query, *found
     )
-    grad_long = to_channels(grad_long_out)
+    heads = jnp.stack([keyed[:, :2], valued[:, :2]])
+    pair_after = passed_along(heads, "context", -1).astype(F32)
+    grad_long = to_channels(ordered(grad_long_out, pair_after))
     product_f, grad_long_f = (product.astype(F32), grad_long.astype(F32))
 
     def finished(total, direct):
@@ -427,7 +430,7 @@
             "grad_product",
             waves,
             [filter_spec, product_spec],
-            [ordered(grad_long, *long_came[1:]), product, skip_row],
+            [ordered(grad_long, long_came[1]), product, skip_row],
             [
                 jax.ShapeDtypeStruct((parts, rows + 2, blk), BF16),
                 jax.ShapeDtypeStruct((blk, seq_len), F32),
@@ -453,8 +456,6 @@
         back_sent = jnp.concatenate([back_blocks, next_heads], 1)
         skip_sum = jnp.sum(grad_long_f * product_f, 0, keepdims=True)
     grad_product = to_positions(back_sent)
-    heads = ordered(jnp.stack([keyed[:, :2], valued[:, :2]]), grad_long_out)
-    pair_after = passed_along(heads, "context", -1).astype(F32)
     long_came = lax.optimization_barrier((*long_came, back_sent, pair_after))[: parts // 2]
 
     piece = jax.ShapeDtypeStruct((rows, chans // parts_dp), BF16)
@@ -465,8 +466,8 @@
     query_heads = gate_grad[:, :2].astype(F32) * long_out[:, :2].astype(F32)
     query_after = passed_along(query_heads, "context", -1)
     early = (grad_product, query_after)
+    cot_all = jnp.concatenate(lax.optimization_barrier((*cots, gates[0]))[:parts_dp], 0)
     gate_all = ordered(jnp.concatenate(gates, 0), *early)
-    cot_all = jnp.concatenate(cots, 0)
     pair, shares = own_share(gate_all, cot_all, parts)
     grad_product = ordered(grad_product, pair)
 

time: 171 us -> 156 us (0.912)
  starting transfers between devices: 60.2 us -> 52.1 us
  local copies, waits for them, and re-layouts: 14.3 us -> 8.27 us
    ppermute x27, starting transfers between devices: 41.1 us -> 33.3 us  [swapped(): lax.ppermute(value, axis, [(i, i ^ mask) for i in range(lax.axis_size(axi...]
    unnamed x31 -> x33, local copies, waits for them, and re-layouts: 8.76 us -> 3.57 us
    ppermute x27, waiting for transfers between devices: 39.8 us -> 35 us  [swapped(): lax.ppermute(value, axis, [(i, i ^ mask) for i in range(lax.axis_size(axi...]
    all_to_all x1, waiting for transfers between devices: 0.01 us -> 4.42 us  [to_positions(): lax.all_to_all(blocks, 'context', split_axis=0, concat_axis=0, tiled=True)]
    convert_element_type x1 -> x0, other arithmetic: 2.09 us -> none  [body(): filter_b = long_filter.astype(BF16)]
  transfers between devices with their start and end apart: 33 -> 33, of which waited for: 16 -> 16; matrix products, arithmetic and copies ran while one was open for 15% -> 12% of each run, Pallas kernels for 11% -> 19%
where the time goes in v12:
time: 156 us; the launch traced here: 155 us
  starting transfers between devices  52.1 us (33%)
  waiting for transfers between devices  39.4 us (25%)
  Pallas kernels  34.5 us (22%)
  matrix products  12.2 us (8%)
  local copies, waits for them, and re-layouts  8.27 us (5%)
  other arithmetic  7.56 us (5%)
    ppermute x27, waiting for transfers between devices, swapped(): lax.ppermute(value, axis, [(i, i ^ mask) for i in range(lax.axis_size(axi...  35 us
    ppermute x27, starting transfers between devices, swapped(): lax.ppermute(value, axis, [(i, i ^ mask) for i in range(lax.axis_size(axi...  33.3 us
    pallas_call x3, Pallas kernels, chunked(): pl.pallas_call(kernel, out_shape=spec_out + outs, grid=(freqs // size,),...  21.6 us
    pallas_call x4, Pallas kernels, call(): pl.pallas_call(run, out_shape=outs, in_specs=[SMEM] * smem + [anywhere] *...  12.9 us
    dot_general x6, matrix products, dot(): lax.dot_general(left, right, (((left_dim,), (right_dim,)), ((), ())), pre...  12.2 us
    all_to_all x2, starting transfers between devices, to_channels(): lax.all_to_all(blocks, 'context', split_axis=0, concat_axis=0, tiled=True)  10.1 us
    all_to_all x1, starting transfers between devices, to_positions(): lax.all_to_all(blocks, 'context', split_axis=0, concat_axis=0, tiled=True)  4.48 us
    all_to_all x1, waiting for transfers between devices, to_positions(): lax.all_to_all(blocks, 'context', split_axis=0, concat_axis=0, tiled=True)  4.42 us
  transfers between devices with their start and end apart: 33, of which 16 were waited for; matrix products, arithmetic and copies ran while one was open for 12% of the time, Pallas kernels for 19%

profile of v12, /device:TPU:0, one launch (start us, length us, event | category | flops | bytes accessed | tf_op | source)
XLA Modules:
  0.0 155.0 jit_solution(16307412083000342733)
XLA Ops:
  0.6 3.0 %collective-permute-start.1 = (bf16[128,2048]{1,0:T(8,128)(2,1)}, bf16[128,2048]{1,0:T(8,128)(2,1)S(1)}, u32[]{:S(2)}, u32[]{:S(2)}) collective-permute-start(bf16[128,2048]{1,0:T(8,128)(2,1)} %param.12), channel_id=1, source_target_pairs={{0,8},{8,0},{16,24},{24,16},{1,9},{9,1},{17,25},{25,17},{2,10},{10... | collective-permute-start | bytes 1572872 | tf_op jit(solution)/shard_map/ppermute | solution.py:22
  3.6 0.9 slice.22
  4.6 1.5 collective-permute-start
  6.0 1.6 %collective-permute-start.3 = (bf16[128,2048]{1,0:T(8,128)(2,1)}, bf16[128,2048]{1,0:T(8,128)(2,1)S(1)}, u32[]{:S(2)}, u32[]{:S(2)}) collective-permute-start(bf16[128,2048]{1,0:T(8,128)(2,1)} %param.12), channel_id=1, source_target_pairs={{0,16},{8,24},{16,0},{24,8},{1,17},{9,25},{17,1},{25,9},{2,18},{10... | collective-permute-start | bytes 1572872 | tf_op jit(solution)/shard_map/ppermute | solution.py:22
  8.0 5.5 %filter_spectrum.1.filter_spec_ref = f32[2,256,1024]{2,1,0:T(8,128)} custom-call(bf16[2,1024,1024]{2,1,0:T(8,128)(2,1)} %constant.82.clone.waves_ref, f32[256,1024]{1,0:T(8,128)} %filter_ref.1), custom_call_target="tpu_custom_call" | custom-call | tf_op jit(solution)/shard_map/filter_spectrum/pallas_call | solution.py:276
  13.5 0.6 convert_element_type.77.refs_1_
  14.1 3.6 %short_convs.1 = (bf16[8,128,256]{2,1,0:T(8,128)(2,1)}, bf16[8,128,256]{2,1,0:T(8,128)(2,1)}, bf16[8,128,256]{2,1,0:T(8,128)(2,1)}, bf16[8,128,256]{2,1,0:T(8,128)(2,1)}) custom-call(bf16[128,6144]{1,0:T(8,128)(2,1)} %refs_0_.3, f32[2,6144]{1,0:T(2,128)} %convert_element_type.77.refs_1_, f32[3,6144]{1,0:T(4,128)} %refs_2_.3), custom_call_target="tpu_custom_call" | custom-call | tf_op jit(solution)/shard_map/short_convs/pallas_call | solution.py:67
  17.7 5.5 %all-to-all-start = ((bf16[8,128,256]{2,1,0:T(8,128)(2,1)}), bf16[8,128,256]{2,1,0:T(8,128)(2,1)}, u32[]{:S(2)}, u32[]{:S(2)}) async-start(bf16[8,128,256]{2,1,0:T(8,128)(2,1)} %get-tuple-element.43), calls=%async_computation | async-start | bytes 1048576 | tf_op jit(solution)/shard_map/all_to_all | solution.py:351
  23.2 0.8 slice_bitcast_fusion
  24.0 0.6 pad_maximum_fusion.1
  24.6 1.3 collective-permute-start.11
  25.9 1.5 fusion.2
  27.4 1.5 collective-permute-start.2
  28.9 2.3 %collective-permute-done.3 = bf16[128,2048]{1,0:T(8,128)(2,1)S(1)} collective-permute-done((bf16[128,2048]{1,0:T(8,128)(2,1)}, bf16[128,2048]{1,0:T(8,128)(2,1)S(1)}, u32[]{:S(2)}, u32[]{:S(2)}) %collective-permute-start.3) | collective-permute-done | bytes 524320 | tf_op jit(solution)/shard_map/ppermute | solution.py:22
  31.2 1.5 fusion.3
  32.6 1.5 collective-permute-start.4
  34.2 2.5 %fusion.4 = bf16[128,512]{1,0:T(8,128)(2,1)} fusion(bf16[512,2048]{1,0:T(8,128)(2,1)S(1)} %copy-done, bf16[128,2048]{1,0:T(8,128)(2,1)} %collective-permute-done.5), kind=kOutput, calls=%fused_computation.10 | convolution fusion | flops 268500992 | bytes 2752512 | tf_op jit(solution)/shard_map/dot_general | solution.py:187
  37.1 0.8 fusion.1.refs_2_
  37.9 0.6 convert_element_type.86.refs_9_
  38.9 5.2 %collective-permute-done.6.refs_5_ = bf16[128,512]{1,0:T(8,128)(2,1)S(1)} collective-permute-done((bf16[128,512]{1,0:T(8,128)(2,1)}, bf16[128,512]{1,0:T(8,128)(2,1)S(1)}, u32[]{:S(2)}, u32[]{:S(2)}) %collective-permute-start.6) | collective-permute-done | bytes 131104 | tf_op jit(solution)/shard_map/ppermute | solution.py:22
  44.1 0.7 copy-done.5
  44.8 0.9 copy-done.6
  45.7 1.0 grad_long.1
  46.7 0.8 copy-done.4
  47.5 4.6 %all-to-all-start.1 = ((bf16[8,128,256]{2,1,0:T(8,128)(2,1)}), bf16[8,128,256]{2,1,0:T(8,128)(2,1)}, u32[]{:S(2)}, u32[]{:S(2)}) async-start(bf16[8,128,256]{2,1,0:T(8,128)(2,1)} %copy-done.4), calls=%async_computation.1 | async-start | bytes 1048576 | tf_op jit(solution)/shard_map/all_to_all | solution.py:351
  52.0 7.4 %long_out.1 = (f32[2,256,1024]{2,1,0:T(8,128)}, bf16[1024,256]{1,0:T(8,128)(2,1)}) custom-call(bf16[2,1024,1024]{2,1,0:T(8,128)(2,1)} %constant.82.clone.waves_ref, f32[2,256,1024]{2,1,0:T(8,128)} %filter_spectrum.1.filter_spec_ref, bf16[1024,256]{1,0:T(8,128)(2,1)} %bitcast.6.product_ref, f32[1,256]{1,0:T(1,128)} %bitcast.56), custom_call_target="tpu_custom_call" | custom-call | tf_op jit(solution)/shard_map/long_out/pallas_call | solution.py:276
  59.4 1.8 %dynamic-slice_bitcast_fusion.3 = (bf16[4,128,256]{2,1,0:T(8,128)(2,1)}, bf16[4,1,128,256]{3,2,1,0:T(8,128)(2,1)S(1)}) fusion(bf16[4,2,128,256]{3,2,1,0:T(8,128)(2,1)} %bitcast.54, s32[]{:T(128)S(6)} %select_n.59, s32[]{:T(128)S(6)} %select_n.58), kind=kLoop, calls=%fused_computation.32 | loop fusion | bytes 1048584 | tf_op jit(solution)/shard_map/jit(dynamic_index_in_dim)/squeeze | solution.py:407
  61.7 1.5 collective-permute-done.7
  63.2 1.7 %fusion.10 = (bf16[2,128,256]{2,1,0:T(8,128)(2,1)}, bf16[2,128,256]{2,1,0:T(8,128)(2,1)S(1)}, bf16[2,128,256]{2,1,0:T(8,128)(2,1)}, bf16[2,128,256]{2,1,0:T(8,128)(2,1)}) fusion(s32[]{:T(128)S(6)} %select_n.64, bf16[4,1,128,256]{3,2,1,0:T(8,128)(2,1)S(1)} %get-tuple-element.86, bf16[4,1,128,256]{3,2,1,0:T(8,128)(2,1)} %bitcast.10, s32[]{:T(128)S(6)} %select_n.61, ...), kind=kLoop, calls=%fused_computation.34 | loop fusion | flops 262144 | bytes 1048592 | tf_op jit(solution)/shard_map/jit(dynamic_index_in_dim)/squeeze | solution.py:411
  64.9 1.9 %collective-permute-start.8 = (bf16[2,128,256]{2,1,0:T(8,128)(2,1)}, bf16[2,128,256]{2,1,0:T(8,128)(2,1)S(1)}, u32[]{:S(2)}, u32[]{:S(2)}) collective-permute-start(bf16[2,128,256]{2,1,0:T(8,128)(2,1)} %get-tuple-element.83), channel_id=1, source_target_pairs={{0,2},{1,3},{2,0},{3,1},{4,6},{5,7},{6,4},{7,5},{8,10},{9,11},{10,... | collective-permute-start | bytes 393224 | tf_op jit(solution)/shard_map/ppermute | solution.py:22
  66.8 2.4 %collective-permute-start.9 = (bf16[2,128,256]{2,1,0:T(8,128)(2,1)}, bf16[2,128,256]{2,1,0:T(8,128)(2,1)S(1)}, u32[]{:S(2)}, u32[]{:S(2)}) collective-permute-start(bf16[2,128,256]{2,1,0:T(8,128)(2,1)} %get-tuple-element.84), channel_id=1, source_target_pairs={{0,4},{1,5},{2,6},{3,7},{4,0},{5,1},{6,2},{7,3},{8,12},{9,13},{10,... | collective-permute-start | bytes 393224 | tf_op jit(solution)/shard_map/ppermute | solution.py:22
  69.3 3.5 %collective-permute-done.8.refs_4_ = bf16[2,128,256]{2,1,0:T(8,128)(2,1)S(1)} collective-permute-done((bf16[2,128,256]{2,1,0:T(8,128)(2,1)}, bf16[2,128,256]{2,1,0:T(8,128)(2,1)S(1)}, u32[]{:S(2)}, u32[]{:S(2)}) %collective-permute-start.8) | collective-permute-done | bytes 131104 | tf_op jit(solution)/shard_map/ppermute | solution.py:22
  72.7 8.8 %grad_product.1 = (bf16[8,130,256]{2,1,0:T(8,128)(2,1)}, f32[256,1024]{1,0:T(8,128)}, f32[1,256]{1,0:T(1,128)}) custom-call(bf16[2,1024,1024]{2,1,0:T(8,128)(2,1)} %constant.82.clone.waves_ref, f32[2,256,1024]{2,1,0:T(8,128)} %filter_spectrum.1.filter_spec_ref, f32[2,256,1024]{2,1,0:T(8,128)} %get-tuple-element.47.spec_ref, ...), custom_call_target="tpu_custom_call" | custom-call | tf_op jit(solution)/shard_map/grad_product/pallas_call | solution.py:276
  81.5 4.5 %all-to-all-start.2 = ((bf16[8,130,256]{2,1,0:T(8,128)(2,1)}), bf16[8,130,256]{2,1,0:T(8,128)(2,1)}, u32[]{:S(2)}, u32[]{:S(2)}) async-start(bf16[8,130,256]{2,1,0:T(8,128)(2,1)} %get-tuple-element.52), calls=%async_computation.2 | async-start | bytes 1114112 | tf_op jit(solution)/shard_map/all_to_all | solution.py:356
  86.0 2.6 %gate.1 = (bf16[8,128,256]{2,1,0:T(8,128)(2,1)S(1)}, bf16[128,512]{1,0:T(8,128)(2,1)S(1)}, bf16[128,512]{1,0:T(8,128)(2,1)S(1)}, bf16[128,512]{1,0:T(8,128)(2,1)S(1)}, bf16[128,512]{1,0:T(8,128)(2,1)S(1)}) custom-call(s32[1]{0:T(128)} %bitcast.5.refs_0_, s32[1]{0:T(128)} %bitcast.refs_0_.refs_1_, bf16[8,128,256]{2,1,0:T(8,128)(2,1)S(1)} %copy-done.1, ...), custom_call_target="tpu_custom_call" | custom-call | tf_op jit(solution)/shard_map/gate/pallas_call | solution.py:67
  89.2 1.5 collective-permute-start.13
  90.8 1.5 collective-permute-start.12
  92.3 1.5 collective-permute-start.15
  93.7 1.1 constant_dynamic-update-slice_fusion.3
  94.9 1.1 constant_dynamic-update-slice_fusion
  96.0 1.6 %collective-permute-done.13 = bf16[128,512]{1,0:T(8,128)(2,1)S(1)} collective-permute-done((bf16[128,512]{1,0:T(8,128)(2,1)S(1)}, bf16[128,512]{1,0:T(8,128)(2,1)S(1)}, u32[]{:S(2)}, u32[]{:S(2)}) %collective-permute-start.13) | collective-permute-done | bytes 131104 | tf_op jit(solution)/shard_map/ppermute | solution.py:22
  97.7 4.4 %all-to-all-done.2.refs_5_ = bf16[8,130,256]{2,1,0:T(8,128)(2,1)} async-done(((bf16[8,130,256]{2,1,0:T(8,128)(2,1)}), bf16[8,130,256]{2,1,0:T(8,128)(2,1)}, u32[]{:S(2)}, u32[]{:S(2)}) %all-to-all-start.2) | async-done | bytes 532512 | tf_op jit(solution)/shard_map/all_to_all | solution.py:356
  102.2 3.3 %convolution_convert_fusion = bf16[256,2048]{1,0:T(8,128)(2,1)} fusion(bf16[512,2048]{1,0:T(8,128)(2,1)} %copy-done.7, bf16[512,512]{1,0:T(8,128)(2,1)S(1)} %pad_maximum_fusion, s32[]{:T(128)S(6)} %select_n.66), kind=kOutput, calls=%fused_computation.2 | convolution fusion | flops 537395200 | bytes 3407876 | tf_op jit(solution)/shard_map/dot_general | solution.py:187
  105.5 3.0 %collective-permute-done.16 = bf16[256,2048]{1,0:T(8,128)(2,1)} collective-permute-done((bf16[256,2048]{1,0:T(8,128)(2,1)}, bf16[256,2048]{1,0:T(8,128)(2,1)}, u32[]{:S(2)}, u32[]{:S(2)}) %collective-permute-start.16) | collective-permute-done | bytes 1048608 | tf_op jit(solution)/shard_map/ppermute | solution.py:22
  108.5 2.6 %fusion = bf16[256,2048]{1,0:T(8,128)(2,1)S(1)} fusion(bf16[512,256]{1,0:T(8,128)(2,1)S(1)} %constant_dynamic-slice_fusion, bf16[512,2048]{1,0:T(8,128)(2,1)} %copy-done.7, bf16[256,2048]{1,0:T(8,128)(2,1)} %collective-permute-done.16), kind=kOutput, calls=%fused_computation.1 | convolution fusion | flops 538443776 | bytes 4456448 | tf_op jit(solution)/shard_map/dot_general | solution.py:187
  111.1 5.7 %stream_grads.1 = (bf16[128,6144]{1,0:T(8,128)(2,1)}, f32[4,6144]{1,0:T(4,128)}) custom-call(bf16[128,6144]{1,0:T(8,128)(2,1)} %refs_0_.3, f32[2,6144]{1,0:T(2,128)} %convert_element_type.77.refs_1_, f32[3,6144]{1,0:T(4,128)} %refs_2_.3, bf16[8,128,256]{2,1,0:T(8,128)(2,1)} %copy-done.2, bf16[8,128,256]{2,1,0:T(8,128)(2,1)} %copy-done.3, ...), custom_call_target="tpu_custom_call" | custom-call | tf_op jit(solution)/shard_map/stream_grads/pallas_call | solution.py:67
  117.4 1.5 collective-permute-start.19
  118.9 1.5 collective-permute-start.17
  120.6 1.7 %collective-permute-start.22 = (bf16[64,2048]{1,0:T(8,128)(2,1)S(1)}, bf16[64,2048]{1,0:T(8,128)(2,1)S(1)}, u32[]{:S(2)}, u32[]{:S(2)}) collective-permute-start(bf16[64,2048]{1,0:T(8,128)(2,1)S(1)} %get-tuple-element.79), channel_id=1, source_target_pairs={{0,4},{1,5},{2,6},{3,7},{4,0},{5,1},{6,2},{7,3},{8,12},{9,13},{10,... | collective-permute-start | bytes 786440 | tf_op jit(solution)/shard_map/ppermute | solution.py:22
  122.4 1.6 %collective-permute-done.18 = f32[4,6144]{1,0:T(4,128)S(1)} collective-permute-done((f32[4,6144]{1,0:T(4,128)}, f32[4,6144]{1,0:T(4,128)S(1)}, u32[]{:S(2)}, u32[]{:S(2)}) %collective-permute-start.18) | collective-permute-done | bytes 98336 | tf_op jit(solution)/shard_map/ppermute | solution.py:22
  123.9 1.3 collective-permute-start.23
  125.2 0.9 add_add_fusion
  127.6 1.5 collective-permute-start.28
  129.1 4.2 %collective-permute-done.29 = bf16[256,256]{1,0:T(8,128)(2,1)S(1)} collective-permute-done((bf16[256,256]{1,0:T(8,128)(2,1)S(1)}, bf16[256,256]{1,0:T(8,128)(2,1)S(1)}, u32[]{:S(2)}, u32[]{:S(2)}) %collective-permute-start.29) | collective-permute-done | bytes 131104 | tf_op jit(solution)/shard_map/ppermute | solution.py:22
  133.9 2.0 %collective-permute-done.28 = bf16[256,256]{1,0:T(8,128)(2,1)S(1)} collective-permute-done((bf16[256,256]{1,0:T(8,128)(2,1)S(1)}, bf16[256,256]{1,0:T(8,128)(2,1)S(1)}, u32[]{:S(2)}, u32[]{:S(2)}) %collective-permute-start.28) | collective-permute-done | bytes 131104 | tf_op jit(solution)/shard_map/ppermute | solution.py:22
  136.0 2.4 %collective-permute-done.27 = bf16[256,256]{1,0:T(8,128)(2,1)S(1)} collective-permute-done((bf16[256,256]{1,0:T(8,128)(2,1)S(1)}, bf16[256,256]{1,0:T(8,128)(2,1)S(1)}, u32[]{:S(2)}, u32[]{:S(2)}) %collective-permute-start.27) | collective-permute-done | bytes 131104 | tf_op jit(solution)/shard_map/ppermute | solution.py:22
  138.3 0.8 add_multiply_fusion
  139.1 2.9 %collective-permute-done.22 = bf16[64,2048]{1,0:T(8,128)(2,1)S(1)} collective-permute-done((bf16[64,2048]{1,0:T(8,128)(2,1)S(1)}, bf16[64,2048]{1,0:T(8,128)(2,1)S(1)}, u32[]{:S(2)}, u32[]{:S(2)}) %collective-permute-start.22) | collective-permute-done | bytes 262176 | tf_op jit(solution)/shard_map/ppermute | solution.py:22
  142.0 4.4 %collective-permute-start.25 = (f32[3,6144]{1,0:T(4,128)S(1)}, f32[3,6144]{1,0:T(4,128)S(1)}, u32[]{:S(2)}, u32[]{:S(2)}) collective-permute-start(f32[3,6144]{1,0:T(4,128)S(1)} %slice_add_fusion), channel_id=1, source_target_pairs={{0,4},{1,5},{2,6},{3,7},{4,0},{5,1},{6,2},{7,3},{8,12},{9,13},{10,... | collective-permute-start | bytes 221192 | tf_op jit(solution)/shard_map/ppermute | solution.py:22
  146.4 2.6 %collective-permute-start.26 = (f32[3,6144]{1,0:T(4,128)S(1)}, f32[3,6144]{1,0:T(4,128)S(1)}, u32[]{:S(2)}, u32[]{:S(2)}) collective-permute-start(f32[3,6144]{1,0:T(4,128)S(1)} %slice_add_fusion), channel_id=1, source_target_pairs={{0,6},{1,7},{2,4},{3,5},{4,2},{5,3},{6,0},{7,1},{8,14},{9,15},{10,... | collective-permute-start | bytes 221192 | tf_op jit(solution)/shard_map/ppermute | solution.py:22
  149.0 0.9 fusion.7
  150.0 3.4 %collective-permute-done.25 = f32[3,6144]{1,0:T(4,128)S(1)} collective-permute-done((f32[3,6144]{1,0:T(4,128)S(1)}, f32[3,6144]{1,0:T(4,128)S(1)}, u32[]{:S(2)}, u32[]{:S(2)}) %collective-permute-start.25) | collective-permute-done | bytes 73760 | tf_op jit(solution)/shard_map/ppermute | solution.py:22
  153.4 1.0 collective-permute-done.24
  154.4 0.7 add_multiply_fusion.1
  (67 shorter events, 5.4 us)
Async XLA Ops:
  0.6 25.3 %copy-start = (bf16[512,2048]{1,0:T(8,128)(2,1)S(1)}, bf16[512,2048]{1,0:T(8,128)(2,1)}, u32[]{:S(2)}) copy-start(bf16[512,2048]{1,0:T(8,128)(2,1)} %param.11) | copy-start | bytes 6291460
  0.6 25.2 %collective-permute-start.1 = (bf16[128,2048]{1,0:T(8,128)(2,1)}, bf16[128,2048]{1,0:T(8,128)(2,1)S(1)}, u32[]{:S(2)}, u32[]{:S(2)}) collective-permute-start(bf16[128,2048]{1,0:T(8,128)(2,1)} %param.12), channel_id=1, source_target_pairs={{0,8},{8,0},{16,24},{24,16},{1,9},{9,1},{17,25},{25,17},{2,10},{10... | collective-permute-start | bytes 1572872 | tf_op jit(solution)/shard_map/ppermute | solution.py:22
  4.6 8.9 %collective-permute-start = (bf16[2,6144]{1,0:T(2,128)(2,1)S(1)}, bf16[2,6144]{1,0:T(2,128)(2,1)S(1)}, u32[]{:S(2)}, u32[]{:S(2)}) collective-permute-start(bf16[2,6144]{1,0:T(2,128)(2,1)S(1)} %slice.22), channel_id=1, source_target_pairs={{0,1},{1,2},{2,3},{3,4},{4,5},{5,6},{6,7},{8,9},{9,10},{10,11},{11... | collective-permute-start | bytes 73736 | tf_op jit(solution)/shard_map/ppermute | solution.py:18
  6.0 25.1 %collective-permute-start.3 = (bf16[128,2048]{1,0:T(8,128)(2,1)}, bf16[128,2048]{1,0:T(8,128)(2,1)S(1)}, u32[]{:S(2)}, u32[]{:S(2)}) collective-permute-start(bf16[128,2048]{1,0:T(8,128)(2,1)} %param.12), channel_id=1, source_target_pairs={{0,16},{8,24},{16,0},{24,8},{1,17},{9,25},{17,1},{25,9},{2,18},{10... | collective-permute-start | bytes 1572872 | tf_op jit(solution)/shard_map/ppermute | solution.py:22
  7.6 26.5 %collective-permute-start.5 = (bf16[128,2048]{1,0:T(8,128)(2,1)}, bf16[128,2048]{1,0:T(8,128)(2,1)}, u32[]{:S(2)}, u32[]{:S(2)}) collective-permute-start(bf16[128,2048]{1,0:T(8,128)(2,1)} %param.12), channel_id=1, source_target_pairs={{0,24},{8,16},{16,8},{24,0},{1,25},{9,17},{17,9},{25,1},{2,26},{10... | collective-permute-start | bytes 1572872 | tf_op jit(solution)/shard_map/ppermute | solution.py:22
  17.7 29.8 %all-to-all-start = ((bf16[8,128,256]{2,1,0:T(8,128)(2,1)}), bf16[8,128,256]{2,1,0:T(8,128)(2,1)}, u32[]{:S(2)}, u32[]{:S(2)}) async-start(bf16[8,128,256]{2,1,0:T(8,128)(2,1)} %get-tuple-element.43), calls=%async_computation | async-start | bytes 1048576 | tf_op jit(solution)/shard_map/all_to_all | solution.py:351
  24.6 13.3 %collective-permute-start.11 = (bf16[2,8,2,256]{3,2,1,0:T(2,128)(2,1)}, bf16[2,8,2,256]{3,2,1,0:T(2,128)(2,1)S(1)}, u32[]{:S(2)}, u32[]{:S(2)}) collective-permute-start(bf16[2,8,2,256]{3,2,1,0:T(2,128)(2,1)} %pad_maximum_fusion.1), channel_id=1, source_target_pairs={{1,0},{2,1},{3,2},{4,3},{5,4},{6,5},{7,6},{9,8},{10,9},{11,10},{12... | collective-permute-start | bytes 49160 | tf_op jit(solution)/shard_map/ppermute | solution.py:18
  25.9 5.2 %copy-start.9 = (bf16[128,2048]{1,0:T(8,128)(2,1)}, bf16[128,2048]{1,0:T(8,128)(2,1)S(1)}, u32[]{:S(2)}) copy-start(bf16[128,2048]{1,0:T(8,128)(2,1)S(1)} %collective-permute-done.1) | copy-start | bytes 1572868
  27.4 9.6 %copy-start.8 = (bf16[128,2048]{1,0:T(8,128)(2,1)S(1)}, bf16[128,2048]{1,0:T(8,128)(2,1)}, u32[]{:S(2)}) copy-start(bf16[128,2048]{1,0:T(8,128)(2,1)} %param.12) | copy-start | bytes 1572868
  27.4 11.1 %collective-permute-start.2 = (bf16[128,512]{1,0:T(8,128)(2,1)}, bf16[128,512]{1,0:T(8,128)(2,1)S(1)}, u32[]{:S(2)}, u32[]{:S(2)}) collective-permute-start(bf16[128,512]{1,0:T(8,128)(2,1)} %fusion.2), channel_id=1, source_target_pairs={{0,8},{8,0},{16,24},{24,16},{1,9},{9,1},{17,25},{25,17},{2,10},{10... | collective-permute-start | bytes 393224 | tf_op jit(solution)/shard_map/ppermute | solution.py:22
  31.2 3.0 %copy-start.11 = (bf16[128,2048]{1,0:T(8,128)(2,1)}, bf16[128,2048]{1,0:T(8,128)(2,1)S(1)}, u32[]{:S(2)}) copy-start(bf16[128,2048]{1,0:T(8,128)(2,1)S(1)} %collective-permute-done.3) | copy-start | bytes 1572868
  32.6 12.1 %copy-start.1 = (bf16[8,128,256]{2,1,0:T(8,128)(2,1)S(1)}, bf16[8,128,256]{2,1,0:T(8,128)(2,1)}, u32[]{:S(2)}) copy-start(bf16[8,128,256]{2,1,0:T(8,128)(2,1)} %get-tuple-element.40.refs_1_.refs_2_) | copy-start | bytes 1572868
  32.6 6.2 %collective-permute-start.4 = (bf16[128,512]{1,0:T(8,128)(2,1)}, bf16[128,512]{1,0:T(8,128)(2,1)S(1)}, u32[]{:S(2)}, u32[]{:S(2)}) collective-permute-start(bf16[128,512]{1,0:T(8,128)(2,1)} %fusion.3), channel_id=1, source_target_pairs={{0,16},{8,24},{16,0},{24,8},{1,17},{9,25},{17,1},{25,9},{2,18},{10... | collective-permute-start | bytes 393224 | tf_op jit(solution)/shard_map/ppermute | solution.py:22
  36.7 7.4 %collective-permute-start.6 = (bf16[128,512]{1,0:T(8,128)(2,1)}, bf16[128,512]{1,0:T(8,128)(2,1)S(1)}, u32[]{:S(2)}, u32[]{:S(2)}) collective-permute-start(bf16[128,512]{1,0:T(8,128)(2,1)} %fusion.4), channel_id=1, source_target_pairs={{0,24},{8,16},{16,8},{24,0},{1,25},{9,17},{17,9},{25,1},{2,26},{10... | collective-permute-start | bytes 393224 | tf_op jit(solution)/shard_map/ppermute | solution.py:22
  44.1 0.7 copy-start.5
  44.8 0.9 copy-start.6
  46.7 0.8 copy-start.4
  47.5 44.8 %copy-start.2 = (bf16[8,128,256]{2,1,0:T(8,128)(2,1)}, bf16[8,128,256]{2,1,0:T(8,128)(2,1)S(1)}, u32[]{:S(2)}) copy-start(bf16[8,128,256]{2,1,0:T(8,128)(2,1)S(1)} %get-tuple-element.42.refs_3_) | copy-start | bytes 1572868
  47.5 25.3 %all-to-all-start.1 = ((bf16[8,128,256]{2,1,0:T(8,128)(2,1)}), bf16[8,128,256]{2,1,0:T(8,128)(2,1)}, u32[]{:S(2)}, u32[]{:S(2)}) async-start(bf16[8,128,256]{2,1,0:T(8,128)(2,1)} %copy-done.4), calls=%async_computation.1 | async-start | bytes 1048576 | tf_op jit(solution)/shard_map/all_to_all | solution.py:351
  61.2 2.0 %collective-permute-start.7 = (bf16[4,128,256]{2,1,0:T(8,128)(2,1)}, bf16[4,128,256]{2,1,0:T(8,128)(2,1)}, u32[]{:S(2)}, u32[]{:S(2)}) collective-permute-start(bf16[4,128,256]{2,1,0:T(8,128)(2,1)} %get-tuple-element.85), channel_id=1, source_target_pairs={{0,1},{1,0},{2,3},{3,2},{4,5},{5,4},{6,7},{7,6},{8,9},{9,8},{10,11... | collective-permute-start | bytes 786440 | tf_op jit(solution)/shard_map/ppermute | solution.py:22
  64.9 7.9 %collective-permute-start.8 = (bf16[2,128,256]{2,1,0:T(8,128)(2,1)}, bf16[2,128,256]{2,1,0:T(8,128)(2,1)S(1)}, u32[]{:S(2)}, u32[]{:S(2)}) collective-permute-start(bf16[2,128,256]{2,1,0:T(8,128)(2,1)} %get-tuple-element.83), channel_id=1, source_target_pairs={{0,2},{1,3},{2,0},{3,1},{4,6},{5,7},{6,4},{7,5},{8,10},{9,11},{10,... | collective-permute-start | bytes 393224 | tf_op jit(solution)/shard_map/ppermute | solution.py:22
  66.8 19.3 %collective-permute-start.9 = (bf16[2,128,256]{2,1,0:T(8,128)(2,1)}, bf16[2,128,256]{2,1,0:T(8,128)(2,1)S(1)}, u32[]{:S(2)}, u32[]{:S(2)}) collective-permute-start(bf16[2,128,256]{2,1,0:T(8,128)(2,1)} %get-tuple-element.84), channel_id=1, source_target_pairs={{0,4},{1,5},{2,6},{3,7},{4,0},{5,1},{6,2},{7,3},{8,12},{9,13},{10,... | collective-permute-start | bytes 393224 | tf_op jit(solution)/shard_map/ppermute | solution.py:22
  69.1 16.9 %collective-permute-start.10 = (bf16[2,128,256]{2,1,0:T(8,128)(2,1)}, bf16[2,128,256]{2,1,0:T(8,128)(2,1)}, u32[]{:S(2)}, u32[]{:S(2)}) collective-permute-start(bf16[2,128,256]{2,1,0:T(8,128)(2,1)} %get-tuple-element.81), channel_id=1, source_target_pairs={{0,6},{1,7},{2,4},{3,5},{4,2},{5,3},{6,0},{7,1},{8,14},{9,15},{10,... | collective-permute-start | bytes 393224 | tf_op jit(solution)/shard_map/ppermute | solution.py:22
  81.5 20.6 %all-to-all-start.2 = ((bf16[8,130,256]{2,1,0:T(8,128)(2,1)}), bf16[8,130,256]{2,1,0:T(8,128)(2,1)}, u32[]{:S(2)}, u32[]{:S(2)}) async-start(bf16[8,130,256]{2,1,0:T(8,128)(2,1)} %get-tuple-element.52), calls=%async_computation.2 | async-start | bytes 1114112 | tf_op jit(solution)/shard_map/all_to_all | solution.py:356
  86.0 8.8 %copy-start.10 = (bf16[128,2048]{1,0:T(8,128)(2,1)S(1)}, bf16[128,2048]{1,0:T(8,128)(2,1)}, u32[]{:S(2)}) copy-start(bf16[128,2048]{1,0:T(8,128)(2,1)} %copy-done.9) | copy-start | bytes 1572868
  86.0 8.9 %copy-start.12 = (bf16[128,2048]{1,0:T(8,128)(2,1)S(1)}, bf16[128,2048]{1,0:T(8,128)(2,1)}, u32[]{:S(2)}) copy-start(bf16[128,2048]{1,0:T(8,128)(2,1)} %copy-done.11) | copy-start | bytes 1572868
  88.7 3.6 %copy-start.3 = (bf16[8,128,256]{2,1,0:T(8,128)(2,1)}, bf16[8,128,256]{2,1,0:T(8,128)(2,1)S(1)}, u32[]{:S(2)}) copy-start(bf16[8,128,256]{2,1,0:T(8,128)(2,1)S(1)} %get-tuple-element.57.refs_4_) | copy-start | bytes 1572868
  88.7 7.4 %collective-permute-start.14 = (bf16[128,512]{1,0:T(8,128)(2,1)S(1)}, bf16[128,512]{1,0:T(8,128)(2,1)S(1)}, u32[]{:S(2)}, u32[]{:S(2)}) collective-permute-start(bf16[128,512]{1,0:T(8,128)(2,1)S(1)} %get-tuple-element.61), channel_id=1, source_target_pairs={{0,24},{8,16},{16,8},{24,0},{1,25},{9,17},{17,9},{25,1},{2,26},{10... | collective-permute-start | bytes 393224 | tf_op jit(solution)/shard_map/ppermute | solution.py:22
  89.2 8.4 %collective-permute-start.13 = (bf16[128,512]{1,0:T(8,128)(2,1)S(1)}, bf16[128,512]{1,0:T(8,128)(2,1)S(1)}, u32[]{:S(2)}, u32[]{:S(2)}) collective-permute-start(bf16[128,512]{1,0:T(8,128)(2,1)S(1)} %get-tuple-element.60), channel_id=1, source_target_pairs={{0,16},{8,24},{16,0},{24,8},{1,17},{9,25},{17,1},{25,9},{2,18},{10... | collective-permute-start | bytes 393224 | tf_op jit(solution)/shard_map/ppermute | solution.py:22
  90.8 6.9 %collective-permute-start.12 = (bf16[128,512]{1,0:T(8,128)(2,1)S(1)}, bf16[128,512]{1,0:T(8,128)(2,1)S(1)}, u32[]{:S(2)}, u32[]{:S(2)}) collective-permute-start(bf16[128,512]{1,0:T(8,128)(2,1)S(1)} %get-tuple-element.59), channel_id=1, source_target_pairs={{0,8},{8,0},{16,24},{24,16},{1,9},{9,1},{17,25},{25,17},{2,10},{10... | collective-permute-start | bytes 393224 | tf_op jit(solution)/shard_map/ppermute | solution.py:22
  92.3 5.5 %collective-permute-start.15 = (f32[8,2,256]{2,1,0:T(2,128)S(1)}, f32[8,2,256]{2,1,0:T(2,128)S(1)}, u32[]{:S(2)}, u32[]{:S(2)}) collective-permute-start(f32[8,2,256]{2,1,0:T(2,128)S(1)} %convert_multiply_fusion), channel_id=1, source_target_pairs={{1,0},{2,1},{3,2},{4,3},{5,4},{6,5},{7,6},{9,8},{10,9},{11,10},{12... | collective-permute-start | bytes 49160 | tf_op jit(solution)/shard_map/ppermute | solution.py:18
  96.0 1.7 %copy-start.7 = (bf16[512,2048]{1,0:T(8,128)(2,1)}, bf16[512,2048]{1,0:T(8,128)(2,1)S(1)}, u32[]{:S(2)}) copy-start(bf16[512,2048]{1,0:T(8,128)(2,1)S(1)} %constant_dynamic-update-slice_fusion) | copy-start | bytes 6291460
  97.7 13.3 %copy-start.14 = (f32[8,2,256]{2,1,0:T(2,128)}, f32[8,2,256]{2,1,0:T(2,128)S(1)}, u32[]{:S(2)}) copy-start(f32[8,2,256]{2,1,0:T(2,128)S(1)} %collective-permute-done.15.refs_8_) | copy-start | bytes 49156
  105.5 3.0 %collective-permute-start.16 = (bf16[256,2048]{1,0:T(8,128)(2,1)}, bf16[256,2048]{1,0:T(8,128)(2,1)}, u32[]{:S(2)}, u32[]{:S(2)}) collective-permute-start(bf16[256,2048]{1,0:T(8,128)(2,1)} %convolution_convert_fusion), channel_id=1, source_target_pairs={{0,1},{1,0},{2,3},{3,2},{4,5},{5,4},{6,7},{7,6},{8,9},{9,8},{10,11... | collective-permute-start | bytes 3145736 | tf_op jit(solution)/shard_map/ppermute | solution.py:22
  116.8 9.4 %copy-start.13 = (f32[256,1024]{1,0:T(8,128)S(1)}, f32[256,1024]{1,0:T(8,128)}, u32[]{:S(2)}) copy-start(f32[256,1024]{1,0:T(8,128)} %get-tuple-element.74) | copy-start | bytes 3145732
  116.8 7.1 %collective-permute-start.18 = (f32[4,6144]{1,0:T(4,128)}, f32[4,6144]{1,0:T(4,128)S(1)}, u32[]{:S(2)}, u32[]{:S(2)}) collective-permute-start(f32[4,6144]{1,0:T(4,128)} %get-tuple-element.71), channel_id=1, source_target_pairs={{0,16},{8,24},{16,0},{24,8},{1,17},{9,25},{17,1},{25,9},{2,18},{10... | collective-permute-start | bytes 294920 | tf_op jit(solution)/shard_map/ppermute | solution.py:22
  117.4 7.8 %collective-permute-start.19 = (f32[4,6144]{1,0:T(4,128)}, f32[4,6144]{1,0:T(4,128)S(1)}, u32[]{:S(2)}, u32[]{:S(2)}) collective-permute-start(f32[4,6144]{1,0:T(4,128)} %get-tuple-element.71), channel_id=1, source_target_pairs={{0,24},{8,16},{16,8},{24,0},{1,25},{9,17},{17,9},{25,1},{2,26},{10... | collective-permute-start | bytes 294920 | tf_op jit(solution)/shard_map/ppermute | solution.py:22
  118.9 6.3 %collective-permute-start.17 = (f32[4,6144]{1,0:T(4,128)}, f32[4,6144]{1,0:T(4,128)S(1)}, u32[]{:S(2)}, u32[]{:S(2)}) collective-permute-start(f32[4,6144]{1,0:T(4,128)} %get-tuple-element.71), channel_id=1, source_target_pairs={{0,8},{8,0},{16,24},{24,16},{1,9},{9,1},{17,25},{25,17},{2,10},{10... | collective-permute-start | bytes 294920 | tf_op jit(solution)/shard_map/ppermute | solution.py:22
  120.5 18.6 %collective-permute-start.21 = (bf16[64,2048]{1,0:T(8,128)(2,1)S(1)}, bf16[64,2048]{1,0:T(8,128)(2,1)S(1)}, u32[]{:S(2)}, u32[]{:S(2)}) collective-permute-start(bf16[64,2048]{1,0:T(8,128)(2,1)S(1)} %get-tuple-element.80), channel_id=1, source_target_pairs={{0,2},{1,3},{2,0},{3,1},{4,6},{5,7},{6,4},{7,5},{8,10},{9,11},{10,... | collective-permute-start | bytes 786440 | tf_op jit(solution)/shard_map/ppermute | solution.py:22
  120.6 21.4 %collective-permute-start.22 = (bf16[64,2048]{1,0:T(8,128)(2,1)S(1)}, bf16[64,2048]{1,0:T(8,128)(2,1)S(1)}, u32[]{:S(2)}, u32[]{:S(2)}) collective-permute-start(bf16[64,2048]{1,0:T(8,128)(2,1)S(1)} %get-tuple-element.79), channel_id=1, source_target_pairs={{0,4},{1,5},{2,6},{3,7},{4,0},{5,1},{6,2},{7,3},{8,12},{9,13},{10,... | collective-permute-start | bytes 786440 | tf_op jit(solution)/shard_map/ppermute | solution.py:22
  123.9 18.1 %collective-permute-start.23 = (bf16[64,2048]{1,0:T(8,128)(2,1)S(1)}, bf16[64,2048]{1,0:T(8,128)(2,1)S(1)}, u32[]{:S(2)}, u32[]{:S(2)}) collective-permute-start(bf16[64,2048]{1,0:T(8,128)(2,1)S(1)} %get-tuple-element.78), channel_id=1, source_target_pairs={{0,6},{1,7},{2,4},{3,5},{4,2},{5,3},{6,0},{7,1},{8,14},{9,15},{10,... | collective-permute-start | bytes 786440 | tf_op jit(solution)/shard_map/ppermute | solution.py:22
  126.2 1.4 collective-permute-start.20
  126.3 6.9 %collective-permute-start.29 = (bf16[256,256]{1,0:T(8,128)(2,1)S(1)}, bf16[256,256]{1,0:T(8,128)(2,1)S(1)}, u32[]{:S(2)}, u32[]{:S(2)}) collective-permute-start(bf16[256,256]{1,0:T(8,128)(2,1)S(1)} %get-tuple-element.76), channel_id=1, source_target_pairs={{0,24},{8,16},{16,8},{24,0},{1,25},{9,17},{17,9},{25,1},{2,26},{10... | collective-permute-start | bytes 393224 | tf_op jit(solution)/shard_map/ppermute | solution.py:22
  127.6 8.4 %collective-permute-start.28 = (bf16[256,256]{1,0:T(8,128)(2,1)S(1)}, bf16[256,256]{1,0:T(8,128)(2,1)S(1)}, u32[]{:S(2)}, u32[]{:S(2)}) collective-permute-start(bf16[256,256]{1,0:T(8,128)(2,1)S(1)} %get-tuple-element.77), channel_id=1, source_target_pairs={{0,16},{8,24},{16,0},{24,8},{1,17},{9,25},{17,1},{25,9},{2,18},{10... | collective-permute-start | bytes 393224 | tf_op jit(solution)/shard_map/ppermute | solution.py:22
  133.3 5.0 %collective-permute-start.27 = (bf16[256,256]{1,0:T(8,128)(2,1)S(1)}, bf16[256,256]{1,0:T(8,128)(2,1)S(1)}, u32[]{:S(2)}, u32[]{:S(2)}) collective-permute-start(bf16[256,256]{1,0:T(8,128)(2,1)S(1)} %get-tuple-element.75), channel_id=1, source_target_pairs={{0,8},{8,0},{16,24},{24,16},{1,9},{9,1},{17,25},{25,17},{2,10},{10... | collective-permute-start | bytes 393224 | tf_op jit(solution)/shard_map/ppermute | solution.py:22
  142.0 11.4 %collective-permute-start.25 = (f32[3,6144]{1,0:T(4,128)S(1)}, f32[3,6144]{1,0:T(4,128)S(1)}, u32[]{:S(2)}, u32[]{:S(2)}) collective-permute-start(f32[3,6144]{1,0:T(4,128)S(1)} %slice_add_fusion), channel_id=1, source_target_pairs={{0,4},{1,5},{2,6},{3,7},{4,0},{5,1},{6,2},{7,3},{8,12},{9,13},{10,... | collective-permute-start | bytes 221192 | tf_op jit(solution)/shard_map/ppermute | solution.py:22
  146.4 7.0 %collective-permute-start.26 = (f32[3,6144]{1,0:T(4,128)S(1)}, f32[3,6144]{1,0:T(4,128)S(1)}, u32[]{:S(2)}, u32[]{:S(2)}) collective-permute-start(f32[3,6144]{1,0:T(4,128)S(1)} %slice_add_fusion), channel_id=1, source_target_pairs={{0,6},{1,7},{2,4},{3,5},{4,2},{5,3},{6,0},{7,1},{8,14},{9,15},{10,... | collective-permute-start | bytes 221192 | tf_op jit(solution)/shard_map/ppermute | solution.py:22
  149.0 5.3 %collective-permute-start.24 = (f32[3,6144]{1,0:T(4,128)S(1)}, f32[3,6144]{1,0:T(4,128)S(1)}, u32[]{:S(2)}, u32[]{:S(2)}) collective-permute-start(f32[3,6144]{1,0:T(4,128)S(1)} %slice_add_fusion), channel_id=1, source_target_pairs={{0,2},{1,3},{2,0},{3,1},{4,6},{5,7},{6,4},{7,5},{8,10},{9,11},{10,... | collective-permute-start | bytes 221192 | tf_op jit(solution)/shard_map/ppermute | solution.py:22

commit v13 on v12

--- a/solution.py
+++ b/solution.py
@@ -387,12 +387,13 @@
             filter_kernel, "filter_spectrum", waves, [], [long_filter], [], [spec], []
         )
         weights = ordered(out_proj, filter_spec)
-    found = [dot(cot, weights, 1, 1).astype(BF16) for cot in cots]
-    found = [found[0]] + [swapped(found[k], "dp", k) for k in range(1, parts_dp)]
+    formed = [dot(cot, weights, 1, 1).astype(BF16) for cot in cots]
+    found = [formed[0]] + [swapped(formed[k], "dp", k) for k in range(1, parts_dp)]
     gate_grad, grad_long_out = call(
         grad_long_kernel, "grad_long", [plane] * 2, 1, 12, me_dp, query, *found
     )
-    heads = jnp.stack([keyed[:, :2], valued[:, :2]])
+    heads = lax.optimization_barrier((keyed[:, :2], valued[:, :2], *formed))[:2]
+    heads = jnp.stack(heads)
     pair_after = passed_along(heads, "context", -1).astype(F32)
     grad_long = to_channels(ordered(grad_long_out, pair_after))
     product_f, grad_long_f = (product.astype(F32), grad_long.astype(F32))

time: 156 us -> 153 us (0.981)
  waiting for transfers between devices: 39.4 us -> 34.1 us
  starting transfers between devices: 52.1 us -> 54.7 us
    ppermute x27, waiting for transfers between devices: 35 us -> 29.1 us  [swapped(): lax.ppermute(value, axis, [(i, i ^ mask) for i in range(lax.axis_size(axi...]
    ppermute x27, starting transfers between devices: 33.3 us -> 35.4 us  [swapped(): lax.ppermute(value, axis, [(i, i ^ mask) for i in range(lax.axis_size(axi...]
    ppermute x3, waiting for transfers between devices: 0.01 us -> 1.78 us  [passed_along(): lax.ppermute(value, axis, [(source, source + steps) for source in range(i...]
  transfers between devices with their start and end apart: 33 -> 33, of which waited for: 16 -> 17; matrix products, arithmetic and copies ran while one was open for 12% -> 12% of each run, Pallas kernels for 19% -> 19%
where the time goes in v13:
time: 153 us; the launch traced here: 152 us
  starting transfers between devices  54.7 us (36%)
  Pallas kernels  34.5 us (23%)
  waiting for transfers between devices  34.1 us (22%)
  matrix products  11.6 us (8%)
  local copies, waits for them, and re-layouts  9.01 us (6%)
  other arithmetic  6.94 us (5%)
    ppermute x27, starting transfers between devices, swapped(): lax.ppermute(value, axis, [(i, i ^ mask) for i in range(lax.axis_size(axi...  35.4 us
    ppermute x27, waiting for transfers between devices, swapped(): lax.ppermute(value, axis, [(i, i ^ mask) for i in range(lax.axis_size(axi...  29.1 us
    pallas_call x3, Pallas kernels, chunked(): pl.pallas_call(kernel, out_shape=spec_out + outs, grid=(freqs // size,),...  21.6 us
    pallas_call x4, Pallas kernels, call(): pl.pallas_call(run, out_shape=outs, in_specs=[SMEM] * smem + [anywhere] *...  12.9 us
    dot_general x6, matrix products, dot(): lax.dot_general(left, right, (((left_dim,), (right_dim,)), ((), ())), pre...  11.6 us
    all_to_all x2, starting transfers between devices, to_channels(): lax.all_to_all(blocks, 'context', split_axis=0, concat_axis=0, tiled=True)  11 us
    all_to_all x1, starting transfers between devices, to_positions(): lax.all_to_all(blocks, 'context', split_axis=0, concat_axis=0, tiled=True)  4.18 us
    ppermute x3, starting transfers between devices, passed_along(): lax.ppermute(value, axis, [(source, source + steps) for source in range(i...  4.06 us
  transfers between devices with their start and end apart: 33, of which 17 were waited for; matrix products, arithmetic and copies ran while one was open for 12% of the time, Pallas kernels for 19%

profile of v13, /device:TPU:0, one launch (start us, length us, event | category | flops | bytes accessed | tf_op | source)
XLA Modules:
  0.0 151.9 jit_solution(15737608214132598917)
XLA Ops:
  0.6 3.0 %collective-permute-start.1 = (bf16[128,2048]{1,0:T(8,128)(2,1)}, bf16[128,2048]{1,0:T(8,128)(2,1)S(1)}, u32[]{:S(2)}, u32[]{:S(2)}) collective-permute-start(bf16[128,2048]{1,0:T(8,128)(2,1)} %param.12), channel_id=1, source_target_pairs={{0,8},{8,0},{16,24},{24,16},{1,9},{9,1},{17,25},{25,17},{2,10},{10... | collective-permute-start | bytes 1572872 | tf_op jit(solution)/shard_map/ppermute | solution.py:22
  3.6 1.5 %collective-permute-start.3 = (bf16[128,2048]{1,0:T(8,128)(2,1)}, bf16[128,2048]{1,0:T(8,128)(2,1)S(1)}, u32[]{:S(2)}, u32[]{:S(2)}) collective-permute-start(bf16[128,2048]{1,0:T(8,128)(2,1)} %param.12), channel_id=1, source_target_pairs={{0,16},{8,24},{16,0},{24,8},{1,17},{9,25},{17,1},{25,9},{2,18},{10... | collective-permute-start | bytes 1572872 | tf_op jit(solution)/shard_map/ppermute | solution.py:22
  5.2 0.9 slice.22
  6.1 1.3 collective-permute-start
  7.8 5.5 %filter_spectrum.1.filter_spec_ref = f32[2,256,1024]{2,1,0:T(8,128)} custom-call(bf16[2,1024,1024]{2,1,0:T(8,128)(2,1)} %constant.82.clone.waves_ref, f32[256,1024]{1,0:T(8,128)} %filter_ref.1), custom_call_target="tpu_custom_call" | custom-call | tf_op jit(solution)/shard_map/filter_spectrum/pallas_call | solution.py:276
  13.3 0.6 convert_element_type.77.refs_1_
  13.9 3.6 %short_convs.1 = (bf16[8,128,256]{2,1,0:T(8,128)(2,1)}, bf16[8,128,256]{2,1,0:T(8,128)(2,1)}, bf16[8,128,256]{2,1,0:T(8,128)(2,1)}, bf16[8,128,256]{2,1,0:T(8,128)(2,1)}) custom-call(bf16[128,6144]{1,0:T(8,128)(2,1)} %refs_0_.3, f32[2,6144]{1,0:T(2,128)} %convert_element_type.77.refs_1_, f32[3,6144]{1,0:T(4,128)} %refs_2_.3), custom_call_target="tpu_custom_call" | custom-call | tf_op jit(solution)/shard_map/short_convs/pallas_call | solution.py:67
  17.5 5.6 %all-to-all-start = ((bf16[8,128,256]{2,1,0:T(8,128)(2,1)}), bf16[8,128,256]{2,1,0:T(8,128)(2,1)}, u32[]{:S(2)}, u32[]{:S(2)}) async-start(bf16[8,128,256]{2,1,0:T(8,128)(2,1)} %get-tuple-element.45), calls=%async_computation | async-start | bytes 1048576 | tf_op jit(solution)/shard_map/all_to_all | solution.py:351
  23.2 1.5 fusion.2
  24.7 1.5 collective-permute-start.2
  26.2 2.3 %collective-permute-done.3 = bf16[128,2048]{1,0:T(8,128)(2,1)S(1)} collective-permute-done((bf16[128,2048]{1,0:T(8,128)(2,1)}, bf16[128,2048]{1,0:T(8,128)(2,1)S(1)}, u32[]{:S(2)}, u32[]{:S(2)}) %collective-permute-start.3) | collective-permute-done | bytes 524320 | tf_op jit(solution)/shard_map/ppermute | solution.py:22
  28.5 1.5 fusion.3
  30.0 1.5 collective-permute-start.4
  31.5 1.9 %fusion.4 = bf16[128,512]{1,0:T(8,128)(2,1)S(1)} fusion(bf16[512,2048]{1,0:T(8,128)(2,1)S(1)} %copy-done, bf16[128,2048]{1,0:T(8,128)(2,1)} %collective-permute-done.5), kind=kOutput, calls=%fused_computation.10 | convolution fusion | flops 268500992 | bytes 2752512 | tf_op jit(solution)/shard_map/dot_general | solution.py:187
  33.5 0.8 fusion.1.refs_2_
  34.3 0.8 slice.23
  35.1 0.8 slice.24
  35.9 1.3 collective-permute-start.11
  37.2 1.8 %collective-permute-done.11 = bf16[2,8,2,256]{3,2,1,0:T(2,128)(2,1)S(1)} collective-permute-done((bf16[2,8,2,256]{3,2,1,0:T(2,128)(2,1)S(1)}, bf16[2,8,2,256]{3,2,1,0:T(2,128)(2,1)S(1)}, u32[]{:S(2)}, u32[]{:S(2)}) %collective-permute-start.11) | collective-permute-done | bytes 16416 | tf_op jit(solution)/shard_map/ppermute | solution.py:18
  39.6 0.6 copy-done.5
  40.3 0.9 copy-done.6
  41.2 1.0 grad_long.1
  42.2 0.8 copy-done.4
  43.0 5.4 %all-to-all-start.1 = ((bf16[8,128,256]{2,1,0:T(8,128)(2,1)}), bf16[8,128,256]{2,1,0:T(8,128)(2,1)}, u32[]{:S(2)}, u32[]{:S(2)}) async-start(bf16[8,128,256]{2,1,0:T(8,128)(2,1)} %copy-done.4), calls=%async_computation.1 | async-start | bytes 1048576 | tf_op jit(solution)/shard_map/all_to_all | solution.py:351
  48.4 7.4 %long_out.1 = (f32[2,256,1024]{2,1,0:T(8,128)}, bf16[1024,256]{1,0:T(8,128)(2,1)}) custom-call(bf16[2,1024,1024]{2,1,0:T(8,128)(2,1)} %constant.82.clone.waves_ref, f32[2,256,1024]{2,1,0:T(8,128)} %filter_spectrum.1.filter_spec_ref, bf16[1024,256]{1,0:T(8,128)(2,1)} %bitcast.6.product_ref, f32[1,256]{1,0:T(1,128)} %bitcast.56), custom_call_target="tpu_custom_call" | custom-call | tf_op jit(solution)/shard_map/long_out/pallas_call | solution.py:276
  55.7 1.8 %dynamic-slice_bitcast_fusion.3 = (bf16[4,128,256]{2,1,0:T(8,128)(2,1)}, bf16[4,1,128,256]{3,2,1,0:T(8,128)(2,1)S(1)}) fusion(bf16[4,2,128,256]{3,2,1,0:T(8,128)(2,1)} %bitcast.52, s32[]{:T(128)S(6)} %select_n.59, s32[]{:T(128)S(6)} %select_n.58), kind=kLoop, calls=%fused_computation.32 | loop fusion | bytes 1048584 | tf_op jit(solution)/shard_map/jit(dynamic_index_in_dim)/squeeze | solution.py:408
  57.5 0.7 collective-permute-start.7
  58.2 1.5 collective-permute-done.7
  59.7 1.7 %fusion.10 = (bf16[2,128,256]{2,1,0:T(8,128)(2,1)}, bf16[2,128,256]{2,1,0:T(8,128)(2,1)S(1)}, bf16[2,128,256]{2,1,0:T(8,128)(2,1)}, bf16[2,128,256]{2,1,0:T(8,128)(2,1)}) fusion(s32[]{:T(128)S(6)} %select_n.64, bf16[4,1,128,256]{3,2,1,0:T(8,128)(2,1)S(1)} %get-tuple-element.90, bf16[4,1,128,256]{3,2,1,0:T(8,128)(2,1)} %bitcast.10, s32[]{:T(128)S(6)} %select_n.61, ...), kind=kLoop, calls=%fused_computation.34 | loop fusion | flops 262144 | bytes 1048592 | tf_op jit(solution)/shard_map/jit(dynamic_index_in_dim)/squeeze | solution.py:412
  61.4 1.7 %collective-permute-start.8 = (bf16[2,128,256]{2,1,0:T(8,128)(2,1)}, bf16[2,128,256]{2,1,0:T(8,128)(2,1)S(1)}, u32[]{:S(2)}, u32[]{:S(2)}) collective-permute-start(bf16[2,128,256]{2,1,0:T(8,128)(2,1)} %get-tuple-element.87), channel_id=1, source_target_pairs={{0,2},{1,3},{2,0},{3,1},{4,6},{5,7},{6,4},{7,5},{8,10},{9,11},{10,... | collective-permute-start | bytes 393224 | tf_op jit(solution)/shard_map/ppermute | solution.py:22
  63.1 2.4 %collective-permute-start.9 = (bf16[2,128,256]{2,1,0:T(8,128)(2,1)}, bf16[2,128,256]{2,1,0:T(8,128)(2,1)S(1)}, u32[]{:S(2)}, u32[]{:S(2)}) collective-permute-start(bf16[2,128,256]{2,1,0:T(8,128)(2,1)} %get-tuple-element.88), channel_id=1, source_target_pairs={{0,4},{1,5},{2,6},{3,7},{4,0},{5,1},{6,2},{7,3},{8,12},{9,13},{10,... | collective-permute-start | bytes 393224 | tf_op jit(solution)/shard_map/ppermute | solution.py:22
  65.8 3.7 %collective-permute-done.8.refs_4_ = bf16[2,128,256]{2,1,0:T(8,128)(2,1)S(1)} collective-permute-done((bf16[2,128,256]{2,1,0:T(8,128)(2,1)}, bf16[2,128,256]{2,1,0:T(8,128)(2,1)S(1)}, u32[]{:S(2)}, u32[]{:S(2)}) %collective-permute-start.8) | collective-permute-done | bytes 131104 | tf_op jit(solution)/shard_map/ppermute | solution.py:22
  69.4 8.8 %grad_product.1 = (bf16[8,130,256]{2,1,0:T(8,128)(2,1)}, f32[256,1024]{1,0:T(8,128)}, f32[1,256]{1,0:T(1,128)}) custom-call(bf16[2,1024,1024]{2,1,0:T(8,128)(2,1)} %constant.82.clone.waves_ref, f32[2,256,1024]{2,1,0:T(8,128)} %filter_spectrum.1.filter_spec_ref, f32[2,256,1024]{2,1,0:T(8,128)} %get-tuple-element.49.spec_ref, ...), custom_call_target="tpu_custom_call" | custom-call | tf_op jit(solution)/shard_map/grad_product/pallas_call | solution.py:276
  78.2 4.2 %all-to-all-start.2 = ((bf16[8,130,256]{2,1,0:T(8,128)(2,1)}), bf16[8,130,256]{2,1,0:T(8,128)(2,1)}, u32[]{:S(2)}, u32[]{:S(2)}) async-start(bf16[8,130,256]{2,1,0:T(8,128)(2,1)} %get-tuple-element.56), calls=%async_computation.2 | async-start | bytes 1114112 | tf_op jit(solution)/shard_map/all_to_all | solution.py:356
  82.4 2.6 %gate.1 = (bf16[8,128,256]{2,1,0:T(8,128)(2,1)S(1)}, bf16[128,512]{1,0:T(8,128)(2,1)S(1)}, bf16[128,512]{1,0:T(8,128)(2,1)S(1)}, bf16[128,512]{1,0:T(8,128)(2,1)S(1)}, bf16[128,512]{1,0:T(8,128)(2,1)S(1)}) custom-call(s32[1]{0:T(128)} %bitcast.5.refs_0_, s32[1]{0:T(128)} %bitcast.refs_0_.refs_1_, bf16[8,128,256]{2,1,0:T(8,128)(2,1)S(1)} %copy-done.1, ...), custom_call_target="tpu_custom_call" | custom-call | tf_op jit(solution)/shard_map/gate/pallas_call | solution.py:67
  85.1 3.0 %collective-permute-start.14 = (bf16[128,512]{1,0:T(8,128)(2,1)S(1)}, bf16[128,512]{1,0:T(8,128)(2,1)S(1)}, u32[]{:S(2)}, u32[]{:S(2)}) collective-permute-start(bf16[128,512]{1,0:T(8,128)(2,1)S(1)} %get-tuple-element.65), channel_id=1, source_target_pairs={{0,24},{8,16},{16,8},{24,0},{1,25},{9,17},{17,9},{25,1},{2,26},{10... | collective-permute-start | bytes 393224 | tf_op jit(solution)/shard_map/ppermute | solution.py:22
  88.7 1.5 collective-permute-start.15
  90.2 1.1 constant_dynamic-update-slice_fusion.3
  91.4 1.1 constant_dynamic-update-slice_fusion
  92.5 2.4 %collective-permute-done.13 = bf16[128,512]{1,0:T(8,128)(2,1)S(1)} collective-permute-done((bf16[128,512]{1,0:T(8,128)(2,1)S(1)}, bf16[128,512]{1,0:T(8,128)(2,1)S(1)}, u32[]{:S(2)}, u32[]{:S(2)}) %collective-permute-start.13) | collective-permute-done | bytes 131104 | tf_op jit(solution)/shard_map/ppermute | solution.py:22
  95.3 3.2 %all-to-all-done.2.refs_5_ = bf16[8,130,256]{2,1,0:T(8,128)(2,1)} async-done(((bf16[8,130,256]{2,1,0:T(8,128)(2,1)}), bf16[8,130,256]{2,1,0:T(8,128)(2,1)}, u32[]{:S(2)}, u32[]{:S(2)}) %all-to-all-start.2) | async-done | bytes 532512 | tf_op jit(solution)/shard_map/all_to_all | solution.py:356
  98.5 3.3 %convolution_convert_fusion = bf16[256,2048]{1,0:T(8,128)(2,1)} fusion(bf16[512,2048]{1,0:T(8,128)(2,1)} %copy-done.7, bf16[512,512]{1,0:T(8,128)(2,1)S(1)} %pad_maximum_fusion, s32[]{:T(128)S(6)} %select_n.66), kind=kOutput, calls=%fused_computation.2 | convolution fusion | flops 537395200 | bytes 3407876 | tf_op jit(solution)/shard_map/dot_general | solution.py:187
  101.8 3.0 %collective-permute-done.16 = bf16[256,2048]{1,0:T(8,128)(2,1)} collective-permute-done((bf16[256,2048]{1,0:T(8,128)(2,1)}, bf16[256,2048]{1,0:T(8,128)(2,1)}, u32[]{:S(2)}, u32[]{:S(2)}) %collective-permute-start.16) | collective-permute-done | bytes 1048608 | tf_op jit(solution)/shard_map/ppermute | solution.py:22
  104.8 2.6 %fusion = bf16[256,2048]{1,0:T(8,128)(2,1)S(1)} fusion(bf16[512,256]{1,0:T(8,128)(2,1)S(1)} %constant_dynamic-slice_fusion, bf16[512,2048]{1,0:T(8,128)(2,1)} %copy-done.7, bf16[256,2048]{1,0:T(8,128)(2,1)} %collective-permute-done.16), kind=kOutput, calls=%fused_computation.1 | convolution fusion | flops 538443776 | bytes 4456448 | tf_op jit(solution)/shard_map/dot_general | solution.py:187
  107.4 5.7 %stream_grads.1 = (bf16[128,6144]{1,0:T(8,128)(2,1)}, f32[4,6144]{1,0:T(4,128)}) custom-call(bf16[128,6144]{1,0:T(8,128)(2,1)} %refs_0_.3, f32[2,6144]{1,0:T(2,128)} %convert_element_type.77.refs_1_, f32[3,6144]{1,0:T(4,128)} %refs_2_.3, bf16[8,128,256]{2,1,0:T(8,128)(2,1)} %copy-done.2, bf16[8,128,256]{2,1,0:T(8,128)(2,1)} %copy-done.3, ...), custom_call_target="tpu_custom_call" | custom-call | tf_op jit(solution)/shard_map/stream_grads/pallas_call | solution.py:67
  113.1 2.0 %collective-permute-start.18 = (f32[4,6144]{1,0:T(4,128)}, f32[4,6144]{1,0:T(4,128)S(1)}, u32[]{:S(2)}, u32[]{:S(2)}) collective-permute-start(f32[4,6144]{1,0:T(4,128)} %get-tuple-element.75), channel_id=1, source_target_pairs={{0,16},{8,24},{16,0},{24,8},{1,17},{9,25},{17,1},{25,9},{2,18},{10... | collective-permute-start | bytes 294920 | tf_op jit(solution)/shard_map/ppermute | solution.py:22
  115.2 1.4 collective-permute-start.19
  117.0 1.7 %collective-permute-start.22 = (bf16[64,2048]{1,0:T(8,128)(2,1)S(1)}, bf16[64,2048]{1,0:T(8,128)(2,1)S(1)}, u32[]{:S(2)}, u32[]{:S(2)}) collective-permute-start(bf16[64,2048]{1,0:T(8,128)(2,1)S(1)} %get-tuple-element.83), channel_id=1, source_target_pairs={{0,4},{1,5},{2,6},{3,7},{4,0},{5,1},{6,2},{7,3},{8,12},{9,13},{10,... | collective-permute-start | bytes 786440 | tf_op jit(solution)/shard_map/ppermute | solution.py:22
  118.7 1.3 collective-permute-done.18
  120.0 1.3 collective-permute-start.23
  121.9 0.9 add_add_fusion
  123.0 2.6 %collective-permute-start.29 = (bf16[256,256]{1,0:T(8,128)(2,1)S(1)}, bf16[256,256]{1,0:T(8,128)(2,1)S(1)}, u32[]{:S(2)}, u32[]{:S(2)}) collective-permute-start(bf16[256,256]{1,0:T(8,128)(2,1)S(1)} %get-tuple-element.80), channel_id=1, source_target_pairs={{0,24},{8,16},{16,8},{24,0},{1,25},{9,17},{17,9},{25,1},{2,26},{10... | collective-permute-start | bytes 393224 | tf_op jit(solution)/shard_map/ppermute | solution.py:22
  126.7 3.2 %collective-permute-done.29 = bf16[256,256]{1,0:T(8,128)(2,1)S(1)} collective-permute-done((bf16[256,256]{1,0:T(8,128)(2,1)S(1)}, bf16[256,256]{1,0:T(8,128)(2,1)S(1)}, u32[]{:S(2)}, u32[]{:S(2)}) %collective-permute-start.29) | collective-permute-done | bytes 131104 | tf_op jit(solution)/shard_map/ppermute | solution.py:22
  130.0 1.6 %collective-permute-start.27 = (bf16[256,256]{1,0:T(8,128)(2,1)S(1)}, bf16[256,256]{1,0:T(8,128)(2,1)S(1)}, u32[]{:S(2)}, u32[]{:S(2)}) collective-permute-start(bf16[256,256]{1,0:T(8,128)(2,1)S(1)} %get-tuple-element.79), channel_id=1, source_target_pairs={{0,8},{8,0},{16,24},{24,16},{1,9},{9,1},{17,25},{25,17},{2,10},{10... | collective-permute-start | bytes 393224 | tf_op jit(solution)/shard_map/ppermute | solution.py:22
  131.6 1.1 collective-permute-done.28
  132.7 2.3 %collective-permute-done.27 = bf16[256,256]{1,0:T(8,128)(2,1)S(1)} collective-permute-done((bf16[256,256]{1,0:T(8,128)(2,1)S(1)}, bf16[256,256]{1,0:T(8,128)(2,1)S(1)}, u32[]{:S(2)}, u32[]{:S(2)}) %collective-permute-start.27) | collective-permute-done | bytes 131104 | tf_op jit(solution)/shard_map/ppermute | solution.py:22
  135.0 0.8 add_multiply_fusion
  135.7 2.6 %collective-permute-done.22 = bf16[64,2048]{1,0:T(8,128)(2,1)S(1)} collective-permute-done((bf16[64,2048]{1,0:T(8,128)(2,1)S(1)}, bf16[64,2048]{1,0:T(8,128)(2,1)S(1)}, u32[]{:S(2)}, u32[]{:S(2)}) %collective-permute-start.22) | collective-permute-done | bytes 262176 | tf_op jit(solution)/shard_map/ppermute | solution.py:22
  138.3 4.7 %collective-permute-start.25 = (f32[3,6144]{1,0:T(4,128)S(1)}, f32[3,6144]{1,0:T(4,128)S(1)}, u32[]{:S(2)}, u32[]{:S(2)}) collective-permute-start(f32[3,6144]{1,0:T(4,128)S(1)} %slice_add_fusion), channel_id=1, source_target_pairs={{0,4},{1,5},{2,6},{3,7},{4,0},{5,1},{6,2},{7,3},{8,12},{9,13},{10,... | collective-permute-start | bytes 221192 | tf_op jit(solution)/shard_map/ppermute | solution.py:22
  143.0 2.4 %collective-permute-start.26 = (f32[3,6144]{1,0:T(4,128)S(1)}, f32[3,6144]{1,0:T(4,128)S(1)}, u32[]{:S(2)}, u32[]{:S(2)}) collective-permute-start(f32[3,6144]{1,0:T(4,128)S(1)} %slice_add_fusion), channel_id=1, source_target_pairs={{0,6},{1,7},{2,4},{3,5},{4,2},{5,3},{6,0},{7,1},{8,14},{9,15},{10,... | collective-permute-start | bytes 221192 | tf_op jit(solution)/shard_map/ppermute | solution.py:22
  145.5 0.9 fusion.7
  146.4 3.8 %collective-permute-done.25 = f32[3,6144]{1,0:T(4,128)S(1)} collective-permute-done((f32[3,6144]{1,0:T(4,128)S(1)}, f32[3,6144]{1,0:T(4,128)S(1)}, u32[]{:S(2)}, u32[]{:S(2)}) %collective-permute-start.25) | collective-permute-done | bytes 73760 | tf_op jit(solution)/shard_map/ppermute | solution.py:22
  150.2 1.0 collective-permute-done.24
  151.2 0.7 add_multiply_fusion.1
  (68 shorter events, 4.9 us)
Async XLA Ops:
  0.6 22.5 %copy-start = (bf16[512,2048]{1,0:T(8,128)(2,1)S(1)}, bf16[512,2048]{1,0:T(8,128)(2,1)}, u32[]{:S(2)}) copy-start(bf16[512,2048]{1,0:T(8,128)(2,1)} %param.11) | copy-start | bytes 6291460
  0.6 22.5 %collective-permute-start.1 = (bf16[128,2048]{1,0:T(8,128)(2,1)}, bf16[128,2048]{1,0:T(8,128)(2,1)S(1)}, u32[]{:S(2)}, u32[]{:S(2)}) collective-permute-start(bf16[128,2048]{1,0:T(8,128)(2,1)} %param.12), channel_id=1, source_target_pairs={{0,8},{8,0},{16,24},{24,16},{1,9},{9,1},{17,25},{25,17},{2,10},{10... | collective-permute-start | bytes 1572872 | tf_op jit(solution)/shard_map/ppermute | solution.py:22
  3.6 24.8 %collective-permute-start.3 = (bf16[128,2048]{1,0:T(8,128)(2,1)}, bf16[128,2048]{1,0:T(8,128)(2,1)S(1)}, u32[]{:S(2)}, u32[]{:S(2)}) collective-permute-start(bf16[128,2048]{1,0:T(8,128)(2,1)} %param.12), channel_id=1, source_target_pairs={{0,16},{8,24},{16,0},{24,8},{1,17},{9,25},{17,1},{25,9},{2,18},{10... | collective-permute-start | bytes 1572872 | tf_op jit(solution)/shard_map/ppermute | solution.py:22
  6.1 7.2 %collective-permute-start = (bf16[2,6144]{1,0:T(2,128)(2,1)S(1)}, bf16[2,6144]{1,0:T(2,128)(2,1)S(1)}, u32[]{:S(2)}, u32[]{:S(2)}) collective-permute-start(bf16[2,6144]{1,0:T(2,128)(2,1)S(1)} %slice.22), channel_id=1, source_target_pairs={{0,1},{1,2},{2,3},{3,4},{4,5},{5,6},{6,7},{8,9},{9,10},{10,11},{11... | collective-permute-start | bytes 73736 | tf_op jit(solution)/shard_map/ppermute | solution.py:18
  7.4 24.1 %collective-permute-start.5 = (bf16[128,2048]{1,0:T(8,128)(2,1)}, bf16[128,2048]{1,0:T(8,128)(2,1)}, u32[]{:S(2)}, u32[]{:S(2)}) collective-permute-start(bf16[128,2048]{1,0:T(8,128)(2,1)} %param.12), channel_id=1, source_target_pairs={{0,24},{8,16},{16,8},{24,0},{1,25},{9,17},{17,9},{25,1},{2,26},{10... | collective-permute-start | bytes 1572872 | tf_op jit(solution)/shard_map/ppermute | solution.py:22
  17.5 25.4 %all-to-all-start = ((bf16[8,128,256]{2,1,0:T(8,128)(2,1)}), bf16[8,128,256]{2,1,0:T(8,128)(2,1)}, u32[]{:S(2)}, u32[]{:S(2)}) async-start(bf16[8,128,256]{2,1,0:T(8,128)(2,1)} %get-tuple-element.45), calls=%async_computation | async-start | bytes 1048576 | tf_op jit(solution)/shard_map/all_to_all | solution.py:351
  23.2 6.8 %copy-start.9 = (bf16[128,2048]{1,0:T(8,128)(2,1)}, bf16[128,2048]{1,0:T(8,128)(2,1)S(1)}, u32[]{:S(2)}) copy-start(bf16[128,2048]{1,0:T(8,128)(2,1)S(1)} %collective-permute-done.1) | copy-start | bytes 1572868
  24.7 8.8 %copy-start.8 = (bf16[128,2048]{1,0:T(8,128)(2,1)S(1)}, bf16[128,2048]{1,0:T(8,128)(2,1)}, u32[]{:S(2)}) copy-start(bf16[128,2048]{1,0:T(8,128)(2,1)} %param.12) | copy-start | bytes 1572868
  24.7 14.9 %collective-permute-start.2 = (bf16[128,512]{1,0:T(8,128)(2,1)}, bf16[128,512]{1,0:T(8,128)(2,1)S(1)}, u32[]{:S(2)}, u32[]{:S(2)}) collective-permute-start(bf16[128,512]{1,0:T(8,128)(2,1)} %fusion.2), channel_id=1, source_target_pairs={{0,8},{8,0},{16,24},{24,16},{1,9},{9,1},{17,25},{25,17},{2,10},{10... | collective-permute-start | bytes 393224 | tf_op jit(solution)/shard_map/ppermute | solution.py:22
  28.5 3.0 %copy-start.11 = (bf16[128,2048]{1,0:T(8,128)(2,1)}, bf16[128,2048]{1,0:T(8,128)(2,1)S(1)}, u32[]{:S(2)}) copy-start(bf16[128,2048]{1,0:T(8,128)(2,1)S(1)} %collective-permute-done.3) | copy-start | bytes 1572868
  30.0 9.6 %collective-permute-start.4 = (bf16[128,512]{1,0:T(8,128)(2,1)}, bf16[128,512]{1,0:T(8,128)(2,1)S(1)}, u32[]{:S(2)}, u32[]{:S(2)}) collective-permute-start(bf16[128,512]{1,0:T(8,128)(2,1)} %fusion.3), channel_id=1, source_target_pairs={{0,16},{8,24},{16,0},{24,8},{1,17},{9,25},{17,1},{25,9},{2,18},{10... | collective-permute-start | bytes 393224 | tf_op jit(solution)/shard_map/ppermute | solution.py:22
  33.4 6.9 %copy-start.1 = (bf16[8,128,256]{2,1,0:T(8,128)(2,1)S(1)}, bf16[8,128,256]{2,1,0:T(8,128)(2,1)}, u32[]{:S(2)}) copy-start(bf16[8,128,256]{2,1,0:T(8,128)(2,1)} %get-tuple-element.42.refs_1_.refs_2_) | copy-start | bytes 1572868
  33.4 6.2 %collective-permute-start.6 = (bf16[128,512]{1,0:T(8,128)(2,1)S(1)}, bf16[128,512]{1,0:T(8,128)(2,1)S(1)}, u32[]{:S(2)}, u32[]{:S(2)}) collective-permute-start(bf16[128,512]{1,0:T(8,128)(2,1)S(1)} %fusion.4), channel_id=1, source_target_pairs={{0,24},{8,16},{16,8},{24,0},{1,25},{9,17},{17,9},{25,1},{2,26},{10... | collective-permute-start | bytes 393224 | tf_op jit(solution)/shard_map/ppermute | solution.py:22
  35.9 3.1 %collective-permute-start.11 = (bf16[2,8,2,256]{3,2,1,0:T(2,128)(2,1)S(1)}, bf16[2,8,2,256]{3,2,1,0:T(2,128)(2,1)S(1)}, u32[]{:S(2)}, u32[]{:S(2)}) collective-permute-start(bf16[2,8,2,256]{3,2,1,0:T(2,128)(2,1)S(1)} %pad_maximum_fusion.1), channel_id=1, source_target_pairs={{1,0},{2,1},{3,2},{4,3},{5,4},{6,5},{7,6},{9,8},{10,9},{11,10},{12... | collective-permute-start | bytes 49160 | tf_op jit(solution)/shard_map/ppermute | solution.py:18
  39.6 0.7 copy-start.5
  40.3 0.9 copy-start.6
  42.1 0.8 copy-start.4
  42.9 45.7 %copy-start.2 = (bf16[8,128,256]{2,1,0:T(8,128)(2,1)}, bf16[8,128,256]{2,1,0:T(8,128)(2,1)S(1)}, u32[]{:S(2)}) copy-start(bf16[8,128,256]{2,1,0:T(8,128)(2,1)S(1)} %get-tuple-element.44.refs_3_) | copy-start | bytes 1572868
  43.0 26.5 %all-to-all-start.1 = ((bf16[8,128,256]{2,1,0:T(8,128)(2,1)}), bf16[8,128,256]{2,1,0:T(8,128)(2,1)}, u32[]{:S(2)}, u32[]{:S(2)}) async-start(bf16[8,128,256]{2,1,0:T(8,128)(2,1)} %copy-done.4), calls=%async_computation.1 | async-start | bytes 1048576 | tf_op jit(solution)/shard_map/all_to_all | solution.py:351
  57.5 2.2 %collective-permute-start.7 = (bf16[4,128,256]{2,1,0:T(8,128)(2,1)}, bf16[4,128,256]{2,1,0:T(8,128)(2,1)}, u32[]{:S(2)}, u32[]{:S(2)}) collective-permute-start(bf16[4,128,256]{2,1,0:T(8,128)(2,1)} %get-tuple-element.89), channel_id=1, source_target_pairs={{0,1},{1,0},{2,3},{3,2},{4,5},{5,4},{6,7},{7,6},{8,9},{9,8},{10,11... | collective-permute-start | bytes 786440 | tf_op jit(solution)/shard_map/ppermute | solution.py:22
  61.4 8.1 %collective-permute-start.8 = (bf16[2,128,256]{2,1,0:T(8,128)(2,1)}, bf16[2,128,256]{2,1,0:T(8,128)(2,1)S(1)}, u32[]{:S(2)}, u32[]{:S(2)}) collective-permute-start(bf16[2,128,256]{2,1,0:T(8,128)(2,1)} %get-tuple-element.87), channel_id=1, source_target_pairs={{0,2},{1,3},{2,0},{3,1},{4,6},{5,7},{6,4},{7,5},{8,10},{9,11},{10,... | collective-permute-start | bytes 393224 | tf_op jit(solution)/shard_map/ppermute | solution.py:22
  63.1 19.3 %collective-permute-start.9 = (bf16[2,128,256]{2,1,0:T(8,128)(2,1)}, bf16[2,128,256]{2,1,0:T(8,128)(2,1)S(1)}, u32[]{:S(2)}, u32[]{:S(2)}) collective-permute-start(bf16[2,128,256]{2,1,0:T(8,128)(2,1)} %get-tuple-element.88), channel_id=1, source_target_pairs={{0,4},{1,5},{2,6},{3,7},{4,0},{5,1},{6,2},{7,3},{8,12},{9,13},{10,... | collective-permute-start | bytes 393224 | tf_op jit(solution)/shard_map/ppermute | solution.py:22
  65.5 17.0 %collective-permute-start.10 = (bf16[2,128,256]{2,1,0:T(8,128)(2,1)}, bf16[2,128,256]{2,1,0:T(8,128)(2,1)}, u32[]{:S(2)}, u32[]{:S(2)}) collective-permute-start(bf16[2,128,256]{2,1,0:T(8,128)(2,1)} %get-tuple-element.85), channel_id=1, source_target_pairs={{0,6},{1,7},{2,4},{3,5},{4,2},{5,3},{6,0},{7,1},{8,14},{9,15},{10,... | collective-permute-start | bytes 393224 | tf_op jit(solution)/shard_map/ppermute | solution.py:22
  78.2 20.3 %all-to-all-start.2 = ((bf16[8,130,256]{2,1,0:T(8,128)(2,1)}), bf16[8,130,256]{2,1,0:T(8,128)(2,1)}, u32[]{:S(2)}, u32[]{:S(2)}) async-start(bf16[8,130,256]{2,1,0:T(8,128)(2,1)} %get-tuple-element.56), calls=%async_computation.2 | async-start | bytes 1114112 | tf_op jit(solution)/shard_map/all_to_all | solution.py:356
  82.4 8.9 %copy-start.10 = (bf16[128,2048]{1,0:T(8,128)(2,1)S(1)}, bf16[128,2048]{1,0:T(8,128)(2,1)}, u32[]{:S(2)}) copy-start(bf16[128,2048]{1,0:T(8,128)(2,1)} %copy-done.9) | copy-start | bytes 1572868
  82.4 8.9 %copy-start.12 = (bf16[128,2048]{1,0:T(8,128)(2,1)S(1)}, bf16[128,2048]{1,0:T(8,128)(2,1)}, u32[]{:S(2)}) copy-start(bf16[128,2048]{1,0:T(8,128)(2,1)} %copy-done.11) | copy-start | bytes 1572868
  85.1 3.6 %copy-start.3 = (bf16[8,128,256]{2,1,0:T(8,128)(2,1)}, bf16[8,128,256]{2,1,0:T(8,128)(2,1)S(1)}, u32[]{:S(2)}) copy-start(bf16[8,128,256]{2,1,0:T(8,128)(2,1)S(1)} %get-tuple-element.61.refs_4_) | copy-start | bytes 1572868
  85.1 7.4 %collective-permute-start.14 = (bf16[128,512]{1,0:T(8,128)(2,1)S(1)}, bf16[128,512]{1,0:T(8,128)(2,1)S(1)}, u32[]{:S(2)}, u32[]{:S(2)}) collective-permute-start(bf16[128,512]{1,0:T(8,128)(2,1)S(1)} %get-tuple-element.65), channel_id=1, source_target_pairs={{0,24},{8,16},{16,8},{24,0},{1,25},{9,17},{17,9},{25,1},{2,26},{10... | collective-permute-start | bytes 393224 | tf_op jit(solution)/shard_map/ppermute | solution.py:22
  88.0 6.9 %collective-permute-start.13 = (bf16[128,512]{1,0:T(8,128)(2,1)S(1)}, bf16[128,512]{1,0:T(8,128)(2,1)S(1)}, u32[]{:S(2)}, u32[]{:S(2)}) collective-permute-start(bf16[128,512]{1,0:T(8,128)(2,1)S(1)} %get-tuple-element.64), channel_id=1, source_target_pairs={{0,16},{8,24},{16,0},{24,8},{1,17},{9,25},{17,1},{25,9},{2,18},{10... | collective-permute-start | bytes 393224 | tf_op jit(solution)/shard_map/ppermute | solution.py:22
  88.5 6.7 %collective-permute-start.12 = (bf16[128,512]{1,0:T(8,128)(2,1)S(1)}, bf16[128,512]{1,0:T(8,128)(2,1)S(1)}, u32[]{:S(2)}, u32[]{:S(2)}) collective-permute-start(bf16[128,512]{1,0:T(8,128)(2,1)S(1)} %get-tuple-element.63), channel_id=1, source_target_pairs={{0,8},{8,0},{16,24},{24,16},{1,9},{9,1},{17,25},{25,17},{2,10},{10... | collective-permute-start | bytes 393224 | tf_op jit(solution)/shard_map/ppermute | solution.py:22
  88.7 6.6 %collective-permute-start.15 = (f32[8,2,256]{2,1,0:T(2,128)S(1)}, f32[8,2,256]{2,1,0:T(2,128)S(1)}, u32[]{:S(2)}, u32[]{:S(2)}) collective-permute-start(f32[8,2,256]{2,1,0:T(2,128)S(1)} %convert_multiply_fusion), channel_id=1, source_target_pairs={{1,0},{2,1},{3,2},{4,3},{5,4},{6,5},{7,6},{9,8},{10,9},{11,10},{12... | collective-permute-start | bytes 49160 | tf_op jit(solution)/shard_map/ppermute | solution.py:18
  92.5 2.8 %copy-start.7 = (bf16[512,2048]{1,0:T(8,128)(2,1)}, bf16[512,2048]{1,0:T(8,128)(2,1)S(1)}, u32[]{:S(2)}) copy-start(bf16[512,2048]{1,0:T(8,128)(2,1)S(1)} %constant_dynamic-update-slice_fusion) | copy-start | bytes 6291460
  95.3 12.1 %copy-start.14 = (f32[8,2,256]{2,1,0:T(2,128)}, f32[8,2,256]{2,1,0:T(2,128)S(1)}, u32[]{:S(2)}) copy-start(f32[8,2,256]{2,1,0:T(2,128)S(1)} %collective-permute-done.15.refs_8_) | copy-start | bytes 49156
  101.8 3.0 %collective-permute-start.16 = (bf16[256,2048]{1,0:T(8,128)(2,1)}, bf16[256,2048]{1,0:T(8,128)(2,1)}, u32[]{:S(2)}, u32[]{:S(2)}) collective-permute-start(bf16[256,2048]{1,0:T(8,128)(2,1)} %convolution_convert_fusion), channel_id=1, source_target_pairs={{0,1},{1,0},{2,3},{3,2},{4,5},{5,4},{6,7},{7,6},{8,9},{9,8},{10,11... | collective-permute-start | bytes 3145736 | tf_op jit(solution)/shard_map/ppermute | solution.py:22
  113.1 9.8 %copy-start.13 = (f32[256,1024]{1,0:T(8,128)S(1)}, f32[256,1024]{1,0:T(8,128)}, u32[]{:S(2)}) copy-start(f32[256,1024]{1,0:T(8,128)} %get-tuple-element.78) | copy-start | bytes 3145732
  113.1 6.9 %collective-permute-start.18 = (f32[4,6144]{1,0:T(4,128)}, f32[4,6144]{1,0:T(4,128)S(1)}, u32[]{:S(2)}, u32[]{:S(2)}) collective-permute-start(f32[4,6144]{1,0:T(4,128)} %get-tuple-element.75), channel_id=1, source_target_pairs={{0,16},{8,24},{16,0},{24,8},{1,17},{9,25},{17,1},{25,9},{2,18},{10... | collective-permute-start | bytes 294920 | tf_op jit(solution)/shard_map/ppermute | solution.py:22
  115.2 6.7 %collective-permute-start.19 = (f32[4,6144]{1,0:T(4,128)}, f32[4,6144]{1,0:T(4,128)S(1)}, u32[]{:S(2)}, u32[]{:S(2)}) collective-permute-start(f32[4,6144]{1,0:T(4,128)} %get-tuple-element.75), channel_id=1, source_target_pairs={{0,24},{8,16},{16,8},{24,0},{1,25},{9,17},{17,9},{25,1},{2,26},{10... | collective-permute-start | bytes 294920 | tf_op jit(solution)/shard_map/ppermute | solution.py:22
  116.6 5.3 %collective-permute-start.17 = (f32[4,6144]{1,0:T(4,128)}, f32[4,6144]{1,0:T(4,128)S(1)}, u32[]{:S(2)}, u32[]{:S(2)}) collective-permute-start(f32[4,6144]{1,0:T(4,128)} %get-tuple-element.75), channel_id=1, source_target_pairs={{0,8},{8,0},{16,24},{24,16},{1,9},{9,1},{17,25},{25,17},{2,10},{10... | collective-permute-start | bytes 294920 | tf_op jit(solution)/shard_map/ppermute | solution.py:22
  116.8 18.9 %collective-permute-start.21 = (bf16[64,2048]{1,0:T(8,128)(2,1)S(1)}, bf16[64,2048]{1,0:T(8,128)(2,1)S(1)}, u32[]{:S(2)}, u32[]{:S(2)}) collective-permute-start(bf16[64,2048]{1,0:T(8,128)(2,1)S(1)} %get-tuple-element.84), channel_id=1, source_target_pairs={{0,2},{1,3},{2,0},{3,1},{4,6},{5,7},{6,4},{7,5},{8,10},{9,11},{10,... | collective-permute-start | bytes 786440 | tf_op jit(solution)/shard_map/ppermute | solution.py:22
  117.0 21.4 %collective-permute-start.22 = (bf16[64,2048]{1,0:T(8,128)(2,1)S(1)}, bf16[64,2048]{1,0:T(8,128)(2,1)S(1)}, u32[]{:S(2)}, u32[]{:S(2)}) collective-permute-start(bf16[64,2048]{1,0:T(8,128)(2,1)S(1)} %get-tuple-element.83), channel_id=1, source_target_pairs={{0,4},{1,5},{2,6},{3,7},{4,0},{5,1},{6,2},{7,3},{8,12},{9,13},{10,... | collective-permute-start | bytes 786440 | tf_op jit(solution)/shard_map/ppermute | solution.py:22
  120.0 18.3 %collective-permute-start.23 = (bf16[64,2048]{1,0:T(8,128)(2,1)S(1)}, bf16[64,2048]{1,0:T(8,128)(2,1)S(1)}, u32[]{:S(2)}, u32[]{:S(2)}) collective-permute-start(bf16[64,2048]{1,0:T(8,128)(2,1)S(1)} %get-tuple-element.82), channel_id=1, source_target_pairs={{0,6},{1,7},{2,4},{3,5},{4,2},{5,3},{6,0},{7,1},{8,14},{9,15},{10,... | collective-permute-start | bytes 786440 | tf_op jit(solution)/shard_map/ppermute | solution.py:22
  122.9 3.3 %collective-permute-start.20 = (f32[3,6144]{1,0:T(4,128)S(1)}, f32[3,6144]{1,0:T(4,128)S(1)}, u32[]{:S(2)}, u32[]{:S(2)}) collective-permute-start(f32[3,6144]{1,0:T(4,128)S(1)} %bitcast.53), channel_id=1, source_target_pairs={{0,1},{1,0},{2,3},{3,2},{4,5},{5,4},{6,7},{7,6},{8,9},{9,8},{10,11... | collective-permute-start | bytes 221192 | tf_op jit(solution)/shard_map/ppermute | solution.py:22
  123.0 6.9 %collective-permute-start.29 = (bf16[256,256]{1,0:T(8,128)(2,1)S(1)}, bf16[256,256]{1,0:T(8,128)(2,1)S(1)}, u32[]{:S(2)}, u32[]{:S(2)}) collective-permute-start(bf16[256,256]{1,0:T(8,128)(2,1)S(1)} %get-tuple-element.80), channel_id=1, source_target_pairs={{0,24},{8,16},{16,8},{24,0},{1,25},{9,17},{17,9},{25,1},{2,26},{10... | collective-permute-start | bytes 393224 | tf_op jit(solution)/shard_map/ppermute | solution.py:22
  126.2 6.5 %collective-permute-start.28 = (bf16[256,256]{1,0:T(8,128)(2,1)S(1)}, bf16[256,256]{1,0:T(8,128)(2,1)S(1)}, u32[]{:S(2)}, u32[]{:S(2)}) collective-permute-start(bf16[256,256]{1,0:T(8,128)(2,1)S(1)} %get-tuple-element.81), channel_id=1, source_target_pairs={{0,16},{8,24},{16,0},{24,8},{1,17},{9,25},{17,1},{25,9},{2,18},{10... | collective-permute-start | bytes 393224 | tf_op jit(solution)/shard_map/ppermute | solution.py:22
  130.0 5.0 %collective-permute-start.27 = (bf16[256,256]{1,0:T(8,128)(2,1)S(1)}, bf16[256,256]{1,0:T(8,128)(2,1)S(1)}, u32[]{:S(2)}, u32[]{:S(2)}) collective-permute-start(bf16[256,256]{1,0:T(8,128)(2,1)S(1)} %get-tuple-element.79), channel_id=1, source_target_pairs={{0,8},{8,0},{16,24},{24,16},{1,9},{9,1},{17,25},{25,17},{2,10},{10... | collective-permute-start | bytes 393224 | tf_op jit(solution)/shard_map/ppermute | solution.py:22
  138.3 11.9 %collective-permute-start.25 = (f32[3,6144]{1,0:T(4,128)S(1)}, f32[3,6144]{1,0:T(4,128)S(1)}, u32[]{:S(2)}, u32[]{:S(2)}) collective-permute-start(f32[3,6144]{1,0:T(4,128)S(1)} %slice_add_fusion), channel_id=1, source_target_pairs={{0,4},{1,5},{2,6},{3,7},{4,0},{5,1},{6,2},{7,3},{8,12},{9,13},{10,... | collective-permute-start | bytes 221192 | tf_op jit(solution)/shard_map/ppermute | solution.py:22
  143.0 7.2 %collective-permute-start.26 = (f32[3,6144]{1,0:T(4,128)S(1)}, f32[3,6144]{1,0:T(4,128)S(1)}, u32[]{:S(2)}, u32[]{:S(2)}) collective-permute-start(f32[3,6144]{1,0:T(4,128)S(1)} %slice_add_fusion), channel_id=1, source_target_pairs={{0,6},{1,7},{2,4},{3,5},{4,2},{5,3},{6,0},{7,1},{8,14},{9,15},{10,... | collective-permute-start | bytes 221192 | tf_op jit(solution)/shard_map/ppermute | solution.py:22
  145.5 5.7 %collective-permute-start.24 = (f32[3,6144]{1,0:T(4,128)S(1)}, f32[3,6144]{1,0:T(4,128)S(1)}, u32[]{:S(2)}, u32[]{:S(2)}) collective-permute-start(f32[3,6144]{1,0:T(4,128)S(1)} %slice_add_fusion), channel_id=1, source_target_pairs={{0,2},{1,3},{2,0},{3,1},{4,6},{5,7},{6,4},{7,5},{8,10},{9,11},{10,... | collective-permute-start | bytes 221192 | tf_op jit(solution)/shard_map/ppermute | solution.py:22

commit v14 on v13

--- a/solution.py
+++ b/solution.py
@@ -88,7 +88,7 @@
         def mixed(stream):
             cols = columns(stream * parts + b, blk)
             values = proj_ref[:, cols].astype(F32)
-            before = prev_ref[:, cols]
+            before = prev_ref[:, cols].astype(F32)
             taps = taps_ref[:, cols]
             total = taps[0:1] * values + taps[1:2] * rows_down(values, 1, before)
             return (total + taps[2:3] * rows_down(values, 2, before)).astype(BF16)
@@ -144,8 +144,8 @@
                 gate_grad_ref[b].astype(F32) * long_ref[b].astype(F32),
                 query_after_ref[b],
             ),
-            (back * valued_ref[b].astype(F32), back_after * pair_after_ref[1, b]),
-            (back * keyed_ref[b].astype(F32), back_after * pair_after_ref[0, b]),
+            (back * valued_ref[b].astype(F32), back_after * pair_after_ref[1, b].astype(F32)),
+            (back * keyed_ref[b].astype(F32), back_after * pair_after_ref[0, b].astype(F32)),
         )
         for stream, (grad, after) in enumerate(grads):
             cols = columns(stream * parts + b, blk)
@@ -153,7 +153,7 @@
             total = taps[0:1] * grad + taps[1:2] * rows_up(grad, 1, after)
             out_ref[:, cols] = (total + taps[2:3] * rows_up(grad, 2, after)).astype(BF16)
             values = proj_ref[:, cols].astype(F32)
-            before = prev_ref[:, cols]
+            before = prev_ref[:, cols].astype(F32)
             for j in range(3):
                 moved = rows_down(values, j, before) if j else values
                 sums_ref[j : j + 1, cols] = jnp.sum(grad * moved, 0, keepdims=True)
@@ -367,7 +367,7 @@
     me_dp = lax.axis_index("dp").astype(jnp.int32)[None]
     plane = jax.ShapeDtypeStruct((parts, rows, blk), BF16)
 
-    prev_rows = passed_along(projected[rows - 2 :], "context", 1).astype(F32)
+    prev_rows = passed_along(projected[rows - 2 :], "context", 1)
     cots = [cotangent] + [swapped(cotangent, "dp", k) for k in range(1, parts_dp)]
     query, keyed, valued, product_out = call(
         short_kernel, "short_convs", [plane] * 4, 0, 60, projected, prev_rows, short_taps
@@ -394,7 +394,7 @@
     )
     heads = lax.optimization_barrier((keyed[:, :2], valued[:, :2], *formed))[:2]
     heads = jnp.stack(heads)
-    pair_after = passed_along(heads, "context", -1).astype(F32)
+    pair_after = passed_along(heads, "context", -1)
     grad_long = to_channels(ordered(grad_long_out, pair_after))
     product_f, grad_long_f = (product.astype(F32), grad_long.astype(F32))
 

time: 153 us -> 152 us (level)
    ppermute x3, waiting for transfers between devices: 1.78 us -> 0.01 us  [passed_along(): lax.ppermute(value, axis, [(source, source + steps) for source in range(i...]
    unnamed x33 -> x37, local copies, waits for them, and re-layouts: 3.56 us -> 4.2 us
  transfers between devices with their start and end apart: 33 -> 33, of which waited for: 17 -> 15; matrix products, arithmetic and copies ran while one was open for 12% -> 12% of each run, Pallas kernels for 19% -> 19%
where the time goes in v14:
time: 152 us; the launch traced here: 151 us
  starting transfers between devices  53.6 us (35%)
  Pallas kernels  34.6 us (23%)
  waiting for transfers between devices  33.9 us (22%)
  matrix products  11.6 us (8%)
  local copies, waits for them, and re-layouts  9.66 us (6%)
  other arithmetic  6.3 us (4%)
    ppermute x27, starting transfers between devices, swapped(): lax.ppermute(value, axis, [(i, i ^ mask) for i in range(lax.axis_size(axi...  34.5 us
    ppermute x27, waiting for transfers between devices, swapped(): lax.ppermute(value, axis, [(i, i ^ mask) for i in range(lax.axis_size(axi...  30.2 us
    pallas_call x3, Pallas kernels, chunked(): pl.pallas_call(kernel, out_shape=spec_out + outs, grid=(freqs // size,),...  21.6 us
    pallas_call x4, Pallas kernels, call(): pl.pallas_call(run, out_shape=outs, in_specs=[SMEM] * smem + [anywhere] *...  13 us
    dot_general x6, matrix products, dot(): lax.dot_general(left, right, (((left_dim,), (right_dim,)), ((), ())), pre...  11.6 us
    all_to_all x2, starting transfers between devices, to_channels(): lax.all_to_all(blocks, 'context', split_axis=0, concat_axis=0, tiled=True)  10.5 us
    all_to_all x1, starting transfers between devices, to_positions(): lax.all_to_all(blocks, 'context', split_axis=0, concat_axis=0, tiled=True)  4.46 us
    unnamed x37, local copies, waits for them, and re-layouts  4.2 us
  transfers between devices with their start and end apart: 33, of which 15 were waited for; matrix products, arithmetic and copies ran while one was open for 12% of the time, Pallas kernels for 19%

profile of v14, /device:TPU:0, one launch (start us, length us, event | category | flops | bytes accessed | tf_op | source)
XLA Modules:
  0.0 150.7 jit_solution(10638837492631102112)
XLA Ops:
  0.6 3.0 %collective-permute-start.1 = (bf16[128,2048]{1,0:T(8,128)(2,1)}, bf16[128,2048]{1,0:T(8,128)(2,1)S(1)}, u32[]{:S(2)}, u32[]{:S(2)}) collective-permute-start(bf16[128,2048]{1,0:T(8,128)(2,1)} %param.12), channel_id=1, source_target_pairs={{0,8},{8,0},{16,24},{24,16},{1,9},{9,1},{17,25},{25,17},{2,10},{10... | collective-permute-start | bytes 1572872 | tf_op jit(solution)/shard_map/ppermute | solution.py:22
  3.6 1.5 %collective-permute-start.3 = (bf16[128,2048]{1,0:T(8,128)(2,1)}, bf16[128,2048]{1,0:T(8,128)(2,1)S(1)}, u32[]{:S(2)}, u32[]{:S(2)}) collective-permute-start(bf16[128,2048]{1,0:T(8,128)(2,1)} %param.12), channel_id=1, source_target_pairs={{0,16},{8,24},{16,0},{24,8},{1,17},{9,25},{17,1},{25,9},{2,18},{10... | collective-permute-start | bytes 1572872 | tf_op jit(solution)/shard_map/ppermute | solution.py:22
  5.2 0.9 slice.22
  6.1 1.3 collective-permute-start
  7.8 5.5 %filter_spectrum.1.filter_spec_ref = f32[2,256,1024]{2,1,0:T(8,128)} custom-call(bf16[2,1024,1024]{2,1,0:T(8,128)(2,1)} %constant.82.clone.waves_ref, f32[256,1024]{1,0:T(8,128)} %filter_ref.1), custom_call_target="tpu_custom_call" | custom-call | tf_op jit(solution)/shard_map/filter_spectrum/pallas_call | solution.py:276
  13.9 3.6 %short_convs.1 = (bf16[8,128,256]{2,1,0:T(8,128)(2,1)}, bf16[8,128,256]{2,1,0:T(8,128)(2,1)}, bf16[8,128,256]{2,1,0:T(8,128)(2,1)}, bf16[8,128,256]{2,1,0:T(8,128)(2,1)}) custom-call(bf16[128,6144]{1,0:T(8,128)(2,1)} %refs_0_.3, bf16[2,6144]{1,0:T(2,128)(2,1)} %copy-done.14, f32[3,6144]{1,0:T(4,128)} %refs_2_.3), custom_call_target="tpu_custom_call" | custom-call | tf_op jit(solution)/shard_map/short_convs/pallas_call | solution.py:67
  17.5 5.6 %all-to-all-start = ((bf16[8,128,256]{2,1,0:T(8,128)(2,1)}), bf16[8,128,256]{2,1,0:T(8,128)(2,1)}, u32[]{:S(2)}, u32[]{:S(2)}) async-start(bf16[8,128,256]{2,1,0:T(8,128)(2,1)} %get-tuple-element.45), calls=%async_computation | async-start | bytes 1048576 | tf_op jit(solution)/shard_map/all_to_all | solution.py:351
  23.2 1.5 fusion.2
  24.7 1.5 collective-permute-start.2
  26.2 2.3 %collective-permute-done.3 = bf16[128,2048]{1,0:T(8,128)(2,1)S(1)} collective-permute-done((bf16[128,2048]{1,0:T(8,128)(2,1)}, bf16[128,2048]{1,0:T(8,128)(2,1)S(1)}, u32[]{:S(2)}, u32[]{:S(2)}) %collective-permute-start.3) | collective-permute-done | bytes 524320 | tf_op jit(solution)/shard_map/ppermute | solution.py:22
  28.5 1.5 fusion.3
  30.0 1.5 %collective-permute-start.4 = (bf16[128,512]{1,0:T(8,128)(2,1)}, bf16[128,512]{1,0:T(8,128)(2,1)S(1)}, u32[]{:S(2)}, u32[]{:S(2)}) collective-permute-start(bf16[128,512]{1,0:T(8,128)(2,1)} %fusion.3), channel_id=1, source_target_pairs={{0,16},{8,24},{16,0},{24,8},{1,17},{9,25},{17,1},{25,9},{2,18},{10... | collective-permute-start | bytes 393224 | tf_op jit(solution)/shard_map/ppermute | solution.py:22
  31.5 1.9 %fusion.4 = bf16[128,512]{1,0:T(8,128)(2,1)S(1)} fusion(bf16[512,2048]{1,0:T(8,128)(2,1)S(1)} %copy-done, bf16[128,2048]{1,0:T(8,128)(2,1)} %collective-permute-done.5), kind=kOutput, calls=%fused_computation.10 | convolution fusion | flops 268500992 | bytes 2752512 | tf_op jit(solution)/shard_map/dot_general | solution.py:187
  33.5 0.8 fusion.1.refs_2_
  34.3 0.8 slice.23
  35.1 0.8 slice.24
  36.5 1.3 collective-permute-start.11
  37.8 1.5 %collective-permute-done.6.refs_5_ = bf16[128,512]{1,0:T(8,128)(2,1)S(1)} collective-permute-done((bf16[128,512]{1,0:T(8,128)(2,1)S(1)}, bf16[128,512]{1,0:T(8,128)(2,1)S(1)}, u32[]{:S(2)}, u32[]{:S(2)}) %collective-permute-start.6) | collective-permute-done | bytes 131104 | tf_op jit(solution)/shard_map/ppermute | solution.py:22
  39.3 0.7 copy-done.5
  40.0 0.9 copy-done.6
  40.9 1.0 grad_long.1
  41.9 0.8 copy-done.4
  42.7 4.9 %all-to-all-start.1 = ((bf16[8,128,256]{2,1,0:T(8,128)(2,1)}), bf16[8,128,256]{2,1,0:T(8,128)(2,1)}, u32[]{:S(2)}, u32[]{:S(2)}) async-start(bf16[8,128,256]{2,1,0:T(8,128)(2,1)} %copy-done.4), calls=%async_computation.1 | async-start | bytes 1048576 | tf_op jit(solution)/shard_map/all_to_all | solution.py:351
  47.6 7.4 %long_out.1 = (f32[2,256,1024]{2,1,0:T(8,128)}, bf16[1024,256]{1,0:T(8,128)(2,1)}) custom-call(bf16[2,1024,1024]{2,1,0:T(8,128)(2,1)} %constant.82.clone.waves_ref, f32[2,256,1024]{2,1,0:T(8,128)} %filter_spectrum.1.filter_spec_ref, bf16[1024,256]{1,0:T(8,128)(2,1)} %bitcast.6.product_ref, f32[1,256]{1,0:T(1,128)} %bitcast.56), custom_call_target="tpu_custom_call" | custom-call | tf_op jit(solution)/shard_map/long_out/pallas_call | solution.py:276
  55.0 1.8 %dynamic-slice_bitcast_fusion.3 = (bf16[4,128,256]{2,1,0:T(8,128)(2,1)}, bf16[4,1,128,256]{3,2,1,0:T(8,128)(2,1)S(1)}) fusion(bf16[4,2,128,256]{3,2,1,0:T(8,128)(2,1)} %bitcast.52, s32[]{:T(128)S(6)} %select_n.59, s32[]{:T(128)S(6)} %select_n.58), kind=kLoop, calls=%fused_computation.32 | loop fusion | bytes 1048584 | tf_op jit(solution)/shard_map/jit(dynamic_index_in_dim)/squeeze | solution.py:408
  57.3 1.5 collective-permute-done.7
  58.8 1.7 %fusion.10 = (bf16[2,128,256]{2,1,0:T(8,128)(2,1)}, bf16[2,128,256]{2,1,0:T(8,128)(2,1)S(1)}, bf16[2,128,256]{2,1,0:T(8,128)(2,1)}, bf16[2,128,256]{2,1,0:T(8,128)(2,1)}) fusion(s32[]{:T(128)S(6)} %select_n.64, bf16[4,1,128,256]{3,2,1,0:T(8,128)(2,1)S(1)} %get-tuple-element.90, bf16[4,1,128,256]{3,2,1,0:T(8,128)(2,1)} %bitcast.10, s32[]{:T(128)S(6)} %select_n.61, ...), kind=kLoop, calls=%fused_computation.34 | loop fusion | flops 262144 | bytes 1048592 | tf_op jit(solution)/shard_map/jit(dynamic_index_in_dim)/squeeze | solution.py:412
  60.5 1.9 %collective-permute-start.8 = (bf16[2,128,256]{2,1,0:T(8,128)(2,1)}, bf16[2,128,256]{2,1,0:T(8,128)(2,1)S(1)}, u32[]{:S(2)}, u32[]{:S(2)}) collective-permute-start(bf16[2,128,256]{2,1,0:T(8,128)(2,1)} %get-tuple-element.87), channel_id=1, source_target_pairs={{0,2},{1,3},{2,0},{3,1},{4,6},{5,7},{6,4},{7,5},{8,10},{9,11},{10,... | collective-permute-start | bytes 393224 | tf_op jit(solution)/shard_map/ppermute | solution.py:22
  62.3 2.4 %collective-permute-start.9 = (bf16[2,128,256]{2,1,0:T(8,128)(2,1)}, bf16[2,128,256]{2,1,0:T(8,128)(2,1)S(1)}, u32[]{:S(2)}, u32[]{:S(2)}) collective-permute-start(bf16[2,128,256]{2,1,0:T(8,128)(2,1)} %get-tuple-element.88), channel_id=1, source_target_pairs={{0,4},{1,5},{2,6},{3,7},{4,0},{5,1},{6,2},{7,3},{8,12},{9,13},{10,... | collective-permute-start | bytes 393224 | tf_op jit(solution)/shard_map/ppermute | solution.py:22
  64.9 3.5 %collective-permute-done.8.refs_4_ = bf16[2,128,256]{2,1,0:T(8,128)(2,1)S(1)} collective-permute-done((bf16[2,128,256]{2,1,0:T(8,128)(2,1)}, bf16[2,128,256]{2,1,0:T(8,128)(2,1)S(1)}, u32[]{:S(2)}, u32[]{:S(2)}) %collective-permute-start.8) | collective-permute-done | bytes 131104 | tf_op jit(solution)/shard_map/ppermute | solution.py:22
  68.3 8.8 %grad_product.1 = (bf16[8,130,256]{2,1,0:T(8,128)(2,1)}, f32[256,1024]{1,0:T(8,128)}, f32[1,256]{1,0:T(1,128)}) custom-call(bf16[2,1024,1024]{2,1,0:T(8,128)(2,1)} %constant.82.clone.waves_ref, f32[2,256,1024]{2,1,0:T(8,128)} %filter_spectrum.1.filter_spec_ref, f32[2,256,1024]{2,1,0:T(8,128)} %get-tuple-element.49.spec_ref, ...), custom_call_target="tpu_custom_call" | custom-call | tf_op jit(solution)/shard_map/grad_product/pallas_call | solution.py:276
  77.1 4.5 %all-to-all-start.2 = ((bf16[8,130,256]{2,1,0:T(8,128)(2,1)}), bf16[8,130,256]{2,1,0:T(8,128)(2,1)}, u32[]{:S(2)}, u32[]{:S(2)}) async-start(bf16[8,130,256]{2,1,0:T(8,128)(2,1)} %get-tuple-element.56), calls=%async_computation.2 | async-start | bytes 1114112 | tf_op jit(solution)/shard_map/all_to_all | solution.py:356
  81.6 2.6 %gate.1 = (bf16[8,128,256]{2,1,0:T(8,128)(2,1)S(1)}, bf16[128,512]{1,0:T(8,128)(2,1)S(1)}, bf16[128,512]{1,0:T(8,128)(2,1)S(1)}, bf16[128,512]{1,0:T(8,128)(2,1)S(1)}, bf16[128,512]{1,0:T(8,128)(2,1)S(1)}) custom-call(s32[1]{0:T(128)} %bitcast.5.refs_0_, s32[1]{0:T(128)} %bitcast.refs_0_.refs_1_, bf16[8,128,256]{2,1,0:T(8,128)(2,1)S(1)} %copy-done.1, ...), custom_call_target="tpu_custom_call" | custom-call | tf_op jit(solution)/shard_map/gate/pallas_call | solution.py:67
  84.2 2.2 %collective-permute-start.14 = (bf16[128,512]{1,0:T(8,128)(2,1)S(1)}, bf16[128,512]{1,0:T(8,128)(2,1)S(1)}, u32[]{:S(2)}, u32[]{:S(2)}) collective-permute-start(bf16[128,512]{1,0:T(8,128)(2,1)S(1)} %get-tuple-element.65), channel_id=1, source_target_pairs={{0,24},{8,16},{16,8},{24,0},{1,25},{9,17},{17,9},{25,1},{2,26},{10... | collective-permute-start | bytes 393224 | tf_op jit(solution)/shard_map/ppermute | solution.py:22
  87.0 0.8 collective-permute-start.12
  87.8 1.5 collective-permute-start.15
  89.3 1.1 constant_dynamic-update-slice_fusion.3
  90.5 1.1 constant_dynamic-update-slice_fusion
  91.6 2.3 %collective-permute-done.13 = bf16[128,512]{1,0:T(8,128)(2,1)S(1)} collective-permute-done((bf16[128,512]{1,0:T(8,128)(2,1)S(1)}, bf16[128,512]{1,0:T(8,128)(2,1)S(1)}, u32[]{:S(2)}, u32[]{:S(2)}) %collective-permute-start.13) | collective-permute-done | bytes 131104 | tf_op jit(solution)/shard_map/ppermute | solution.py:22
  94.0 3.7 %all-to-all-done.2.refs_5_ = bf16[8,130,256]{2,1,0:T(8,128)(2,1)} async-done(((bf16[8,130,256]{2,1,0:T(8,128)(2,1)}), bf16[8,130,256]{2,1,0:T(8,128)(2,1)}, u32[]{:S(2)}, u32[]{:S(2)}) %all-to-all-start.2) | async-done | bytes 532512 | tf_op jit(solution)/shard_map/all_to_all | solution.py:356
  97.7 3.3 %convolution_convert_fusion = bf16[256,2048]{1,0:T(8,128)(2,1)} fusion(bf16[512,2048]{1,0:T(8,128)(2,1)} %copy-done.7, bf16[512,512]{1,0:T(8,128)(2,1)S(1)} %pad_maximum_fusion, s32[]{:T(128)S(6)} %select_n.66), kind=kOutput, calls=%fused_computation.2 | convolution fusion | flops 537395200 | bytes 3407876 | tf_op jit(solution)/shard_map/dot_general | solution.py:187
  101.1 3.0 %collective-permute-done.16 = bf16[256,2048]{1,0:T(8,128)(2,1)} collective-permute-done((bf16[256,2048]{1,0:T(8,128)(2,1)}, bf16[256,2048]{1,0:T(8,128)(2,1)}, u32[]{:S(2)}, u32[]{:S(2)}) %collective-permute-start.16) | collective-permute-done | bytes 1048608 | tf_op jit(solution)/shard_map/ppermute | solution.py:22
  104.0 2.6 %fusion = bf16[256,2048]{1,0:T(8,128)(2,1)S(1)} fusion(bf16[512,256]{1,0:T(8,128)(2,1)S(1)} %constant_dynamic-slice_fusion, bf16[512,2048]{1,0:T(8,128)(2,1)} %copy-done.7, bf16[256,2048]{1,0:T(8,128)(2,1)} %collective-permute-done.16), kind=kOutput, calls=%fused_computation.1 | convolution fusion | flops 538443776 | bytes 4456448 | tf_op jit(solution)/shard_map/dot_general | solution.py:187
  106.6 5.8 %stream_grads.1 = (bf16[128,6144]{1,0:T(8,128)(2,1)}, f32[4,6144]{1,0:T(4,128)}) custom-call(bf16[128,6144]{1,0:T(8,128)(2,1)} %refs_0_.3, bf16[2,6144]{1,0:T(2,128)(2,1)} %copy-done.14, f32[3,6144]{1,0:T(4,128)} %refs_2_.3, bf16[8,128,256]{2,1,0:T(8,128)(2,1)} %copy-done.2, bf16[8,128,256]{2,1,0:T(8,128)(2,1)} %copy-done.3, ...), custom_call_target="tpu_custom_call" | custom-call | tf_op jit(solution)/shard_map/stream_grads/pallas_call | solution.py:67
  112.5 1.3 collective-permute-start.18
  113.7 1.4 collective-permute-start.19
  115.2 0.8 collective-permute-start.17
  116.2 1.7 %collective-permute-start.22 = (bf16[64,2048]{1,0:T(8,128)(2,1)S(1)}, bf16[64,2048]{1,0:T(8,128)(2,1)S(1)}, u32[]{:S(2)}, u32[]{:S(2)}) collective-permute-start(bf16[64,2048]{1,0:T(8,128)(2,1)S(1)} %get-tuple-element.83), channel_id=1, source_target_pairs={{0,4},{1,5},{2,6},{3,7},{4,0},{5,1},{6,2},{7,3},{8,12},{9,13},{10,... | collective-permute-start | bytes 786440 | tf_op jit(solution)/shard_map/ppermute | solution.py:22
  118.0 1.0 collective-permute-done.18
  118.9 1.6 %collective-permute-start.23 = (bf16[64,2048]{1,0:T(8,128)(2,1)S(1)}, bf16[64,2048]{1,0:T(8,128)(2,1)S(1)}, u32[]{:S(2)}, u32[]{:S(2)}) collective-permute-start(bf16[64,2048]{1,0:T(8,128)(2,1)S(1)} %get-tuple-element.82), channel_id=1, source_target_pairs={{0,6},{1,7},{2,4},{3,5},{4,2},{5,3},{6,0},{7,1},{8,14},{9,15},{10,... | collective-permute-start | bytes 786440 | tf_op jit(solution)/shard_map/ppermute | solution.py:22
  120.9 0.9 add_add_fusion
  122.0 2.1 %collective-permute-start.29 = (bf16[256,256]{1,0:T(8,128)(2,1)S(1)}, bf16[256,256]{1,0:T(8,128)(2,1)S(1)}, u32[]{:S(2)}, u32[]{:S(2)}) collective-permute-start(bf16[256,256]{1,0:T(8,128)(2,1)S(1)} %get-tuple-element.80), channel_id=1, source_target_pairs={{0,24},{8,16},{16,8},{24,0},{1,25},{9,17},{17,9},{25,1},{2,26},{10... | collective-permute-start | bytes 393224 | tf_op jit(solution)/shard_map/ppermute | solution.py:22
  125.3 3.7 %collective-permute-done.29 = bf16[256,256]{1,0:T(8,128)(2,1)S(1)} collective-permute-done((bf16[256,256]{1,0:T(8,128)(2,1)S(1)}, bf16[256,256]{1,0:T(8,128)(2,1)S(1)}, u32[]{:S(2)}, u32[]{:S(2)}) %collective-permute-start.29) | collective-permute-done | bytes 131104 | tf_op jit(solution)/shard_map/ppermute | solution.py:22
  128.9 1.2 collective-permute-start.27
  130.2 1.5 collective-permute-done.28
  131.7 2.3 %collective-permute-done.27 = bf16[256,256]{1,0:T(8,128)(2,1)S(1)} collective-permute-done((bf16[256,256]{1,0:T(8,128)(2,1)S(1)}, bf16[256,256]{1,0:T(8,128)(2,1)S(1)}, u32[]{:S(2)}, u32[]{:S(2)}) %collective-permute-start.27) | collective-permute-done | bytes 131104 | tf_op jit(solution)/shard_map/ppermute | solution.py:22
  133.9 0.8 add_multiply_fusion
  134.7 2.9 %collective-permute-done.22 = bf16[64,2048]{1,0:T(8,128)(2,1)S(1)} collective-permute-done((bf16[64,2048]{1,0:T(8,128)(2,1)S(1)}, bf16[64,2048]{1,0:T(8,128)(2,1)S(1)}, u32[]{:S(2)}, u32[]{:S(2)}) %collective-permute-start.22) | collective-permute-done | bytes 262176 | tf_op jit(solution)/shard_map/ppermute | solution.py:22
  137.6 4.4 %collective-permute-start.25 = (f32[3,6144]{1,0:T(4,128)S(1)}, f32[3,6144]{1,0:T(4,128)S(1)}, u32[]{:S(2)}, u32[]{:S(2)}) collective-permute-start(f32[3,6144]{1,0:T(4,128)S(1)} %slice_add_fusion), channel_id=1, source_target_pairs={{0,4},{1,5},{2,6},{3,7},{4,0},{5,1},{6,2},{7,3},{8,12},{9,13},{10,... | collective-permute-start | bytes 221192 | tf_op jit(solution)/shard_map/ppermute | solution.py:22
  142.0 2.6 %collective-permute-start.26 = (f32[3,6144]{1,0:T(4,128)S(1)}, f32[3,6144]{1,0:T(4,128)S(1)}, u32[]{:S(2)}, u32[]{:S(2)}) collective-permute-start(f32[3,6144]{1,0:T(4,128)S(1)} %slice_add_fusion), channel_id=1, source_target_pairs={{0,6},{1,7},{2,4},{3,5},{4,2},{5,3},{6,0},{7,1},{8,14},{9,15},{10,... | collective-permute-start | bytes 221192 | tf_op jit(solution)/shard_map/ppermute | solution.py:22
  144.6 0.9 fusion.7
  145.6 3.4 %collective-permute-done.25 = f32[3,6144]{1,0:T(4,128)S(1)} collective-permute-done((f32[3,6144]{1,0:T(4,128)S(1)}, f32[3,6144]{1,0:T(4,128)S(1)}, u32[]{:S(2)}, u32[]{:S(2)}) %collective-permute-start.25) | collective-permute-done | bytes 73760 | tf_op jit(solution)/shard_map/ppermute | solution.py:22
  149.0 1.0 collective-permute-done.24
  150.0 0.7 add_multiply_fusion.1
  (70 shorter events, 5.1 us)
Async XLA Ops:
  0.6 22.5 %copy-start = (bf16[512,2048]{1,0:T(8,128)(2,1)S(1)}, bf16[512,2048]{1,0:T(8,128)(2,1)}, u32[]{:S(2)}) copy-start(bf16[512,2048]{1,0:T(8,128)(2,1)} %param.11) | copy-start | bytes 6291460
  0.6 22.5 %collective-permute-start.1 = (bf16[128,2048]{1,0:T(8,128)(2,1)}, bf16[128,2048]{1,0:T(8,128)(2,1)S(1)}, u32[]{:S(2)}, u32[]{:S(2)}) collective-permute-start(bf16[128,2048]{1,0:T(8,128)(2,1)} %param.12), channel_id=1, source_target_pairs={{0,8},{8,0},{16,24},{24,16},{1,9},{9,1},{17,25},{25,17},{2,10},{10... | collective-permute-start | bytes 1572872 | tf_op jit(solution)/shard_map/ppermute | solution.py:22
  3.6 24.8 %collective-permute-start.3 = (bf16[128,2048]{1,0:T(8,128)(2,1)}, bf16[128,2048]{1,0:T(8,128)(2,1)S(1)}, u32[]{:S(2)}, u32[]{:S(2)}) collective-permute-start(bf16[128,2048]{1,0:T(8,128)(2,1)} %param.12), channel_id=1, source_target_pairs={{0,16},{8,24},{16,0},{24,8},{1,17},{9,25},{17,1},{25,9},{2,18},{10... | collective-permute-start | bytes 1572872 | tf_op jit(solution)/shard_map/ppermute | solution.py:22
  6.1 7.2 %collective-permute-start = (bf16[2,6144]{1,0:T(2,128)(2,1)S(1)}, bf16[2,6144]{1,0:T(2,128)(2,1)S(1)}, u32[]{:S(2)}, u32[]{:S(2)}) collective-permute-start(bf16[2,6144]{1,0:T(2,128)(2,1)S(1)} %slice.22), channel_id=1, source_target_pairs={{0,1},{1,2},{2,3},{3,4},{4,5},{5,6},{6,7},{8,9},{9,10},{10,11},{11... | collective-permute-start | bytes 73736 | tf_op jit(solution)/shard_map/ppermute | solution.py:18
  7.4 24.1 %collective-permute-start.5 = (bf16[128,2048]{1,0:T(8,128)(2,1)}, bf16[128,2048]{1,0:T(8,128)(2,1)}, u32[]{:S(2)}, u32[]{:S(2)}) collective-permute-start(bf16[128,2048]{1,0:T(8,128)(2,1)} %param.12), channel_id=1, source_target_pairs={{0,24},{8,16},{16,8},{24,0},{1,25},{9,17},{17,9},{25,1},{2,26},{10... | collective-permute-start | bytes 1572872 | tf_op jit(solution)/shard_map/ppermute | solution.py:22
  13.3 0.6 copy-start.14
  17.5 25.2 %all-to-all-start = ((bf16[8,128,256]{2,1,0:T(8,128)(2,1)}), bf16[8,128,256]{2,1,0:T(8,128)(2,1)}, u32[]{:S(2)}, u32[]{:S(2)}) async-start(bf16[8,128,256]{2,1,0:T(8,128)(2,1)} %get-tuple-element.45), calls=%async_computation | async-start | bytes 1048576 | tf_op jit(solution)/shard_map/all_to_all | solution.py:351
  23.2 6.8 %copy-start.9 = (bf16[128,2048]{1,0:T(8,128)(2,1)}, bf16[128,2048]{1,0:T(8,128)(2,1)S(1)}, u32[]{:S(2)}) copy-start(bf16[128,2048]{1,0:T(8,128)(2,1)S(1)} %collective-permute-done.1) | copy-start | bytes 1572868
  24.7 8.8 %copy-start.8 = (bf16[128,2048]{1,0:T(8,128)(2,1)S(1)}, bf16[128,2048]{1,0:T(8,128)(2,1)}, u32[]{:S(2)}) copy-start(bf16[128,2048]{1,0:T(8,128)(2,1)} %param.12) | copy-start | bytes 1572868
  24.7 13.1 %collective-permute-start.2 = (bf16[128,512]{1,0:T(8,128)(2,1)}, bf16[128,512]{1,0:T(8,128)(2,1)S(1)}, u32[]{:S(2)}, u32[]{:S(2)}) collective-permute-start(bf16[128,512]{1,0:T(8,128)(2,1)} %fusion.2), channel_id=1, source_target_pairs={{0,8},{8,0},{16,24},{24,16},{1,9},{9,1},{17,25},{25,17},{2,10},{10... | collective-permute-start | bytes 393224 | tf_op jit(solution)/shard_map/ppermute | solution.py:22
  28.5 3.0 %copy-start.11 = (bf16[128,2048]{1,0:T(8,128)(2,1)}, bf16[128,2048]{1,0:T(8,128)(2,1)S(1)}, u32[]{:S(2)}) copy-start(bf16[128,2048]{1,0:T(8,128)(2,1)S(1)} %collective-permute-done.3) | copy-start | bytes 1572868
  30.0 7.8 %collective-permute-start.4 = (bf16[128,512]{1,0:T(8,128)(2,1)}, bf16[128,512]{1,0:T(8,128)(2,1)S(1)}, u32[]{:S(2)}, u32[]{:S(2)}) collective-permute-start(bf16[128,512]{1,0:T(8,128)(2,1)} %fusion.3), channel_id=1, source_target_pairs={{0,16},{8,24},{16,0},{24,8},{1,17},{9,25},{17,1},{25,9},{2,18},{10... | collective-permute-start | bytes 393224 | tf_op jit(solution)/shard_map/ppermute | solution.py:22
  33.4 6.6 %copy-start.1 = (bf16[8,128,256]{2,1,0:T(8,128)(2,1)S(1)}, bf16[8,128,256]{2,1,0:T(8,128)(2,1)}, u32[]{:S(2)}) copy-start(bf16[8,128,256]{2,1,0:T(8,128)(2,1)} %get-tuple-element.42.refs_1_.refs_2_) | copy-start | bytes 1572868
  33.4 5.9 %collective-permute-start.6 = (bf16[128,512]{1,0:T(8,128)(2,1)S(1)}, bf16[128,512]{1,0:T(8,128)(2,1)S(1)}, u32[]{:S(2)}, u32[]{:S(2)}) collective-permute-start(bf16[128,512]{1,0:T(8,128)(2,1)S(1)} %fusion.4), channel_id=1, source_target_pairs={{0,24},{8,16},{16,8},{24,0},{1,25},{9,17},{17,9},{25,1},{2,26},{10... | collective-permute-start | bytes 393224 | tf_op jit(solution)/shard_map/ppermute | solution.py:22
  36.5 6.2 %collective-permute-start.11 = (bf16[2,8,2,256]{3,2,1,0:T(2,128)(2,1)}, bf16[2,8,2,256]{3,2,1,0:T(2,128)(2,1)S(1)}, u32[]{:S(2)}, u32[]{:S(2)}) collective-permute-start(bf16[2,8,2,256]{3,2,1,0:T(2,128)(2,1)} %pad_maximum_fusion.1), channel_id=1, source_target_pairs={{1,0},{2,1},{3,2},{4,3},{5,4},{6,5},{7,6},{9,8},{10,9},{11,10},{12... | collective-permute-start | bytes 49160 | tf_op jit(solution)/shard_map/ppermute | solution.py:18
  39.3 0.7 copy-start.5
  40.0 0.9 copy-start.6
  41.9 0.8 copy-start.4
  42.7 45.1 %copy-start.2 = (bf16[8,128,256]{2,1,0:T(8,128)(2,1)}, bf16[8,128,256]{2,1,0:T(8,128)(2,1)S(1)}, u32[]{:S(2)}) copy-start(bf16[8,128,256]{2,1,0:T(8,128)(2,1)S(1)} %get-tuple-element.44.refs_3_) | copy-start | bytes 1572868
  42.7 12.3 %copy-start.15 = (bf16[2,8,2,256]{3,2,1,0:T(2,128)(2,1)}, bf16[2,8,2,256]{3,2,1,0:T(2,128)(2,1)S(1)}, u32[]{:S(2)}) copy-start(bf16[2,8,2,256]{3,2,1,0:T(2,128)(2,1)S(1)} %collective-permute-done.11.refs_9_) | copy-start | bytes 49156
  42.7 25.6 %all-to-all-start.1 = ((bf16[8,128,256]{2,1,0:T(8,128)(2,1)}), bf16[8,128,256]{2,1,0:T(8,128)(2,1)}, u32[]{:S(2)}, u32[]{:S(2)}) async-start(bf16[8,128,256]{2,1,0:T(8,128)(2,1)} %copy-done.4), calls=%async_computation.1 | async-start | bytes 1048576 | tf_op jit(solution)/shard_map/all_to_all | solution.py:351
  56.8 2.0 %collective-permute-start.7 = (bf16[4,128,256]{2,1,0:T(8,128)(2,1)}, bf16[4,128,256]{2,1,0:T(8,128)(2,1)}, u32[]{:S(2)}, u32[]{:S(2)}) collective-permute-start(bf16[4,128,256]{2,1,0:T(8,128)(2,1)} %get-tuple-element.89), channel_id=1, source_target_pairs={{0,1},{1,0},{2,3},{3,2},{4,5},{5,4},{6,7},{7,6},{8,9},{9,8},{10,11... | collective-permute-start | bytes 786440 | tf_op jit(solution)/shard_map/ppermute | solution.py:22
  60.5 7.9 %collective-permute-start.8 = (bf16[2,128,256]{2,1,0:T(8,128)(2,1)}, bf16[2,128,256]{2,1,0:T(8,128)(2,1)S(1)}, u32[]{:S(2)}, u32[]{:S(2)}) collective-permute-start(bf16[2,128,256]{2,1,0:T(8,128)(2,1)} %get-tuple-element.87), channel_id=1, source_target_pairs={{0,2},{1,3},{2,0},{3,1},{4,6},{5,7},{6,4},{7,5},{8,10},{9,11},{10,... | collective-permute-start | bytes 393224 | tf_op jit(solution)/shard_map/ppermute | solution.py:22
  62.3 19.2 %collective-permute-start.9 = (bf16[2,128,256]{2,1,0:T(8,128)(2,1)}, bf16[2,128,256]{2,1,0:T(8,128)(2,1)S(1)}, u32[]{:S(2)}, u32[]{:S(2)}) collective-permute-start(bf16[2,128,256]{2,1,0:T(8,128)(2,1)} %get-tuple-element.88), channel_id=1, source_target_pairs={{0,4},{1,5},{2,6},{3,7},{4,0},{5,1},{6,2},{7,3},{8,12},{9,13},{10,... | collective-permute-start | bytes 393224 | tf_op jit(solution)/shard_map/ppermute | solution.py:22
  64.7 16.9 %collective-permute-start.10 = (bf16[2,128,256]{2,1,0:T(8,128)(2,1)}, bf16[2,128,256]{2,1,0:T(8,128)(2,1)}, u32[]{:S(2)}, u32[]{:S(2)}) collective-permute-start(bf16[2,128,256]{2,1,0:T(8,128)(2,1)} %get-tuple-element.85), channel_id=1, source_target_pairs={{0,6},{1,7},{2,4},{3,5},{4,2},{5,3},{6,0},{7,1},{8,14},{9,15},{10,... | collective-permute-start | bytes 393224 | tf_op jit(solution)/shard_map/ppermute | solution.py:22
  77.1 20.6 %all-to-all-start.2 = ((bf16[8,130,256]{2,1,0:T(8,128)(2,1)}), bf16[8,130,256]{2,1,0:T(8,128)(2,1)}, u32[]{:S(2)}, u32[]{:S(2)}) async-start(bf16[8,130,256]{2,1,0:T(8,128)(2,1)} %get-tuple-element.56), calls=%async_computation.2 | async-start | bytes 1114112 | tf_op jit(solution)/shard_map/all_to_all | solution.py:356
  81.6 8.8 %copy-start.10 = (bf16[128,2048]{1,0:T(8,128)(2,1)S(1)}, bf16[128,2048]{1,0:T(8,128)(2,1)}, u32[]{:S(2)}) copy-start(bf16[128,2048]{1,0:T(8,128)(2,1)} %copy-done.9) | copy-start | bytes 1572868
  81.6 8.9 %copy-start.12 = (bf16[128,2048]{1,0:T(8,128)(2,1)S(1)}, bf16[128,2048]{1,0:T(8,128)(2,1)}, u32[]{:S(2)}) copy-start(bf16[128,2048]{1,0:T(8,128)(2,1)} %copy-done.11) | copy-start | bytes 1572868
  84.2 3.6 %copy-start.3 = (bf16[8,128,256]{2,1,0:T(8,128)(2,1)}, bf16[8,128,256]{2,1,0:T(8,128)(2,1)S(1)}, u32[]{:S(2)}) copy-start(bf16[8,128,256]{2,1,0:T(8,128)(2,1)S(1)} %get-tuple-element.61.refs_4_) | copy-start | bytes 1572868
  84.2 7.4 %collective-permute-start.14 = (bf16[128,512]{1,0:T(8,128)(2,1)S(1)}, bf16[128,512]{1,0:T(8,128)(2,1)S(1)}, u32[]{:S(2)}, u32[]{:S(2)}) collective-permute-start(bf16[128,512]{1,0:T(8,128)(2,1)S(1)} %get-tuple-element.65), channel_id=1, source_target_pairs={{0,24},{8,16},{16,8},{24,0},{1,25},{9,17},{17,9},{25,1},{2,26},{10... | collective-permute-start | bytes 393224 | tf_op jit(solution)/shard_map/ppermute | solution.py:22
  86.4 7.5 %collective-permute-start.13 = (bf16[128,512]{1,0:T(8,128)(2,1)S(1)}, bf16[128,512]{1,0:T(8,128)(2,1)S(1)}, u32[]{:S(2)}, u32[]{:S(2)}) collective-permute-start(bf16[128,512]{1,0:T(8,128)(2,1)S(1)} %get-tuple-element.64), channel_id=1, source_target_pairs={{0,16},{8,24},{16,0},{24,8},{1,17},{9,25},{17,1},{25,9},{2,18},{10... | collective-permute-start | bytes 393224 | tf_op jit(solution)/shard_map/ppermute | solution.py:22
  87.0 7.0 %collective-permute-start.12 = (bf16[128,512]{1,0:T(8,128)(2,1)S(1)}, bf16[128,512]{1,0:T(8,128)(2,1)S(1)}, u32[]{:S(2)}, u32[]{:S(2)}) collective-permute-start(bf16[128,512]{1,0:T(8,128)(2,1)S(1)} %get-tuple-element.63), channel_id=1, source_target_pairs={{0,8},{8,0},{16,24},{24,16},{1,9},{9,1},{17,25},{25,17},{2,10},{10... | collective-permute-start | bytes 393224 | tf_op jit(solution)/shard_map/ppermute | solution.py:22
  87.8 6.1 %collective-permute-start.15 = (f32[8,2,256]{2,1,0:T(2,128)S(1)}, f32[8,2,256]{2,1,0:T(2,128)S(1)}, u32[]{:S(2)}, u32[]{:S(2)}) collective-permute-start(f32[8,2,256]{2,1,0:T(2,128)S(1)} %convert_multiply_fusion), channel_id=1, source_target_pairs={{1,0},{2,1},{3,2},{4,3},{5,4},{6,5},{7,6},{9,8},{10,9},{11,10},{12... | collective-permute-start | bytes 49160 | tf_op jit(solution)/shard_map/ppermute | solution.py:18
  91.6 2.4 %copy-start.7 = (bf16[512,2048]{1,0:T(8,128)(2,1)}, bf16[512,2048]{1,0:T(8,128)(2,1)S(1)}, u32[]{:S(2)}) copy-start(bf16[512,2048]{1,0:T(8,128)(2,1)S(1)} %constant_dynamic-update-slice_fusion) | copy-start | bytes 6291460
  94.0 12.7 %copy-start.16 = (f32[8,2,256]{2,1,0:T(2,128)}, f32[8,2,256]{2,1,0:T(2,128)S(1)}, u32[]{:S(2)}) copy-start(f32[8,2,256]{2,1,0:T(2,128)S(1)} %collective-permute-done.15.refs_8_) | copy-start | bytes 49156
  101.0 3.0 %collective-permute-start.16 = (bf16[256,2048]{1,0:T(8,128)(2,1)}, bf16[256,2048]{1,0:T(8,128)(2,1)}, u32[]{:S(2)}, u32[]{:S(2)}) collective-permute-start(bf16[256,2048]{1,0:T(8,128)(2,1)} %convolution_convert_fusion), channel_id=1, source_target_pairs={{0,1},{1,0},{2,3},{3,2},{4,5},{5,4},{6,7},{7,6},{8,9},{9,8},{10,11... | collective-permute-start | bytes 3145736 | tf_op jit(solution)/shard_map/ppermute | solution.py:22
  112.4 9.5 %copy-start.13 = (f32[256,1024]{1,0:T(8,128)S(1)}, f32[256,1024]{1,0:T(8,128)}, u32[]{:S(2)}) copy-start(f32[256,1024]{1,0:T(8,128)} %get-tuple-element.78) | copy-start | bytes 3145732
  112.5 6.5 %collective-permute-start.18 = (f32[4,6144]{1,0:T(4,128)}, f32[4,6144]{1,0:T(4,128)S(1)}, u32[]{:S(2)}, u32[]{:S(2)}) collective-permute-start(f32[4,6144]{1,0:T(4,128)} %get-tuple-element.75), channel_id=1, source_target_pairs={{0,16},{8,24},{16,0},{24,8},{1,17},{9,25},{17,1},{25,9},{2,18},{10... | collective-permute-start | bytes 294920 | tf_op jit(solution)/shard_map/ppermute | solution.py:22
  113.7 6.8 %collective-permute-start.19 = (f32[4,6144]{1,0:T(4,128)}, f32[4,6144]{1,0:T(4,128)S(1)}, u32[]{:S(2)}, u32[]{:S(2)}) collective-permute-start(f32[4,6144]{1,0:T(4,128)} %get-tuple-element.75), channel_id=1, source_target_pairs={{0,24},{8,16},{16,8},{24,0},{1,25},{9,17},{17,9},{25,1},{2,26},{10... | collective-permute-start | bytes 294920 | tf_op jit(solution)/shard_map/ppermute | solution.py:22
  115.2 5.7 %collective-permute-start.17 = (f32[4,6144]{1,0:T(4,128)}, f32[4,6144]{1,0:T(4,128)S(1)}, u32[]{:S(2)}, u32[]{:S(2)}) collective-permute-start(f32[4,6144]{1,0:T(4,128)} %get-tuple-element.75), channel_id=1, source_target_pairs={{0,8},{8,0},{16,24},{24,16},{1,9},{9,1},{17,25},{25,17},{2,10},{10... | collective-permute-start | bytes 294920 | tf_op jit(solution)/shard_map/ppermute | solution.py:22
  116.1 18.6 %collective-permute-start.21 = (bf16[64,2048]{1,0:T(8,128)(2,1)S(1)}, bf16[64,2048]{1,0:T(8,128)(2,1)S(1)}, u32[]{:S(2)}, u32[]{:S(2)}) collective-permute-start(bf16[64,2048]{1,0:T(8,128)(2,1)S(1)} %get-tuple-element.84), channel_id=1, source_target_pairs={{0,2},{1,3},{2,0},{3,1},{4,6},{5,7},{6,4},{7,5},{8,10},{9,11},{10,... | collective-permute-start | bytes 786440 | tf_op jit(solution)/shard_map/ppermute | solution.py:22
  116.2 21.4 %collective-permute-start.22 = (bf16[64,2048]{1,0:T(8,128)(2,1)S(1)}, bf16[64,2048]{1,0:T(8,128)(2,1)S(1)}, u32[]{:S(2)}, u32[]{:S(2)}) collective-permute-start(bf16[64,2048]{1,0:T(8,128)(2,1)S(1)} %get-tuple-element.83), channel_id=1, source_target_pairs={{0,4},{1,5},{2,6},{3,7},{4,0},{5,1},{6,2},{7,3},{8,12},{9,13},{10,... | collective-permute-start | bytes 786440 | tf_op jit(solution)/shard_map/ppermute | solution.py:22
  118.9 18.7 %collective-permute-start.23 = (bf16[64,2048]{1,0:T(8,128)(2,1)S(1)}, bf16[64,2048]{1,0:T(8,128)(2,1)S(1)}, u32[]{:S(2)}, u32[]{:S(2)}) collective-permute-start(bf16[64,2048]{1,0:T(8,128)(2,1)S(1)} %get-tuple-element.82), channel_id=1, source_target_pairs={{0,6},{1,7},{2,4},{3,5},{4,2},{5,3},{6,0},{7,1},{8,14},{9,15},{10,... | collective-permute-start | bytes 786440 | tf_op jit(solution)/shard_map/ppermute | solution.py:22
  121.8 2.9 %collective-permute-start.20 = (f32[3,6144]{1,0:T(4,128)S(1)}, f32[3,6144]{1,0:T(4,128)S(1)}, u32[]{:S(2)}, u32[]{:S(2)}) collective-permute-start(f32[3,6144]{1,0:T(4,128)S(1)} %bitcast.53), channel_id=1, source_target_pairs={{0,1},{1,0},{2,3},{3,2},{4,5},{5,4},{6,7},{7,6},{8,9},{9,8},{10,11... | collective-permute-start | bytes 221192 | tf_op jit(solution)/shard_map/ppermute | solution.py:22
  122.0 6.9 %collective-permute-start.29 = (bf16[256,256]{1,0:T(8,128)(2,1)S(1)}, bf16[256,256]{1,0:T(8,128)(2,1)S(1)}, u32[]{:S(2)}, u32[]{:S(2)}) collective-permute-start(bf16[256,256]{1,0:T(8,128)(2,1)S(1)} %get-tuple-element.80), channel_id=1, source_target_pairs={{0,24},{8,16},{16,8},{24,0},{1,25},{9,17},{17,9},{25,1},{2,26},{10... | collective-permute-start | bytes 393224 | tf_op jit(solution)/shard_map/ppermute | solution.py:22
  124.7 6.9 %collective-permute-start.28 = (bf16[256,256]{1,0:T(8,128)(2,1)S(1)}, bf16[256,256]{1,0:T(8,128)(2,1)S(1)}, u32[]{:S(2)}, u32[]{:S(2)}) collective-permute-start(bf16[256,256]{1,0:T(8,128)(2,1)S(1)} %get-tuple-element.81), channel_id=1, source_target_pairs={{0,16},{8,24},{16,0},{24,8},{1,17},{9,25},{17,1},{25,9},{2,18},{10... | collective-permute-start | bytes 393224 | tf_op jit(solution)/shard_map/ppermute | solution.py:22
  128.9 5.0 %collective-permute-start.27 = (bf16[256,256]{1,0:T(8,128)(2,1)S(1)}, bf16[256,256]{1,0:T(8,128)(2,1)S(1)}, u32[]{:S(2)}, u32[]{:S(2)}) collective-permute-start(bf16[256,256]{1,0:T(8,128)(2,1)S(1)} %get-tuple-element.79), channel_id=1, source_target_pairs={{0,8},{8,0},{16,24},{24,16},{1,9},{9,1},{17,25},{25,17},{2,10},{10... | collective-permute-start | bytes 393224 | tf_op jit(solution)/shard_map/ppermute | solution.py:22
  137.6 11.4 %collective-permute-start.25 = (f32[3,6144]{1,0:T(4,128)S(1)}, f32[3,6144]{1,0:T(4,128)S(1)}, u32[]{:S(2)}, u32[]{:S(2)}) collective-permute-start(f32[3,6144]{1,0:T(4,128)S(1)} %slice_add_fusion), channel_id=1, source_target_pairs={{0,4},{1,5},{2,6},{3,7},{4,0},{5,1},{6,2},{7,3},{8,12},{9,13},{10,... | collective-permute-start | bytes 221192 | tf_op jit(solution)/shard_map/ppermute | solution.py:22
  142.0 7.0 %collective-permute-start.26 = (f32[3,6144]{1,0:T(4,128)S(1)}, f32[3,6144]{1,0:T(4,128)S(1)}, u32[]{:S(2)}, u32[]{:S(2)}) collective-permute-start(f32[3,6144]{1,0:T(4,128)S(1)} %slice_add_fusion), channel_id=1, source_target_pairs={{0,6},{1,7},{2,4},{3,5},{4,2},{5,3},{6,0},{7,1},{8,14},{9,15},{10,... | collective-permute-start | bytes 221192 | tf_op jit(solution)/shard_map/ppermute | solution.py:22
  144.6 5.3 %collective-permute-start.24 = (f32[3,6144]{1,0:T(4,128)S(1)}, f32[3,6144]{1,0:T(4,128)S(1)}, u32[]{:S(2)}, u32[]{:S(2)}) collective-permute-start(f32[3,6144]{1,0:T(4,128)S(1)} %slice_add_fusion), channel_id=1, source_target_pairs={{0,2},{1,3},{2,0},{3,1},{4,6},{5,7},{6,4},{7,5},{8,10},{9,11},{10,... | collective-permute-start | bytes 221192 | tf_op jit(solution)/shard_map/ppermute | solution.py:22
